TPU v7x, 32 devices: a whole 2x2x4 slice. The times are simulated.
32 devices in a mesh: dp: 8 (over y, x, core), tensor: 4 (over z).
Axes of the slice: x: 2, y: 2, z: 4, core: 2. Of those that a mesh axis runs over, the one named last changes fastest.
Arguments:
- tokens: bfloat16 [4096, 2048], P('dp'), may hold values from -6 to 6
- seq_ids: int32 [4096], replicated, may hold values from 0 to 3, never falling along the last dimension, each value on 1 to 2048 neighbouring positions
- route_ids: int32 [4096, 6], P('dp'), may hold values from 0 to 63, all different within a row; in each aligned block of 512 rows (0 to 511, 512 to 1023, ...) at most 72 rows name the same one
- cotangent: bfloat16 [4096, 2048], P('dp'), may hold values from -6 to 6
- input_gain: float32 [2048], replicated, may hold values from 0.5 to 1.5
- w_query: bfloat16 [2048, 3072], P(None, 'tensor'), may hold values from -0.125 to 0.125
- w_latent: bfloat16 [2048, 576], replicated, may hold values from -0.125 to 0.125
- latent_gain: float32 [512], replicated, may hold values from 0.5 to 1.5
- w_expand: bfloat16 [512, 4096], P(None, 'tensor'), may hold values from -0.25 to 0.25
- w_out: bfloat16 [2048, 2048], P('tensor'), may hold values from -0.5 to 0.5
- middle_gain: float32 [2048], replicated, may hold values from 0.5 to 1.5
- w_router: bfloat16 [2048, 64], replicated, may hold values from -0.0390625 to 0.0390625
- expert_gate: bfloat16 [64, 2048, 1408], P('dp', None, 'tensor'), may hold values from -0.125 to 0.125
- expert_up: bfloat16 [64, 2048, 1408], P('dp', None, 'tensor'), may hold values from -0.125 to 0.125
- expert_down: bfloat16 [64, 1408, 2048], P('dp', 'tensor'), may hold values from -2.5 to 2.5
- shared_gate: bfloat16 [2048, 2816], P(None, 'tensor'), may hold values from -0.125 to 0.125
- shared_up: bfloat16 [2048, 2816], P(None, 'tensor'), may hold values from -0.125 to 0.125
- shared_down: bfloat16 [2816, 2048], P('tensor'), may hold values from -0.21875 to 0.21875
Outputs:
- output: bfloat16 [4096, 2048], P('dp')
- token_grad: bfloat16 [4096, 2048], P('dp')
- grad_input_gain: float32 [2048], P('dp')
- grad_query: float32 [2048, 3072], P('dp', 'tensor')
- grad_latent: float32 [2048, 576], P('dp')
- grad_latent_gain: float32 [512], P('dp')
- grad_expand: float32 [512, 4096], P('dp', 'tensor')
- grad_out_proj: float32 [2048, 2048], P('tensor', 'dp')
- grad_middle_gain: float32 [2048], P('dp')
- grad_router: float32 [2048, 64], P('dp')
- grad_expert_gate: float32 [64, 2048, 1408], P('dp', None, 'tensor')
- grad_expert_up: float32 [64, 2048, 1408], P('dp', None, 'tensor')
- grad_expert_down: float32 [64, 1408, 2048], P('dp', 'tensor')
- grad_shared_gate: float32 [2048, 2816], P('dp', 'tensor')
- grad_shared_up: float32 [2048, 2816], P('dp', 'tensor')
- grad_shared_down: float32 [2816, 2048], P('tensor', 'dp')
Inputs may be any that keep to these rules, and one draw needn't show every extreme that they name: seq_ids never fall; each sequence has 1 to 2048 tokens, one has exactly 2048. `route_ids`: each row names 6 different experts; in the rows of one data block (512 tokens) no expert is named by more than 72 rows, a bound that some block reaches.
All inputs are finite; a program needn't handle non-finite values.
Results may differ from a plain program's by a relative error of at most 0.025.
Values may be sent and summed in bfloat16 or wider, within the bound.
No kernel may reach another device: no remote copies, remote signals or barrier semaphores. Data moves between devices by JAX's collectives and lax.ppermute only.
A program may use at most 448 MiB of HBM per device.

v0:
```python
import jax
import jax.numpy as jnp
from jax import lax
from jax.sharding import PartitionSpec as P

DN = 128
DR = 64
DV = 128
KVR = 512
ROUTED_EXPERTS = 64
TOP = 6
REACH = 4
CAP = 72


epsilon = 1e-06


def passed_along(shard, axis, by):
    peers = lax.axis_size(axis)
    pairs = [(i, i + by) for i in range(peers) if 0 <= i + by < peers]
    return lax.ppermute(shard, axis, pairs)


def normed(values, norm_gain):
    return (
        values * lax.rsqrt(jnp.mean(values * values, axis=-1, keepdims=True) + epsilon) * norm_gain
    )


def rotate(values, cosine, sine_table):
    half_width = values.shape[-1] // 2
    front_half = values[..., :half_width]
    back_half = values[..., half_width:]
    return jnp.concatenate(
        [
            front_half * cosine - back_half * sine_table,
            back_half * cosine + front_half * sine_table,
        ],
        axis=-1,
    )


def rotate_back(upstream, cosine, sine_table):

    def rotated(values):
        return rotate(values, cosine, sine_table)

    _, pullback = jax.vjp(rotated, upstream)
    return pullback(upstream)[0]


def silu_gate(gate_val, up_val):
    return gate_val * jax.nn.sigmoid(gate_val) * up_val


def silu_backward(gate_val, up_val, upstream):
    _, pullback = jax.vjp(silu_gate, gate_val, up_val)
    return pullback(upstream)


def norm_backward(values, norm_gain, upstream):
    _, pullback = jax.vjp(normed, values, norm_gain)
    return pullback(upstream)


def rope_tables(seq_all, seq_here, index_here):
    starts = jnp.searchsorted(seq_all, seq_here, side="left")
    position = (index_here - starts).astype(jnp.float32)
    frequency = 10000.0 ** (-(jnp.arange(DR // 2, dtype=jnp.float32) * 2.0) / DR)
    angle = position[:, None] * frequency[None, :]
    return (jnp.cos(angle), jnp.sin(angle))


def dispatch(buffer_rows, devices, row_width):
    arrived = lax.all_to_all(
        buffer_rows.reshape(devices, -1, row_width), "dp", split_axis=0, concat_axis=0, tiled=True
    )
    return arrived.reshape(devices, -1, CAP, row_width)


def send_back(results, devices):
    row_width = results.shape[-1]
    arrived = lax.all_to_all(
        results.reshape(devices, -1, row_width), "dp", split_axis=0, concat_axis=0, tiled=True
    )
    return arrived.reshape(-1, row_width)


def shards(
    tokens,
    seq_ids,
    route_ids,
    cotangent,
    input_gain,
    w_query,
    w_latent,
    latent_gain,
    w_expand,
    w_out,
    middle_gain,
    w_router,
    expert_gate,
    expert_up,
    expert_down,
    shared_gate,
    shared_up,
    shared_down,
):
    devices = lax.axis_size("dp")
    rank_dp = lax.axis_index("dp")
    tok_rows = tokens.shape[0]
    model_width = tokens.shape[1]
    heads_local = w_query.shape[1] // (DN + DR)
    reach_used = min(REACH, devices - 1)
    window = (reach_used + 1) * tok_rows
    scale = (DN + DR) ** (-0.5)
    index_here = rank_dp * tok_rows + jnp.arange(tok_rows, dtype=jnp.int32)
    seq_here = lax.dynamic_slice_in_dim(seq_ids, rank_dp * tok_rows, tok_rows, 0)
    cosine, sine_table = rope_tables(seq_ids, seq_here, index_here)
    key_index = (rank_dp - reach_used) * tok_rows + jnp.arange(window, dtype=jnp.int32)
    seq_keys = jnp.where(key_index >= 0, jnp.take(seq_ids, jnp.maximum(key_index, 0)), -1)
    allowed = (seq_here[:, None] == seq_keys[None, :]) & (key_index[None, :] <= index_here[:, None])
    token_features = tokens.astype(jnp.float32)
    grad_output = cotangent.astype(jnp.float32)
    hidden_in = normed(token_features, input_gain).astype(jnp.bfloat16)
    query_pre = jnp.dot(hidden_in, w_query, preferred_element_type=jnp.float32).reshape(
        tok_rows, heads_local, DN + DR
    )
    queries = jnp.concatenate(
        [
            query_pre[..., :DN],
            rotate(query_pre[..., DN:], cosine[:, None, :], sine_table[:, None, :]),
        ],
        axis=-1,
    ).astype(jnp.bfloat16)
    latent_full = jnp.dot(hidden_in, w_latent, preferred_element_type=jnp.float32)
    latent_raw = latent_full[:, :KVR]
    latent = normed(latent_raw, latent_gain).astype(jnp.bfloat16)
    rope_key = rotate(latent_full[:, KVR:], cosine, sine_table).astype(jnp.bfloat16)
    latent_list = []
    rope_list = []
    for steps_back in range(reach_used, 0, -1):
        latent_earlier, rope_earlier = passed_along((latent, rope_key), "dp", steps_back)
        latent_list.append(latent_earlier)
        rope_list.append(rope_earlier)
    latent_window = jnp.concatenate(latent_list + [latent], axis=0)
    rope_window = jnp.concatenate(rope_list + [rope_key], axis=0)
    expanded = (
        jnp.dot(latent_window, w_expand, preferred_element_type=jnp.float32)
        .astype(jnp.bfloat16)
        .reshape(window, heads_local, DN + DV)
    )
    key_nope = expanded[..., :DN]
    key_value = expanded[..., DN:]
    scores = jnp.einsum(
        "qhd,khd->hqk", queries[..., :DN], key_nope, preferred_element_type=jnp.float32
    ) + jnp.einsum(
        "qhd,kd->hqk", queries[..., DN:], rope_window, preferred_element_type=jnp.float32
    )
    scores = jnp.where(allowed[None], scores * scale, -1e30)
    probs = jax.nn.softmax(scores, axis=-1)
    probs_low = probs.astype(jnp.bfloat16)
    attended = (
        jnp.einsum("hqk,khd->qhd", probs_low, key_value, preferred_element_type=jnp.float32)
        .astype(jnp.bfloat16)
        .reshape(tok_rows, heads_local * DV)
    )
    attention = lax.psum(
        jnp.dot(attended, w_out, preferred_element_type=jnp.float32).astype(jnp.bfloat16), "tensor"
    ).astype(jnp.float32)
    middle = token_features + attention
    hidden_mid = normed(middle, middle_gain).astype(jnp.bfloat16)
    logits = jnp.dot(hidden_mid, w_router, preferred_element_type=jnp.float32)
    router_probs = jax.nn.softmax(logits, axis=-1)
    gates = jnp.take_along_axis(router_probs, route_ids, axis=1)
    flat_expert = route_ids.reshape(-1)
    onehot = (flat_expert[:, None] == jnp.arange(ROUTED_EXPERTS, dtype=jnp.int32)[None, :]).astype(
        jnp.int32
    )
    rank_within = jnp.sum((jnp.cumsum(onehot, axis=0) - onehot) * onehot, axis=1)
    slot_index = flat_expert * CAP + rank_within
    entries = tok_rows * TOP
    slot_source = (
        jnp.zeros((ROUTED_EXPERTS * CAP,), jnp.int32)
        .at[slot_index]
        .set(jnp.arange(entries, dtype=jnp.int32) + 1)
    )
    filled = slot_source > 0
    slot_entry = jnp.maximum(slot_source - 1, 0)
    slot_token = slot_entry // TOP
    send_rows = jnp.where(filled[:, None], hidden_mid[slot_token], jnp.zeros((), jnp.bfloat16))
    shared_gate_val = jnp.dot(hidden_mid, shared_gate, preferred_element_type=jnp.float32)
    shared_up_val = jnp.dot(hidden_mid, shared_up, preferred_element_type=jnp.float32)
    shared_active = silu_gate(shared_gate_val, shared_up_val).astype(jnp.bfloat16)
    shared_result = jnp.dot(shared_active, shared_down, preferred_element_type=jnp.float32)
    received = dispatch(send_rows, devices, model_width)
    gate_val = jnp.einsum(
        "secd,edf->secf", received, expert_gate, preferred_element_type=jnp.float32
    )
    up_val = jnp.einsum("secd,edf->secf", received, expert_up, preferred_element_type=jnp.float32)
    active = silu_gate(gate_val, up_val).astype(jnp.bfloat16)
    expert_result = jnp.einsum(
        "secf,efd->secd", active, expert_down, preferred_element_type=jnp.float32
    ).astype(jnp.bfloat16)
    returned = send_back(expert_result, devices)
    slot_result = returned[slot_index].reshape(tok_rows, TOP, model_width).astype(jnp.float32)
    routed = jnp.sum(slot_result * gates[:, :, None], axis=1)
    feedforward = lax.psum((routed + shared_result).astype(jnp.bfloat16), "tensor").astype(
        jnp.float32
    )
    output = (middle + feedforward).astype(jnp.bfloat16)
    shared_active_grad = jnp.einsum(
        "td,fd->tf", cotangent, shared_down, preferred_element_type=jnp.float32
    )
    shared_gate_grad, shared_up_grad = silu_backward(
        shared_gate_val, shared_up_val, shared_active_grad
    )
    shared_gate_grad = shared_gate_grad.astype(jnp.bfloat16)
    shared_up_grad = shared_up_grad.astype(jnp.bfloat16)
    grad_shared_down = jnp.einsum(
        "tf,td->fd", shared_active, cotangent, preferred_element_type=jnp.float32
    )
    grad_shared_gate = jnp.einsum(
        "td,tf->df", hidden_mid, shared_gate_grad, preferred_element_type=jnp.float32
    )
    grad_shared_up = jnp.einsum(
        "td,tf->df", hidden_mid, shared_up_grad, preferred_element_type=jnp.float32
    )
    mid_from_shared = jnp.einsum(
        "tf,df->td", shared_gate_grad, shared_gate, preferred_element_type=jnp.float32
    ) + jnp.einsum("tf,df->td", shared_up_grad, shared_up, preferred_element_type=jnp.float32)
    gate_grad_part = jnp.sum(slot_result * grad_output[:, None, :], axis=2)
    slot_gates = gates.reshape(-1)[slot_entry]
    slot_grad = jnp.where(
        filled[:, None], slot_gates[:, None] * grad_output[slot_token], 0.0
    ).astype(jnp.bfloat16)
    received_grad = dispatch(slot_grad, devices, model_width)
    active_grad = jnp.einsum(
        "secd,efd->secf", received_grad, expert_down, preferred_element_type=jnp.float32
    )
    gate_val_grad, up_val_grad = silu_backward(gate_val, up_val, active_grad)
    gate_val_grad = gate_val_grad.astype(jnp.bfloat16)
    up_val_grad = up_val_grad.astype(jnp.bfloat16)
    grad_expert_down = jnp.einsum(
        "secf,secd->efd", active, received_grad, preferred_element_type=jnp.float32
    )
    grad_expert_gate = jnp.einsum(
        "secd,secf->edf", received, gate_val_grad, preferred_element_type=jnp.float32
    )
    grad_expert_up = jnp.einsum(
        "secd,secf->edf", received, up_val_grad, preferred_element_type=jnp.float32
    )
    expert_input_grad = (
        jnp.einsum("secf,edf->secd", gate_val_grad, expert_gate, preferred_element_type=jnp.float32)
        + jnp.einsum("secf,edf->secd", up_val_grad, expert_up, preferred_element_type=jnp.float32)
    ).astype(jnp.bfloat16)
    returned_grad = send_back(expert_input_grad, devices)
    mid_from_routed = jnp.sum(
        returned_grad[slot_index].reshape(tok_rows, TOP, model_width).astype(jnp.float32), axis=1
    )
    mid_grad_sum, gate_grad = (
        lax.psum((mid_from_routed + mid_from_shared).astype(jnp.bfloat16), "tensor").astype(
            jnp.float32
        ),
        lax.psum(gate_grad_part.astype(jnp.bfloat16), "tensor").astype(jnp.float32),
    )
    route_table = (
        route_ids[:, :, None] == jnp.arange(ROUTED_EXPERTS, dtype=jnp.int32)[None, None, :]
    ).astype(jnp.float32)
    probs_grad = jnp.sum(gate_grad[:, :, None] * route_table, axis=1)
    logit_grad = (
        router_probs * (probs_grad - jnp.sum(router_probs * probs_grad, axis=-1, keepdims=True))
    ).astype(jnp.bfloat16)
    grad_router = jnp.einsum(
        "td,te->de", hidden_mid, logit_grad, preferred_element_type=jnp.float32
    )
    mid_grad = mid_grad_sum + jnp.einsum(
        "te,de->td", logit_grad, w_router, preferred_element_type=jnp.float32
    )
    middle_from_norm, grad_middle_gain = norm_backward(middle, middle_gain, mid_grad)
    middle_grad = grad_output + middle_from_norm
    middle_low = middle_grad.astype(jnp.bfloat16)
    grad_out_proj = jnp.einsum(
        "tc,td->cd", attended, middle_low, preferred_element_type=jnp.float32
    )
    attended_grad = (
        jnp.einsum("td,cd->tc", middle_low, w_out, preferred_element_type=jnp.float32)
        .astype(jnp.bfloat16)
        .reshape(tok_rows, heads_local, DV)
    )
    probs_grad_att = jnp.einsum(
        "qhd,khd->hqk", attended_grad, key_value, preferred_element_type=jnp.float32
    )
    score_grad = (
        probs * (probs_grad_att - jnp.sum(probs * probs_grad_att, axis=-1, keepdims=True))
    ).astype(jnp.bfloat16)
    query_nope_grad = (
        jnp.einsum("hqk,khd->qhd", score_grad, key_nope, preferred_element_type=jnp.float32) * scale
    )
    query_rope_grad = (
        jnp.einsum("hqk,kd->qhd", score_grad, rope_window, preferred_element_type=jnp.float32)
        * scale
    )
    key_nope_grad = (
        jnp.einsum(
            "hqk,qhd->khd", score_grad, queries[..., :DN], preferred_element_type=jnp.float32
        )
        * scale
    )
    rope_window_grad = (
        jnp.einsum("hqk,qhd->kd", score_grad, queries[..., DN:], preferred_element_type=jnp.float32)
        * scale
    )
    value_grad = jnp.einsum(
        "hqk,qhd->khd", probs_low, attended_grad, preferred_element_type=jnp.float32
    )
    expanded_grad = (
        jnp.concatenate([key_nope_grad, value_grad], axis=-1)
        .astype(jnp.bfloat16)
        .reshape(window, heads_local * (DN + DV))
    )
    latent_window_grad = jnp.einsum(
        "wc,kc->wk", expanded_grad, w_expand, preferred_element_type=jnp.float32
    )
    grad_expand = jnp.einsum(
        "wk,wc->kc", latent_window, expanded_grad, preferred_element_type=jnp.float32
    )
    own_start = reach_used * tok_rows
    latent_grad = latent_window_grad[own_start:]
    rope_grad = rope_window_grad[own_start:]
    for steps_back in range(reach_used, 0, -1):
        start_row = (reach_used - steps_back) * tok_rows
        piece_latent = latent_window_grad[start_row : start_row + tok_rows]
        piece_rope = rope_window_grad[start_row : start_row + tok_rows]
        latent_later, rope_later = (
            passed_along(piece_latent.astype(jnp.bfloat16), "dp", -steps_back).astype(
                piece_latent.dtype
            ),
            passed_along(piece_rope.astype(jnp.bfloat16), "dp", -steps_back).astype(
                piece_rope.dtype
            ),
        )
        latent_grad = latent_grad + latent_later
        rope_grad = rope_grad + rope_later
    query_grad = (
        jnp.concatenate(
            [
                query_nope_grad,
                rotate_back(query_rope_grad, cosine[:, None, :], sine_table[:, None, :]),
            ],
            axis=-1,
        )
        .astype(jnp.bfloat16)
        .reshape(tok_rows, heads_local * (DN + DR))
    )
    grad_query = jnp.einsum("td,tc->dc", hidden_in, query_grad, preferred_element_type=jnp.float32)
    input_from_query = jnp.einsum(
        "tc,dc->td", query_grad, w_query, preferred_element_type=jnp.float32
    )
    latent_grad, rope_grad, input_from_query = (
        lax.psum(latent_grad.astype(jnp.bfloat16), "tensor").astype(jnp.float32),
        lax.psum(rope_grad.astype(jnp.bfloat16), "tensor").astype(jnp.float32),
        lax.psum(input_from_query.astype(jnp.bfloat16), "tensor").astype(jnp.float32),
    )
    latent_raw_grad, grad_latent_gain = norm_backward(latent_raw, latent_gain, latent_grad)
    rope_raw_grad = rotate_back(rope_grad, cosine, sine_table)
    latent_full_grad = jnp.concatenate([latent_raw_grad, rope_raw_grad], axis=-1).astype(
        jnp.bfloat16
    )
    grad_latent = jnp.einsum(
        "td,tc->dc", hidden_in, latent_full_grad, preferred_element_type=jnp.float32
    )
    input_grad = input_from_query + jnp.einsum(
        "tc,dc->td", latent_full_grad, w_latent, preferred_element_type=jnp.float32
    )
    token_from_norm, grad_input_gain = norm_backward(token_features, input_gain, input_grad)
    token_grad = (middle_grad + token_from_norm).astype(jnp.bfloat16)
    (
        grad_input_gain,
        grad_query,
        grad_latent,
        grad_latent_gain,
        grad_expand,
        grad_middle_gain,
        grad_router,
        grad_shared_gate,
        grad_shared_up,
    ) = (
        lax.psum_scatter(
            grad_input_gain.astype(jnp.bfloat16), "dp", scatter_dimension=0, tiled=True
        ).astype(jnp.float32),
        lax.psum_scatter(
            grad_query.astype(jnp.bfloat16), "dp", scatter_dimension=0, tiled=True
        ).astype(jnp.float32),
        lax.psum_scatter(
            grad_latent.astype(jnp.bfloat16), "dp", scatter_dimension=0, tiled=True
        ).astype(jnp.float32),
        lax.psum_scatter(
            grad_latent_gain.astype(jnp.bfloat16), "dp", scatter_dimension=0, tiled=True
        ).astype(jnp.float32),
        lax.psum_scatter(
            grad_expand.astype(jnp.bfloat16), "dp", scatter_dimension=0, tiled=True
        ).astype(jnp.float32),
        lax.psum_scatter(
            grad_middle_gain.astype(jnp.bfloat16), "dp", scatter_dimension=0, tiled=True
        ).astype(jnp.float32),
        lax.psum_scatter(
            grad_router.astype(jnp.bfloat16), "dp", scatter_dimension=0, tiled=True
        ).astype(jnp.float32),
        lax.psum_scatter(
            grad_shared_gate.astype(jnp.bfloat16), "dp", scatter_dimension=0, tiled=True
        ).astype(jnp.float32),
        lax.psum_scatter(
            grad_shared_up.astype(jnp.bfloat16), "dp", scatter_dimension=0, tiled=True
        ).astype(jnp.float32),
    )
    grad_out_proj, grad_shared_down = (
        lax.psum_scatter(
            grad_out_proj.astype(jnp.bfloat16), "dp", scatter_dimension=1, tiled=True
        ).astype(jnp.float32),
        lax.psum_scatter(
            grad_shared_down.astype(jnp.bfloat16), "dp", scatter_dimension=1, tiled=True
        ).astype(jnp.float32),
    )
    return (
        output,
        token_grad,
        grad_input_gain,
        grad_query,
        grad_latent,
        grad_latent_gain,
        grad_expand,
        grad_out_proj,
        grad_middle_gain,
        grad_router,
        grad_expert_gate,
        grad_expert_up,
        grad_expert_down,
        grad_shared_gate,
        grad_shared_up,
        grad_shared_down,
    )


def solution(mesh):
    placed = (
        P("dp", None),
        P(),
        P("dp", None),
        P("dp", None),
        P(),
        P(None, "tensor"),
        P(),
        P(),
        P(None, "tensor"),
        P("tensor", None),
        P(),
        P(),
        P("dp", None, "tensor"),
        P("dp", None, "tensor"),
        P("dp", "tensor", None),
        P(None, "tensor"),
        P(None, "tensor"),
        P("tensor", None),
    )
    return jax.shard_map(
        shards,
        mesh=mesh,
        in_specs=placed,
        out_specs=(
            P("dp", None),
            P("dp", None),
            P("dp"),
            P("dp", "tensor"),
            P("dp", None),
            P("dp"),
            P("dp", "tensor"),
            P("tensor", "dp"),
            P("dp"),
            P("dp", None),
            P("dp", None, "tensor"),
            P("dp", None, "tensor"),
            P("dp", "tensor", None),
            P("dp", "tensor"),
            P("dp", "tensor"),
            P("tensor", "dp"),
        ),
        check_vma=False,
    )
```

profile of v0, /device:TPU:0, one launch (start us, length us, event | category | flops | bytes accessed | tf_op | source)
XLA Modules:
  0.0 1902.7 jit_solution(3197887144351945432)
XLA Ops:
  30.0 42.1 %while.24 = (s32[]{:T(128)}, u32[512]{0:T(512)S(1)}, u32[512]{0:T(512)S(1)}, s32[4096]{0:T(1024)S(1)}, s32[512]{0:T(512)S(1)}, /*index=5*/s32[]{:T(128)}, s32[]{:T(128)}, s32[]{}) while((s32[]{:T(128)}, u32[512]{0:T(512)S(1)}, u32[512]{0:T(512)S(1)}, s32[4096]{0:T(1024)S(1)}, s32[512]{0:T(512)S(1)}, /*index=5*/s32[]{:T(128)}, ...), condition=%wide.region_3.4_spmd.clone, body=%wide.region_2.3_spmd.clone.sunk | while | flops 10244 | bytes 40053 | solution.py:68
  79.5 13.6 gather_fusion.1
  115.1 8.9 fusion.53
  124.1 13.6 fusion.2
  137.7 23.7 %fusion.134 = (f32[4,512]{1,0:T(4,128)S(1)}, f32[4,512,2560]{2,1,0:T(8,128)}) fusion(f32[4,512,2560]{2,1,0:T(8,128)} %fusion.2), kind=kOutput, calls=%fused_computation.255 | output fusion | flops 10488319 | bytes 41951232 | tf_op jit(solution)/shard_map/sub | solution.py:162
  161.4 17.4 fusion.70
  185.0 34.9 %reduce-window.6 = s32[64,24,128]{2,1,0:T(8,128)} reduce-window(s32[64,24,128]{2,1,0:T(8,128)} %fusion.93, s32[]{:T(128)} %constant.121.clone.1), window={size=1x1x128 pad=0_0x0_0x127_0}, to_apply=%region_7.8 | reduce-window | flops 24969216 | bytes 1572868 | tf_op jit(solution)/shard_map/reduce-window
  225.6 12.0 scatter_custom_fusion
  238.3 37.8 %all-reduce.13.cloned.1.call-done = bf16[512,2048]{1,0:T(8,128)(2,1)} async-done(((bf16[512,2048]{1,0:T(8,128)(2,1)}), bf16[512,2048]{1,0:T(8,128)(2,1)}) %all-reduce.13.cloned.1.call-update) | async-done | bytes 2097168 | tf_op jit(solution)/shard_map/psum | solution.py:169
  282.0 36.9 %gather_fusion.2 = bf16[4608,2048]{1,0:T(8,128)(2,1)} fusion(bf16[512,2048]{1,0:T(8,128)(2,1)} %multiply_convert_fusion.2, s32[5120]{0:T(1024)S(1)} %pad_clamp_fusion.2), kind=kCustom, calls=%fused_computation.2 | custom fusion | bytes 37767168 | tf_op jit(solution)/shard_map/gather | solution.py:192
  318.9 16.8 broadcast_select_fusion
  345.7 36.1 %gather_fusion.5 = f32[4608,2048]{1,0:T(8,128)} fusion(f32[512,2048]{1,0:T(8,128)} %convert_element_type.292, s32[5120]{0:T(1024)S(1)} %pad_clamp_fusion.2), kind=kCustom, calls=%fused_computation.5 | custom fusion | bytes 75515904 | tf_op jit(solution)/shard_map/gather | solution.py:236
  385.8 24.9 %gather_fusion.7 = f32[3072]{0:T(1024)S(1)} fusion(f32[512,64]{0,1:T(8,128)S(1)} %fusion.100, s32[3072]{0:T(1024)S(1)} %reshape.444), kind=kCustom, calls=%fused_computation.7 | custom fusion | bytes 49152 | tf_op jit(solution)/shard_map/jit(take_along_axis)/gather | solution.py:176
  413.1 24.1 %gather_fusion.4 = f32[4608]{0:T(1024)S(1)} fusion(f32[3072]{0:T(1024)S(1)} %select_n.94, s32[5120]{0:T(1024)S(1)} %pad_clamp_fusion.1), kind=kCustom, calls=%fused_computation.4 | custom fusion | bytes 55296 | tf_op jit(solution)/shard_map/gather | solution.py:234
  437.3 21.1 %select_convert_fusion = bf16[8,576,2048]{2,1,0:T(8,128)(2,1)} fusion(f32[8,576,2048]{2,1,0:T(8,128)} %bitcast.189, f32[8,576]{1,0:T(8,128)S(1)} %mul.490, pred[8,576]{1,0:T(8,128)(4,1)S(1)} %copy-done.46), kind=kLoop, calls=%fused_computation.15 | loop fusion | flops 28311552 | bytes 56646144 | tf_op jit(solution)/shard_map/convert_element_type | solution.py:237
  458.4 89.6 %all-to-all-done = bf16[8,576,2048]{2,1,0:T(8,128)(2,1)} async-done(((bf16[8,576,2048]{2,1,0:T(8,128)(2,1)}), bf16[8,576,2048]{2,1,0:T(8,128)(2,1)}, u32[]{:S(2)}, u32[]{:S(2)}) %all-to-all-start) | async-done | bytes 18874400 | tf_op jit(solution)/shard_map/all_to_all | solution.py:76
  554.2 20.0 %fusion.10 = f32[8,8,72,352]{3,2,1,0:T(8,128)} fusion(bf16[8,8,72,2048]{3,2,1,0:T(8,128)(2,1)} %bitcast.12, bf16[8,2048,352]{1,2,0:T(8,128)(2,1)} %param.32), kind=kOutput, calls=%fused_computation.33 | convolution fusion | flops 6643777536 | bytes 36896768 | tf_op jit(solution)/shard_map/secd,edf->secf/dot_general | solution.py:198
  574.2 20.0 %fusion.8 = f32[8,8,72,352]{3,2,1,0:T(8,128)} fusion(bf16[8,8,72,2048]{3,2,1,0:T(8,128)(2,1)} %bitcast.12, bf16[8,2048,352]{1,2,0:T(8,128)(2,1)} %param.33), kind=kOutput, calls=%fused_computation.31 | convolution fusion | flops 6643777536 | bytes 36896768 | tf_op jit(solution)/shard_map/secd,edf->secf/dot_general | solution.py:201
  594.2 166.4 %all-to-all-done.2 = bf16[8,576,2048]{2,1,0:T(8,128)(2,1)} async-done(((bf16[8,576,2048]{2,1,0:T(8,128)(2,1)}), bf16[8,576,2048]{2,1,0:T(8,128)(2,1)}, u32[]{:S(2)}, u32[]{:S(2)}) %all-to-all-start.2) | async-done | bytes 18874400 | tf_op jit(solution)/shard_map/all_to_all | solution.py:76
  760.6 22.7 %fusion.25 = (bf16[8,8,72,352]{3,2,0,1:T(8,128)(2,1)}, bf16[8,8,72,352]{3,2,0,1:T(8,128)(2,1)}, bf16[8,8,72,352]{3,2,0,1:T(8,128)(2,1)}) fusion(f32[8,8,72,352]{3,2,1,0:T(8,128)} %fusion.10, f32[8,8,72,352]{3,2,1,0:T(8,128)} %fusion.8, bf16[8,352,2048]{2,1,0:T(8,128)(2,1)} %param.34, bf16[8,8,72,2048]{3,2,1,0:T(8,128)(2,1)} %bitcast.26), kind=kOutput, calls=%fused_computation.57 | convolution fusion | flops 6669729792 | bytes 53116928 | tf_op jit(solution)/shard_map/secd,efd->secf/dot_general | solution.py:239
  783.3 21.3 %fusion.14 = f32[8,8,72,2048]{3,2,1,0:T(8,128)} fusion(bf16[8,8,72,352]{3,2,0,1:T(8,128)(2,1)} %get-tuple-element.128, bf16[8,2048,352]{1,2,0:T(8,128)(2,1)} %param.32), kind=kOutput, calls=%fused_computation.37 | convolution fusion | flops 6643777536 | bytes 52527104 | tf_op jit(solution)/shard_map/secf,edf->secd/dot_general | solution.py:255
  804.6 24.5 %fusion.3 = bf16[8,8,72,2048]{3,2,0,1:T(8,128)(2,1)} fusion(f32[8,8,72,2048]{3,2,1,0:T(8,128)} %fusion.14, bf16[8,8,72,352]{3,2,0,1:T(8,128)(2,1)} %get-tuple-element.127, bf16[8,2048,352]{1,2,0:T(8,128)(2,1)} %param.33), kind=kOutput, calls=%fused_computation.24 | convolution fusion | flops 6662651904 | bytes 71401472 | tf_op jit(solution)/shard_map/secf,edf->secd/dot_general | solution.py:256
  829.1 16.9 copy.179
  852.0 17.6 convert_bitcast_fusion
  869.6 16.9 copy.173
  886.5 171.9 %all-to-all-done.3 = bf16[8,576,2048]{2,1,0:T(8,128)(2,1)} async-done(((bf16[8,576,2048]{2,1,0:T(8,128)(2,1)}), bf16[8,576,2048]{2,1,0:T(8,128)(2,1)}, u32[]{:S(2)}, u32[]{:S(2)}) %all-to-all-start.3) | async-done | bytes 18874400 | tf_op jit(solution)/shard_map/all_to_all | solution.py:84
  1078.9 32.8 %gather_fusion.6 = bf16[3072,2048]{1,0:T(8,128)(2,1)} fusion(bf16[4608,2048]{1,0:T(8,128)(2,1)} %bitcast.33, s32[3072]{0:T(1024)S(1)} %broadcast_clamp_fusion), kind=kCustom, calls=%fused_computation.6 | custom fusion | bytes 25178112 | tf_op jit(solution)/shard_map/gather | solution.py:260
  1111.7 22.2 %reshape.387 = f32[512,6,2048]{2,1,0:T(8,128)} reshape(bf16[3072,2048]{1,0:T(8,128)(2,1)} %gather_fusion.6) | data formatting | bytes 37748736 | tf_op jit(solution)/shard_map/convert_element_type | solution.py:260
  1133.9 17.9 reduce_sum.175
  1175.0 96.0 %all-to-all-done.1 = bf16[8,576,2048]{2,1,0:T(8,128)(2,1)} async-done(((bf16[8,576,2048]{2,1,0:T(8,128)(2,1)}), bf16[8,576,2048]{2,1,0:T(8,128)(2,1)}, u32[]{:S(2)}, u32[]{:S(2)}) %all-to-all-start.1) | async-done | bytes 18874400 | tf_op jit(solution)/shard_map/all_to_all | solution.py:84
  1271.0 33.1 %gather_fusion.3 = bf16[3072,2048]{1,0:T(8,128)(2,1)} fusion(bf16[4608,2048]{1,0:T(8,128)(2,1)} %bitcast.23, s32[3072]{0:T(1024)S(1)} %broadcast_clamp_fusion), kind=kCustom, calls=%fused_computation.3 | custom fusion | bytes 25178112 | tf_op jit(solution)/shard_map/gather | solution.py:207
  1304.2 22.5 %reshape.386 = f32[512,6,2048]{2,1,0:T(8,128)} reshape(bf16[3072,2048]{1,0:T(8,128)(2,1)} %gather_fusion.3) | data formatting | bytes 37748736 | tf_op jit(solution)/shard_map/convert_element_type | solution.py:207
  1326.7 21.0 %multiply_reduce_fusion = (bf16[512,6]{1,0:T(8,128)(2,1)}, f32[512,2048]{1,0:T(8,128)}) fusion(f32[512,6,2048]{2,1,0:T(8,128)} %reshape.386, f32[512,2048]{1,0:T(8,128)} %convert_element_type.292, f32[512,6]{1,0:T(8,128)S(1)} %copy-done.19), kind=kLoop, calls=%fused_computation.16 | loop fusion | flops 24114176 | bytes 33572864 | tf_op jit(solution)/shard_map/reduce_sum | solution.py:233
  1348.7 10.3 psum.52
  1378.0 19.6 %fusion.46 = bf16[2560,4,128]{0,2,1:T(8,128)(2,1)} fusion(bf16[512,4,128]{0,2,1:T(8,128)(2,1)} %bitcast.212, f32[4,512]{1,0:T(4,128)S(1)} %copy-done.53, f32[4,512,2560]{2,1,0:T(8,128)} %fusion.2), kind=kOutput, calls=%fused_computation.95 | convolution fusion | flops 1359221248 | bytes 24125440 | tf_op jit(solution)/shard_map/hqk,qhd->khd/dot_general | solution.py:315
  1397.6 14.5 multiply_reduce_fusion.2
  1412.1 14.1 multiply_convert_fusion
  1467.6 8.9 collective-permute-done.10
  1518.5 19.2 %convolution_bitcast_fusion.1 = f32[8,2048,352]{1,2,0:T(8,128)} fusion(bf16[8,8,72,2048]{3,2,1,0:T(8,128)(2,1)} %bitcast.12, bf16[8,8,72,352]{3,2,0,1:T(8,128)(2,1)} %get-tuple-element.128), kind=kOutput, calls=%fused_computation.51 | convolution fusion | flops 6643777536 | bytes 45187072 | tf_op jit(solution)/shard_map/secd,secf->edf/dot_general | solution.py:248
  1537.7 18.2 fusion.19
  1555.9 121.3 %all-reduce.17.cloned.1.call-done = (bf16[512,2048]{1,0:T(8,128)(2,1)}, bf16[512,2048]{1,0:T(8,128)(2,1)}, bf16[512,64]{0,1:T(8,128)(2,1)}, bf16[512,512]{0,1:T(8,128)(2,1)}) async-done(((bf16[512,2048]{1,0:T(8,128)(2,1)}, bf16[512,2048]{1,0:T(8,128)(2,1)}, bf16[512,64]{0,1:T(8,128)(2,1)}, bf16[512,512]{0,1:T(8,128)(2,1)}), (bf16[512,2048]{1,0:T(8,128)(2,1)}, bf16[512,2048]{1,0:T(8,128)(2,1)}, ...) | async-done | bytes 4784144 | tf_op jit(solution)/shard_map/psum | solution.py:209
  1685.9 19.4 %convolution_bitcast_fusion = f32[8,2048,352]{1,2,0:T(8,128)} fusion(bf16[8,8,72,2048]{3,2,1,0:T(8,128)(2,1)} %bitcast.12, bf16[8,8,72,352]{3,2,0,1:T(8,128)(2,1)} %get-tuple-element.127), kind=kOutput, calls=%fused_computation.50 | convolution fusion | flops 6643777536 | bytes 45187072 | tf_op jit(solution)/shard_map/secd,secf->edf/dot_general | solution.py:251
  1705.3 8.1 reduce-scatter.17.cloned.1.call-done
  1714.8 38.2 %reduce-scatter.13.cloned.1.call-done = bf16[64,1024]{1,0:T(8,128)(2,1)} async-done(((bf16[512,1024]{1,0:T(8,128)(2,1)}), bf16[64,1024]{1,0:T(8,128)(2,1)}) %reduce-scatter.13.cloned.1.call-update) | async-done | bytes 131088 | tf_op jit(solution)/shard_map/reduce_scatter | solution.py:402
  1754.6 43.9 %reduce-scatter.15.cloned.1.call-done = bf16[512,256]{1,0:T(8,128)(2,1)} async-done(((bf16[512,2048]{1,0:T(8,128)(2,1)}), bf16[512,256]{1,0:T(8,128)(2,1)}) %reduce-scatter.15.cloned.1.call-update) | async-done | bytes 262160 | tf_op jit(solution)/shard_map/reduce_scatter | solution.py:419
  1800.2 47.7 %reduce-scatter.9.cloned.1.call-done = bf16[256,768]{1,0:T(8,128)(2,1)} async-done(((bf16[2048,768]{1,0:T(8,128)(2,1)}), bf16[256,768]{1,0:T(8,128)(2,1)}) %reduce-scatter.9.cloned.1.call-update) | async-done | bytes 393232 | tf_op jit(solution)/shard_map/reduce_scatter | solution.py:393
  1857.7 13.2 all-reduce.7
  1880.6 13.6 reduce-scatter.11.cloned.1.call-done
  (419 shorter events, 319.7 us)
Async XLA Ops:
  7.2 67.5 %copy-start = (bf16[2048,768]{1,0:T(8,128)(2,1)S(1)}, bf16[2048,768]{1,0:T(8,128)(2,1)}, u32[]{:S(2)}) copy-start(bf16[2048,768]{1,0:T(8,128)(2,1)} %param.25) | copy-start | bytes 9437188
  7.2 268.9 %all-reduce.13.cloned.1.call-start = ((), (), s32[]{:S(2)}) async-start(), calls=%async_computation.12 | async-start | bytes 4194304 | tf_op jit(solution)/shard_map/psum | solution.py:169
  10.0 64.7 %copy-start.66 = (f32[512]{0:T(512)}, f32[512]{0:T(512)S(1)}, u32[]{:S(2)}) copy-start(f32[512]{0:T(512)S(1)} %fusion.119) | copy-start | bytes 6148
  14.9 96.2 %copy-start.40 = (f32[512]{0:T(512)}, f32[512]{0:T(512)S(1)}, u32[]{:S(2)}) copy-start(f32[512]{0:T(512)S(1)} %fusion.120) | copy-start | bytes 6148
  15.8 90.8 %collective-permute-start = (bf16[512,512]{0,1:T(8,128)(2,1)}, bf16[512,512]{0,1:T(8,128)(2,1)}, u32[]{:S(2)}, u32[]{:S(2)}) collective-permute-start(bf16[512,512]{0,1:T(8,128)(2,1)} %multiply_convert_fusion.5), channel_id=1, source_target_pairs={{0,16},{4,20},{8,24},{12,28},{1,17},{5,21},{9,25},{13,29},{2,18},{... | collective-permute-start | bytes 1572872 | tf_op jit(solution)/shard_map/ppermute | solution.py:22
  21.5 86.3 %collective-permute-start.1 = (bf16[512,512]{0,1:T(8,128)(2,1)}, bf16[512,512]{0,1:T(8,128)(2,1)}, u32[]{:S(2)}, u32[]{:S(2)}) collective-permute-start(bf16[512,512]{0,1:T(8,128)(2,1)} %multiply_convert_fusion.5), channel_id=1, source_target_pairs={{0,12},{4,16},{8,20},{12,24},{16,28},{1,13},{5,17},{9,21},{13,25},... | collective-permute-start | bytes 1572872 | tf_op jit(solution)/shard_map/ppermute | solution.py:22
  24.8 84.1 %collective-permute-start.2 = (bf16[512,512]{0,1:T(8,128)(2,1)}, bf16[512,512]{0,1:T(8,128)(2,1)}, u32[]{:S(2)}, u32[]{:S(2)}) collective-permute-start(bf16[512,512]{0,1:T(8,128)(2,1)} %multiply_convert_fusion.5), channel_id=1, source_target_pairs={{0,8},{4,12},{8,16},{12,20},{16,24},{20,28},{1,9},{5,13},{9,17},{1... | collective-permute-start | bytes 1572872 | tf_op jit(solution)/shard_map/ppermute | solution.py:22
  27.8 82.2 %collective-permute-start.3 = (bf16[512,512]{0,1:T(8,128)(2,1)}, bf16[512,512]{0,1:T(8,128)(2,1)}, u32[]{:S(2)}, u32[]{:S(2)}) collective-permute-start(bf16[512,512]{0,1:T(8,128)(2,1)} %multiply_convert_fusion.5), channel_id=1, source_target_pairs={{0,4},{4,8},{8,12},{12,16},{16,20},{20,24},{24,28},{1,5},{5,9},{9,... | collective-permute-start | bytes 1572872 | tf_op jit(solution)/shard_map/ppermute | solution.py:22
  29.9 42.2 %copy-start.69 = (f32[32]{0:T(128)}, f32[32]{0:T(128)S(1)}, u32[]{:S(2)}) copy-start(f32[32]{0:T(128)S(1)} %multiply_power_fusion) | copy-start | bytes 388
  30.0 44.7 %copy-start.64 = (f32[2048]{0:T(1024)S(1)}, f32[2048]{0:T(1024)}, u32[]{:S(2)}) copy-start(f32[2048]{0:T(1024)} %param.24) | copy-start | bytes 24580
  73.3 22.1 %collective-permute-start.4 = (bf16[512,64]{0,1:T(8,128)(2,1)S(1)}, bf16[512,64]{0,1:T(8,128)(2,1)S(1)}, u32[]{:S(2)}, u32[]{:S(2)}) collective-permute-start(bf16[512,64]{0,1:T(8,128)(2,1)S(1)} %pad_maximum_fusion.8), channel_id=1, source_target_pairs={{0,16},{4,20},{8,24},{12,28},{1,17},{5,21},{9,25},{13,29},{2,18},{... | collective-permute-start | bytes 196616 | tf_op jit(solution)/shard_map/ppermute | solution.py:22
  95.5 3.2 collective-permute-start.5
  98.7 3.2 collective-permute-start.6
  101.9 4.7 collective-permute-start.7
  222.2 57.1 %copy-start.47 = (f32[2048]{0:T(1024)S(1)}, f32[2048]{0:T(1024)}, u32[]{:S(2)}) copy-start(f32[2048]{0:T(1024)} %param.30) | copy-start | bytes 24580
  225.6 56.4 %copy-start.43 = (s32[3072,1]{0,1:T(1,128)}, s32[3072,1]{0,1:T(1,128)S(1)}, u32[]{:S(2)}) copy-start(s32[3072,1]{0,1:T(1,128)S(1)} %compare_select_fusion) | copy-start | bytes 36868
  237.7 81.2 %copy-start.45 = (pred[8,576]{1,0:T(8,128)(4,1)}, pred[8,576]{1,0:T(8,128)(4,1)S(1)}, u32[]{:S(2)}) copy-start(pred[8,576]{1,0:T(8,128)(4,1)S(1)} %broadcast_in_dim.84) | copy-start | bytes 13828
  279.3 39.7 %copy-start.60 = (f32[512]{0:T(512)}, f32[512]{0:T(512)S(1)}, u32[]{:S(2)}) copy-start(f32[512]{0:T(512)S(1)} %multiply_reduce_fusion.5) | copy-start | bytes 6148
  279.6 39.3 %copy-start.62 = (f32[512]{0:T(512)}, f32[512]{0:T(512)S(1)}, u32[]{:S(2)}) copy-start(f32[512]{0:T(512)S(1)} %fusion.121) | copy-start | bytes 6148
  335.7 212.3 %all-to-all-start = ((bf16[8,576,2048]{2,1,0:T(8,128)(2,1)}), bf16[8,576,2048]{2,1,0:T(8,128)(2,1)}, u32[]{:S(2)}, u32[]{:S(2)}) async-start(bf16[8,576,2048]{2,1,0:T(8,128)(2,1)} %broadcast_select_fusion), calls=%async_computation | async-start | bytes 37748736 | tf_op jit(solution)/shard_map/all_to_all | solution.py:76
  345.7 36.1 %copy-start.35 = (s32[512,6]{0,1:T(8,128)S(1)}, s32[512,6]{0,1:T(8,128)}, u32[]{:S(2)}) copy-start(s32[512,6]{0,1:T(8,128)} %param.22) | copy-start | bytes 36868
  345.7 36.5 %copy-start.39 = (s32[4608]{0:T(1024)S(1)}, s32[4608]{0:T(1024)}, u32[]{:S(2)}) copy-start(s32[4608]{0:T(1024)} %get-tuple-element.151) | copy-start | bytes 55300
  548.0 212.6 %all-to-all-start.2 = ((bf16[8,576,2048]{2,1,0:T(8,128)(2,1)}), bf16[8,576,2048]{2,1,0:T(8,128)(2,1)}, u32[]{:S(2)}, u32[]{:S(2)}) async-start(bf16[8,576,2048]{2,1,0:T(8,128)(2,1)} %select_convert_fusion), calls=%async_computation.2 | async-start | bytes 37748736 | tf_op jit(solution)/shard_map/all_to_all | solution.py:76
  846.1 212.4 %all-to-all-start.3 = ((bf16[8,576,2048]{2,1,0:T(8,128)(2,1)}), bf16[8,576,2048]{2,1,0:T(8,128)(2,1)}, u32[]{:S(2)}, u32[]{:S(2)}) async-start(bf16[8,576,2048]{2,1,0:T(8,128)(2,1)} %bitcast.192), calls=%async_computation.3 | async-start | bytes 37748736 | tf_op jit(solution)/shard_map/all_to_all | solution.py:84
  1058.4 212.6 %all-to-all-start.1 = ((bf16[8,576,2048]{2,1,0:T(8,128)(2,1)}), bf16[8,576,2048]{2,1,0:T(8,128)(2,1)}, u32[]{:S(2)}, u32[]{:S(2)}) async-start(bf16[8,576,2048]{2,1,0:T(8,128)(2,1)} %bitcast.191), calls=%async_computation.1 | async-start | bytes 37748736 | tf_op jit(solution)/shard_map/all_to_all | solution.py:84
  1064.6 302.4 %all-reduce.15.cloned.1.call-start = ((), (), s32[]{:S(2)}) async-start(), calls=%async_computation.13 | async-start | bytes 4194304 | tf_op jit(solution)/shard_map/psum | solution.py:263
  1159.5 347.2 %reduce-scatter.19.cloned.1.call-start = ((), (), s32[]{:S(2)}) async-start(), calls=%async_computation.19 | async-start | bytes 3244032 | tf_op jit(solution)/shard_map/reduce_scatter | solution.py:411
  1164.7 344.1 %reduce-scatter.21.cloned.1.call-start = ((), (), s32[]{:S(2)}) async-start(), calls=%async_computation.20 | async-start | bytes 3244032 | tf_op jit(solution)/shard_map/reduce_scatter | solution.py:414
  1169.8 340.8 %reduce-scatter.23.cloned.1.call-start = ((), (), s32[]{:S(2)}) async-start(), calls=%async_computation.21 | async-start | bytes 3244032 | tf_op jit(solution)/shard_map/reduce_scatter | solution.py:422
  1175.0 502.2 %all-reduce.17.cloned.1.call-start = ((), (), s32[]{:S(2)}) async-start(), calls=%async_computation.22 | async-start | bytes 9568256 | tf_op jit(solution)/shard_map/psum | solution.py:209
  1430.5 28.3 %collective-permute-start.15 = (bf16[512,64]{0,1:T(8,128)(2,1)}, bf16[512,64]{0,1:T(8,128)(2,1)}, u32[]{:S(2)}, u32[]{:S(2)}) collective-permute-start(bf16[512,64]{0,1:T(8,128)(2,1)} %get-tuple-element.146), channel_id=1, source_target_pairs={{4,0},{8,4},{12,8},{16,12},{20,16},{24,20},{28,24},{5,1},{9,5},{13... | collective-permute-start | bytes 196616 | tf_op jit(solution)/shard_map/ppermute | solution.py:22
  1431.8 28.4 %collective-permute-start.14 = (bf16[512,64]{0,1:T(8,128)(2,1)}, bf16[512,64]{0,1:T(8,128)(2,1)}, u32[]{:S(2)}, u32[]{:S(2)}) collective-permute-start(bf16[512,64]{0,1:T(8,128)(2,1)} %get-tuple-element.147), channel_id=1, source_target_pairs={{8,0},{12,4},{16,8},{20,12},{24,16},{28,20},{9,1},{13,5},{17,9},{2... | collective-permute-start | bytes 196616 | tf_op jit(solution)/shard_map/ppermute | solution.py:22
  1433.1 28.4 %collective-permute-start.13 = (bf16[512,64]{0,1:T(8,128)(2,1)}, bf16[512,64]{0,1:T(8,128)(2,1)}, u32[]{:S(2)}, u32[]{:S(2)}) collective-permute-start(bf16[512,64]{0,1:T(8,128)(2,1)} %get-tuple-element.148), channel_id=1, source_target_pairs={{12,0},{16,4},{20,8},{24,12},{28,16},{13,1},{17,5},{21,9},{25,13},... | collective-permute-start | bytes 196616 | tf_op jit(solution)/shard_map/ppermute | solution.py:22
  1434.4 31.5 %collective-permute-start.12 = (bf16[512,64]{0,1:T(8,128)(2,1)}, bf16[512,64]{0,1:T(8,128)(2,1)}, u32[]{:S(2)}, u32[]{:S(2)}) collective-permute-start(bf16[512,64]{0,1:T(8,128)(2,1)} %get-tuple-element.145), channel_id=1, source_target_pairs={{16,0},{20,4},{24,8},{28,12},{17,1},{21,5},{25,9},{29,13},{18,2},{... | collective-permute-start | bytes 196616 | tf_op jit(solution)/shard_map/ppermute | solution.py:22
  1448.6 19.0 %collective-permute-start.11 = (bf16[512,512]{0,1:T(8,128)(2,1)}, bf16[512,512]{0,1:T(8,128)(2,1)S(1)}, u32[]{:S(2)}, u32[]{:S(2)}) collective-permute-start(bf16[512,512]{0,1:T(8,128)(2,1)} %get-tuple-element.134), channel_id=1, source_target_pairs={{4,0},{8,4},{12,8},{16,12},{20,16},{24,20},{28,24},{5,1},{9,5},{13... | collective-permute-start | bytes 1572872 | tf_op jit(solution)/shard_map/ppermute | solution.py:22
  1458.9 17.6 collective-permute-start.10
  1460.2 22.6 %collective-permute-start.9 = (bf16[512,512]{0,1:T(8,128)(2,1)}, bf16[512,512]{0,1:T(8,128)(2,1)S(1)}, u32[]{:S(2)}, u32[]{:S(2)}) collective-permute-start(bf16[512,512]{0,1:T(8,128)(2,1)} %get-tuple-element.136), channel_id=1, source_target_pairs={{12,0},{16,4},{20,8},{24,12},{28,16},{13,1},{17,5},{21,9},{25,13},... | collective-permute-start | bytes 1572872 | tf_op jit(solution)/shard_map/ppermute | solution.py:22
  1461.5 25.6 %collective-permute-start.8 = (bf16[512,512]{0,1:T(8,128)(2,1)S(1)}, bf16[512,512]{0,1:T(8,128)(2,1)S(1)}, u32[]{:S(2)}, u32[]{:S(2)}) collective-permute-start(bf16[512,512]{0,1:T(8,128)(2,1)S(1)} %get-tuple-element.133), channel_id=1, source_target_pairs={{16,0},{20,4},{24,8},{28,12},{17,1},{21,5},{25,9},{29,13},{18,2},{... | collective-permute-start | bytes 1572872 | tf_op jit(solution)/shard_map/ppermute | solution.py:22
  1489.5 223.9 %reduce-scatter.17.cloned.1.call-start = ((), (), s32[]{:S(2)}) async-start(), calls=%async_computation.18 | async-start | bytes 294912 | tf_op jit(solution)/shard_map/reduce_scatter | solution.py:408
  1492.4 260.6 %reduce-scatter.13.cloned.1.call-start = ((), (), s32[]{:S(2)}) async-start(), calls=%async_computation.16 | async-start | bytes 1179648 | tf_op jit(solution)/shard_map/reduce_scatter | solution.py:402
  1499.7 298.7 %reduce-scatter.15.cloned.1.call-start = ((), (), s32[]{:S(2)}) async-start(), calls=%async_computation.17 | async-start | bytes 2359296 | tf_op jit(solution)/shard_map/reduce_scatter | solution.py:419
  1504.8 343.2 %reduce-scatter.9.cloned.1.call-start = ((), (), s32[]{:S(2)}) async-start(), calls=%async_computation.14 | async-start | bytes 3538944 | tf_op jit(solution)/shard_map/reduce_scatter | solution.py:393
  1518.0 376.1 %reduce-scatter.11.cloned.1.call-start = ((), (), s32[]{:S(2)}) async-start(), calls=%async_computation.15 | async-start | bytes 2654208 | tf_op jit(solution)/shard_map/reduce_scatter | solution.py:396
  1537.7 140.5 %copy-start.55 = (f32[512]{0:T(512)S(1)}, f32[512]{0:T(512)}, u32[]{:S(2)}) copy-start(f32[512]{0:T(512)} %copy-done.54) | copy-start | bytes 6148
  1537.7 140.5 %copy-start.70 = (f32[32]{0:T(128)S(1)}, f32[32]{0:T(128)}, u32[]{:S(2)}) copy-start(f32[32]{0:T(128)} %copy-done.69) | copy-start | bytes 388
  1537.7 140.8 %copy-start.41 = (f32[512]{0:T(512)S(1)}, f32[512]{0:T(512)}, u32[]{:S(2)}) copy-start(f32[512]{0:T(512)} %copy-done.40) | copy-start | bytes 6148
  1537.7 140.8 %copy-start.50 = (f32[512]{0:T(512)S(1)}, f32[512]{0:T(512)}, u32[]{:S(2)}) copy-start(f32[512]{0:T(512)} %param.27) | copy-start | bytes 6148
  1537.7 142.7 %copy-start.59 = (f32[512]{0:T(512)S(1)}, f32[512]{0:T(512)}, u32[]{:S(2)}) copy-start(f32[512]{0:T(512)} %copy-done.58) | copy-start | bytes 6148
  (60 other events, 573.9 us)
Sparse Core Ops, SparseCore 0:
  183.3 92.7 all-reduce.12
  1159.7 85.8 all-reduce.14
  1249.0 43.8 reduce-scatter.18
  1296.5 44.8 reduce-scatter.20
  1344.6 44.8 reduce-scatter.22
  1489.7 187.4 all-reduce.16
  1680.8 32.6 reduce-scatter.16
  1716.9 36.0 reduce-scatter.12
  1757.2 41.2 reduce-scatter.14
  1801.7 46.2 reduce-scatter.8
  1851.7 42.4 reduce-scatter.10
where the time goes:
time: 1920 us; the launch traced here: 1900 us
  waiting for transfers between devices  859 us (45%)
  matrix products  380 us (20%)
  local copies, waits for them, and re-layouts  355 us (18%)
  other arithmetic  210 us (11%)
  starting transfers between devices  57.7 us (3%)
  blocking collectives  23.5 us (1%)
    all_to_all x2, waiting for transfers between devices, send_back(): lax.all_to_all(results.reshape(devices, -1, row_width), 'dp', split_axis=...  268 us
    all_to_all x2, waiting for transfers between devices, dispatch(): lax.all_to_all(buffer_rows.reshape(devices, -1, row_width), 'dp', split_a...  256 us
    psum x1, waiting for transfers between devices, shards(): lax.psum((routed + shared_result).astype(jnp.bfloat16), 'tensor')  121 us
    reduce_scatter x1, waiting for transfers between devices, shards(): lax.psum_scatter(grad_query.astype(jnp.bfloat16), 'dp', scatter_dimension...  47.7 us
    reduce_scatter x1, waiting for transfers between devices, shards(): lax.psum_scatter(grad_out_proj.astype(jnp.bfloat16), 'dp', scatter_dimens...  43.9 us
    gather x13, local copies, waits for them, and re-layouts, rope_tables(): starts = jnp.searchsorted(seq_all, seq_here, side='left')  40.9 us
    another operation x7, other arithmetic  39.3 us
  transfers between devices with their start and end apart: 31, of which 17 were waited for; matrix products, arithmetic and copies ran while one was open for 37% of the time, Pallas kernels for 0%

commit v1 on v0

v1 whole, which is shorter than its diff:
```python
import jax
import jax.numpy as jnp
from jax import lax
from jax.sharding import PartitionSpec as P

DN = 128
DR = 64
DV = 128
KVR = 512
REACH = 4
CAP = 72
BF = jnp.bfloat16
F32 = jnp.float32

epsilon = 1e-06


def dot(eq, a, b):
    return jnp.einsum(eq, a, b, preferred_element_type=F32)


def passed_along(shard, axis, by):
    peers = lax.axis_size(axis)
    pairs = [(i, i + by) for i in range(peers) if 0 <= i + by < peers]
    return lax.ppermute(shard, axis, pairs)


def normed(values, norm_gain):
    return (
        values * lax.rsqrt(jnp.mean(values * values, axis=-1, keepdims=True) + epsilon) * norm_gain
    )


def norm_backward(values, norm_gain, upstream):
    _, pullback = jax.vjp(normed, values, norm_gain)
    return pullback(upstream)


def rotate(values, cosine, sine):
    half = values.shape[-1] // 2
    front, back = values[..., :half], values[..., half:]
    return jnp.concatenate([front * cosine - back * sine, back * cosine + front * sine], axis=-1)


def rotate_back(upstream, cosine, sine):
    return rotate(upstream, cosine, -sine)


def silu_gate(gate_val, up_val):
    return gate_val * jax.nn.sigmoid(gate_val) * up_val


def silu_backward(gate_val, up_val, upstream):
    _, pullback = jax.vjp(silu_gate, gate_val, up_val)
    return pullback(upstream)


def rope_tables(seq_all, seq_here, index_here):
    starts = jnp.sum((seq_all[None, :] < seq_here[:, None]).astype(jnp.int32), axis=1)
    position = (index_here - starts).astype(F32)
    frequency = 10000.0 ** (-(jnp.arange(DR // 2, dtype=F32) * 2.0) / DR)
    angle = position[:, None] * frequency[None, :]
    return jnp.cos(angle), jnp.sin(angle)


def scatter_sum(parts):
    joined = jnp.concatenate(parts, axis=1)
    summed = lax.psum_scatter(joined, "dp", scatter_dimension=0, tiled=True)
    out, at = [], 0
    for part in parts:
        out.append(summed[:, at : at + part.shape[1]].astype(F32))
        at += part.shape[1]
    return out


def shards(
    tokens,
    seq_ids,
    route_ids,
    cotangent,
    input_gain,
    w_query,
    w_latent,
    latent_gain,
    w_expand,
    w_out,
    middle_gain,
    w_router,
    expert_gate,
    expert_up,
    expert_down,
    shared_gate,
    shared_up,
    shared_down,
):
    devices = lax.axis_size("dp")
    rank_dp = lax.axis_index("dp")
    tok_rows, width = tokens.shape
    experts_local = expert_gate.shape[0]
    heads_local = w_query.shape[1] // (DN + DR)
    reach = min(REACH, devices - 1)
    window = (reach + 1) * tok_rows
    scale = (DN + DR) ** (-0.5)

    cot_all = lax.all_gather(cotangent, "dp", tiled=True)
    route_all = lax.all_gather(route_ids, "dp", tiled=True)

    index_here = rank_dp * tok_rows + jnp.arange(tok_rows, dtype=jnp.int32)
    seq_here = lax.dynamic_slice_in_dim(seq_ids, rank_dp * tok_rows, tok_rows, 0)
    cosine, sine = rope_tables(seq_ids, seq_here, index_here)
    key_index = (rank_dp - reach) * tok_rows + jnp.arange(window, dtype=jnp.int32)
    seq_padded = jnp.concatenate([jnp.full((reach * tok_rows,), -1, jnp.int32), seq_ids])
    seq_keys = lax.dynamic_slice_in_dim(seq_padded, rank_dp * tok_rows, window, 0)
    allowed = (seq_here[:, None] == seq_keys[None, :]) & (key_index[None, :] <= index_here[:, None])

    token_features = tokens.astype(F32)
    grad_output = cotangent.astype(F32)
    hidden_in = normed(token_features, input_gain).astype(BF)
    latent_full = jnp.dot(hidden_in, w_latent, preferred_element_type=F32)
    latent_raw = latent_full[:, :KVR]
    latent = normed(latent_raw, latent_gain).astype(BF)
    rope_key = rotate(latent_full[:, KVR:], cosine, sine).astype(BF)
    own_keys = jnp.concatenate([latent, rope_key], axis=1)
    earlier = [passed_along(own_keys, "dp", back) for back in range(reach, 0, -1)]
    keys_window = jnp.concatenate(earlier + [own_keys], axis=0)
    latent_window = keys_window[:, :KVR]
    rope_window = keys_window[:, KVR:]
    query_pre = jnp.dot(hidden_in, w_query, preferred_element_type=F32).reshape(
        tok_rows, heads_local, DN + DR
    )
    queries = jnp.concatenate(
        [
            query_pre[..., :DN],
            rotate(query_pre[..., DN:], cosine[:, None, :], sine[:, None, :]),
        ],
        axis=-1,
    ).astype(BF)
    expanded = (
        jnp.dot(latent_window, w_expand, preferred_element_type=F32)
        .astype(BF)
        .reshape(window, heads_local, DN + DV)
    )
    key_nope = expanded[..., :DN]
    key_value = expanded[..., DN:]
    scores = dot("qhd,khd->hqk", queries[..., :DN], key_nope) + dot(
        "qhd,kd->hqk", queries[..., DN:], rope_window
    )
    scores = jnp.where(allowed[None], scores * scale, -1e30)
    probs = jax.nn.softmax(scores, axis=-1)
    probs_low = probs.astype(BF)
    attended = (
        dot("hqk,khd->qhd", probs_low, key_value).astype(BF).reshape(tok_rows, heads_local * DV)
    )
    attention = lax.psum(
        jnp.dot(attended, w_out, preferred_element_type=F32).astype(BF), "tensor"
    ).astype(F32)
    middle = token_features + attention
    hidden_mid = normed(middle, middle_gain).astype(BF)
    hidden_all = lax.all_gather(hidden_mid, "dp", tiled=True)

    shared_gate_val = jnp.dot(hidden_mid, shared_gate, preferred_element_type=F32)
    shared_up_val = jnp.dot(hidden_mid, shared_up, preferred_element_type=F32)
    shared_active = silu_gate(shared_gate_val, shared_up_val).astype(BF)
    shared_result = jnp.dot(shared_active, shared_down, preferred_element_type=F32)
    shared_active_grad = dot("td,fd->tf", cotangent, shared_down)
    shared_gate_grad, shared_up_grad = silu_backward(
        shared_gate_val, shared_up_val, shared_active_grad
    )
    shared_gate_grad = shared_gate_grad.astype(BF)
    shared_up_grad = shared_up_grad.astype(BF)
    mid_from_shared = dot("tf,df->td", shared_gate_grad, shared_gate) + dot(
        "tf,df->td", shared_up_grad, shared_up
    )
    grad_shared_down = dot("td,tf->df", cotangent, shared_active).astype(BF)
    grad_shared_gate = dot("td,tf->df", hidden_mid, shared_gate_grad).astype(BF)
    grad_shared_up = dot("td,tf->df", hidden_mid, shared_up_grad).astype(BF)

    local_ids = rank_dp * experts_local + jnp.arange(experts_local, dtype=jnp.int32)
    named = jnp.any(route_all[:, :, None] == local_ids[None, None, :], axis=1)
    named_block = named.reshape(devices, tok_rows, experts_local)
    before = jnp.tril(jnp.ones((tok_rows, tok_rows), BF), -1)
    rank_within = dot("ts,bse->bet", before, named_block.astype(BF)).astype(jnp.int32)
    slot = jnp.where(named_block.transpose(0, 2, 1), rank_within, -1)
    chosen = (slot[:, :, None, :] == jnp.arange(CAP, dtype=jnp.int32)[None, None, :, None]).astype(
        BF
    )

    logits = jnp.dot(hidden_all, w_router, preferred_element_type=F32)
    router_probs = jax.nn.softmax(logits, axis=-1)
    local_probs = lax.dynamic_slice_in_dim(
        router_probs, rank_dp * experts_local, experts_local, 1
    ).reshape(devices, tok_rows, experts_local)
    slot_gates = jnp.sum(
        chosen.astype(F32) * local_probs.transpose(0, 2, 1)[:, :, None, :], axis=-1
    )

    cot_rows = dot("bect,btd->becd", chosen, cot_all.reshape(devices, tok_rows, width)).astype(BF)
    rows = dot("bect,btd->becd", chosen, hidden_all.reshape(devices, tok_rows, width)).astype(BF)
    gate_val = dot("becd,edf->becf", rows, expert_gate)
    up_val = dot("becd,edf->becf", rows, expert_up)
    down_back = dot("becd,efd->becf", cot_rows, expert_down)
    active = silu_gate(gate_val, up_val).astype(BF)
    gated_active = active.astype(F32) * slot_gates[..., None]
    gate_grad = jnp.sum(active.astype(F32) * down_back, axis=-1)
    gate_val_grad, up_val_grad = silu_backward(gate_val, up_val, down_back * slot_gates[..., None])
    gate_val_grad = gate_val_grad.astype(BF)
    up_val_grad = up_val_grad.astype(BF)
    gated_active = gated_active.astype(BF)
    row_grad = (
        dot("becf,edf->becd", gate_val_grad, expert_gate)
        + dot("becf,edf->becd", up_val_grad, expert_up)
    ).astype(BF)
    row_out = dot("becf,efd->becd", gated_active, expert_down).astype(BF)

    probs_grad = dot("bect,bec->bte", chosen, gate_grad.astype(BF)).reshape(-1, experts_local)
    probs_grad = lax.dynamic_update_slice_in_dim(
        jnp.zeros_like(router_probs), probs_grad, rank_dp * experts_local, 1
    )
    logit_grad = (
        router_probs * (probs_grad - jnp.sum(router_probs * probs_grad, axis=-1, keepdims=True))
    ).astype(BF)
    grad_router = dot("td,te->de", hidden_all, logit_grad)
    mid_part = dot("bect,becd->btd", chosen, row_grad).reshape(-1, width) + dot(
        "te,de->td", logit_grad, w_router
    )
    mid_block = lax.psum_scatter(mid_part.astype(BF), "dp", scatter_dimension=0, tiled=True)
    mid_grad = lax.psum((mid_block.astype(F32) + mid_from_shared).astype(BF), "tensor").astype(F32)

    routed_part = dot("bect,becd->btd", chosen, row_out).reshape(-1, width).astype(BF)
    routed_part, _ = lax.optimization_barrier((routed_part, mid_block))
    routed_block = lax.psum_scatter(routed_part, "dp", scatter_dimension=0, tiled=True)

    grad_expert_down = dot("becf,becd->efd", gated_active, cot_rows)
    grad_expert_gate = dot("becd,becf->edf", rows, gate_val_grad)
    grad_expert_up = dot("becd,becf->edf", rows, up_val_grad)

    middle_from_norm, grad_middle_gain = norm_backward(middle, middle_gain, mid_grad)
    middle_grad = grad_output + middle_from_norm
    middle_low = middle_grad.astype(BF)
    grad_out_proj = dot("td,tc->dc", middle_low, attended).astype(BF)
    attended_grad = (
        dot("td,cd->tc", middle_low, w_out).astype(BF).reshape(tok_rows, heads_local, DV)
    )
    probs_grad_att = dot("qhd,khd->hqk", attended_grad, key_value)
    score_grad = (
        probs * (probs_grad_att - jnp.sum(probs * probs_grad_att, axis=-1, keepdims=True))
    ).astype(BF)
    query_nope_grad = dot("hqk,khd->qhd", score_grad, key_nope) * scale
    query_rope_grad = dot("hqk,kd->qhd", score_grad, rope_window) * scale
    key_nope_grad = dot("hqk,qhd->khd", score_grad, queries[..., :DN]) * scale
    rope_window_grad = dot("hqk,qhd->kd", score_grad, queries[..., DN:]) * scale
    value_grad = dot("hqk,qhd->khd", probs_low, attended_grad)
    expanded_grad = (
        jnp.concatenate([key_nope_grad, value_grad], axis=-1)
        .astype(BF)
        .reshape(window, heads_local * (DN + DV))
    )
    latent_window_grad = dot("wc,kc->wk", expanded_grad, w_expand)
    grad_expand = dot("wk,wc->kc", latent_window, expanded_grad).astype(BF)
    window_grad = jnp.concatenate([latent_window_grad, rope_window_grad], axis=1)
    keys_grad = window_grad[reach * tok_rows :]
    for back in range(reach, 0, -1):
        start = (reach - back) * tok_rows
        piece = window_grad[start : start + tok_rows].astype(BF)
        keys_grad = keys_grad + passed_along(piece, "dp", -back).astype(F32)
    query_grad = (
        jnp.concatenate(
            [
                query_nope_grad,
                rotate_back(query_rope_grad, cosine[:, None, :], sine[:, None, :]),
            ],
            axis=-1,
        )
        .astype(BF)
        .reshape(tok_rows, heads_local * (DN + DR))
    )
    grad_query = dot("td,tc->dc", hidden_in, query_grad).astype(BF)
    input_from_query = dot("tc,dc->td", query_grad, w_query)
    keys_grad = lax.psum(keys_grad.astype(BF), "tensor").astype(F32)
    latent_raw_grad, grad_latent_gain = norm_backward(latent_raw, latent_gain, keys_grad[:, :KVR])
    rope_raw_grad = rotate_back(keys_grad[:, KVR:], cosine, sine)
    latent_full_grad = jnp.concatenate([latent_raw_grad, rope_raw_grad], axis=-1).astype(BF)
    grad_latent = dot("td,tc->dc", hidden_in, latent_full_grad).astype(BF)
    input_grad = lax.psum(input_from_query.astype(BF), "tensor").astype(F32) + dot(
        "tc,dc->td", latent_full_grad, w_latent
    )
    token_from_norm, grad_input_gain = norm_backward(token_features, input_gain, input_grad)
    token_grad = (middle_grad + token_from_norm).astype(BF)

    routed_block, _ = lax.optimization_barrier((routed_block, mid_grad))
    feedforward = lax.psum((routed_block.astype(F32) + shared_result).astype(BF), "tensor")
    output = (middle + feedforward.astype(F32)).astype(BF)

    grad_shared_down, grad_shared_gate, grad_shared_up = scatter_sum(
        [grad_shared_down, grad_shared_gate, grad_shared_up]
    )
    grad_router = lax.psum(grad_router.astype(BF), "tensor")
    gains = jnp.stack(
        [grad_middle_gain, grad_input_gain, jnp.repeat(grad_latent_gain, width // KVR)], axis=1
    ).astype(BF)
    grad_out_proj, grad_query, grad_latent, grad_expand, grad_router, gains = scatter_sum(
        [
            grad_out_proj,
            grad_query,
            grad_latent,
            grad_expand.reshape(width, -1),
            grad_router,
            gains,
        ]
    )
    grad_expand = grad_expand.reshape(KVR // devices, -1)
    return (
        output,
        token_grad,
        gains[:, 1],
        grad_query,
        grad_latent,
        gains[:: width // KVR, 2],
        grad_expand,
        grad_out_proj.T,
        gains[:, 0],
        grad_router,
        grad_expert_gate,
        grad_expert_up,
        grad_expert_down,
        grad_shared_gate,
        grad_shared_up,
        grad_shared_down.T,
    )


def solution(mesh):
    placed = (
        P("dp", None),
        P(),
        P("dp", None),
        P("dp", None),
        P(),
        P(None, "tensor"),
        P(),
        P(),
        P(None, "tensor"),
        P("tensor", None),
        P(),
        P(),
        P("dp", None, "tensor"),
        P("dp", None, "tensor"),
        P("dp", "tensor", None),
        P(None, "tensor"),
        P(None, "tensor"),
        P("tensor", None),
    )
    return jax.shard_map(
        shards,
        mesh=mesh,
        in_specs=placed,
        out_specs=(
            P("dp", None),
            P("dp", None),
            P("dp"),
            P("dp", "tensor"),
            P("dp", None),
            P("dp"),
            P("dp", "tensor"),
            P("tensor", "dp"),
            P("dp"),
            P("dp", None),
            P("dp", None, "tensor"),
            P("dp", None, "tensor"),
            P("dp", "tensor", None),
            P("dp", "tensor"),
            P("dp", "tensor"),
            P("tensor", "dp"),
        ),
        check_vma=False,
    )
```

time: 1920 us -> 1200 us (0.62)
  waiting for transfers between devices: 859 us -> 498 us
  local copies, waits for them, and re-layouts: 355 us -> 67.1 us
  other arithmetic: 210 us -> 111 us
  matrix products: 380 us -> 471 us
  starting transfers between devices: 57.7 us -> 20.8 us
    all_to_all x4 -> x0, waiting for transfers between devices: 524 us -> none  [the longest x2 268 us: send_back(): lax.all_to_all(results.reshape(devices, -1, row_width), 'dp', split_axis=...]
    gather x24 -> x0, local copies, waits for them, and re-layouts: 245 us -> none  [the longest x13 40.9 us: rope_tables(): starts = jnp.searchsorted(seq_all, seq_here, side='left')]
    psum x3, waiting for transfers between devices: 159 us -> 317 us  [the longest x1 179 us: shards(): lax.psum((routed_block.astype(F32) + shared_result).astype(BF), 'tensor')]
    dot_general x42 -> x46, matrix products: 380 us -> 471 us  [the longest x38 433 us: dot(): return jnp.einsum(eq, a, b, preferred_element_type=F32)]
    convert_element_type x4 -> x0, local copies, waits for them, and re-layouts: 78.6 us -> none  [the longest x1 22.5 us: shards(): returned[slot_index].reshape(tok_rows, TOP, model_width).astype(jnp.float32)]
    all_gather x0 -> x2, waiting for transfers between devices: none -> 59.2 us  [the longest x1 59.2 us: shards(): hidden_all = lax.all_gather(hidden_mid, 'dp', tiled=True)]
    reduce_scatter x8 -> x4, waiting for transfers between devices: 151 us -> 96.5 us  [the longest x1 95.9 us: shards(): lax.psum_scatter(mid_part.astype(BF), 'dp', scatter_dimension=0, tiled=True)]
    concatenate x0 -> x1, local copies, waits for them, and re-layouts: none -> 40.1 us  [scatter_sum(): joined = jnp.concatenate(parts, axis=1)]
  transfers between devices with their start and end apart: 31 -> 17, of which waited for: 17 -> 7; matrix products, arithmetic and copies ran while one was open for 37% -> 29% of each run, Pallas kernels for 0% -> 0%
where the time goes in v1:
time: 1200 us
  waiting for transfers between devices  498 us (42%)
  matrix products  471 us (39%)
  other arithmetic  111 us (9%)
  local copies, waits for them, and re-layouts  67.1 us (6%)
  starting transfers between devices  20.8 us (2%)
  between operations  16.7 us (1%)
    dot_general x38, matrix products, dot(): return jnp.einsum(eq, a, b, preferred_element_type=F32)  433 us
    psum x1, waiting for transfers between devices, shards(): lax.psum((routed_block.astype(F32) + shared_result).astype(BF), 'tensor')  179 us
    reduce_scatter x1, waiting for transfers between devices, shards(): lax.psum_scatter(mid_part.astype(BF), 'dp', scatter_dimension=0, tiled=True)  95.9 us
    psum x1, waiting for transfers between devices, shards(): lax.psum(jnp.dot(attended, w_out, preferred_element_type=F32).astype(BF),...  91.4 us
    all_gather x1, waiting for transfers between devices, shards(): hidden_all = lax.all_gather(hidden_mid, 'dp', tiled=True)  59.2 us
    psum x1, waiting for transfers between devices, shards(): lax.psum((mid_block.astype(F32) + mid_from_shared).astype(BF), 'tensor')  46.8 us
    concatenate x1, local copies, waits for them, and re-layouts, scatter_sum(): joined = jnp.concatenate(parts, axis=1)  40.1 us
    ppermute x8, waiting for transfers between devices, passed_along(): return lax.ppermute(shard, axis, pairs)  25.1 us
  transfers between devices with their start and end apart: 17, of which 7 were waited for; matrix products, arithmetic and copies ran while one was open for 29% of the time, Pallas kernels for 0%

profile of v1, /device:TPU:0, one launch (start us, length us, event | category | flops | bytes accessed | tf_op | source)
XLA Modules:
  0.0 1195.1 jit_solution(14079437632044810351)
XLA Ops:
  13.4 3.8 fusion.161
  20.9 5.7 collective-permute-start
  40.0 25.1 %collective-permute-done = bf16[512,576]{0,1:T(8,128)(2,1)} collective-permute-done((bf16[512,576]{0,1:T(8,128)(2,1)}, bf16[512,576]{0,1:T(8,128)(2,1)}, u32[]{:S(2)}, u32[]{:S(2)}) %collective-permute-start) | collective-permute-done | bytes 589856 | tf_op jit(solution)/shard_map/ppermute | solution.py:25
  73.0 8.9 fusion.82
  82.0 13.6 %fusion.3 = f32[4,512,2560]{2,1,0:T(8,128)} fusion(f32[4,512,2560]{2,1,0:T(8,128)} %fusion.82, pred[512,2560]{1,0:T(8,128)(4,1)S(1)} %compare_and_fusion, bf16[2560,576]{0,1:T(8,128)(2,1)} %copy-done.37, bf16[512,4,32]{0,2,1:T(8,128)(2,1)S(1)} %get-tuple-element.126, bf16[512,4,32]{0,2,1:T(8,128)(2,1)S(1)} %get-tuple-element.125), kind=kOutput, calls=%fused_computation.7 | convolution fusion | flops 687341568 | bytes 43843584 | tf_op jit(solution)/shard_map/qhd,kd->hqk/dot_general | solution.py:19
  95.6 23.5 %fusion.169 = (f32[4,512]{1,0:T(4,128)S(1)}, f32[4,512,2560]{2,1,0:T(8,128)}) fusion(f32[4,512,2560]{2,1,0:T(8,128)} %fusion.3), kind=kOutput, calls=%fused_computation.251 | output fusion | flops 10488319 | bytes 41951232 | tf_op jit(solution)/shard_map/sub | solution.py:149
  119.1 17.4 %fusion.105 = bf16[4,128,512]{2,1,0:T(8,128)(2,1)} fusion(bf16[2560,4,256]{0,2,1:T(8,128)(2,1)} %bitcast.238, f32[4,512]{1,0:T(4,128)S(1)} %get-tuple-element.144, f32[4,512,2560]{2,1,0:T(8,128)} %fusion.3), kind=kOutput, calls=%fused_computation.147 | convolution fusion | flops 1358172672 | bytes 45096960 | tf_op jit(solution)/shard_map/hqk,khd->qhd/dot_general | solution.py:19
  136.5 4.4 convolution_convert_fusion.10
  141.5 91.4 %all-reduce.6.cloned.1.call-done = bf16[512,2048]{1,0:T(8,128)(2,1)} async-done(((bf16[512,2048]{1,0:T(8,128)(2,1)}), bf16[512,2048]{1,0:T(8,128)(2,1)}) %all-reduce.6.cloned.1.call-update) | async-done | bytes 2097168 | tf_op jit(solution)/shard_map/psum | solution.py:154
  239.6 9.4 all_gather.9
  252.7 18.8 %convolution_convert_fusion = bf16[8,8,72,2048]{3,2,1,0:T(8,128)(2,1)} fusion(bf16[8,512,2048,1]{2,1,3,0:T(8,128)(2,1)} %bitcast.249, s32[8,8,512]{2,1,0:T(8,128)S(1)} %fusion.120), kind=kOutput, calls=%fused_computation.26 | convolution fusion | flops 9675472896 | bytes 35782656 | tf_op jit(solution)/shard_map/bect,btd->becd/dot_general | solution.py:19
  271.4 59.2 %all-gather.3.cloned.1.call-done = bf16[4096,2048]{1,0:T(8,128)(2,1)} async-done(((bf16[512,2048]{1,0:T(8,128)(2,1)}), bf16[4096,2048]{1,0:T(8,128)(2,1)}) %all-gather.3.cloned.1.call-update) | async-done | bytes 16777232 | tf_op jit(solution)/shard_map/all_gather | solution.py:159
  330.6 18.8 %convolution_convert_fusion.1 = bf16[8,8,72,2048]{3,2,1,0:T(8,128)(2,1)} fusion(bf16[8,512,2048,1]{2,1,3,0:T(8,128)(2,1)} %bitcast.222, s32[8,8,512]{2,1,0:T(8,128)S(1)} %fusion.120), kind=kOutput, calls=%fused_computation.27 | convolution fusion | flops 9675472896 | bytes 35782656 | tf_op jit(solution)/shard_map/bect,btd->becd/dot_general | solution.py:19
  349.4 20.0 %fusion.18 = f32[8,8,72,352]{3,2,1,0:T(8,128)} fusion(bf16[8,8,72,2048]{3,2,1,0:T(8,128)(2,1)} %convolution_convert_fusion.1, bf16[8,2048,352]{1,2,0:T(8,128)(2,1)} %param.31), kind=kOutput, calls=%fused_computation.22 | convolution fusion | flops 6643777536 | bytes 36896768 | tf_op jit(solution)/shard_map/becd,edf->becf/dot_general | solution.py:19
  369.4 20.4 %fusion.20 = f32[8,8,72,352]{3,2,1,0:T(8,128)} fusion(bf16[8,8,72,2048]{3,2,1,0:T(8,128)(2,1)} %convolution_convert_fusion.1, bf16[8,2048,352]{1,2,0:T(8,128)(2,1)} %param.30), kind=kOutput, calls=%fused_computation.24 | convolution fusion | flops 6643777536 | bytes 36896768 | tf_op jit(solution)/shard_map/becd,edf->becf/dot_general | solution.py:19
  389.9 24.2 %fusion.39 = (bf16[8,8,72]{2,0,1:T(8,128)(2,1)S(1)}, bf16[8,8,72,352]{3,2,0,1:T(8,128)(2,1)}, f32[8,8,72,352]{3,2,1,0:T(8,128)}) fusion(f32[8,8,72,352]{3,2,1,0:T(8,128)} %fusion.18, f32[8,8,72,352]{3,2,1,0:T(8,128)} %fusion.20, bf16[8,352,2048]{2,1,0:T(8,128)(2,1)} %param.32, bf16[8,8,72,2048]{3,2,1,0:T(8,128)(2,1)} %convolution_convert_fusion), kind=kOutput, calls=%fused_computation.56 | convolution fusion | flops 6658371072 | bytes 53126144 | tf_op jit(solution)/shard_map/becd,efd->becf/dot_general | solution.py:19
  415.7 11.1 fusion.170
  429.9 6.7 multiply_convert_fusion.1
  436.6 21.0 %fusion.31 = f32[8,8,72,2048]{3,2,0,1:T(8,128)} fusion(bf16[8,2048,352]{1,2,0:T(8,128)(2,1)} %param.30, bf16[8,8,72,352]{3,2,0,1:T(8,128)(2,1)} %get-tuple-element.115), kind=kOutput, calls=%fused_computation.33 | convolution fusion | flops 6643777536 | bytes 52527104 | tf_op jit(solution)/shard_map/becf,edf->becd/dot_general | solution.py:19
  457.6 40.2 %fusion.5 = f32[8,512,2048,1]{2,1,3,0:T(8,128)} fusion(f32[8,8,72,2048]{3,2,0,1:T(8,128)} %fusion.31, bf16[8,2048,352]{1,2,0:T(8,128)(2,1)} %param.31, bf16[8,8,72,352]{3,2,0,1:T(8,128)(2,1)} %get-tuple-element.114, pred[8,8,72,512]{3,2,1,0:T(8,128)(4,1)} %iota_compare_fusion.14), kind=kOutput, calls=%fused_computation.12 | convolution fusion | flops 16326328320 | bytes 88440832 | tf_op jit(solution)/shard_map/bect,becd->btd/dot_general | solution.py:19
  497.8 17.1 %fusion.1 = bf16[4096,2048]{1,0:T(8,128)(2,1)} fusion(f32[8,512,2048,1]{2,1,3,0:T(8,128)} %fusion.5, bf16[4096,64]{0,1:T(8,128)(2,1)} %multiply_convert_fusion.6, bf16[2048,64]{0,1:T(8,128)(2,1)S(1)} %copy-done.31), kind=kOutput, calls=%fused_computation.3 | convolution fusion | flops 1090519040 | bytes 51118080 | tf_op jit(solution)/shard_map/te,de->td/dot_general | solution.py:19
  518.3 4.8 fusion.171
  530.8 4.1 fusion.173
  534.9 95.9 %reduce-scatter.5.cloned.1.call-done = bf16[512,2048]{1,0:T(8,128)(2,1)} async-done(((bf16[4096,2048]{1,0:T(8,128)(2,1)}), bf16[512,2048]{1,0:T(8,128)(2,1)}) %reduce-scatter.5.cloned.1.call-update) | async-done | bytes 2097168 | tf_op jit(solution)/shard_map/reduce_scatter | solution.py:226
  630.9 7.1 add_convert_fusion.3
  638.2 29.4 %bitcast_convert_fusion = bf16[8,512,2048]{2,1,0:T(8,128)(2,1)} fusion(bf16[8,352,2048]{2,1,0:T(8,128)(2,1)} %param.32, bf16[8,8,72,352]{3,2,0,1:T(8,128)(2,1)} %get-tuple-element.136, pred[8,8,72,512]{3,2,1,0:T(8,128)(4,1)} %iota_compare_fusion.13), kind=kOutput, calls=%fused_computation.4 | convolution fusion | flops 16325279744 | bytes 33914880 | tf_op jit(solution)/shard_map/bect,becd->btd/dot_general | solution.py:19
  667.7 10.2 convolution_convert_fusion.11
  677.9 46.8 %all-reduce.8.cloned.1.call-done = bf16[512,2048]{1,0:T(8,128)(2,1)} async-done(((bf16[512,2048]{1,0:T(8,128)(2,1)}), bf16[512,2048]{1,0:T(8,128)(2,1)}) %all-reduce.8.cloned.1.call-update) | async-done | bytes 2097168 | tf_op jit(solution)/shard_map/psum | solution.py:227
  724.7 4.9 multiply_reduce_fusion.2
  729.7 5.4 convolution_convert_fusion.12
  735.0 19.7 %fusion.69 = bf16[2560,4,128]{0,2,1:T(8,128)(2,1)} fusion(bf16[512,4,128]{0,2,1:T(8,128)(2,1)} %bitcast.252, f32[4,512]{1,0:T(4,128)S(1)} %copy-done.48, f32[4,512,2560]{2,1,0:T(8,128)} %fusion.3), kind=kOutput, calls=%fused_computation.106 | convolution fusion | flops 1359221248 | bytes 24125440 | tf_op jit(solution)/shard_map/hqk,qhd->khd/dot_general | solution.py:19
  754.7 15.2 %multiply_reduce_fusion = (f32[4,512]{1,0:T(4,128)S(1)}, f32[4,512,2560]{2,1,0:T(8,128)}) fusion(f32[4,512,2560]{2,1,0:T(8,128)} %get-tuple-element.145, f32[4,512]{1,0:T(4,128)S(1)} %copy-done.48, bf16[512,4,128]{0,2,1:T(8,128)(2,1)} %bitcast.253, bf16[2560,4,256]{0,2,1:T(8,128)(2,1)} %bitcast.239), kind=kOutput, calls=%fused_computation.9 | convolution fusion | flops 1357903872 | bytes 45105152 | tf_op jit(solution)/shard_map/qhd,khd->hqk/dot_general | solution.py:19
  769.9 14.6 %multiply_convert_fusion = bf16[4,512,2560]{2,1,0:T(8,128)(2,1)S(1)} fusion(f32[4,512,2560]{2,1,0:T(8,128)} %get-tuple-element.150, f32[4,512]{1,0:T(4,128)S(1)} %get-tuple-element.149, f32[4,512,2560]{2,1,0:T(8,128)} %get-tuple-element.145, f32[4,512]{1,0:T(4,128)S(1)} %copy-done.48), kind=kLoop, calls=%fused_computation.8 | loop fusion | flops 20971520 | bytes 52445184 | tf_op jit(solution)/shard_map/convert_element_type | solution.py:247
  786.2 4.5 pad_maximum_fusion.2
  808.3 4.2 fusion.113
  813.2 6.0 fusion.110
  826.3 5.8 add_convert_fusion.2
  839.3 4.1 pad_maximum_fusion
  843.4 7.2 fusion.92
  855.6 5.6 convolution_convert_fusion.3
  864.7 178.7 %all-reduce.10.cloned.1.call-done = (bf16[512,2048]{1,0:T(8,128)(2,1)}, bf16[512,2048]{1,0:T(8,128)(2,1)}, bf16[512,576]{0,1:T(8,128)(2,1)}, bf16[2048,64]{0,1:T(8,128)(2,1)}) async-done(((bf16[512,2048]{1,0:T(8,128)(2,1)}, bf16[512,2048]{1,0:T(8,128)(2,1)}, bf16[512,576]{0,1:T(8,128)(2,1)}, bf16[2048,64]{0,1:T(8,128)(2,1)}), (bf16[512,2048]{1,0:T(8,128)(2,1)}, bf16[512,2048]{1,0:T(8,128)(2,1)}, ...) | async-done | bytes 5046288 | tf_op jit(solution)/shard_map/psum | solution.py:291
  1047.5 6.6 fusion.63
  1054.4 4.7 convolution_convert_fusion.7
  1059.2 40.1 %concatenate.47 = bf16[2048,2179]{0,1:T(8,128)(2,1)} concatenate(bf16[2048,512]{0,1:T(8,128)(2,1)} %convolution_convert_fusion.8, bf16[2048,768]{0,1:T(8,128)(2,1)} %convolution_convert_fusion.3, bf16[2048,576]{0,1:T(8,128)(2,1)} %convolution_convert_fusion.7, bf16[2048,256]{0,1:T(8,128)(2,1)} %copy.126, bf16[2048,64]{0,1:T(8,128)(2,1)S(1)} %copy-done.39, ...), dimensions={1} | concatenate | bytes 17850368 | tf_op jit(solution)/shard_map/concatenate | solution.py:67
  1101.9 21.4 %convolution_bitcast_fusion = f32[8,2048,352]{1,2,0:T(8,128)} fusion(bf16[8,8,72,2048]{3,2,1,0:T(8,128)(2,1)} %convolution_convert_fusion.1, bf16[8,8,72,352]{3,2,0,1:T(8,128)(2,1)} %get-tuple-element.114), kind=kOutput, calls=%fused_computation.53 | convolution fusion | flops 6643777536 | bytes 45187072 | tf_op jit(solution)/shard_map/becd,becf->edf/dot_general | solution.py:19
  1123.3 22.3 %convolution_bitcast_fusion.1 = f32[8,2048,352]{1,2,0:T(8,128)} fusion(bf16[8,8,72,2048]{3,2,1,0:T(8,128)(2,1)} %convolution_convert_fusion.1, bf16[8,8,72,352]{3,2,0,1:T(8,128)(2,1)S(1)} %copy-done.8), kind=kOutput, calls=%fused_computation.54 | convolution fusion | flops 6643777536 | bytes 45187072 | tf_op jit(solution)/shard_map/becd,becf->edf/dot_general | solution.py:19
  1145.6 18.2 %fusion.35 = f32[8,352,2048]{2,1,0:T(8,128)} fusion(bf16[8,8,72,352]{3,2,0,1:T(8,128)(2,1)} %get-tuple-element.136, bf16[8,8,72,2048]{3,2,1,0:T(8,128)(2,1)} %convolution_convert_fusion), kind=kOutput, calls=%fused_computation.52 | convolution fusion | flops 6643777536 | bytes 45187072 | tf_op jit(solution)/shard_map/becf,becd->efd/dot_general | solution.py:19
  1163.7 8.7 fusion.66
  (283 shorter events, 121.6 us)
Async XLA Ops:
  8.0 28.3 %copy-start = (bf16[2048,768]{1,0:T(8,128)(2,1)S(1)}, bf16[2048,768]{1,0:T(8,128)(2,1)}, u32[]{:S(2)}) copy-start(bf16[2048,768]{1,0:T(8,128)(2,1)} %param.23) | copy-start | bytes 9437188
  8.0 224.8 %all-reduce.6.cloned.1.call-start = ((), (), s32[]{:S(2)}) async-start(), calls=%async_computation.4 | async-start | bytes 4194304 | tf_op jit(solution)/shard_map/psum | solution.py:154
  8.1 9.3 copy-start.65
  13.4 22.9 %copy-start.63 = (f32[512]{0:T(512)}, f32[512]{0:T(512)S(1)}, u32[]{:S(2)}) copy-start(f32[512]{0:T(512)S(1)} %fusion.148) | copy-start | bytes 6148
  17.2 17.8 %copy-start.49 = (s32[4096]{0:T(1024)S(1)}, s32[4096]{0:T(1024)}, u32[]{:S(2)}) copy-start(s32[4096]{0:T(1024)} %param.19) | copy-start | bytes 49156
  17.2 19.0 %copy-start.61 = (f32[2048]{0:T(1024)S(1)}, f32[2048]{0:T(1024)}, u32[]{:S(2)}) copy-start(f32[2048]{0:T(1024)} %param.22) | copy-start | bytes 24580
  19.0 20.8 %copy-start.35 = (f32[512,32]{0,1:T(8,128)}, f32[512,32]{0,1:T(8,128)S(1)}, u32[]{:S(2)}) copy-start(f32[512,32]{0,1:T(8,128)S(1)} %get-tuple-element.143) | copy-start | bytes 196612
  20.9 44.2 %collective-permute-start = (bf16[512,576]{0,1:T(8,128)(2,1)}, bf16[512,576]{0,1:T(8,128)(2,1)}, u32[]{:S(2)}, u32[]{:S(2)}) collective-permute-start(bf16[512,576]{0,1:T(8,128)(2,1)} %pad_maximum_fusion.4), channel_id=1, source_target_pairs={{0,16},{4,20},{8,24},{12,28},{1,17},{5,21},{9,25},{13,29},{2,18},{... | collective-permute-start | bytes 1769480 | tf_op jit(solution)/shard_map/ppermute | solution.py:25
  26.6 39.6 %collective-permute-start.1 = (bf16[512,576]{0,1:T(8,128)(2,1)}, bf16[512,576]{0,1:T(8,128)(2,1)}, u32[]{:S(2)}, u32[]{:S(2)}) collective-permute-start(bf16[512,576]{0,1:T(8,128)(2,1)} %pad_maximum_fusion.4), channel_id=1, source_target_pairs={{0,12},{4,16},{8,20},{12,24},{16,28},{1,13},{5,17},{9,21},{13,25},... | collective-permute-start | bytes 1769480 | tf_op jit(solution)/shard_map/ppermute | solution.py:25
  29.9 37.3 %collective-permute-start.2 = (bf16[512,576]{0,1:T(8,128)(2,1)}, bf16[512,576]{0,1:T(8,128)(2,1)}, u32[]{:S(2)}, u32[]{:S(2)}) collective-permute-start(bf16[512,576]{0,1:T(8,128)(2,1)} %pad_maximum_fusion.4), channel_id=1, source_target_pairs={{0,8},{4,12},{8,16},{12,20},{16,24},{20,28},{1,9},{5,13},{9,17},{1... | collective-permute-start | bytes 1769480 | tf_op jit(solution)/shard_map/ppermute | solution.py:25
  32.9 35.5 %collective-permute-start.3 = (bf16[512,576]{0,1:T(8,128)(2,1)}, bf16[512,576]{0,1:T(8,128)(2,1)}, u32[]{:S(2)}, u32[]{:S(2)}) collective-permute-start(bf16[512,576]{0,1:T(8,128)(2,1)} %pad_maximum_fusion.4), channel_id=1, source_target_pairs={{0,4},{4,8},{8,12},{12,16},{16,20},{20,24},{24,28},{1,5},{5,9},{9,... | collective-permute-start | bytes 1769480 | tf_op jit(solution)/shard_map/ppermute | solution.py:25
  39.8 33.2 %copy-start.22 = (f32[512,768]{0,1:T(8,128)}, f32[512,768]{0,1:T(8,128)S(1)}, u32[]{:S(2)}) copy-start(f32[512,768]{0,1:T(8,128)S(1)} %fusion.159) | copy-start | bytes 4718596
  39.8 29.7 %copy-start.21 = (bf16[512,512]{0,1:T(8,128)(2,1)S(1)}, bf16[512,512]{0,1:T(8,128)(2,1)}, u32[]{:S(2)}) copy-start(bf16[512,512]{0,1:T(8,128)(2,1)} %copy-done.20) | copy-start | bytes 1572868
  39.8 29.7 %copy-start.69 = (bf16[512,1024]{1,0:T(8,128)(2,1)S(1)}, bf16[512,1024]{1,0:T(8,128)(2,1)}, u32[]{:S(2)}) copy-start(bf16[512,1024]{1,0:T(8,128)(2,1)} %param.26) | copy-start | bytes 3145732
  39.9 42.0 %copy-start.27 = (bf16[512,4,32]{0,2,1:T(8,128)(2,1)}, bf16[512,4,32]{0,2,1:T(8,128)(2,1)S(1)}, u32[]{:S(2)}) copy-start(bf16[512,4,32]{0,2,1:T(8,128)(2,1)S(1)} %get-tuple-element.125) | copy-start | bytes 393220
  40.0 42.0 %copy-start.29 = (bf16[512,4,32]{0,2,1:T(8,128)(2,1)}, bf16[512,4,32]{0,2,1:T(8,128)(2,1)S(1)}, u32[]{:S(2)}) copy-start(bf16[512,4,32]{0,2,1:T(8,128)(2,1)S(1)} %get-tuple-element.126) | copy-start | bytes 393220
  119.1 17.4 %copy-start.47 = (f32[4,512]{1,0:T(4,128)}, f32[4,512]{1,0:T(4,128)S(1)}, u32[]{:S(2)}) copy-start(f32[4,512]{1,0:T(4,128)S(1)} %get-tuple-element.144) | copy-start | bytes 24580
  140.8 96.3 %copy-start.41 = (f32[2048]{0:T(1024)S(1)}, f32[2048]{0:T(1024)}, u32[]{:S(2)}) copy-start(f32[2048]{0:T(1024)} %param.28) | copy-start | bytes 24580
  140.9 111.8 %all-gather.5.cloned.1.call-start = ((), (), s32[]{:S(2)}) async-start(), calls=%async_computation.6 | async-start | bytes 18874368 | tf_op jit(solution)/shard_map/all_gather | solution.py:105
  141.4 189.2 %all-gather.3.cloned.1.call-start = ((), (), s32[]{:S(2)}) async-start(), calls=%async_computation.5 | async-start | bytes 18874368 | tf_op jit(solution)/shard_map/all_gather | solution.py:159
  239.6 391.3 %reduce-scatter.5.cloned.1.call-start = ((), (), s32[]{:S(2)}) async-start(), calls=%async_computation.7 | async-start | bytes 18874368 | tf_op jit(solution)/shard_map/reduce_scatter | solution.py:226
  389.9 25.7 %copy-start.31 = (bf16[2048,64]{0,1:T(8,128)(2,1)S(1)}, bf16[2048,64]{0,1:T(8,128)(2,1)}, u32[]{:S(2)}) copy-start(bf16[2048,64]{0,1:T(8,128)(2,1)} %param.29) | copy-start | bytes 786436
  415.6 14.2 %slice-start.2 = ((s8[7077888]{0:T(1024)(128)(4,1)}), s8[4194304]{0:T(1024)(128)(4,1)S(1)}, s32[]{:S(2)}) async-start(s8[7077888]{0:T(1024)(128)(4,1)} %bitcast.226), calls=%async_computation.15 | async-start | bytes 8388608
  415.6 14.2 %slice-start.4 = ((s8[7077888]{0:T(1024)(128)(4,1)}), s8[4194304]{0:T(1024)(128)(4,1)S(1)}, s32[]{:S(2)}) async-start(s8[7077888]{0:T(1024)(128)(4,1)} %bitcast.228), calls=%async_computation.17 | async-start | bytes 8388608
  415.6 14.2 %slice-start.6 = ((s8[7077888]{0:T(1024)(128)(4,1)}), s8[4194304]{0:T(1024)(128)(4,1)S(1)}, s32[]{:S(2)}) async-start(s8[7077888]{0:T(1024)(128)(4,1)} %bitcast.230), calls=%async_computation.19 | async-start | bytes 8388608
  415.6 14.2 %slice-start.3 = ((s8[7077888]{0:T(1024)(128)(4,1)}), s8[2883584]{0:T(1024)(128)(4,1)S(1)}, s32[]{:S(2)}) async-start(s8[7077888]{0:T(1024)(128)(4,1)} %bitcast.226), calls=%async_computation.16 | async-start | bytes 5767168
  415.6 14.2 %slice-start.5 = ((s8[7077888]{0:T(1024)(128)(4,1)}), s8[2883584]{0:T(1024)(128)(4,1)S(1)}, s32[]{:S(2)}) async-start(s8[7077888]{0:T(1024)(128)(4,1)} %bitcast.228), calls=%async_computation.18 | async-start | bytes 5767168
  415.6 14.2 %slice-start.7 = ((s8[7077888]{0:T(1024)(128)(4,1)}), s8[2883584]{0:T(1024)(128)(4,1)S(1)}, s32[]{:S(2)}) async-start(s8[7077888]{0:T(1024)(128)(4,1)} %bitcast.230), calls=%async_computation.20 | async-start | bytes 5767168
  514.9 209.8 %all-reduce.8.cloned.1.call-start = ((), (), s32[]{:S(2)}) async-start(), calls=%async_computation.9 | async-start | bytes 4194304 | tf_op jit(solution)/shard_map/psum | solution.py:227
  638.0 188.3 %reduce-scatter.7.cloned.1.call-start = ((), (), s32[]{:S(2)}) async-start(), calls=%async_computation.8 | async-start | bytes 18874368 | tf_op jit(solution)/shard_map/reduce_scatter | solution.py:231
  667.6 57.1 %copy-start.42 = (f32[2048]{0:T(1024)S(1)}, f32[2048]{0:T(1024)}, u32[]{:S(2)}) copy-start(f32[2048]{0:T(1024)} %param.28) | copy-start | bytes 24580
  667.6 57.1 %copy-start.44 = (f32[512]{0:T(512)S(1)}, f32[512]{0:T(512)}, u32[]{:S(2)}) copy-start(f32[512]{0:T(512)} %copy-done.43) | copy-start | bytes 6148
  667.6 375.7 %all-reduce.10.cloned.1.call-start = ((), (), s32[]{:S(2)}) async-start(), calls=%async_computation.12 | async-start | bytes 10092544 | tf_op jit(solution)/shard_map/psum | solution.py:291
  677.9 51.7 %copy-start.57 = (f32[512]{0:T(512)S(1)}, f32[512]{0:T(512)}, u32[]{:S(2)}) copy-start(f32[512]{0:T(512)} %copy-done.56) | copy-start | bytes 6148
  769.9 14.7 %copy-start.23 = (f32[512,768]{0,1:T(8,128)S(1)}, f32[512,768]{0,1:T(8,128)}, u32[]{:S(2)}) copy-start(f32[512,768]{0,1:T(8,128)} %copy-done.22) | copy-start | bytes 4718596
  802.5 21.2 %collective-permute-start.4 = (bf16[512,576]{0,1:T(8,128)(2,1)}, bf16[512,576]{0,1:T(8,128)(2,1)S(1)}, u32[]{:S(2)}, u32[]{:S(2)}) collective-permute-start(bf16[512,576]{0,1:T(8,128)(2,1)} %get-tuple-element.118), channel_id=1, source_target_pairs={{16,0},{20,4},{24,8},{28,12},{17,1},{21,5},{25,9},{29,13},{18,2},{... | collective-permute-start | bytes 1769480 | tf_op jit(solution)/shard_map/ppermute | solution.py:25
  803.8 19.9 %collective-permute-start.5 = (bf16[512,576]{0,1:T(8,128)(2,1)}, bf16[512,576]{0,1:T(8,128)(2,1)S(1)}, u32[]{:S(2)}, u32[]{:S(2)}) collective-permute-start(bf16[512,576]{0,1:T(8,128)(2,1)} %get-tuple-element.121), channel_id=1, source_target_pairs={{12,0},{16,4},{20,8},{24,12},{28,16},{13,1},{17,5},{21,9},{25,13},... | collective-permute-start | bytes 1769480 | tf_op jit(solution)/shard_map/ppermute | solution.py:25
  805.1 18.6 %collective-permute-start.6 = (bf16[512,576]{0,1:T(8,128)(2,1)}, bf16[512,576]{0,1:T(8,128)(2,1)}, u32[]{:S(2)}, u32[]{:S(2)}) collective-permute-start(bf16[512,576]{0,1:T(8,128)(2,1)} %get-tuple-element.120), channel_id=1, source_target_pairs={{8,0},{12,4},{16,8},{20,12},{24,16},{28,20},{9,1},{13,5},{17,9},{2... | collective-permute-start | bytes 1769480 | tf_op jit(solution)/shard_map/ppermute | solution.py:25
  806.4 17.3 %collective-permute-start.7 = (bf16[512,576]{0,1:T(8,128)(2,1)S(1)}, bf16[512,576]{0,1:T(8,128)(2,1)}, u32[]{:S(2)}, u32[]{:S(2)}) collective-permute-start(bf16[512,576]{0,1:T(8,128)(2,1)S(1)} %get-tuple-element.119), channel_id=1, source_target_pairs={{4,0},{8,4},{12,8},{16,12},{20,16},{24,20},{28,24},{5,1},{9,5},{13... | collective-permute-start | bytes 1769480 | tf_op jit(solution)/shard_map/ppermute | solution.py:25
  832.1 267.1 %reduce-scatter.11.cloned.1.call-start = ((), (), s32[]{:S(2)}) async-start(), calls=%async_computation.11 | async-start | bytes 9732096 | tf_op jit(solution)/shard_map/reduce_scatter | solution.py:68
  843.4 329.7 %reduce-scatter.9.cloned.1.call-start = ((), (), s32[]{:S(2)}) async-start(), calls=%async_computation.10 | async-start | bytes 10063872 | tf_op jit(solution)/shard_map/reduce_scatter | solution.py:68
  861.2 183.5 %copy-start.46 = (f32[512]{0:T(512)S(1)}, f32[512]{0:T(512)}, u32[]{:S(2)}) copy-start(f32[512]{0:T(512)} %copy-done.45) | copy-start | bytes 6148
  861.2 183.5 %copy-start.59 = (f32[512]{0:T(512)S(1)}, f32[512]{0:T(512)}, u32[]{:S(2)}) copy-start(f32[512]{0:T(512)} %param.25) | copy-start | bytes 6148
  861.2 185.6 %copy-start.55 = (f32[512]{0:T(512)S(1)}, f32[512]{0:T(512)}, u32[]{:S(2)}) copy-start(f32[512]{0:T(512)} %copy-done.54) | copy-start | bytes 6148
  861.2 185.6 %copy-start.51 = (f32[512]{0:T(512)S(1)}, f32[512]{0:T(512)}, u32[]{:S(2)}) copy-start(f32[512]{0:T(512)} %copy-done.50) | copy-start | bytes 6148
  861.2 185.6 %copy-start.66 = (f32[32]{0:T(128)S(1)}, f32[32]{0:T(128)}, u32[]{:S(2)}) copy-start(f32[32]{0:T(128)} %copy-done.65) | copy-start | bytes 388
  1101.9 21.4 %copy-start.8 = (bf16[8,8,72,352]{3,2,0,1:T(8,128)(2,1)S(1)}, bf16[8,8,72,352]{3,2,0,1:T(8,128)(2,1)}, u32[]{:S(2)}) copy-start(bf16[8,8,72,352]{3,2,0,1:T(8,128)(2,1)} %get-tuple-element.115) | copy-start | bytes 9732100
  1145.5 18.2 %copy-start.53 = (f32[512]{0:T(512)S(1)}, f32[512]{0:T(512)}, u32[]{:S(2)}) copy-start(f32[512]{0:T(512)} %copy-done.52) | copy-start | bytes 6148
  (50 other events, 194.1 us)
Sparse Core Ops, SparseCore 0:
  141.0 91.8 all-reduce.5
  638.1 86.5 all-reduce.7
  832.3 211.0 all-reduce.9
Sparse Core Ops, SparseCore 1:
  143.4 95.0 all-gather.4
  240.9 89.7 all-gather.2
  515.0 115.8 reduce-scatter.4
  667.7 115.8 reduce-scatter.6
  843.5 99.9 reduce-scatter.10
  1099.3 73.7 reduce-scatter.8

commit v2 on v1

v2 whole, which is shorter than its diff:
```python
import functools

import jax
import jax.numpy as jnp
from jax import lax
from jax.experimental import pallas as pl
from jax.experimental.pallas import tpu as pltpu
from jax.sharding import PartitionSpec as P

DN = 128
DR = 64
DV = 128
KVR = 512
REACH = 4
SLOTS = 80
BF = jnp.bfloat16
F32 = jnp.float32
VMEM_BYTES = 60 * 1024 * 1024
epsilon = 1e-06


def mm(a, b, ca, cb):
    return lax.dot_general(a, b, (((ca,), (cb,)), ((), ())), preferred_element_type=F32)


def cost(flops, nbytes, trans=0):
    return pl.CostEstimate(flops=int(flops), bytes_accessed=int(nbytes), transcendentals=int(trans))


def bias_rows(seq_q, seq_k, pos_q, pos_k):
    return jnp.where((seq_q == seq_k) & (pos_k <= pos_q), 0.0, -1e30)


def attend_kernel(scale, step, q_ref, kv_ref, kr_ref, sq_ref, sk_ref, o_ref, lse_ref, key_ref, bias_ref):
    rows = q_ref.shape[1]

    @pl.when(pl.program_id(0) == 0)
    def _():
        for at in range(0, rows, step):
            part = pl.ds(at, step)
            bias_ref[part, :] = bias_rows(
                sq_ref[part, 0:1], sk_ref[0:1, :], sq_ref[part, 1:2], sk_ref[1:2, :]
            ).astype(BF)
        key_ref[:, DN:] = kr_ref[...]

    key_ref[:, :DN] = kv_ref[:, :DN]
    for at in range(0, rows, step):
        part = pl.ds(at, step)
        s = mm(q_ref[0, part, :], key_ref[...], 1, 1) * scale + bias_ref[part, :].astype(F32)
        top = jnp.max(s, axis=-1, keepdims=True)
        p = jnp.exp(s - top)
        total = jnp.sum(p, axis=-1, keepdims=True)
        o = mm((p * (1.0 / total)).astype(BF), kv_ref[:, DN:], 1, 0)
        o_ref[part, :] = o.astype(BF)
        lse_ref[0, part, :] = top + jnp.log(total)


def attend(queries, expanded, rope_window, seq_pos_q, seq_pos_k):
    heads, rows, qw = queries.shape
    window = expanded.shape[0]
    kvw = DN + DV
    step = rows // 2
    return pl.pallas_call(
        functools.partial(attend_kernel, qw ** (-0.5), step),
        name="attend",
        grid=(heads,),
        in_specs=[
            pl.BlockSpec((1, rows, qw), lambda h: (h, 0, 0)),
            pl.BlockSpec((window, kvw), lambda h: (0, h)),
            pl.BlockSpec((window, DR), lambda h: (0, 0)),
            pl.BlockSpec(seq_pos_q.shape, lambda h: (0, 0)),
            pl.BlockSpec(seq_pos_k.shape, lambda h: (0, 0)),
        ],
        out_specs=[
            pl.BlockSpec((rows, DV), lambda h: (0, h)),
            pl.BlockSpec((1, rows, 1), lambda h: (h, 0, 0)),
        ],
        out_shape=[
            jax.ShapeDtypeStruct((rows, heads * DV), BF),
            jax.ShapeDtypeStruct((heads, rows, 1), F32),
        ],
        scratch_shapes=[pltpu.VMEM((window, qw), BF), pltpu.VMEM((rows, window), BF)],
        compiler_params=pltpu.CompilerParams(vmem_limit_bytes=VMEM_BYTES),
        cost_estimate=cost(
            2 * heads * rows * window * 512, heads * window * 512, heads * rows * window
        ),
    )(queries, expanded, rope_window, seq_pos_q, seq_pos_k)


def attend_back_kernel(
    scale, step, q_ref, kv_ref, kr_ref, sq_ref, sk_ref, lse_ref, do_ref,
    dq_ref, dkv_ref, dkr_ref, key_ref, bias_ref, dk_ref, dv_ref,
):
    rows = q_ref.shape[1]
    head = pl.program_id(0)

    @pl.when(head == 0)
    def _():
        for at in range(0, rows, step):
            part = pl.ds(at, step)
            bias_ref[part, :] = bias_rows(
                sq_ref[part, 0:1], sk_ref[0:1, :], sq_ref[part, 1:2], sk_ref[1:2, :]
            ).astype(BF)
        key_ref[:, DN:] = kr_ref[...]

    key_ref[:, :DN] = kv_ref[:, :DN]
    for at in range(0, rows, step):
        part = pl.ds(at, step)
        q = q_ref[0, part, :]
        do = do_ref[part, :]
        s = mm(q, key_ref[...], 1, 1) * scale + bias_ref[part, :].astype(F32)
        p = jnp.exp(s - lse_ref[0, part, :])
        dp = mm(do, kv_ref[:, DN:], 1, 1)
        ds = (p * (dp - jnp.sum(p * dp, axis=-1, keepdims=True))).astype(BF)
        dq_ref[0, part, :] = mm(ds, key_ref[...], 1, 0) * scale
        dk = mm(ds, q, 0, 0) * scale
        dv = mm(p.astype(BF), do, 0, 0)
        if at == 0:
            dk_ref[...] = dk
            dv_ref[...] = dv
        else:
            dk_ref[...] += dk
            dv_ref[...] += dv
    dkv_ref[:, :DN] = dk_ref[:, :DN].astype(BF)
    dkv_ref[:, DN:] = dv_ref[...].astype(BF)

    @pl.when(head == 0)
    def _():
        dkr_ref[...] = dk_ref[:, DN:]

    @pl.when(head != 0)
    def _():
        dkr_ref[...] += dk_ref[:, DN:]


def attend_back(queries, expanded, rope_window, seq_pos_q, seq_pos_k, lse, attended_grad):
    heads, rows, qw = queries.shape
    window = expanded.shape[0]
    kvw = DN + DV
    step = rows // 2
    return pl.pallas_call(
        functools.partial(attend_back_kernel, qw ** (-0.5), step),
        name="attend_back",
        grid=(heads,),
        in_specs=[
            pl.BlockSpec((1, rows, qw), lambda h: (h, 0, 0)),
            pl.BlockSpec((window, kvw), lambda h: (0, h)),
            pl.BlockSpec((window, DR), lambda h: (0, 0)),
            pl.BlockSpec(seq_pos_q.shape, lambda h: (0, 0)),
            pl.BlockSpec(seq_pos_k.shape, lambda h: (0, 0)),
            pl.BlockSpec((1, rows, 1), lambda h: (h, 0, 0)),
            pl.BlockSpec((rows, DV), lambda h: (0, h)),
        ],
        out_specs=[
            pl.BlockSpec((1, rows, qw), lambda h: (h, 0, 0)),
            pl.BlockSpec((window, kvw), lambda h: (0, h)),
            pl.BlockSpec((window, DR), lambda h: (0, 0)),
        ],
        out_shape=[
            jax.ShapeDtypeStruct((heads, rows, qw), F32),
            jax.ShapeDtypeStruct((window, heads * kvw), BF),
            jax.ShapeDtypeStruct((window, DR), F32),
        ],
        scratch_shapes=[
            pltpu.VMEM((window, qw), BF),
            pltpu.VMEM((rows, window), BF),
            pltpu.VMEM((window, qw), F32),
            pltpu.VMEM((window, DV), F32),
        ],
        compiler_params=pltpu.CompilerParams(vmem_limit_bytes=VMEM_BYTES),
        cost_estimate=cost(
            2 * heads * rows * window * 1280, heads * window * 1024, heads * rows * window
        ),
    )(queries, expanded, rope_window, seq_pos_q, seq_pos_k, lse, attended_grad)


def one_hot(slot_ref):
    experts, rows = slot_ref.shape[0], slot_ref.shape[-1]
    place = lax.broadcasted_iota(jnp.int32, (SLOTS, rows), 0)
    return jnp.concatenate(
        [(slot_ref[e, 0] == place).astype(F32).astype(BF) for e in range(experts)], axis=0
    )


def pick_kernel(slot_ref, x_ref, o_ref):
    experts = slot_ref.shape[0]
    picked = mm(one_hot(slot_ref), x_ref[...], 1, 0).astype(BF)
    o_ref[...] = picked.reshape(o_ref.shape)


def pick(slot, values):
    experts, blocks, _, rows = slot.shape
    width = values.shape[1]
    return pl.pallas_call(
        pick_kernel,
        name="pick",
        grid=(blocks,),
        in_specs=[
            pl.BlockSpec((experts, 1, 1, rows), lambda b: (0, b, 0, 0)),
            pl.BlockSpec((rows, width), lambda b: (b, 0)),
        ],
        out_specs=pl.BlockSpec((experts, 1, SLOTS, width), lambda b: (0, b, 0, 0)),
        out_shape=jax.ShapeDtypeStruct((experts, blocks, SLOTS, width), BF),
        compiler_params=pltpu.CompilerParams(vmem_limit_bytes=VMEM_BYTES),
        cost_estimate=cost(
            2 * experts * blocks * SLOTS * rows * width,
            2 * blocks * width * (rows + experts * SLOTS),
        ),
    )(slot, values)


def put_kernel(place_ref, r_ref, *rest):
    total = mm(place_ref[0], r_ref[...].reshape(-1, r_ref.shape[-1]), 1, 0)
    if len(rest) == 3:
        total += mm(rest[0][...], rest[1][...], 1, 0)
    rest[-1][...] = total.astype(BF)


def put(places, picked, extra=()):
    blocks, rows, slots = places.shape
    experts, width = picked.shape[0], picked.shape[3]
    specs = [
        pl.BlockSpec((1, rows, slots), lambda b: (b, 0, 0)),
        pl.BlockSpec((experts, 1, SLOTS, width), lambda b: (0, b, 0, 0)),
    ]
    if extra:
        lanes = extra[0].shape[1]
        specs += [
            pl.BlockSpec((rows, lanes), lambda b: (b, 0)),
            pl.BlockSpec((lanes, width), lambda b: (0, 0)),
        ]
    return pl.pallas_call(
        put_kernel,
        name="put",
        grid=(blocks,),
        in_specs=specs,
        out_specs=pl.BlockSpec((rows, width), lambda b: (b, 0)),
        out_shape=jax.ShapeDtypeStruct((blocks * rows, width), BF),
        compiler_params=pltpu.CompilerParams(vmem_limit_bytes=VMEM_BYTES),
        cost_estimate=cost(
            2 * blocks * slots * rows * width, 2 * blocks * width * (rows + slots)
        ),
    )(places, picked, *extra)


def down_back_kernel(x_ref, w_ref, o_ref):
    ff = w_ref.shape[1]
    wide = o_ref.shape[-1]
    back = mm(x_ref[...].reshape(-1, x_ref.shape[-1]), w_ref[0], 1, 1)
    o_ref[0, :, :ff] = back
    if wide > ff:
        o_ref[0, :, ff:] = jnp.zeros((o_ref.shape[1], wide - ff), F32)


def down_back(rows, down):
    experts, blocks, slots, width = rows.shape
    ff = down.shape[1]
    wide = -(-ff // 128) * 128
    count = blocks * slots
    return pl.pallas_call(
        down_back_kernel,
        name="down_back",
        grid=(experts,),
        in_specs=[
            pl.BlockSpec((1, blocks, slots, width), lambda e: (e, 0, 0, 0)),
            pl.BlockSpec((1, ff, width), lambda e: (e, 0, 0)),
        ],
        out_specs=pl.BlockSpec((1, count, wide), lambda e: (e, 0, 0)),
        out_shape=jax.ShapeDtypeStruct((experts, count, wide), F32),
        compiler_params=pltpu.CompilerParams(vmem_limit_bytes=VMEM_BYTES),
        cost_estimate=cost(
            2 * experts * count * width * ff,
            experts * (2 * count * width + 2 * ff * width + 4 * count * wide),
        ),
    )(rows, down)


def row_out_kernel(x_ref, w_ref, o_ref):
    ff = w_ref.shape[1]
    o_ref[...] = mm(x_ref[0, :, :ff], w_ref[0], 1, 0).astype(BF).reshape(o_ref.shape)


def row_out(active, down, blocks):
    experts, count, wide = active.shape
    ff, width = down.shape[1:]
    slots = count // blocks
    return pl.pallas_call(
        row_out_kernel,
        name="row_out",
        grid=(experts,),
        in_specs=[
            pl.BlockSpec((1, count, wide), lambda e: (e, 0, 0)),
            pl.BlockSpec((1, ff, width), lambda e: (e, 0, 0)),
        ],
        out_specs=pl.BlockSpec((1, blocks, slots, width), lambda e: (e, 0, 0, 0)),
        out_shape=jax.ShapeDtypeStruct((experts, blocks, slots, width), BF),
        compiler_params=pltpu.CompilerParams(vmem_limit_bytes=VMEM_BYTES),
        cost_estimate=cost(
            2 * experts * count * width * ff,
            2 * experts * (count * width + ff * width + count * wide),
        ),
    )(active, down)


def expert_kernel(
    x_ref, gate_ref, up_ref, back_ref, slot_ref, prob_ref,
    ga_ref, dg_ref, du_ref, dx_ref, pg_ref, w_ref, d_ref,
):
    ff = gate_ref.shape[1]
    wide = back_ref.shape[2]
    blocks, rows = slot_ref.shape[1], slot_ref.shape[3]

    @pl.when(pl.program_id(0) == 0)
    def _():
        w_ref[...] = jnp.zeros_like(w_ref)

    w_ref[:ff, :] = gate_ref[0]
    w_ref[wide : wide + ff, :] = up_ref[0]
    x = x_ref[...].reshape(-1, x_ref.shape[-1])
    both = mm(x, w_ref[...], 1, 1)
    a = both[:, :wide]
    b = both[:, wide:]
    place = lax.broadcasted_iota(jnp.int32, (SLOTS, rows), 0)
    slot_gate = jnp.concatenate(
        [
            jnp.sum(
                jnp.where(slot_ref[0, i] == place, prob_ref[0, i], 0.0), axis=-1, keepdims=True
            )
            for i in range(blocks)
        ],
        axis=0,
    )
    back = back_ref[0]
    sig = jax.nn.sigmoid(a)
    swish = a * sig
    active = swish * b
    gate_grad = jnp.sum(active * back, axis=-1, keepdims=True)
    for i in range(blocks):
        part = gate_grad[i * SLOTS : (i + 1) * SLOTS, :]
        pg_ref[0, i] = jnp.sum(
            jnp.where(slot_ref[0, i] == place, part, 0.0), axis=0, keepdims=True
        )
    gated = back * slot_gate
    ga_ref[0] = (active * slot_gate).astype(BF)
    dg = (gated * b * (sig + swish * (1.0 - sig))).astype(BF)
    du = (gated * swish).astype(BF)
    dg_ref[0] = dg
    du_ref[0] = du
    d_ref[:, :wide] = dg
    d_ref[:, wide:] = du
    dx_ref[...] = mm(d_ref[...], w_ref[...], 1, 0).astype(BF).reshape(dx_ref.shape)


def expert_step(rows, gate_t, up_t, back, slot, probs):
    experts, blocks, slots, width = rows.shape
    ff = gate_t.shape[1]
    wide = back.shape[2]
    count = blocks * slots
    whole = pl.BlockSpec((1, blocks, slots, width), lambda e: (e, 0, 0, 0))
    flat = lambda n: pl.BlockSpec((1, count, n), lambda e: (e, 0, 0))
    shape = lambda n, dtype: jax.ShapeDtypeStruct((experts, count, n), dtype)
    weight = pl.BlockSpec((1, ff, width), lambda e: (e, 0, 0))
    by_token = pl.BlockSpec((1,) + slot.shape[1:], lambda e: (e, 0, 0, 0))
    return pl.pallas_call(
        expert_kernel,
        name="expert_step",
        grid=(experts,),
        in_specs=[whole, weight, weight, flat(wide), by_token, by_token],
        out_specs=[flat(wide), flat(wide), flat(wide), whole, by_token],
        out_shape=[
            shape(wide, BF),
            shape(wide, BF),
            shape(wide, BF),
            jax.ShapeDtypeStruct(rows.shape, BF),
            jax.ShapeDtypeStruct(slot.shape, F32),
        ],
        scratch_shapes=[pltpu.VMEM((2 * wide, width), BF), pltpu.VMEM((count, 2 * wide), BF)],
        compiler_params=pltpu.CompilerParams(vmem_limit_bytes=VMEM_BYTES),
        cost_estimate=cost(
            8 * experts * count * width * wide,
            2 * experts * (2 * count * width + 2 * width * wide + 5 * count * wide),
            experts * count * wide,
        ),
    )(rows, gate_t, up_t, back, slot, probs)


def dot(eq, a, b):
    return jnp.einsum(eq, a, b, preferred_element_type=F32)


def passed_along(shard, axis, by):
    peers = lax.axis_size(axis)
    pairs = [(i, i + by) for i in range(peers) if 0 <= i + by < peers]
    return lax.ppermute(shard, axis, pairs)


def normed(values, norm_gain):
    return (
        values * lax.rsqrt(jnp.mean(values * values, axis=-1, keepdims=True) + epsilon) * norm_gain
    )


def norm_backward(values, norm_gain, upstream):
    _, pullback = jax.vjp(normed, values, norm_gain)
    return pullback(upstream)


def rotate(values, cosine, sine):
    half = values.shape[-1] // 2
    front, back = values[..., :half], values[..., half:]
    return jnp.concatenate([front * cosine - back * sine, back * cosine + front * sine], axis=-1)


def rotate_back(upstream, cosine, sine):
    return rotate(upstream, cosine, -sine)


def silu_gate(gate_val, up_val):
    return gate_val * jax.nn.sigmoid(gate_val) * up_val


def silu_backward(gate_val, up_val, upstream):
    _, pullback = jax.vjp(silu_gate, gate_val, up_val)
    return pullback(upstream)


def rope_tables(seq_all, seq_here, index_here):
    starts = jnp.sum((seq_all[None, :] < seq_here[:, None]).astype(jnp.int32), axis=1)
    position = (index_here - starts).astype(F32)
    frequency = 10000.0 ** (-(jnp.arange(DR // 2, dtype=F32) * 2.0) / DR)
    angle = position[:, None] * frequency[None, :]
    return jnp.cos(angle), jnp.sin(angle)


def after(value, *others):
    return lax.optimization_barrier((value,) + others)[0]


def scatter_sum(parts):
    joined = parts if not isinstance(parts, list) else jnp.concatenate(parts, axis=1)
    return lax.psum_scatter(joined, "dp", scatter_dimension=0, tiled=True)


def shards(
    tokens,
    seq_ids,
    route_ids,
    cotangent,
    input_gain,
    w_query,
    w_latent,
    latent_gain,
    w_expand,
    w_out,
    middle_gain,
    w_router,
    expert_gate,
    expert_up,
    expert_down,
    shared_gate,
    shared_up,
    shared_down,
):
    devices = lax.axis_size("dp")
    rank_dp = lax.axis_index("dp")
    tok_rows, width = tokens.shape
    experts_local = expert_gate.shape[0]
    all_experts = w_router.shape[1]
    ff_local = expert_gate.shape[2]
    heads_local = w_query.shape[1] // (DN + DR)
    reach = min(REACH, devices - 1)
    window = (reach + 1) * tok_rows

    cot_all = lax.all_gather(cotangent, "dp", tiled=True)
    route_all = lax.all_gather(route_ids, "dp", tiled=True)

    index_here = rank_dp * tok_rows + jnp.arange(tok_rows, dtype=jnp.int32)
    seq_here = lax.dynamic_slice_in_dim(seq_ids, rank_dp * tok_rows, tok_rows, 0)
    cosine, sine = rope_tables(seq_ids, seq_here, index_here)
    key_index = (rank_dp - reach) * tok_rows + jnp.arange(window, dtype=jnp.int32)
    seq_padded = jnp.concatenate([jnp.full((reach * tok_rows,), -1, jnp.int32), seq_ids])
    seq_keys = lax.dynamic_slice_in_dim(seq_padded, rank_dp * tok_rows, window, 0)
    place_q = jnp.stack([seq_here, index_here], axis=1)
    place_k = jnp.stack([seq_keys, key_index], axis=0)

    token_features = tokens.astype(F32)
    grad_output = cotangent.astype(F32)
    hidden_in = normed(token_features, input_gain).astype(BF)
    latent_full = jnp.dot(hidden_in, w_latent, preferred_element_type=F32)
    latent_raw = latent_full[:, :KVR]
    latent = normed(latent_raw, latent_gain).astype(BF)
    rope_key = rotate(latent_full[:, KVR:], cosine, sine).astype(BF)
    own_keys = jnp.concatenate([latent, rope_key], axis=1)
    earlier = [passed_along(own_keys, "dp", back) for back in range(reach, 0, -1)]
    keys_window = jnp.concatenate(earlier + [own_keys], axis=0)
    latent_window = keys_window[:, :KVR]
    rope_window = keys_window[:, KVR:]
    query_pre = jnp.dot(hidden_in, w_query, preferred_element_type=F32).reshape(
        tok_rows, heads_local, DN + DR
    )
    queries = (
        jnp.concatenate(
            [
                query_pre[..., :DN],
                rotate(query_pre[..., DN:], cosine[:, None, :], sine[:, None, :]),
            ],
            axis=-1,
        )
        .astype(BF)
        .transpose(1, 0, 2)
    )
    expanded = jnp.dot(latent_window, w_expand, preferred_element_type=F32).astype(BF)
    attended, lse = attend(queries, expanded, rope_window, place_q, place_k)
    attention = lax.psum(
        jnp.dot(attended, w_out, preferred_element_type=F32).astype(BF), "tensor"
    )
    attention = after(attention, cot_all)
    middle = token_features + attention.astype(F32)
    hidden_mid = normed(middle, middle_gain).astype(BF)
    hidden_all = lax.all_gather(hidden_mid, "dp", tiled=True)

    local_ids = rank_dp * experts_local + jnp.arange(experts_local, dtype=jnp.int32)
    named = jnp.any(route_all[:, :, None] == local_ids[None, None, :], axis=1)
    named_block = named.reshape(devices, tok_rows, experts_local)
    before = jnp.tril(jnp.ones((tok_rows, tok_rows), BF), -1)
    rank_within = dot("ts,bse->bte", before, named_block.astype(BF))
    slot_of = jnp.where(named_block, rank_within, -1.0)
    slot = slot_of.astype(jnp.int32).transpose(2, 0, 1)[:, :, None, :]
    columns = jnp.arange(experts_local * SLOTS, dtype=jnp.int32)
    spread = (columns[None, :] // SLOTS == jnp.arange(experts_local, dtype=jnp.int32)[:, None]).astype(
        BF
    )
    places = (
        dot("bte,en->btn", slot_of.astype(BF), spread) == (columns % SLOTS).astype(F32)
    ).astype(BF)
    gate_t = expert_gate.swapaxes(1, 2)
    up_t = expert_up.swapaxes(1, 2)
    cot_rows = pick(slot, cot_all)
    back = down_back(cot_rows, expert_down)

    shared_gate_val = jnp.dot(hidden_mid, shared_gate, preferred_element_type=F32)
    shared_up_val = jnp.dot(hidden_mid, shared_up, preferred_element_type=F32)
    shared_active = silu_gate(shared_gate_val, shared_up_val).astype(BF)
    shared_result = jnp.dot(shared_active, shared_down, preferred_element_type=F32)
    shared_active_grad = dot("td,fd->tf", cotangent, shared_down)
    shared_gate_grad, shared_up_grad = silu_backward(
        shared_gate_val, shared_up_val, shared_active_grad
    )
    shared_gate_grad = shared_gate_grad.astype(BF)
    shared_up_grad = shared_up_grad.astype(BF)
    mid_from_shared = dot("tf,df->td", shared_gate_grad, shared_gate) + dot(
        "tf,df->td", shared_up_grad, shared_up
    )
    shared_grads = jnp.concatenate(
        [
            dot("td,tf->df", cotangent, shared_active).astype(BF),
            dot("td,tf->df", hidden_mid, shared_gate_grad).astype(BF),
            dot("td,tf->df", hidden_mid, shared_up_grad).astype(BF),
        ],
        axis=1,
    )

    hidden_all = after(hidden_all, back, shared_grads)
    logits = jnp.dot(hidden_all, w_router, preferred_element_type=F32)
    router_probs = jax.nn.softmax(logits, axis=-1)
    local_probs = (
        lax.dynamic_slice_in_dim(router_probs, rank_dp * experts_local, experts_local, 1)
        .reshape(devices, tok_rows, experts_local)
        .transpose(2, 0, 1)[:, :, None, :]
    )
    rows = pick(slot, hidden_all)
    shared_sums = scatter_sum(shared_grads)
    gated_active, gate_val_grad, up_val_grad, row_grad, probs_grad = expert_step(
        rows, gate_t, up_t, back, slot, local_probs
    )
    probs_grad = lax.dynamic_update_slice_in_dim(
        jnp.zeros_like(router_probs),
        probs_grad[:, :, 0, :].transpose(1, 2, 0).reshape(-1, experts_local),
        rank_dp * experts_local,
        1,
    )
    logit_grad = (
        router_probs * (probs_grad - jnp.sum(router_probs * probs_grad, axis=-1, keepdims=True))
    ).astype(BF)
    lanes = -(-all_experts // 128) * 128 - all_experts
    mid_part = put(
        places,
        row_grad,
        (jnp.pad(logit_grad, ((0, 0), (0, lanes))), jnp.pad(w_router.T, ((0, lanes), (0, 0)))),
    )
    mid_part = after(mid_part, shared_sums)
    mid_block = lax.psum_scatter(mid_part, "dp", scatter_dimension=0, tiled=True)
    grad_router = dot("td,te->de", hidden_all, logit_grad).astype(BF)
    routed_part = put(places, row_out(gated_active, expert_down, devices))
    rows_flat = rows.reshape(experts_local, -1, width)
    grad_expert_down = dot(
        "ecf,ecd->efd",
        gated_active[..., :ff_local],
        cot_rows.reshape(experts_local, -1, width),
    )
    grad_expert_gate = dot("ecd,ecf->edf", rows_flat, gate_val_grad[..., :ff_local])
    grad_expert_up = dot("ecd,ecf->edf", rows_flat, up_val_grad[..., :ff_local])

    routed_block = scatter_sum(after(routed_part, mid_block))
    mid_block = after(
        mid_block, routed_part, grad_router, grad_expert_down, grad_expert_gate, grad_expert_up
    )
    mid_grad = lax.psum((mid_block.astype(F32) + mid_from_shared).astype(BF), "tensor")
    routed_block = after(routed_block, mid_grad)
    mid_grad = mid_grad.astype(F32)

    middle_from_norm, grad_middle_gain = norm_backward(middle, middle_gain, mid_grad)
    middle_grad = grad_output + middle_from_norm
    middle_low = middle_grad.astype(BF)
    attended_grad = dot("td,cd->tc", middle_low, w_out).astype(BF)
    query_back, expanded_grad, rope_window_grad = attend_back(
        queries, expanded, rope_window, place_q, place_k, lse, attended_grad
    )
    ff_part = (routed_block.astype(F32) + shared_result).astype(BF)
    expanded_grad = after(expanded_grad, ff_part)
    window_grad = jnp.concatenate(
        [dot("wc,kc->wk", expanded_grad, w_expand), rope_window_grad], axis=1
    )
    keys_grad = window_grad[reach * tok_rows :]
    for step in range(reach, 0, -1):
        start = (reach - step) * tok_rows
        piece = window_grad[start : start + tok_rows].astype(BF)
        keys_grad = keys_grad + passed_along(piece, "dp", -step).astype(F32)
    query_back = query_back.transpose(1, 0, 2)
    query_grad = (
        jnp.concatenate(
            [
                query_back[..., :DN],
                rotate_back(query_back[..., DN:], cosine[:, None, :], sine[:, None, :]),
            ],
            axis=-1,
        )
        .astype(BF)
        .reshape(tok_rows, heads_local * (DN + DR))
    )
    latent_raw_grad, grad_latent_gain = norm_backward(latent_raw, latent_gain, keys_grad[:, :KVR])
    rope_raw_grad = rotate_back(keys_grad[:, KVR:], cosine, sine)
    latent_full_grad = jnp.concatenate([latent_raw_grad, rope_raw_grad], axis=-1).astype(BF)
    input_part = dot("tc,dc->td", query_grad, w_query) + dot(
        "tc,dc->td", latent_full_grad, w_latent
    )
    _, grad_input_gain = norm_backward(token_features, input_gain, input_part)

    feedforward = lax.psum(ff_part, "tensor")
    output = (middle + feedforward.astype(F32)).astype(BF)
    input_part, grad_input_gain = lax.optimization_barrier((input_part.astype(BF), grad_input_gain))
    input_part = after(input_part, feedforward)
    input_grad = lax.psum(input_part, "tensor").astype(F32)
    token_from_norm, _ = norm_backward(token_features, input_gain, input_grad)
    token_grad = (middle_grad + token_from_norm).astype(BF)

    gains = jnp.concatenate(
        [
            grad_middle_gain[None, :],
            grad_input_gain[None, :],
            jnp.repeat(grad_latent_gain, width // KVR)[None, :],
            jnp.zeros((125, width), F32),
        ],
        axis=0,
    )
    query_width = heads_local * (DN + DR)
    out_width = heads_local * DV
    expand_width = w_expand.shape[1] * KVR // width
    latent_width = KVR + DR
    sums = scatter_sum(
        [
            dot("td,tc->dc", middle_low, attended).astype(BF),
            dot("td,tc->dc", hidden_in, query_grad).astype(BF),
            dot("wk,wc->kc", latent_window, expanded_grad).astype(BF).reshape(width, expand_width),
            dot("td,tc->dc", hidden_in, latent_full_grad).astype(BF),
            grad_router,
            gains.astype(BF).T,
        ]
    )
    at = out_width + query_width + expand_width
    grad_out_proj = sums[:, :out_width].astype(F32).T
    grad_query = sums[:, out_width : out_width + query_width].astype(F32)
    grad_expand = sums[:, out_width + query_width : at].astype(F32).reshape(KVR // devices, -1)
    gain_at = at + latent_width + all_experts
    grad_middle_gain = sums[:, gain_at].astype(F32)
    partial_sums = lax.psum(sums[:, at : gain_at + 3].astype(F32), "tensor")
    shared_sums = shared_sums.astype(F32)
    sw = shared_gate.shape[1]
    return (
        output,
        token_grad,
        partial_sums[:, -2],
        grad_query,
        partial_sums[:, :latent_width],
        partial_sums[:: width // KVR, -1],
        grad_expand,
        grad_out_proj,
        grad_middle_gain,
        partial_sums[:, latent_width : latent_width + all_experts],
        grad_expert_gate,
        grad_expert_up,
        grad_expert_down,
        shared_sums[:, sw : 2 * sw],
        shared_sums[:, 2 * sw :],
        shared_sums[:, :sw].T,
    )


def solution(mesh):
    placed = (
        P("dp", None),
        P(),
        P("dp", None),
        P("dp", None),
        P(),
        P(None, "tensor"),
        P(),
        P(),
        P(None, "tensor"),
        P("tensor", None),
        P(),
        P(),
        P("dp", None, "tensor"),
        P("dp", None, "tensor"),
        P("dp", "tensor", None),
        P(None, "tensor"),
        P(None, "tensor"),
        P("tensor", None),
    )
    return jax.shard_map(
        shards,
        mesh=mesh,
        in_specs=placed,
        out_specs=(
            P("dp", None),
            P("dp", None),
            P("dp"),
            P("dp", "tensor"),
            P("dp", None),
            P("dp"),
            P("dp", "tensor"),
            P("tensor", "dp"),
            P("dp"),
            P("dp", None),
            P("dp", None, "tensor"),
            P("dp", None, "tensor"),
            P("dp", "tensor", None),
            P("dp", "tensor"),
            P("dp", "tensor"),
            P("tensor", "dp"),
        ),
        check_vma=False,
    )
```

time: 1200 us -> 995 us (0.83)
  matrix products: 471 us -> 177 us
  Pallas kernels: 0 us -> 216 us
  waiting for transfers between devices: 498 us -> 361 us
  local copies, waits for them, and re-layouts: 67.1 us -> 112 us
  other arithmetic: 111 us -> 75.3 us
    dot_general x38 -> x20, matrix products: 433 us -> 137 us  [dot(): return jnp.einsum(eq, a, b, preferred_element_type=F32)]
    pallas_call x0 -> x9, Pallas kernels: none -> 216 us  [the longest x1 49.9 us: expert_step(): pl.pallas_call(expert_kernel, name='expert_step', grid=(experts,), in_spe...]
    reduce_scatter x4, waiting for transfers between devices: 96.5 us -> 1.87 us  [the longest x3 1.87 us: scatter_sum(): return lax.psum_scatter(joined, 'dp', scatter_dimension=0, tiled=True)]
    all_gather x1, waiting for transfers between devices: 59.2 us -> 17.2 us  [shards(): hidden_all = lax.all_gather(hidden_mid, 'dp', tiled=True)]
    psum x1, waiting for transfers between devices: 46.8 us -> 86.8 us  [shards(): lax.psum((mid_block.astype(F32) + mid_from_shared).astype(BF), 'tensor')]
    psum x1 -> x3, waiting for transfers between devices: 179 us -> 143 us  [the longest x1 58.6 us: shards(): input_grad = lax.psum(input_part, 'tensor').astype(F32)]
    concatenate x1 -> x3, local copies, waits for them, and re-layouts: 40.1 us -> 4.9 us  [the longest x1 2.19 us: shards(): jnp.concatenate([query_back[..., :DN], rotate_back(query_back[..., DN:],...]
    convert_element_type x8 -> x4, other arithmetic: 31.1 us -> 6.55 us  [the longest x1 1.96 us: shards(): grad_query = sums[:, out_width:out_width + query_width].astype(F32)]
  transfers between devices with their start and end apart: 17 -> 19, of which waited for: 7 -> 11; matrix products, arithmetic and copies ran while one was open for 29% -> 29% of each run, Pallas kernels for 0% -> 20%
where the time goes in v2:
time: 995 us; the launch traced here: 988 us
  waiting for transfers between devices  361 us (36%)
  Pallas kernels  216 us (22%)
  matrix products  177 us (18%)
  local copies, waits for them, and re-layouts  112 us (11%)
  other arithmetic  75.3 us (8%)
  starting transfers between devices  20.5 us (2%)
  between operations  16.7 us (2%)
    dot_general x20, matrix products, dot(): return jnp.einsum(eq, a, b, preferred_element_type=F32)  137 us
    psum x1, waiting for transfers between devices, shards(): lax.psum(jnp.dot(attended, w_out, preferred_element_type=F32).astype(BF),...  90.1 us
    psum x1, waiting for transfers between devices, shards(): lax.psum((mid_block.astype(F32) + mid_from_shared).astype(BF), 'tensor')  86.8 us
    psum x1, waiting for transfers between devices, shards(): input_grad = lax.psum(input_part, 'tensor').astype(F32)  58.6 us
    psum x1, waiting for transfers between devices, shards(): feedforward = lax.psum(ff_part, 'tensor')  53.6 us
    pallas_call x1, Pallas kernels, expert_step(): pl.pallas_call(expert_kernel, name='expert_step', grid=(experts,), in_spe...  49.9 us
    pallas_call x2, Pallas kernels, put(): pl.pallas_call(put_kernel, name='put', grid=(blocks,), in_specs=specs, ou...  45 us
    pallas_call x2, Pallas kernels, pick(): pl.pallas_call(pick_kernel, name='pick', grid=(blocks,), in_specs=[pl.Blo...  39 us
  transfers between devices with their start and end apart: 19, of which 11 were waited for; matrix products, arithmetic and copies ran while one was open for 29% of the time, Pallas kernels for 20%

profile of v2, /device:TPU:0, one launch (start us, length us, event | category | flops | bytes accessed | tf_op | source)
XLA Modules:
  0.0 988.2 jit_solution(1735993649484260873)
XLA Ops:
  14.1 4.2 fusion.90
  25.0 5.7 collective-permute-start
  30.7 3.4 collective-permute-start.1
  39.3 3.5 fusion.92
  62.5 6.6 collective-permute-done
  88.0 6.4 convolution_convert_fusion.kv_ref
  94.4 15.2 %attend.1 = (bf16[512,512]{1,0:T(8,128)(2,1)}, f32[4,512,1]{2,1,0:T(8,128)}) custom-call(bf16[4,512,192]{2,1,0:T(8,128)(2,1)} %maximum_bitcast_fusion.q_ref, bf16[2560,1024]{1,0:T(8,128)(2,1)} %convolution_convert_fusion.kv_ref, bf16[2560,64]{1,0:T(8,128)(2,1)} %slice.161.kr_ref, s32[512,2]{1,0:T(8,128)} %copy.165.sq_ref, s32[2,2560]{1,0:T(2,128)} %pad_add_fusion.sk_ref), custom_call_target="tpu_custom_call" | custom-call | flops 5368709120 | bytes 5242880 | tf_op jit(solution)/shard_map/attend/pallas_call | solution.py:63
  109.6 4.3 convolution_convert_fusion.7
  114.9 90.1 %all-reduce.9.cloned.1.call-done = bf16[512,2048]{1,0:T(8,128)(2,1)} async-done(((bf16[512,2048]{1,0:T(8,128)(2,1)}), bf16[512,2048]{1,0:T(8,128)(2,1)}) %all-reduce.9.cloned.1.call-update) | async-done | bytes 2097168 | tf_op jit(solution)/shard_map/psum | solution.py:514
  205.0 5.6 all-gather.3.cloned.1.call-done.x_ref
  217.3 4.3 fusion.105
  231.2 4.1 pad_maximum_fusion.1
  235.9 9.7 all_gather.10
  247.8 4.0 compare_convert_fusion.place_ref
  251.8 19.4 %pick.2.x_ref = bf16[8,8,80,2048]{3,2,1,0:T(8,128)(2,1)} custom-call(s32[8,8,1,512]{3,2,1,0:T(1,128)} %broadcast_in_dim.36.slot_ref, bf16[4096,2048]{1,0:T(8,128)(2,1)} %all-gather.3.cloned.1.call-done.x_ref), custom_call_target="tpu_custom_call" | custom-call | flops 10737418240 | bytes 37748736 | tf_op jit(solution)/shard_map/pick/pallas_call | solution.py:194
  271.2 19.2 %down_back.1.back_ref = f32[8,640,384]{2,1,0:T(8,128)} custom-call(bf16[8,8,80,2048]{3,2,1,0:T(8,128)(2,1)} %pick.2.x_ref, bf16[8,352,2048]{2,1,0:T(8,128)(2,1)} %w_ref.3), custom_call_target="tpu_custom_call" | custom-call | flops 7381975040 | bytes 40370176 | tf_op jit(solution)/shard_map/down_back/pallas_call | solution.py:260
  290.4 17.2 %all-gather.5.cloned.1.call-done.x_ref = bf16[4096,2048]{1,0:T(8,128)(2,1)} async-done(((bf16[512,2048]{1,0:T(8,128)(2,1)}), bf16[4096,2048]{1,0:T(8,128)(2,1)}) %all-gather.5.cloned.1.call-update) | async-done | bytes 16777232 | tf_op jit(solution)/shard_map/all_gather | solution.py:520
  307.6 11.9 %fusion.99 = (f32[4096]{0:T(1024)S(1)}, f32[4096,64]{0,1:T(8,128)}) fusion(bf16[4096,2048]{1,0:T(8,128)(2,1)} %all-gather.5.cloned.1.call-done.x_ref, bf16[2048,64]{0,1:T(8,128)(2,1)S(1)} %copy-done.32), kind=kOutput, calls=%fused_computation.185 | convolution fusion | flops 1073999872 | bytes 18104320 | tf_op jit(solution)/shard_map/dot_general | solution.py:564
  319.5 3.3 copy.167
  333.0 19.6 %pick.3.x_ref = bf16[8,8,80,2048]{3,2,1,0:T(8,128)(2,1)} custom-call(s32[8,8,1,512]{3,2,1,0:T(1,128)} %broadcast_in_dim.36.slot_ref, bf16[4096,2048]{1,0:T(8,128)(2,1)} %all-gather.5.cloned.1.call-done.x_ref), custom_call_target="tpu_custom_call" | custom-call | flops 10737418240 | bytes 37748736 | tf_op jit(solution)/shard_map/pick/pallas_call | solution.py:194
  352.6 49.9 %expert_step.1 = (bf16[8,640,384]{2,1,0:T(8,128)(2,1)}, bf16[8,640,384]{2,1,0:T(8,128)(2,1)}, bf16[8,640,384]{2,1,0:T(8,128)(2,1)}, bf16[8,8,80,2048]{3,2,1,0:T(8,128)(2,1)}, f32[8,8,1,512]{3,2,1,0:T(1,128)}) custom-call(bf16[8,8,80,2048]{3,2,1,0:T(8,128)(2,1)} %pick.3.x_ref, bf16[8,352,2048]{2,1,0:T(8,128)(2,1)} %bitcast.112, ...), custom_call_target="tpu_custom_call" | custom-call | flops 32212254720 | bytes 86769664 | tf_op jit(solution)/shard_map/expert_step/pallas_call | solution.py:364
  406.9 10.3 %dynamic_update_slice.3 = f32[4096,64]{1,0:T(8,128)} dynamic-update-slice(f32[4096,64]{1,0:T(8,128)} %broadcast_in_dim.38, f32[4096,8]{1,0:T(8,128)} %bitcast.98, s32[]{:T(128)} %constant.32.clone.1, s32[]{:T(128)S(6)} %select_n.45) | dynamic-update-slice | bytes 262148 | tf_op jit(solution)/shard_map/dynamic_update_slice | solution.py:576
  417.2 3.7 multiply_reduce_fusion.1
  425.1 23.4 %put.3 = bf16[4096,2048]{1,0:T(8,128)(2,1)} custom-call(bf16[8,512,640]{2,1,0:T(8,128)(2,1)} %compare_convert_fusion.place_ref, bf16[8,8,80,2048]{3,2,1,0:T(8,128)(2,1)} %get-tuple-element.40.r_ref, bf16[4096,128]{1,0:T(8,128)(2,1)} %pad.9.rest_0_, bf16[128,2048]{1,0:T(8,128)(2,1)} %pad.10.rest_1_), custom_call_target="tpu_custom_call" | custom-call | flops 10737418240 | bytes 37748736 | tf_op jit(solution)/shard_map/put/pallas_call | solution.py:232
  448.6 5.9 fusion.106
  454.4 21.0 %row_out.1.r_ref = bf16[8,8,80,2048]{3,2,1,0:T(8,128)(2,1)} custom-call(bf16[8,640,384]{2,1,0:T(8,128)(2,1)} %get-tuple-element.39.x_ref, bf16[8,352,2048]{2,1,0:T(8,128)(2,1)} %w_ref.3), custom_call_target="tpu_custom_call" | custom-call | flops 7381975040 | bytes 36438016 | tf_op jit(solution)/shard_map/row_out/pallas_call | solution.py:287
  475.4 21.6 %put.2 = bf16[4096,2048]{1,0:T(8,128)(2,1)} custom-call(bf16[8,512,640]{2,1,0:T(8,128)(2,1)} %compare_convert_fusion.place_ref, bf16[8,8,80,2048]{3,2,1,0:T(8,128)(2,1)} %row_out.1.r_ref), custom_call_target="tpu_custom_call" | custom-call | flops 10737418240 | bytes 37748736 | tf_op jit(solution)/shard_map/put/pallas_call | solution.py:232
  497.0 9.6 convolution_convert_fusion.8
  506.6 19.4 %fusion.18 = f32[8,352,2048]{2,1,0:T(8,128)} fusion(bf16[8,640,2048]{2,1,0:T(8,128)(2,1)} %bitcast.95, bf16[8,640,384]{2,1,0:T(8,128)(2,1)} %get-tuple-element.39.x_ref), kind=kOutput, calls=%fused_computation.40 | convolution fusion | flops 7381975040 | bytes 47972352 | tf_op jit(solution)/shard_map/ecf,ecd->efd/dot_general | solution.py:388
  526.0 20.1 %fusion.16 = f32[8,2048,352]{1,2,0:T(8,128)} fusion(bf16[8,640,2048]{2,1,0:T(8,128)(2,1)} %bitcast.96, bf16[8,640,384]{2,1,0:T(8,128)(2,1)} %get-tuple-element.44), kind=kOutput, calls=%fused_computation.38 | convolution fusion | flops 7381975040 | bytes 47972352 | tf_op jit(solution)/shard_map/ecd,ecf->edf/dot_general | solution.py:388
  546.1 22.5 %fusion.14 = f32[8,2048,352]{1,2,0:T(8,128)} fusion(bf16[8,640,2048]{2,1,0:T(8,128)(2,1)} %bitcast.97, bf16[8,640,384]{2,1,0:T(8,128)(2,1)S(1)} %copy-done.23), kind=kOutput, calls=%fused_computation.36 | convolution fusion | flops 7381975040 | bytes 47972352 | tf_op jit(solution)/shard_map/ecd,ecf->edf/dot_general | solution.py:388
  568.6 7.1 add_convert_fusion.2
  577.2 86.8 %all-reduce.11.cloned.1.call-done = bf16[512,2048]{1,0:T(8,128)(2,1)} async-done(((bf16[512,2048]{1,0:T(8,128)(2,1)}), bf16[512,2048]{1,0:T(8,128)(2,1)}) %all-reduce.11.cloned.1.call-update) | async-done | bytes 2097168 | tf_op jit(solution)/shard_map/psum | solution.py:608
  664.1 4.8 fusion.8
  668.9 4.9 convolution_convert_fusion.9.do_ref
  673.8 26.3 %attend_back.1 = (f32[4,512,192]{2,1,0:T(8,128)}, bf16[2560,1024]{1,0:T(8,128)(2,1)}, f32[2560,64]{1,0:T(8,128)}) custom-call(bf16[4,512,192]{2,1,0:T(8,128)(2,1)} %maximum_bitcast_fusion.q_ref, bf16[2560,1024]{1,0:T(8,128)(2,1)} %convolution_convert_fusion.kv_ref, bf16[2560,64]{1,0:T(8,128)(2,1)} %slice.161.kr_ref, s32[512,2]{1,0:T(8,128)} %copy.165.sq_ref, ...), custom_call_target="tpu_custom_call" | custom-call | flops 13421772800 | bytes 10485760 | tf_op jit(solution)/shard_map/attend_back/pallas_call | solution.py:141
  702.8 5.8 add_convert_fusion.1
  708.6 5.3 fusion.108
  731.7 7.0 fusion.22
  743.4 6.4 collective-permute-done.6
  772.6 4.0 fusion.6
  776.6 53.6 %all-reduce.13.cloned.1.call-done = bf16[512,2048]{1,0:T(8,128)(2,1)} async-done(((bf16[512,2048]{1,0:T(8,128)(2,1)}), bf16[512,2048]{1,0:T(8,128)(2,1)}) %all-reduce.13.cloned.1.call-update) | async-done | bytes 2097168 | tf_op jit(solution)/shard_map/psum | solution.py:649
  830.5 7.1 fusion.29
  844.8 5.5 fusion.20
  859.9 58.6 %all-reduce.15.cloned.1.call-done = bf16[512,2048]{1,0:T(8,128)(2,1)} async-done(((bf16[512,2048]{1,0:T(8,128)(2,1)}), bf16[512,2048]{1,0:T(8,128)(2,1)}) %all-reduce.15.cloned.1.call-update) | async-done | bytes 2097168 | tf_op jit(solution)/shard_map/psum | solution.py:653
  918.5 3.1 fusion.13
  922.0 7.8 fusion.11
  944.2 30.4 %all-reduce.17.cloned.1.call-done = f32[256,643]{0,1:T(8,128)} async-done(((f32[256,643]{0,1:T(8,128)}), f32[256,643]{0,1:T(8,128)}) %all-reduce.17.cloned.1.call-update) | async-done | bytes 658448 | tf_op jit(solution)/shard_map/psum | solution.py:686
  (301 shorter events, 181.6 us)
Async XLA Ops:
  8.0 31.3 %copy-start = (bf16[2048,768]{1,0:T(8,128)(2,1)S(1)}, bf16[2048,768]{1,0:T(8,128)(2,1)}, u32[]{:S(2)}) copy-start(bf16[2048,768]{1,0:T(8,128)(2,1)} %param.23) | copy-start | bytes 9437188
  8.0 197.0 %all-reduce.9.cloned.1.call-start = ((), (), s32[]{:S(2)}) async-start(), calls=%async_computation.4 | async-start | bytes 4194304 | tf_op jit(solution)/shard_map/psum | solution.py:514
  11.6 27.7 %copy-start.66 = (f32[512]{0:T(512)}, f32[512]{0:T(512)S(1)}, u32[]{:S(2)}) copy-start(f32[512]{0:T(512)S(1)} %fusion.81) | copy-start | bytes 6148
  14.0 6.9 copy-start.62
  18.4 20.9 %copy-start.45 = (f32[2048]{0:T(1024)S(1)}, f32[2048]{0:T(1024)}, u32[]{:S(2)}) copy-start(f32[2048]{0:T(1024)} %param.22) | copy-start | bytes 24580
  20.9 29.8 %copy-start.27 = (f32[512,32]{1,0:T(8,128)}, f32[512,32]{1,0:T(8,128)S(1)}, u32[]{:S(2)}) copy-start(f32[512,32]{1,0:T(8,128)S(1)} %get-tuple-element.167) | copy-start | bytes 196612
  25.0 44.2 %collective-permute-start = (bf16[512,576]{0,1:T(8,128)(2,1)}, bf16[512,576]{0,1:T(8,128)(2,1)}, u32[]{:S(2)}, u32[]{:S(2)}) collective-permute-start(bf16[512,576]{0,1:T(8,128)(2,1)} %copy.157), channel_id=1, source_target_pairs={{0,16},{4,20},{8,24},{12,28},{1,17},{5,21},{9,25},{13,29},{2,18},{... | collective-permute-start | bytes 1769480 | tf_op jit(solution)/shard_map/ppermute | solution.py:394
  30.7 40.6 %collective-permute-start.1 = (bf16[512,576]{0,1:T(8,128)(2,1)}, bf16[512,576]{0,1:T(8,128)(2,1)}, u32[]{:S(2)}, u32[]{:S(2)}) collective-permute-start(bf16[512,576]{0,1:T(8,128)(2,1)} %copy.157), channel_id=1, source_target_pairs={{0,12},{4,16},{8,20},{12,24},{16,28},{1,13},{5,17},{9,21},{13,25},... | collective-permute-start | bytes 1769480 | tf_op jit(solution)/shard_map/ppermute | solution.py:394
  34.0 39.4 %collective-permute-start.2 = (bf16[512,576]{0,1:T(8,128)(2,1)}, bf16[512,576]{0,1:T(8,128)(2,1)}, u32[]{:S(2)}, u32[]{:S(2)}) collective-permute-start(bf16[512,576]{0,1:T(8,128)(2,1)} %copy.157), channel_id=1, source_target_pairs={{0,8},{4,12},{8,16},{12,20},{16,24},{20,28},{1,9},{5,13},{9,17},{1... | collective-permute-start | bytes 1769480 | tf_op jit(solution)/shard_map/ppermute | solution.py:394
  37.0 42.8 %collective-permute-start.3 = (bf16[512,576]{0,1:T(8,128)(2,1)}, bf16[512,576]{0,1:T(8,128)(2,1)}, u32[]{:S(2)}, u32[]{:S(2)}) collective-permute-start(bf16[512,576]{0,1:T(8,128)(2,1)} %copy.157), channel_id=1, source_target_pairs={{0,4},{4,8},{8,12},{12,16},{16,20},{20,24},{24,28},{1,5},{5,9},{9,... | collective-permute-start | bytes 1769480 | tf_op jit(solution)/shard_map/ppermute | solution.py:394
  76.8 7.3 copy-start.31
  82.0 6.1 copy-start.74
  114.0 100.9 %copy-start.43 = (f32[2048]{0:T(1024)S(1)}, f32[2048]{0:T(1024)}, u32[]{:S(2)}) copy-start(f32[2048]{0:T(1024)} %param.28) | copy-start | bytes 24580
  114.0 96.6 %all-gather.3.cloned.1.call-start = ((), (), s32[]{:S(2)}) async-start(), calls=%async_computation.5 | async-start | bytes 18874368 | tf_op jit(solution)/shard_map/all_gather | solution.py:474
  114.6 193.0 %all-gather.5.cloned.1.call-start = ((), (), s32[]{:S(2)}) async-start(), calls=%async_computation.6 | async-start | bytes 18874368 | tf_op jit(solution)/shard_map/all_gather | solution.py:520
  217.3 231.2 %reduce-scatter.5.cloned.1.call-start = ((), (), s32[]{:S(2)}) async-start(), calls=%async_computation.7 | async-start | bytes 9732096 | tf_op jit(solution)/shard_map/reduce_scatter | solution.py:441
  235.2 11.7 %copy-start.32 = (bf16[2048,64]{0,1:T(8,128)(2,1)S(1)}, bf16[2048,64]{0,1:T(8,128)(2,1)}, u32[]{:S(2)}) copy-start(bf16[2048,64]{0,1:T(8,128)(2,1)} %param.29) | copy-start | bytes 786436
  235.3 333.4 %reduce-scatter.7.cloned.1.call-start = ((), (), s32[]{:S(2)}) async-start(), calls=%async_computation.8 | async-start | bytes 18874368 | tf_op jit(solution)/shard_map/reduce_scatter | solution.py:592
  448.5 215.5 %all-reduce.11.cloned.1.call-start = ((), (), s32[]{:S(2)}) async-start(), calls=%async_computation.10 | async-start | bytes 4194304 | tf_op jit(solution)/shard_map/psum | solution.py:608
  526.0 20.1 %copy-start.23 = (bf16[8,640,384]{2,1,0:T(8,128)(2,1)S(1)}, bf16[8,640,384]{2,1,0:T(8,128)(2,1)}, u32[]{:S(2)}) copy-start(bf16[8,640,384]{2,1,0:T(8,128)(2,1)} %get-tuple-element.45) | copy-start | bytes 11796484
  575.8 88.3 %copy-start.44 = (f32[2048]{0:T(1024)S(1)}, f32[2048]{0:T(1024)}, u32[]{:S(2)}) copy-start(f32[2048]{0:T(1024)} %param.28) | copy-start | bytes 24580
  575.8 88.3 %copy-start.48 = (f32[512]{0:T(512)S(1)}, f32[512]{0:T(512)}, u32[]{:S(2)}) copy-start(f32[512]{0:T(512)} %copy-done.47) | copy-start | bytes 6148
  575.8 127.0 %reduce-scatter.9.cloned.1.call-start = ((), (), s32[]{:S(2)}) async-start(), calls=%async_computation.9 | async-start | bytes 18874368 | tf_op jit(solution)/shard_map/reduce_scatter | solution.py:441
  576.5 253.6 %all-reduce.13.cloned.1.call-start = ((), (), s32[]{:S(2)}) async-start(), calls=%async_computation.11 | async-start | bytes 4194304 | tf_op jit(solution)/shard_map/psum | solution.py:649
  577.2 91.7 %copy-start.61 = (f32[512]{0:T(512)S(1)}, f32[512]{0:T(512)}, u32[]{:S(2)}) copy-start(f32[512]{0:T(512)} %copy-done.60) | copy-start | bytes 6148
  668.9 62.8 %copy-start.64 = (f32[512]{0:T(512)}, f32[512]{0:T(512)S(1)}, u32[]{:S(2)}) copy-start(f32[512]{0:T(512)S(1)} %multiply_multiply_fusion.2) | copy-start | bytes 6148
  708.6 5.3 copy-start.20
  720.0 18.9 %collective-permute-start.4 = (bf16[512,576]{0,1:T(8,128)(2,1)}, bf16[512,576]{0,1:T(8,128)(2,1)}, u32[]{:S(2)}, u32[]{:S(2)}) collective-permute-start(bf16[512,576]{0,1:T(8,128)(2,1)} %copy.177), channel_id=1, source_target_pairs={{16,0},{20,4},{24,8},{28,12},{17,1},{21,5},{25,9},{29,13},{18,2},{... | collective-permute-start | bytes 1769480 | tf_op jit(solution)/shard_map/ppermute | solution.py:394
  723.4 17.8 %collective-permute-start.7 = (bf16[512,576]{0,1:T(8,128)(2,1)}, bf16[512,576]{0,1:T(8,128)(2,1)}, u32[]{:S(2)}, u32[]{:S(2)}) collective-permute-start(bf16[512,576]{0,1:T(8,128)(2,1)} %copy.183), channel_id=1, source_target_pairs={{4,0},{8,4},{12,8},{16,12},{20,16},{24,20},{28,24},{5,1},{9,5},{13... | collective-permute-start | bytes 1769480 | tf_op jit(solution)/shard_map/ppermute | solution.py:394
  726.8 23.0 %collective-permute-start.6 = (bf16[512,576]{0,1:T(8,128)(2,1)}, bf16[512,576]{0,1:T(8,128)(2,1)}, u32[]{:S(2)}, u32[]{:S(2)}) collective-permute-start(bf16[512,576]{0,1:T(8,128)(2,1)} %copy.181), channel_id=1, source_target_pairs={{8,0},{12,4},{16,8},{20,12},{24,16},{28,20},{9,1},{13,5},{17,9},{2... | collective-permute-start | bytes 1769480 | tf_op jit(solution)/shard_map/ppermute | solution.py:394
  730.2 23.7 %collective-permute-start.5 = (bf16[512,576]{0,1:T(8,128)(2,1)}, bf16[512,576]{0,1:T(8,128)(2,1)}, u32[]{:S(2)}, u32[]{:S(2)}) collective-permute-start(bf16[512,576]{0,1:T(8,128)(2,1)} %copy.179), channel_id=1, source_target_pairs={{12,0},{16,4},{20,8},{24,12},{28,16},{13,1},{17,5},{21,9},{25,13},... | collective-permute-start | bytes 1769480 | tf_op jit(solution)/shard_map/ppermute | solution.py:394
  738.8 179.7 %all-reduce.15.cloned.1.call-start = ((), (), s32[]{:S(2)}) async-start(), calls=%async_computation.12 | async-start | bytes 4194304 | tf_op jit(solution)/shard_map/psum | solution.py:653
  756.1 5.7 copy-start.24
  756.1 5.7 copy-start.28
  761.8 10.2 %copy-start.39 = (bf16[512,32]{1,0:T(8,128)(2,1)}, bf16[512,32]{1,0:T(8,128)(2,1)S(1)}, u32[]{:S(2)}) copy-start(bf16[512,32]{1,0:T(8,128)(2,1)S(1)} %get-tuple-element.157) | copy-start | bytes 98308
  762.2 6.0 copy-start.59
  830.2 101.4 %reduce-scatter.11.cloned.1.call-start = ((), (), s32[]{:S(2)}) async-start(), calls=%async_computation.13 | async-start | bytes 10616832 | tf_op jit(solution)/shard_map/reduce_scatter | solution.py:441
  837.7 7.1 copy-start.46
  844.7 5.6 copy-start.22
  844.8 6.7 copy-start.4
  844.8 6.7 copy-start.38
  844.8 6.7 copy-start.40
  844.8 6.6 copy-start.42
  844.8 6.6 copy-start.68
  856.2 118.5 %all-reduce.17.cloned.1.call-start = ((), (), s32[]{:S(2)}) async-start(), calls=%async_computation.14 | async-start | bytes 1327104 | tf_op jit(solution)/shard_map/psum | solution.py:686
  858.7 63.0 %copy-start.57 = (f32[512]{0:T(512)S(1)}, f32[512]{0:T(512)}, u32[]{:S(2)}) copy-start(f32[512]{0:T(512)} %copy-done.56) | copy-start | bytes 6148
  858.7 63.0 %copy-start.49 = (f32[512]{0:T(512)S(1)}, f32[512]{0:T(512)}, u32[]{:S(2)}) copy-start(f32[512]{0:T(512)} %copy-done.47) | copy-start | bytes 6148
  858.7 63.0 %copy-start.65 = (f32[512]{0:T(512)S(1)}, f32[512]{0:T(512)}, u32[]{:S(2)}) copy-start(f32[512]{0:T(512)} %copy-done.64) | copy-start | bytes 6148
  (48 other events, 130.0 us)
Sparse Core Ops, SparseCore 0:
  114.1 90.8 all-reduce.8
  575.9 88.1 all-reduce.10
  738.9 91.2 all-reduce.12
  833.0 85.4 all-reduce.14
  933.6 41.0 all-reduce.16
Sparse Core Ops, SparseCore 1:
  116.5 94.0 all-gather.2
  217.3 90.2 all-gather.4
  312.0 72.5 reduce-scatter.4
  448.6 117.4 reduce-scatter.6
  580.6 117.4 reduce-scatter.8
  856.3 75.3 reduce-scatter.10

commit v3 on v2

v3 whole, which is shorter than its diff:
```python
import functools

import jax
import jax.numpy as jnp
from jax import lax
from jax.experimental import pallas as pl
from jax.experimental.pallas import tpu as pltpu
from jax.sharding import PartitionSpec as P

DN = 128
DR = 64
DV = 128
KVR = 512
REACH = 4
SLOTS = 80
BF = jnp.bfloat16
F32 = jnp.float32
VMEM_BYTES = 60 * 1024 * 1024
epsilon = 1e-06


def mm(a, b, ca, cb):
    return lax.dot_general(a, b, (((ca,), (cb,)), ((), ())), preferred_element_type=F32)


def cost(flops, nbytes, trans=0):
    return pl.CostEstimate(flops=int(flops), bytes_accessed=int(nbytes), transcendentals=int(trans))


def smem():
    return pl.BlockSpec(memory_space=pltpu.SMEM)


def fixed(shape):
    return pl.BlockSpec(shape, lambda *at: (0,) * len(shape))


def params():
    return pltpu.CompilerParams(vmem_limit_bytes=VMEM_BYTES)


def attend_setup(
    head, heads, step, qp_ref, cos_ref, sin_ref, wx_ref, sq_ref, sk_ref, keys,
    q_ref, key_ref, v_ref, bias_ref,
):
    rows = qp_ref.shape[0]

    @pl.when(head == 0)
    def _():
        for at in range(0, rows, step):
            part = pl.ds(at, step)
            allowed = (sq_ref[part, 0:1] == sk_ref[0:1, :]) & (
                sk_ref[1:2, :] <= sq_ref[part, 1:2]
            )
            bias_ref[part, :] = jnp.where(allowed, 0.0, -1e30).astype(BF)
        for i, key in enumerate(keys):
            key_ref[i * rows : (i + 1) * rows, DN:] = key[:, KVR : KVR + DR]

    for k in range(heads):

        @pl.when(head == k)
        def _():
            at = k * (DN + DR)
            front = qp_ref[:, at + DN : at + DN + DR // 2]
            back = qp_ref[:, at + DN + DR // 2 : at + DN + DR]
            cosine, sine = cos_ref[...], sin_ref[...]
            q_ref[:, :DN] = qp_ref[:, at : at + DN].astype(BF)
            q_ref[:, DN : DN + DR // 2] = (front * cosine - back * sine).astype(BF)
            q_ref[:, DN + DR // 2 :] = (back * cosine + front * sine).astype(BF)

    for i, key in enumerate(keys):
        kv = mm(key[:, :KVR], wx_ref[...], 1, 0).astype(BF)
        key_ref[i * rows : (i + 1) * rows, :DN] = kv[:, :DN]
        v_ref[i * rows : (i + 1) * rows, :] = kv[:, DN:]


def attend_kernel(heads, step, qp_ref, cos_ref, sin_ref, wx_ref, sq_ref, sk_ref, *rest):
    keys, (o_ref, lse_ref, q_ref, key_ref, v_ref, bias_ref) = rest[:-6], rest[-6:]
    rows = qp_ref.shape[0]
    scale = (DN + DR) ** (-0.5)
    attend_setup(
        pl.program_id(0), heads, step, qp_ref, cos_ref, sin_ref, wx_ref, sq_ref, sk_ref, keys,
        q_ref, key_ref, v_ref, bias_ref,
    )
    for at in range(0, rows, step):
        part = pl.ds(at, step)
        s = mm(q_ref[part, :], key_ref[...], 1, 1) * scale + bias_ref[part, :].astype(F32)
        top = jnp.max(s, axis=-1, keepdims=True)
        p = jnp.exp(s - top)
        total = jnp.sum(p, axis=-1, keepdims=True)
        o_ref[part, :] = mm((p * (1.0 / total)).astype(BF), v_ref[...], 1, 0).astype(BF)
        lse_ref[0, part, :] = top + jnp.log(total)


def attend_specs(query_pre, cosine, w_expand, place_q, place_k, keys):
    return [
        fixed(query_pre.shape),
        fixed(cosine.shape),
        fixed(cosine.shape),
        pl.BlockSpec((KVR, DN + DV), lambda h: (0, h)),
        fixed(place_q.shape),
        fixed(place_k.shape),
    ], [fixed(keys[0].shape) for _ in keys]


def attend(query_pre, cosine, sine, w_expand, place_q, place_k, keys):
    rows = query_pre.shape[0]
    heads = query_pre.shape[1] // (DN + DR)
    window = rows * len(keys)
    specs, key_specs = attend_specs(query_pre, cosine, w_expand, place_q, place_k, keys)
    return pl.pallas_call(
        functools.partial(attend_kernel, heads, rows // 2),
        name="attend",
        grid=(heads,),
        in_specs=specs + key_specs,
        out_specs=[
            pl.BlockSpec((rows, DV), lambda h: (0, h)),
            pl.BlockSpec((1, rows, 1), lambda h: (h, 0, 0)),
        ],
        out_shape=[
            jax.ShapeDtypeStruct((rows, heads * DV), BF),
            jax.ShapeDtypeStruct((heads, rows, 1), F32),
        ],
        scratch_shapes=[
            pltpu.VMEM((rows, DN + DR), BF),
            pltpu.VMEM((window, DN + DR), BF),
            pltpu.VMEM((window, DV), BF),
            pltpu.VMEM((rows, window), BF),
        ],
        compiler_params=params(),
        cost_estimate=cost(
            2 * heads * window * (rows * 384 + KVR * 256), 2 * window * 640, heads * rows * window
        ),
    )(query_pre, cosine, sine, w_expand, place_q, place_k, *keys)


def attend_back_kernel(
    heads, step, count, qp_ref, cos_ref, sin_ref, wx_ref, sq_ref, sk_ref, lse_ref, do_ref, *rest
):
    keys, rest = rest[:count], rest[count:]
    dq_ref, gx_ref = rest[:2]
    grads = rest[2 : 2 + count]
    q_ref, key_ref, v_ref, bias_ref, dk_ref, dv_ref, dkv_ref, acc_ref, dqs_ref = rest[2 + count :]
    rows = qp_ref.shape[0]
    head = pl.program_id(0)
    scale = (DN + DR) ** (-0.5)
    attend_setup(
        head, heads, step, qp_ref, cos_ref, sin_ref, wx_ref, sq_ref, sk_ref, keys,
        q_ref, key_ref, v_ref, bias_ref,
    )

    @pl.when(head == 0)
    def _():
        acc_ref[...] = jnp.zeros_like(acc_ref)

    for at in range(0, rows, step):
        part = pl.ds(at, step)
        q = q_ref[part, :]
        do = do_ref[part, :]
        s = mm(q, key_ref[...], 1, 1) * scale + bias_ref[part, :].astype(F32)
        p = jnp.exp(s - lse_ref[0, part, :])
        dp = mm(do, v_ref[...], 1, 1)
        ds = (p * (dp - jnp.sum(p * dp, axis=-1, keepdims=True))).astype(BF)
        dqs_ref[part, :] = mm(ds, key_ref[...], 1, 0) * scale
        dk = mm(ds, q, 0, 0) * scale
        dv = mm(p.astype(BF), do, 0, 0)
        if at == 0:
            dk_ref[...] = dk
            dv_ref[...] = dv
        else:
            dk_ref[...] += dk
            dv_ref[...] += dv
    dkv_ref[:, :DN] = dk_ref[:, :DN].astype(BF)
    dkv_ref[:, DN:] = dv_ref[...].astype(BF)
    acc_ref[:, :KVR] += mm(dkv_ref[...], wx_ref[...], 1, 1)
    acc_ref[:, KVR : KVR + DR] += dk_ref[:, DN:]
    expand_grad = jnp.zeros((KVR, DN + DV), F32)
    for i, key in enumerate(keys):
        expand_grad += mm(key[:, :KVR], dkv_ref[i * rows : (i + 1) * rows, :], 0, 0)
    gx_ref[...] = expand_grad.astype(BF)
    for k in range(heads):

        @pl.when(head == k)
        def _():
            at = k * (DN + DR)
            front = dqs_ref[:, DN : DN + DR // 2]
            back = dqs_ref[:, DN + DR // 2 :]
            cosine, sine = cos_ref[...], sin_ref[...]
            dq_ref[:, at : at + DN] = dqs_ref[:, :DN].astype(BF)
            dq_ref[:, at + DN : at + DN + DR // 2] = (front * cosine + back * sine).astype(BF)
            dq_ref[:, at + DN + DR // 2 : at + DN + DR] = (back * cosine - front * sine).astype(BF)

    @pl.when(head == heads - 1)
    def _():
        for i, grad in enumerate(grads):
            grad[...] = acc_ref[i * rows : (i + 1) * rows, :].astype(grad.dtype)


def attend_back(query_pre, cosine, sine, w_expand, place_q, place_k, lse, attended_grad, keys):
    rows = query_pre.shape[0]
    heads = query_pre.shape[1] // (DN + DR)
    window = rows * len(keys)
    count = len(keys)
    specs, key_specs = attend_specs(query_pre, cosine, w_expand, place_q, place_k, keys)
    wide = keys[0].shape[1]
    return pl.pallas_call(
        functools.partial(attend_back_kernel, heads, rows // 2, count),
        name="attend_back",
        grid=(heads,),
        in_specs=specs
        + [
            pl.BlockSpec((1, rows, 1), lambda h: (h, 0, 0)),
            pl.BlockSpec((rows, DV), lambda h: (0, h)),
        ]
        + key_specs,
        out_specs=[fixed(query_pre.shape), pl.BlockSpec((KVR, DN + DV), lambda h: (0, h))]
        + [fixed((rows, wide)) for _ in keys],
        out_shape=[
            jax.ShapeDtypeStruct(query_pre.shape, BF),
            jax.ShapeDtypeStruct(w_expand.shape, BF),
        ]
        + [jax.ShapeDtypeStruct((rows, wide), BF) for _ in keys[1:]]
        + [jax.ShapeDtypeStruct((rows, wide), F32)],
        scratch_shapes=[
            pltpu.VMEM((rows, DN + DR), BF),
            pltpu.VMEM((window, DN + DR), BF),
            pltpu.VMEM((window, DV), BF),
            pltpu.VMEM((rows, window), BF),
            pltpu.VMEM((window, DN + DR), F32),
            pltpu.VMEM((window, DV), F32),
            pltpu.VMEM((window, DN + DV), BF),
            pltpu.VMEM((window, wide), F32),
            pltpu.VMEM((rows, DN + DR), F32),
        ],
        compiler_params=params(),
        cost_estimate=cost(
            2 * heads * window * (rows * 1024 + KVR * 768), 4 * window * 640, heads * rows * window
        ),
    )(query_pre, cosine, sine, w_expand, place_q, place_k, lse, attended_grad, *keys)


def one_hot(slot_ref):
    experts, rows = slot_ref.shape[0], slot_ref.shape[-1]
    place = lax.broadcasted_iota(jnp.int32, (SLOTS, rows), 0)
    return jnp.concatenate(
        [(slot_ref[e, 0] == place).astype(F32).astype(BF) for e in range(experts)], axis=0
    )


def pick_kernel(slot_ref, x_ref, o_ref):
    o_ref[...] = mm(one_hot(slot_ref), x_ref[...], 1, 0).astype(BF).reshape(o_ref.shape)


def pick_route_kernel(count, first_ref, slot_ref, x_ref, w_ref, o_ref, p_ref, g_ref):
    x = x_ref[...]
    logits = mm(x, w_ref[...], 1, 1)
    lane = lax.broadcasted_iota(jnp.int32, logits.shape, 1)
    logits = jnp.where(lane < count, logits, -1e30)
    e = jnp.exp(logits - jnp.max(logits, axis=-1, keepdims=True))
    probs = e / jnp.sum(e, axis=-1, keepdims=True)
    p_ref[...] = probs
    high = probs.astype(BF)
    low = (probs - high.astype(F32)).astype(BF)
    chosen = one_hot(slot_ref)
    o_ref[...] = mm(chosen, x, 1, 0).astype(BF).reshape(o_ref.shape)
    taken = mm(chosen, high, 1, 0) + mm(chosen, low, 1, 0)
    lane = lax.broadcasted_iota(jnp.int32, (SLOTS, taken.shape[1]), 1)
    for i in range(slot_ref.shape[0]):
        part = taken[i * SLOTS : (i + 1) * SLOTS, :]
        g_ref[i, 0] = jnp.sum(
            jnp.where(lane == first_ref[0] + i, part, 0.0), axis=-1, keepdims=True
        )


def pick(slot, values):
    experts, blocks, _, rows = slot.shape
    width = values.shape[1]
    return pl.pallas_call(
        pick_kernel,
        name="pick",
        grid=(blocks,),
        in_specs=[
            pl.BlockSpec((experts, 1, 1, rows), lambda b: (0, b, 0, 0)),
            pl.BlockSpec((rows, width), lambda b: (b, 0)),
        ],
        out_specs=pl.BlockSpec((experts, 1, SLOTS, width), lambda b: (0, b, 0, 0)),
        out_shape=jax.ShapeDtypeStruct((experts, blocks, SLOTS, width), BF),
        compiler_params=params(),
        cost_estimate=cost(
            2 * experts * blocks * SLOTS * rows * width,
            2 * blocks * width * (rows + experts * SLOTS),
        ),
    )(slot, values)


def pick_route(first, slot, values, router_rows, count):
    experts, blocks, _, rows = slot.shape
    width = values.shape[1]
    lanes = router_rows.shape[0]
    return pl.pallas_call(
        functools.partial(pick_route_kernel, count),
        name="pick_route",
        grid=(blocks,),
        in_specs=[
            smem(),
            pl.BlockSpec((experts, 1, 1, rows), lambda b: (0, b, 0, 0)),
            pl.BlockSpec((rows, width), lambda b: (b, 0)),
            fixed(router_rows.shape),
        ],
        out_specs=[
            pl.BlockSpec((experts, 1, SLOTS, width), lambda b: (0, b, 0, 0)),
            pl.BlockSpec((rows, lanes), lambda b: (b, 0)),
            pl.BlockSpec((experts, 1, SLOTS, 1), lambda b: (0, b, 0, 0)),
        ],
        out_shape=[
            jax.ShapeDtypeStruct((experts, blocks, SLOTS, width), BF),
            jax.ShapeDtypeStruct((blocks * rows, lanes), F32),
            jax.ShapeDtypeStruct((experts, blocks, SLOTS, 1), F32),
        ],
        compiler_params=params(),
        cost_estimate=cost(
            2 * experts * blocks * SLOTS * rows * width,
            2 * blocks * width * (rows + experts * SLOTS),
        ),
    )(first, slot, values, router_rows)


def put_kernel(place_ref, r_ref, o_ref):
    o_ref[...] = mm(place_ref[0], r_ref[...].reshape(-1, r_ref.shape[-1]), 1, 0).astype(BF)


def put_route_kernel(first_ref, place_ref, r_ref, p_ref, pg_ref, w_ref, o_ref, lg_ref):
    experts, rows = pg_ref.shape[0], pg_ref.shape[3]
    by_expert = jnp.concatenate(
        [pg_ref[i, 0] for i in range(experts)] + [jnp.zeros((1, rows), F32)] * (-experts % 8), axis=0
    )
    high = by_expert.astype(BF)
    low = (by_expert - high.astype(F32)).astype(BF)
    probs = p_ref[...]
    shape = (by_expert.shape[0], probs.shape[1])
    expert = lax.broadcasted_iota(jnp.int32, shape, 0)
    lane = lax.broadcasted_iota(jnp.int32, shape, 1)
    spread = (lane == first_ref[0] + expert) & (expert < experts)
    spread = spread.astype(F32).astype(BF)
    grad = mm(high, spread, 0, 0) + mm(low, spread, 0, 0)
    back = (probs * (grad - jnp.sum(probs * grad, axis=-1, keepdims=True))).astype(BF)
    lg_ref[...] = back
    total = mm(place_ref[0], r_ref[...].reshape(-1, r_ref.shape[-1]), 1, 0)
    o_ref[...] = (total + mm(back, w_ref[...], 1, 0)).astype(BF)


def put_specs(places, picked):
    blocks, rows, slots = places.shape
    experts, width = picked.shape[0], picked.shape[3]
    return [
        pl.BlockSpec((1, rows, slots), lambda b: (b, 0, 0)),
        pl.BlockSpec((experts, 1, SLOTS, width), lambda b: (0, b, 0, 0)),
    ]


def put_cost(places, width):
    blocks, rows, slots = places.shape
    return cost(2 * blocks * slots * rows * width, 2 * blocks * width * (rows + slots))


def put(places, picked):
    blocks, rows, _ = places.shape
    width = picked.shape[3]
    return pl.pallas_call(
        put_kernel,
        name="put",
        grid=(blocks,),
        in_specs=put_specs(places, picked),
        out_specs=pl.BlockSpec((rows, width), lambda b: (b, 0)),
        out_shape=jax.ShapeDtypeStruct((blocks * rows, width), BF),
        compiler_params=params(),
        cost_estimate=put_cost(places, width),
    )(places, picked)


def put_route(first, places, picked, probs, probs_grad, router_rows):
    blocks, rows, _ = places.shape
    experts, width = picked.shape[0], picked.shape[3]
    lanes = probs.shape[1]
    return pl.pallas_call(
        put_route_kernel,
        name="put_route",
        grid=(blocks,),
        in_specs=[smem()]
        + put_specs(places, picked)
        + [
            pl.BlockSpec((rows, lanes), lambda b: (b, 0)),
            pl.BlockSpec((experts, 1, 1, rows), lambda b: (0, b, 0, 0)),
            fixed(router_rows.shape),
        ],
        out_specs=[
            pl.BlockSpec((rows, width), lambda b: (b, 0)),
            pl.BlockSpec((rows, lanes), lambda b: (b, 0)),
        ],
        out_shape=[
            jax.ShapeDtypeStruct((blocks * rows, width), BF),
            jax.ShapeDtypeStruct((blocks * rows, lanes), BF),
        ],
        compiler_params=params(),
        cost_estimate=put_cost(places, width),
    )(first, places, picked, probs, probs_grad, router_rows)


def down_back_kernel(x_ref, w_ref, o_ref):
    ff = w_ref.shape[1]
    wide = o_ref.shape[-1]
    back = mm(x_ref[...].reshape(-1, x_ref.shape[-1]), w_ref[0], 1, 1)
    o_ref[0, :, :ff] = back
    if wide > ff:
        o_ref[0, :, ff:] = jnp.zeros((o_ref.shape[1], wide - ff), F32)


def down_back(rows, down):
    experts, blocks, slots, width = rows.shape
    ff = down.shape[1]
    wide = -(-ff // 128) * 128
    count = blocks * slots
    return pl.pallas_call(
        down_back_kernel,
        name="down_back",
        grid=(experts,),
        in_specs=[
            pl.BlockSpec((1, blocks, slots, width), lambda e: (e, 0, 0, 0)),
            pl.BlockSpec((1, ff, width), lambda e: (e, 0, 0)),
        ],
        out_specs=pl.BlockSpec((1, count, wide), lambda e: (e, 0, 0)),
        out_shape=jax.ShapeDtypeStruct((experts, count, wide), F32),
        compiler_params=params(),
        cost_estimate=cost(
            2 * experts * count * width * ff,
            experts * (2 * count * width + 2 * ff * width + 4 * count * wide),
        ),
    )(rows, down)


def row_out_kernel(x_ref, w_ref, o_ref):
    ff = w_ref.shape[1]
    o_ref[...] = mm(x_ref[0, :, :ff], w_ref[0], 1, 0).astype(BF).reshape(o_ref.shape)


def row_out(active, down, blocks):
    experts, count, wide = active.shape
    ff, width = down.shape[1:]
    slots = count // blocks
    return pl.pallas_call(
        row_out_kernel,
        name="row_out",
        grid=(experts,),
        in_specs=[
            pl.BlockSpec((1, count, wide), lambda e: (e, 0, 0)),
            pl.BlockSpec((1, ff, width), lambda e: (e, 0, 0)),
        ],
        out_specs=pl.BlockSpec((1, blocks, slots, width), lambda e: (e, 0, 0, 0)),
        out_shape=jax.ShapeDtypeStruct((experts, blocks, slots, width), BF),
        compiler_params=params(),
        cost_estimate=cost(
            2 * experts * count * width * ff,
            2 * experts * (count * width + ff * width + count * wide),
        ),
    )(active, down)


def expert_kernel(
    x_ref, gate_ref, up_ref, back_ref, slot_ref, sg_ref,
    ga_ref, dg_ref, du_ref, dx_ref, pg_ref, w_ref, d_ref,
):
    ff = gate_ref.shape[1]
    wide = back_ref.shape[2]
    blocks, rows = slot_ref.shape[1], slot_ref.shape[3]

    @pl.when(pl.program_id(0) == 0)
    def _():
        w_ref[...] = jnp.zeros_like(w_ref)

    w_ref[:ff, :] = gate_ref[0]
    w_ref[wide : wide + ff, :] = up_ref[0]
    x = x_ref[...].reshape(-1, x_ref.shape[-1])
    both = mm(x, w_ref[...], 1, 1)
    a = both[:, :wide]
    b = both[:, wide:]
    place = lax.broadcasted_iota(jnp.int32, (SLOTS, rows), 0)
    slot_gate = sg_ref[...].reshape(-1, 1)
    back = back_ref[0]
    sig = jax.nn.sigmoid(a)
    swish = a * sig
    active = swish * b
    gate_grad = jnp.sum(active * back, axis=-1, keepdims=True)
    for i in range(blocks):
        part = gate_grad[i * SLOTS : (i + 1) * SLOTS, :]
        pg_ref[0, i] = jnp.sum(
            jnp.where(slot_ref[0, i] == place, part, 0.0), axis=0, keepdims=True
        )
    gated = back * slot_gate
    ga_ref[0] = (active * slot_gate).astype(BF)
    dg = (gated * b * (sig + swish * (1.0 - sig))).astype(BF)
    du = (gated * swish).astype(BF)
    dg_ref[0] = dg
    du_ref[0] = du
    d_ref[:, :wide] = dg
    d_ref[:, wide:] = du
    dx_ref[...] = mm(d_ref[...], w_ref[...], 1, 0).astype(BF).reshape(dx_ref.shape)


def expert_step(rows, gate_t, up_t, back, slot, slot_gates):
    experts, blocks, slots, width = rows.shape
    ff = gate_t.shape[1]
    wide = back.shape[2]
    count = blocks * slots
    whole = pl.BlockSpec((1, blocks, slots, width), lambda e: (e, 0, 0, 0))
    flat = lambda n: pl.BlockSpec((1, count, n), lambda e: (e, 0, 0))
    shape = lambda n, dtype: jax.ShapeDtypeStruct((experts, count, n), dtype)
    weight = pl.BlockSpec((1, ff, width), lambda e: (e, 0, 0))
    by_token = pl.BlockSpec((1,) + slot.shape[1:], lambda e: (e, 0, 0, 0))
    return pl.pallas_call(
        expert_kernel,
        name="expert_step",
        grid=(experts,),
        in_specs=[
            whole,
            weight,
            weight,
            flat(wide),
            by_token,
            pl.BlockSpec((1, blocks, slots, 1), lambda e: (e, 0, 0, 0)),
        ],
        out_specs=[flat(wide), flat(wide), flat(wide), whole, by_token],
        out_shape=[
            shape(wide, BF),
            shape(wide, BF),
            shape(wide, BF),
            jax.ShapeDtypeStruct(rows.shape, BF),
            jax.ShapeDtypeStruct(slot.shape, F32),
        ],
        scratch_shapes=[pltpu.VMEM((2 * wide, width), BF), pltpu.VMEM((count, 2 * wide), BF)],
        compiler_params=params(),
        cost_estimate=cost(
            8 * experts * count * width * wide,
            2 * experts * (2 * count * width + 2 * width * wide + 5 * count * wide),
            experts * count * wide,
        ),
    )(rows, gate_t, up_t, back, slot, slot_gates)


def dot(eq, a, b):
    return jnp.einsum(eq, a, b, preferred_element_type=F32)


def passed_along(shard, axis, by):
    peers = lax.axis_size(axis)
    pairs = [(i, i + by) for i in range(peers) if 0 <= i + by < peers]
    return lax.ppermute(shard, axis, pairs)


def normed(values, norm_gain):
    return (
        values * lax.rsqrt(jnp.mean(values * values, axis=-1, keepdims=True) + epsilon) * norm_gain
    )


def norm_backward(values, norm_gain, upstream):
    _, pullback = jax.vjp(normed, values, norm_gain)
    return pullback(upstream)


def rotate(values, cosine, sine):
    half = values.shape[-1] // 2
    front, back = values[..., :half], values[..., half:]
    return jnp.concatenate([front * cosine - back * sine, back * cosine + front * sine], axis=-1)


def rotate_back(upstream, cosine, sine):
    return rotate(upstream, cosine, -sine)


def silu_gate(gate_val, up_val):
    return gate_val * jax.nn.sigmoid(gate_val) * up_val


def silu_backward(gate_val, up_val, upstream):
    _, pullback = jax.vjp(silu_gate, gate_val, up_val)
    return pullback(upstream)


def rope_tables(seq_all, seq_here, index_here):
    starts = jnp.sum((seq_all[None, :] < seq_here[:, None]).astype(jnp.int32), axis=1)
    position = (index_here - starts).astype(F32)
    frequency = 10000.0 ** (-(jnp.arange(DR // 2, dtype=F32) * 2.0) / DR)
    angle = position[:, None] * frequency[None, :]
    return jnp.cos(angle), jnp.sin(angle)


def after(value, *others):
    return lax.optimization_barrier((value,) + others)[0]


def scatter_sum(parts):
    joined = parts if not isinstance(parts, list) else jnp.concatenate(parts, axis=1)
    return lax.psum_scatter(joined, "dp", scatter_dimension=0, tiled=True)


def tensor_sum(value):
    peers = lax.axis_size("tensor")
    rank = lax.axis_index("tensor")
    rows = value.shape[0] // peers
    piece = lambda at: lax.dynamic_slice_in_dim(value, at * rows, rows, 0)
    turn = lambda piece, by: lax.ppermute(
        piece, "tensor", [(i, (i + by) % peers) for i in range(peers)]
    )
    total = piece(rank).astype(F32)
    for by in range(1, peers):
        total = total + turn(piece((rank + by) % peers), by).astype(F32)
    mine = total.astype(BF)
    out = jnp.zeros(value.shape, F32)
    out = lax.dynamic_update_slice_in_dim(out, total, rank * rows, 0)
    for by in range(1, peers):
        other = turn(mine, by).astype(F32)
        out = lax.dynamic_update_slice_in_dim(out, other, (rank - by) % peers * rows, 0)
    return out


def shards(
    tokens,
    seq_ids,
    route_ids,
    cotangent,
    input_gain,
    w_query,
    w_latent,
    latent_gain,
    w_expand,
    w_out,
    middle_gain,
    w_router,
    expert_gate,
    expert_up,
    expert_down,
    shared_gate,
    shared_up,
    shared_down,
):
    devices = lax.axis_size("dp")
    rank_dp = lax.axis_index("dp")
    tok_rows, width = tokens.shape
    experts_local = expert_gate.shape[0]
    all_experts = w_router.shape[1]
    ff_local = expert_gate.shape[2]
    heads_local = w_query.shape[1] // (DN + DR)
    reach = min(REACH, devices - 1)
    window = (reach + 1) * tok_rows

    cot_all = lax.all_gather(cotangent, "dp", tiled=True)
    route_all = lax.all_gather(route_ids, "dp", tiled=True)

    index_here = rank_dp * tok_rows + jnp.arange(tok_rows, dtype=jnp.int32)
    seq_here = lax.dynamic_slice_in_dim(seq_ids, rank_dp * tok_rows, tok_rows, 0)
    cosine, sine = rope_tables(seq_ids, seq_here, index_here)
    key_index = (rank_dp - reach) * tok_rows + jnp.arange(window, dtype=jnp.int32)
    seq_padded = jnp.concatenate([jnp.full((reach * tok_rows,), -1, jnp.int32), seq_ids])
    seq_keys = lax.dynamic_slice_in_dim(seq_padded, rank_dp * tok_rows, window, 0)
    place_q = jnp.stack([seq_here, index_here], axis=1)
    place_k = jnp.stack([seq_keys, key_index], axis=0)

    token_features = tokens.astype(F32)
    grad_output = cotangent.astype(F32)
    hidden_in = normed(token_features, input_gain).astype(BF)
    latent_full = jnp.dot(hidden_in, w_latent, preferred_element_type=F32)
    latent_raw = latent_full[:, :KVR]
    latent = normed(latent_raw, latent_gain).astype(BF)
    rope_key = rotate(latent_full[:, KVR:], cosine, sine).astype(BF)
    fill = jnp.zeros((tok_rows, -(KVR + DR) % 128), BF)
    own_keys = jnp.concatenate([latent, rope_key, fill], axis=1)
    keys = [passed_along(own_keys, "dp", back) for back in range(reach, 0, -1)] + [own_keys]
    query_pre = jnp.dot(hidden_in, w_query, preferred_element_type=F32)
    attended, lse = attend(query_pre, cosine, sine, w_expand, place_q, place_k, keys)
    attention = lax.psum(
        jnp.dot(attended, w_out, preferred_element_type=F32).astype(BF), "tensor"
    )
    attention = after(attention, cot_all)
    middle = token_features + attention.astype(F32)
    hidden_mid = normed(middle, middle_gain).astype(BF)
    hidden_all = lax.all_gather(hidden_mid, "dp", tiled=True)

    local_ids = rank_dp * experts_local + jnp.arange(experts_local, dtype=jnp.int32)
    named = jnp.any(route_all[:, :, None] == local_ids[None, None, :], axis=1)
    named_block = named.reshape(devices, tok_rows, experts_local)
    before = jnp.tril(jnp.ones((tok_rows, tok_rows), BF), -1)
    rank_within = dot("ts,bse->bte", before, named_block.astype(BF))
    slot_of = jnp.where(named_block, rank_within, -1.0)
    slot = slot_of.astype(jnp.int32).transpose(2, 0, 1)[:, :, None, :]
    columns = jnp.arange(experts_local * SLOTS, dtype=jnp.int32)
    spread = (columns[None, :] // SLOTS == jnp.arange(experts_local, dtype=jnp.int32)[:, None]).astype(
        BF
    )
    places = (
        dot("bte,en->btn", slot_of.astype(BF), spread) == (columns % SLOTS).astype(F32)
    ).astype(BF)
    gate_t = expert_gate.swapaxes(1, 2)
    up_t = expert_up.swapaxes(1, 2)
    cot_rows = pick(slot, cot_all)
    back = down_back(cot_rows, expert_down)

    shared_gate_val = jnp.dot(hidden_mid, shared_gate, preferred_element_type=F32)
    shared_up_val = jnp.dot(hidden_mid, shared_up, preferred_element_type=F32)
    shared_active = silu_gate(shared_gate_val, shared_up_val).astype(BF)
    shared_result = jnp.dot(shared_active, shared_down, preferred_element_type=F32)
    shared_active_grad = dot("td,fd->tf", cotangent, shared_down)
    shared_gate_grad, shared_up_grad = silu_backward(
        shared_gate_val, shared_up_val, shared_active_grad
    )
    shared_gate_grad = shared_gate_grad.astype(BF)
    shared_up_grad = shared_up_grad.astype(BF)
    mid_from_shared = dot("tf,df->td", shared_gate_grad, shared_gate) + dot(
        "tf,df->td", shared_up_grad, shared_up
    )
    shared_grads = jnp.concatenate(
        [
            dot("td,tf->df", cotangent, shared_active).astype(BF),
            dot("td,tf->df", hidden_mid, shared_gate_grad).astype(BF),
            dot("td,tf->df", hidden_mid, shared_up_grad).astype(BF),
        ],
        axis=1,
    )

    hidden_all = after(hidden_all, back, shared_grads)
    first = (rank_dp * experts_local).astype(jnp.int32).reshape(1)
    router_rows = jnp.pad(w_router.T, ((0, -all_experts % 128), (0, 0)))
    rows, router_probs, slot_gates = pick_route(first, slot, hidden_all, router_rows, all_experts)
    shared_sums = scatter_sum(shared_grads)
    gated_active, gate_val_grad, up_val_grad, row_grad, probs_grad = expert_step(
        rows, gate_t, up_t, back, slot, slot_gates
    )
    mid_part, logit_grad = put_route(first, places, row_grad, router_probs, probs_grad, router_rows)
    mid_part = after(mid_part, shared_sums)
    mid_block = lax.psum_scatter(mid_part, "dp", scatter_dimension=0, tiled=True)
    grad_router = dot("td,te->de", hidden_all, logit_grad[:, :all_experts]).astype(BF)
    routed_part = put(places, row_out(gated_active, expert_down, devices))
    rows_flat = rows.reshape(experts_local, -1, width)
    grad_expert_down = dot(
        "ecf,ecd->efd",
        gated_active[..., :ff_local],
        cot_rows.reshape(experts_local, -1, width),
    )
    grad_expert_gate = dot("ecd,ecf->edf", rows_flat, gate_val_grad[..., :ff_local])
    grad_expert_up = dot("ecd,ecf->edf", rows_flat, up_val_grad[..., :ff_local])

    routed_block = scatter_sum(after(routed_part, mid_block))
    mid_block = after(
        mid_block, routed_part, grad_router, grad_expert_down, grad_expert_gate, grad_expert_up
    )
    mid_grad = lax.psum((mid_block.astype(F32) + mid_from_shared).astype(BF), "tensor")
    routed_block = after(routed_block, mid_grad)
    mid_grad = mid_grad.astype(F32)

    middle_from_norm, grad_middle_gain = norm_backward(middle, middle_gain, mid_grad)
    middle_grad = grad_output + middle_from_norm
    middle_low = middle_grad.astype(BF)
    attended_grad = dot("td,cd->tc", middle_low, w_out).astype(BF)
    query_grad, grad_expand, *window_grads = attend_back(
        query_pre, cosine, sine, w_expand, place_q, place_k, lse, attended_grad, keys
    )
    ff_part = (routed_block.astype(F32) + shared_result).astype(BF)
    window_grads = lax.optimization_barrier((*window_grads, ff_part))[:-1]
    keys_grad = window_grads[-1]
    for step in range(reach, 0, -1):
        keys_grad = keys_grad + passed_along(window_grads[reach - step], "dp", -step).astype(F32)
    latent_raw_grad, grad_latent_gain = norm_backward(latent_raw, latent_gain, keys_grad[:, :KVR])
    rope_raw_grad = rotate_back(keys_grad[:, KVR : KVR + DR], cosine, sine)
    latent_full_grad = jnp.concatenate([latent_raw_grad, rope_raw_grad], axis=-1).astype(BF)
    input_part = dot("tc,dc->td", query_grad, w_query) + dot(
        "tc,dc->td", latent_full_grad, w_latent
    )
    _, grad_input_gain = norm_backward(token_features, input_gain, input_part)

    feedforward = lax.psum(ff_part, "tensor")
    output = (middle + feedforward.astype(F32)).astype(BF)
    input_part, grad_input_gain = lax.optimization_barrier((input_part.astype(BF), grad_input_gain))
    input_part = after(input_part, feedforward)
    input_grad = lax.psum(input_part, "tensor").astype(F32)
    tensors = lax.axis_size("tensor")
    query_width = heads_local * (DN + DR)
    out_width = heads_local * DV
    expand_width = w_expand.shape[1] * KVR // width
    latent_width = KVR + DR
    late = scatter_sum(
        [
            dot("td,tc->dc", middle_low, attended).astype(BF),
            dot("td,tc->dc", hidden_in, query_grad).astype(BF),
            grad_expand.reshape(width, expand_width),
        ]
    )
    gains = jnp.concatenate(
        [
            grad_middle_gain[None, :] / tensors,
            grad_input_gain[None, :],
            jnp.repeat(grad_latent_gain, width // KVR)[None, :],
            jnp.zeros((61, width), F32),
        ],
        axis=0,
    )
    parts = scatter_sum(
        [dot("td,tc->dc", hidden_in, latent_full_grad).astype(BF), grad_router, gains.astype(BF).T]
    )
    parts = tensor_sum(parts)
    input_grad = after(input_grad, parts)
    token_from_norm, _ = norm_backward(token_features, input_gain, input_grad)
    token_grad = (middle_grad + token_from_norm).astype(BF)
    sw = shared_gate.shape[1]
    gain_at = latent_width + all_experts
    return (
        output,
        token_grad,
        parts[:, gain_at + 1],
        late[:, out_width : out_width + query_width].astype(F32),
        parts[:, :latent_width],
        parts[:: width // KVR, gain_at + 2],
        late[:, out_width + query_width :].astype(F32).reshape(KVR // devices, -1),
        late[:, :out_width].astype(F32).T,
        parts[:, gain_at],
        parts[:, latent_width:gain_at],
        grad_expert_gate,
        grad_expert_up,
        grad_expert_down,
        shared_sums[:, sw : 2 * sw].astype(F32),
        shared_sums[:, 2 * sw :].astype(F32),
        shared_sums[:, :sw].astype(F32).T,
    )


def solution(mesh):
    placed = (
        P("dp", None),
        P(),
        P("dp", None),
        P("dp", None),
        P(),
        P(None, "tensor"),
        P(),
        P(),
        P(None, "tensor"),
        P("tensor", None),
        P(),
        P(),
        P("dp", None, "tensor"),
        P("dp", None, "tensor"),
        P("dp", "tensor", None),
        P(None, "tensor"),
        P(None, "tensor"),
        P("tensor", None),
    )
    return jax.shard_map(
        shards,
        mesh=mesh,
        in_specs=placed,
        out_specs=(
            P("dp", None),
            P("dp", None),
            P("dp"),
            P("dp", "tensor"),
            P("dp", None),
            P("dp"),
            P("dp", "tensor"),
            P("tensor", "dp"),
            P("dp"),
            P("dp", None),
            P("dp", None, "tensor"),
            P("dp", None, "tensor"),
            P("dp", "tensor", None),
            P("dp", "tensor"),
            P("dp", "tensor"),
            P("tensor", "dp"),
        ),
        check_vma=False,
    )
```

time: 995 us -> 948 us (0.953)
  local copies, waits for them, and re-layouts: 112 us -> 43.9 us
  matrix products: 177 us -> 141 us
  Pallas kernels: 216 us -> 244 us
  waiting for transfers between devices: 361 us -> 388 us
    reduce_scatter x3 -> x4, waiting for transfers between devices: 1.87 us -> 67.8 us  [scatter_sum(): return lax.psum_scatter(joined, 'dp', scatter_dimension=0, tiled=True)]
    pallas_call x4 -> x5, Pallas kernels: 86.5 us -> 136 us  [the longest x1 43.1 us: attend_back(): pl.pallas_call(functools.partial(attend_back_kernel, heads, rows // 2, co...]
    psum x1, waiting for transfers between devices: 58.6 us -> 22.3 us  [shards(): input_grad = lax.psum(input_part, 'tensor').astype(F32)]
    psum x1, waiting for transfers between devices: 53.6 us -> 18.7 us  [shards(): feedforward = lax.psum(ff_part, 'tensor')]
    psum x1 -> x0, waiting for transfers between devices: 30.4 us -> none  [shards(): partial_sums = lax.psum(sums[:, at:gain_at + 3].astype(F32), 'tensor')]
    ppermute x0 -> x6, waiting for transfers between devices: none -> 29.6 us  [tensor_sum(): lax.ppermute(piece, 'tensor', [(i, (i + by) % peers) for i in range(peers)])]
    ppermute x8, waiting for transfers between devices: 15.1 us -> 44.2 us  [passed_along(): return lax.ppermute(shard, axis, pairs)]
    unnamed x164 -> x121, local copies, waits for them, and re-layouts: 27.5 us -> 7.98 us
  transfers between devices with their start and end apart: 19 -> 25, of which waited for: 11 -> 16; matrix products, arithmetic and copies ran while one was open for 29% -> 21% of each run, Pallas kernels for 20% -> 24%
where the time goes in v3:
time: 948 us; the launch traced here: 941 us
  waiting for transfers between devices  388 us (41%)
  Pallas kernels  244 us (26%)
  matrix products  141 us (15%)
  other arithmetic  71.6 us (8%)
  local copies, waits for them, and re-layouts  43.9 us (5%)
  starting transfers between devices  27.2 us (3%)
  between operations  16.5 us (2%)
    dot_general x18, matrix products, dot(): return jnp.einsum(eq, a, b, preferred_element_type=F32)  118 us
    psum x1, waiting for transfers between devices, shards(): lax.psum(jnp.dot(attended, w_out, preferred_element_type=F32).astype(BF),...  93.7 us
    psum x1, waiting for transfers between devices, shards(): lax.psum((mid_block.astype(F32) + mid_from_shared).astype(BF), 'tensor')  87.1 us
    reduce_scatter x4, waiting for transfers between devices, scatter_sum(): return lax.psum_scatter(joined, 'dp', scatter_dimension=0, tiled=True)  67.8 us
    pallas_call x1, Pallas kernels, expert_step(): pl.pallas_call(expert_kernel, name='expert_step', grid=(experts,), in_spe...  49.5 us
    ppermute x8, waiting for transfers between devices, passed_along(): return lax.ppermute(shard, axis, pairs)  44.2 us
    pallas_call x1, Pallas kernels, attend_back(): pl.pallas_call(functools.partial(attend_back_kernel, heads, rows // 2, co...  43.1 us
    ppermute x6, waiting for transfers between devices, tensor_sum(): lax.ppermute(piece, 'tensor', [(i, (i + by) % peers) for i in range(peers)])  29.6 us
  transfers between devices with their start and end apart: 25, of which 16 were waited for; matrix products, arithmetic and copies ran while one was open for 21% of the time, Pallas kernels for 24%

profile of v3, /device:TPU:0, one launch (start us, length us, event | category | flops | bytes accessed | tf_op | source)
XLA Modules:
  0.0 941.5 jit_solution(7424018298726473751)
XLA Ops:
  13.4 4.2 fusion.76
  24.9 4.4 collective-permute-start.2
  29.3 4.3 collective-permute-start.1
  37.7 4.6 fusion.78.qp_ref
  43.9 11.5 %collective-permute-done.1.rest_1_ = bf16[512,640]{1,0:T(8,128)(2,1)} collective-permute-done((bf16[512,640]{1,0:T(8,128)(2,1)}, bf16[512,640]{1,0:T(8,128)(2,1)}, u32[]{:S(2)}, u32[]{:S(2)}) %collective-permute-start.1) | collective-permute-done | bytes 655392 | tf_op jit(solution)/shard_map/ppermute | solution.py:556
  55.4 15.1 %collective-permute-done.rest_0_ = bf16[512,640]{1,0:T(8,128)(2,1)} collective-permute-done((bf16[512,640]{1,0:T(8,128)(2,1)}, bf16[512,640]{1,0:T(8,128)(2,1)}, u32[]{:S(2)}, u32[]{:S(2)}) %collective-permute-start) | collective-permute-done | bytes 655392 | tf_op jit(solution)/shard_map/ppermute | solution.py:556
  70.5 20.8 %attend.1 = (bf16[512,512]{1,0:T(8,128)(2,1)}, f32[4,512,1]{2,1,0:T(8,128)}) custom-call(f32[512,768]{1,0:T(8,128)} %fusion.78.qp_ref, f32[512,32]{1,0:T(8,128)} %get-tuple-element.192.cos_ref, f32[512,32]{1,0:T(8,128)} %get-tuple-element.191.sin_ref, bf16[512,1024]{1,0:T(8,128)(2,1)} %wx_ref.3, s32[512,2]{1,0:T(8,128)} %copy.89.sq_ref, ...), custom_call_target="tpu_custom_call" | custom-call | flops 6710886400 | bytes 3276800 | tf_op jit(solution)/shard_map/attend/pallas_call | solution.py:111
  91.2 4.3 convolution_convert_fusion.6
  96.2 93.7 %all-reduce.7.cloned.1.call-done = bf16[512,2048]{1,0:T(8,128)(2,1)} async-done(((bf16[512,2048]{1,0:T(8,128)(2,1)}), bf16[512,2048]{1,0:T(8,128)(2,1)}) %all-reduce.7.cloned.1.call-update) | async-done | bytes 2097168 | tf_op jit(solution)/shard_map/psum | solution.py:680
  190.0 5.5 all-gather.3.cloned.1.call-done.x_ref
  202.7 4.3 fusion.89
  216.3 3.9 pad_maximum_fusion
  220.9 9.4 all_gather.10
  232.4 3.9 compare_convert_fusion.place_ref
  236.3 19.5 %pick.1.x_ref = bf16[8,8,80,2048]{3,2,1,0:T(8,128)(2,1)} custom-call(s32[8,8,1,512]{3,2,1,0:T(1,128)} %broadcast_in_dim.36.slot_ref, bf16[4096,2048]{1,0:T(8,128)(2,1)} %all-gather.3.cloned.1.call-done.x_ref), custom_call_target="tpu_custom_call" | custom-call | flops 10737418240 | bytes 37748736 | tf_op jit(solution)/shard_map/pick/pallas_call | solution.py:278
  255.9 19.2 %down_back.1.back_ref = f32[8,640,384]{2,1,0:T(8,128)} custom-call(bf16[8,8,80,2048]{3,2,1,0:T(8,128)(2,1)} %pick.1.x_ref, bf16[8,352,2048]{2,1,0:T(8,128)(2,1)} %w_ref.3), custom_call_target="tpu_custom_call" | custom-call | flops 7381975040 | bytes 40370176 | tf_op jit(solution)/shard_map/down_back/pallas_call | solution.py:423
  275.0 17.4 %all-gather.5.cloned.1.call-done.x_ref = bf16[4096,2048]{1,0:T(8,128)(2,1)} async-done(((bf16[512,2048]{1,0:T(8,128)(2,1)}), bf16[4096,2048]{1,0:T(8,128)(2,1)}) %all-gather.5.cloned.1.call-update) | async-done | bytes 16777232 | tf_op jit(solution)/shard_map/all_gather | solution.py:686
  292.4 25.0 %pick_route.1 = (bf16[8,8,80,2048]{3,2,1,0:T(8,128)(2,1)}, f32[4096,128]{1,0:T(8,128)}, f32[8,8,80,1]{3,2,1,0:T(8,128)}) custom-call(s32[1]{0:T(128)} %bitcast.4.first_ref, s32[8,8,1,512]{3,2,1,0:T(1,128)} %broadcast_in_dim.36.slot_ref, bf16[4096,2048]{1,0:T(8,128)(2,1)} %all-gather.5.cloned.1.call-done.x_ref, bf16[128,2048]{1,0:T(8,128)(2,1)} %pad.5.w_ref), custom_call_target="tpu_custom_call" | custom-call | flops 10737418240 | bytes 37748736 | tf_op jit(solution)/shard_map/pick_route/pallas_call | solution.py:300
  317.4 49.5 %expert_step.1 = (bf16[8,640,384]{2,1,0:T(8,128)(2,1)}, bf16[8,640,384]{2,1,0:T(8,128)(2,1)}, bf16[8,640,384]{2,1,0:T(8,128)(2,1)}, bf16[8,8,80,2048]{3,2,1,0:T(8,128)(2,1)}, f32[8,8,1,512]{3,2,1,0:T(1,128)}) custom-call(bf16[8,8,80,2048]{3,2,1,0:T(8,128)(2,1)} %get-tuple-element.53.x_ref, bf16[8,352,2048]{2,1,0:T(8,128)(2,1)} %bitcast.82, ...), custom_call_target="tpu_custom_call" | custom-call | flops 32212254720 | bytes 86769664 | tf_op jit(solution)/shard_map/expert_step/pallas_call | solution.py:519
  367.0 24.7 %put_route.1 = (bf16[4096,2048]{1,0:T(8,128)(2,1)}, bf16[4096,128]{1,0:T(8,128)(2,1)}) custom-call(s32[1]{0:T(128)} %bitcast.4.first_ref, bf16[8,512,640]{2,1,0:T(8,128)(2,1)} %compare_convert_fusion.place_ref, bf16[8,8,80,2048]{3,2,1,0:T(8,128)(2,1)} %get-tuple-element.56.r_ref, f32[4096,128]{1,0:T(8,128)} %get-tuple-element.57.p_ref, ...), custom_call_target="tpu_custom_call" | custom-call | flops 10737418240 | bytes 37748736 | tf_op jit(solution)/shard_map/put_route/pallas_call | solution.py:385
  391.8 6.0 fusion.90
  397.8 20.5 %row_out.1.r_ref = bf16[8,8,80,2048]{3,2,1,0:T(8,128)(2,1)} custom-call(bf16[8,640,384]{2,1,0:T(8,128)(2,1)} %get-tuple-element.55.x_ref, bf16[8,352,2048]{2,1,0:T(8,128)(2,1)} %w_ref.3), custom_call_target="tpu_custom_call" | custom-call | flops 7381975040 | bytes 36438016 | tf_op jit(solution)/shard_map/row_out/pallas_call | solution.py:450
  418.3 21.9 %put.1 = bf16[4096,2048]{1,0:T(8,128)(2,1)} custom-call(bf16[8,512,640]{2,1,0:T(8,128)(2,1)} %compare_convert_fusion.place_ref, bf16[8,8,80,2048]{3,2,1,0:T(8,128)(2,1)} %row_out.1.r_ref), custom_call_target="tpu_custom_call" | custom-call | flops 10737418240 | bytes 37748736 | tf_op jit(solution)/shard_map/put/pallas_call | solution.py:369
  440.1 9.6 %convolution_convert_fusion.7 = bf16[2048,64]{0,1:T(8,128)(2,1)S(1)} fusion(bf16[4096,2048]{1,0:T(8,128)(2,1)} %all-gather.5.cloned.1.call-done.x_ref, bf16[4096,128]{1,0:T(8,128)(2,1)} %get-tuple-element.62), kind=kOutput, calls=%fused_computation.47 | convolution fusion | flops 1073872896 | bytes 18087936 | tf_op jit(solution)/shard_map/td,te->de/dot_general | solution.py:550
  449.8 19.5 %fusion.17 = f32[8,352,2048]{2,1,0:T(8,128)} fusion(bf16[8,640,2048]{2,1,0:T(8,128)(2,1)} %bitcast.74, bf16[8,640,384]{2,1,0:T(8,128)(2,1)} %get-tuple-element.55.x_ref), kind=kOutput, calls=%fused_computation.35 | convolution fusion | flops 7381975040 | bytes 47972352 | tf_op jit(solution)/shard_map/ecf,ecd->efd/dot_general | solution.py:550
  469.3 20.1 %fusion.15 = f32[8,2048,352]{1,2,0:T(8,128)} fusion(bf16[8,640,2048]{2,1,0:T(8,128)(2,1)} %bitcast.75, bf16[8,640,384]{2,1,0:T(8,128)(2,1)} %get-tuple-element.63), kind=kOutput, calls=%fused_computation.33 | convolution fusion | flops 7381975040 | bytes 47972352 | tf_op jit(solution)/shard_map/ecd,ecf->edf/dot_general | solution.py:550
  489.4 22.4 %fusion.13 = f32[8,2048,352]{1,2,0:T(8,128)} fusion(bf16[8,640,2048]{2,1,0:T(8,128)(2,1)} %bitcast.76, bf16[8,640,384]{2,1,0:T(8,128)(2,1)S(1)} %copy-done.19), kind=kOutput, calls=%fused_computation.31 | convolution fusion | flops 7381975040 | bytes 47972352 | tf_op jit(solution)/shard_map/ecd,ecf->edf/dot_general | solution.py:550
  511.8 7.1 add_convert_fusion.2
  519.8 87.1 %all-reduce.9.cloned.1.call-done = bf16[512,2048]{1,0:T(8,128)(2,1)} async-done(((bf16[512,2048]{1,0:T(8,128)(2,1)}), bf16[512,2048]{1,0:T(8,128)(2,1)}) %all-reduce.9.cloned.1.call-update) | async-done | bytes 2097168 | tf_op jit(solution)/shard_map/psum | solution.py:755
  606.9 4.8 fusion.7
  611.8 4.9 convolution_convert_fusion.8.do_ref
  616.6 43.1 %attend_back.1 = (bf16[512,768]{1,0:T(8,128)(2,1)}, bf16[512,1024]{1,0:T(8,128)(2,1)}, bf16[512,640]{1,0:T(8,128)(2,1)}, bf16[512,640]{1,0:T(8,128)(2,1)}, bf16[...) custom-call(f32[512,768]{1,0:T(8,128)} %fusion.78.qp_ref, ...), custom_call_target="tpu_custom_call" | custom-call | flops 18790481920 | bytes 6553600 | tf_op jit(solution)/shard_map/attend_back/pallas_call | solution.py:206
  659.8 5.8 add_convert_fusion.1
  670.6 3.9 convolution_convert_fusion
  677.1 11.2 %pad_maximum_fusion.1 = bf16[2048,1536]{0,1:T(8,128)(2,1)} fusion(bf16[2048,256]{0,1:T(8,128)(2,1)S(1)} %copy-done.18, bf16[2048,768]{0,1:T(8,128)(2,1)S(1)} %convolution_convert_fusion, bf16[2048,512]{0,1:T(8,128)(2,1)S(1)} %convolution_convert_fusion.5), kind=kLoop, calls=%fused_computation.8 | loop fusion | flops 18874368 | bytes 12582912 | tf_op jit(solution)/shard_map/concatenate | solution.py:602
  695.0 12.3 %collective-permute-done.4 = bf16[512,640]{1,0:T(8,128)(2,1)S(1)} collective-permute-done((bf16[512,640]{1,0:T(8,128)(2,1)}, bf16[512,640]{1,0:T(8,128)(2,1)S(1)}, u32[]{:S(2)}, u32[]{:S(2)}) %collective-permute-start.4) | collective-permute-done | bytes 655392 | tf_op jit(solution)/shard_map/ppermute | solution.py:556
  707.4 3.6 collective-permute-done.6
  723.0 3.9 fusion.5
  733.0 18.7 %all-reduce.11.cloned.1.call-done = bf16[512,2048]{1,0:T(8,128)(2,1)} async-done(((bf16[512,2048]{1,0:T(8,128)(2,1)}), bf16[512,2048]{1,0:T(8,128)(2,1)}) %all-reduce.11.cloned.1.call-update) | async-done | bytes 2097168 | tf_op jit(solution)/shard_map/psum | solution.py:779
  754.4 17.8 %reduce-scatter.14.cloned.1.call-done = bf16[256,1536]{0,1:T(8,128)(2,1)} async-done(((bf16[2048,1536]{0,1:T(8,128)(2,1)}), bf16[256,1536]{0,1:T(8,128)(2,1)}) %reduce-scatter.14.cloned.1.call-update) | async-done | bytes 786448 | tf_op jit(solution)/shard_map/reduce_scatter | solution.py:603
  774.1 50.0 %reduce-scatter.12.cloned.1.call-done = bf16[256,704]{0,1:T(8,128)(2,1)} async-done(((bf16[2048,704]{0,1:T(8,128)(2,1)}), bf16[256,704]{0,1:T(8,128)(2,1)}) %reduce-scatter.12.cloned.1.call-update) | async-done | bytes 360464 | tf_op jit(solution)/shard_map/reduce_scatter | solution.py:603
  834.8 6.8 collective-permute-done.10
  841.6 19.7 %collective-permute-done.9 = bf16[64,704]{0,1:T(8,128)(2,1)S(1)} collective-permute-done((bf16[64,704]{0,1:T(8,128)(2,1)S(1)}, bf16[64,704]{0,1:T(8,128)(2,1)S(1)}, u32[]{:S(2)}, u32[]{:S(2)}) %collective-permute-start.9) | collective-permute-done | bytes 90144 | tf_op jit(solution)/shard_map/ppermute | solution.py:611
  872.5 22.3 %all-reduce.13.cloned.1.call-done = bf16[512,2048]{1,0:T(8,128)(2,1)} async-done(((bf16[512,2048]{1,0:T(8,128)(2,1)}), bf16[512,2048]{1,0:T(8,128)(2,1)}) %all-reduce.13.cloned.1.call-update) | async-done | bytes 2097168 | tf_op jit(solution)/shard_map/psum | solution.py:783
  894.7 4.1 convert_element_type.206
  912.0 3.7 dynamic_update_slice.15
  921.8 3.6 fusion.12
  926.5 7.7 fusion.10
  (241 shorter events, 117.5 us)
Async XLA Ops:
  8.0 29.7 %copy-start = (bf16[2048,768]{1,0:T(8,128)(2,1)S(1)}, bf16[2048,768]{1,0:T(8,128)(2,1)}, u32[]{:S(2)}) copy-start(bf16[2048,768]{1,0:T(8,128)(2,1)} %param.23) | copy-start | bytes 9437188
  8.0 182.0 %all-reduce.7.cloned.1.call-start = ((), (), s32[]{:S(2)}) async-start(), calls=%async_computation.5 | async-start | bytes 4194304 | tf_op jit(solution)/shard_map/psum | solution.py:680
  8.1 10.6 %copy-start.52 = (f32[32]{0:T(128)}, f32[32]{0:T(128)S(1)}, u32[]{:S(2)}) copy-start(f32[32]{0:T(128)S(1)} %multiply_power_fusion) | copy-start | bytes 388
  10.9 26.8 %copy-start.48 = (f32[512]{0:T(512)}, f32[512]{0:T(512)S(1)}, u32[]{:S(2)}) copy-start(f32[512]{0:T(512)S(1)} %fusion.67) | copy-start | bytes 6148
  13.4 5.4 copy-start.37
  13.4 5.2 copy-start.43
  17.6 18.5 %copy-start.36 = (s32[4096]{0:T(1024)S(1)}, s32[4096]{0:T(1024)}, u32[]{:S(2)}) copy-start(s32[4096]{0:T(1024)} %param.19) | copy-start | bytes 49156
  17.6 20.1 %copy-start.27 = (f32[2048]{0:T(1024)S(1)}, f32[2048]{0:T(1024)}, u32[]{:S(2)}) copy-start(f32[2048]{0:T(1024)} %param.22) | copy-start | bytes 24580
  21.7 20.6 %collective-permute-start.3 = (bf16[512,640]{1,0:T(8,128)(2,1)}, bf16[512,640]{1,0:T(8,128)(2,1)}, u32[]{:S(2)}, u32[]{:S(2)}) collective-permute-start(bf16[512,640]{1,0:T(8,128)(2,1)} %maximum_maximum_fusion.rest_4_), channel_id=1, source_target_pairs={{0,4},{4,8},{8,12},{12,16},{16,20},{20,24},{24,28},{1,5},{5,9},{9,... | collective-permute-start | bytes 1966088 | tf_op jit(solution)/shard_map/ppermute | solution.py:556
  24.9 19.0 %collective-permute-start.2 = (bf16[512,640]{1,0:T(8,128)(2,1)}, bf16[512,640]{1,0:T(8,128)(2,1)}, u32[]{:S(2)}, u32[]{:S(2)}) collective-permute-start(bf16[512,640]{1,0:T(8,128)(2,1)} %maximum_maximum_fusion.rest_4_), channel_id=1, source_target_pairs={{0,8},{4,12},{8,16},{12,20},{16,24},{20,28},{1,9},{5,13},{9,17},{1... | collective-permute-start | bytes 1966088 | tf_op jit(solution)/shard_map/ppermute | solution.py:556
  29.3 26.1 %collective-permute-start.1 = (bf16[512,640]{1,0:T(8,128)(2,1)}, bf16[512,640]{1,0:T(8,128)(2,1)}, u32[]{:S(2)}, u32[]{:S(2)}) collective-permute-start(bf16[512,640]{1,0:T(8,128)(2,1)} %maximum_maximum_fusion.rest_4_), channel_id=1, source_target_pairs={{0,12},{4,16},{8,20},{12,24},{16,28},{1,13},{5,17},{9,21},{13,25},... | collective-permute-start | bytes 1966088 | tf_op jit(solution)/shard_map/ppermute | solution.py:556
  33.6 36.9 %collective-permute-start = (bf16[512,640]{1,0:T(8,128)(2,1)}, bf16[512,640]{1,0:T(8,128)(2,1)}, u32[]{:S(2)}, u32[]{:S(2)}) collective-permute-start(bf16[512,640]{1,0:T(8,128)(2,1)} %maximum_maximum_fusion.rest_4_), channel_id=1, source_target_pairs={{0,16},{4,20},{8,24},{12,28},{1,17},{5,21},{9,25},{13,29},{2,18},{... | collective-permute-start | bytes 1966088 | tf_op jit(solution)/shard_map/ppermute | solution.py:556
  95.6 104.1 %copy-start.25 = (f32[2048]{0:T(1024)S(1)}, f32[2048]{0:T(1024)}, u32[]{:S(2)}) copy-start(f32[2048]{0:T(1024)} %param.28) | copy-start | bytes 24580
  95.6 99.9 %all-gather.3.cloned.1.call-start = ((), (), s32[]{:S(2)}) async-start(), calls=%async_computation.6 | async-start | bytes 18874368 | tf_op jit(solution)/shard_map/all_gather | solution.py:656
  96.2 196.2 %all-gather.5.cloned.1.call-start = ((), (), s32[]{:S(2)}) async-start(), calls=%async_computation.7 | async-start | bytes 18874368 | tf_op jit(solution)/shard_map/all_gather | solution.py:686
  202.1 189.6 %reduce-scatter.6.cloned.1.call-start = ((), (), s32[]{:S(2)}) async-start(), calls=%async_computation.8 | async-start | bytes 9732096 | tf_op jit(solution)/shard_map/reduce_scatter | solution.py:603
  220.2 11.4 %copy-start.23 = (bf16[2048,64]{0,1:T(8,128)(2,1)S(1)}, bf16[2048,64]{0,1:T(8,128)(2,1)}, u32[]{:S(2)}) copy-start(bf16[2048,64]{0,1:T(8,128)(2,1)} %param.29) | copy-start | bytes 786436
  220.2 291.6 %reduce-scatter.8.cloned.1.call-start = ((), (), s32[]{:S(2)}) async-start(), calls=%async_computation.9 | async-start | bytes 18874368 | tf_op jit(solution)/shard_map/reduce_scatter | solution.py:739
  391.8 215.1 %all-reduce.9.cloned.1.call-start = ((), (), s32[]{:S(2)}) async-start(), calls=%async_computation.11 | async-start | bytes 4194304 | tf_op jit(solution)/shard_map/psum | solution.py:755
  469.3 20.1 %copy-start.19 = (bf16[8,640,384]{2,1,0:T(8,128)(2,1)S(1)}, bf16[8,640,384]{2,1,0:T(8,128)(2,1)}, u32[]{:S(2)}) copy-start(bf16[8,640,384]{2,1,0:T(8,128)(2,1)} %get-tuple-element.64) | copy-start | bytes 11796484
  519.0 87.9 %copy-start.26 = (f32[2048]{0:T(1024)S(1)}, f32[2048]{0:T(1024)}, u32[]{:S(2)}) copy-start(f32[2048]{0:T(1024)} %param.28) | copy-start | bytes 24580
  519.0 87.9 %copy-start.30 = (f32[512]{0:T(512)S(1)}, f32[512]{0:T(512)}, u32[]{:S(2)}) copy-start(f32[512]{0:T(512)} %copy-done.29) | copy-start | bytes 6148
  519.0 140.8 %reduce-scatter.10.cloned.1.call-start = ((), (), s32[]{:S(2)}) async-start(), calls=%async_computation.10 | async-start | bytes 18874368 | tf_op jit(solution)/shard_map/reduce_scatter | solution.py:603
  519.7 92.0 %copy-start.42 = (f32[512]{0:T(512)S(1)}, f32[512]{0:T(512)}, u32[]{:S(2)}) copy-start(f32[512]{0:T(512)} %copy-done.41) | copy-start | bytes 6148
  519.8 231.9 %all-reduce.11.cloned.1.call-start = ((), (), s32[]{:S(2)}) async-start(), calls=%async_computation.12 | async-start | bytes 4194304 | tf_op jit(solution)/shard_map/psum | solution.py:779
  606.9 4.9 copy-start.2
  606.9 4.9 copy-start.8
  606.9 4.9 copy-start.14
  611.8 62.7 %copy-start.46 = (f32[512]{0:T(512)}, f32[512]{0:T(512)S(1)}, u32[]{:S(2)}) copy-start(f32[512]{0:T(512)S(1)} %multiply_multiply_fusion.2) | copy-start | bytes 6148
  665.7 4.9 copy-start.28
  665.7 4.9 copy-start.49
  665.7 106.5 %reduce-scatter.14.cloned.1.call-start = ((), (), s32[]{:S(2)}) async-start(), calls=%async_computation.15 | async-start | bytes 7077888 | tf_op jit(solution)/shard_map/reduce_scatter | solution.py:603
  688.4 24.6 %copy-start.35 = (f32[512]{0:T(512)S(1)}, f32[512]{0:T(512)}, u32[]{:S(2)}) copy-start(f32[512]{0:T(512)} %copy-done.34) | copy-start | bytes 6148
  688.4 24.6 %copy-start.44 = (f32[512]{0:T(512)S(1)}, f32[512]{0:T(512)}, u32[]{:S(2)}) copy-start(f32[512]{0:T(512)} %param.25) | copy-start | bytes 6148
  688.4 135.7 %reduce-scatter.12.cloned.1.call-start = ((), (), s32[]{:S(2)}) async-start(), calls=%async_computation.14 | async-start | bytes 3244032 | tf_op jit(solution)/shard_map/reduce_scatter | solution.py:603
  688.5 24.5 %copy-start.11 = (f32[512,576]{1,0:T(8,128)S(1)}, f32[512,576]{1,0:T(8,128)}, u32[]{:S(2)}) copy-start(f32[512,576]{1,0:T(8,128)} %copy-done.10) | copy-start | bytes 3538948
  688.5 18.9 %collective-permute-start.4 = (bf16[512,640]{1,0:T(8,128)(2,1)}, bf16[512,640]{1,0:T(8,128)(2,1)S(1)}, u32[]{:S(2)}, u32[]{:S(2)}) collective-permute-start(bf16[512,640]{1,0:T(8,128)(2,1)} %get-tuple-element.75), channel_id=1, source_target_pairs={{16,0},{20,4},{24,8},{28,12},{17,1},{21,5},{25,9},{29,13},{18,2},{... | collective-permute-start | bytes 1966088 | tf_op jit(solution)/shard_map/ppermute | solution.py:556
  689.9 17.5 %collective-permute-start.5 = (bf16[512,640]{1,0:T(8,128)(2,1)}, bf16[512,640]{1,0:T(8,128)(2,1)S(1)}, u32[]{:S(2)}, u32[]{:S(2)}) collective-permute-start(bf16[512,640]{1,0:T(8,128)(2,1)} %get-tuple-element.76), channel_id=1, source_target_pairs={{12,0},{16,4},{20,8},{24,12},{28,16},{13,1},{17,5},{21,9},{25,13},... | collective-permute-start | bytes 1966088 | tf_op jit(solution)/shard_map/ppermute | solution.py:556
  691.2 19.8 %collective-permute-start.6 = (bf16[512,640]{1,0:T(8,128)(2,1)}, bf16[512,640]{1,0:T(8,128)(2,1)S(1)}, u32[]{:S(2)}, u32[]{:S(2)}) collective-permute-start(bf16[512,640]{1,0:T(8,128)(2,1)} %get-tuple-element.77), channel_id=1, source_target_pairs={{8,0},{12,4},{16,8},{20,12},{24,16},{28,20},{9,1},{13,5},{17,9},{2... | collective-permute-start | bytes 1966088 | tf_op jit(solution)/shard_map/ppermute | solution.py:556
  692.5 18.5 %collective-permute-start.7 = (bf16[512,640]{1,0:T(8,128)(2,1)}, bf16[512,640]{1,0:T(8,128)(2,1)S(1)}, u32[]{:S(2)}, u32[]{:S(2)}) collective-permute-start(bf16[512,640]{1,0:T(8,128)(2,1)} %get-tuple-element.78), channel_id=1, source_target_pairs={{4,0},{8,4},{12,8},{16,12},{20,16},{24,20},{28,24},{5,1},{9,5},{13... | collective-permute-start | bytes 1966088 | tf_op jit(solution)/shard_map/ppermute | solution.py:556
  715.0 6.2 copy-start.55
  732.9 161.8 %all-reduce.13.cloned.1.call-start = ((), (), s32[]{:S(2)}) async-start(), calls=%async_computation.13 | async-start | bytes 4194304 | tf_op jit(solution)/shard_map/psum | solution.py:783
  825.4 9.3 collective-permute-start.8
  827.0 14.6 %collective-permute-start.10 = (bf16[64,704]{0,1:T(8,128)(2,1)S(1)}, bf16[64,704]{0,1:T(8,128)(2,1)S(1)}, u32[]{:S(2)}, u32[]{:S(2)}) collective-permute-start(bf16[64,704]{0,1:T(8,128)(2,1)S(1)} %get-tuple-element.187), channel_id=1, source_target_pairs={{0,3},{1,0},{2,1},{3,2},{4,7},{5,4},{6,5},{7,6},{8,11},{9,8},{10,9... | collective-permute-start | bytes 270344 | tf_op jit(solution)/shard_map/ppermute | solution.py:611
  829.3 32.0 %collective-permute-start.9 = (bf16[64,704]{0,1:T(8,128)(2,1)S(1)}, bf16[64,704]{0,1:T(8,128)(2,1)S(1)}, u32[]{:S(2)}, u32[]{:S(2)}) collective-permute-start(bf16[64,704]{0,1:T(8,128)(2,1)S(1)} %get-tuple-element.188), channel_id=1, source_target_pairs={{0,2},{1,3},{2,0},{3,1},{4,6},{5,7},{6,4},{7,5},{8,10},{9,11},{10,... | collective-permute-start | bytes 270344 | tf_op jit(solution)/shard_map/ppermute | solution.py:611
  863.0 48.0 %collective-permute-start.13 = (bf16[64,704]{0,1:T(8,128)(2,1)}, bf16[64,704]{0,1:T(8,128)(2,1)}, u32[]{:S(2)}, u32[]{:S(2)}) collective-permute-start(bf16[64,704]{0,1:T(8,128)(2,1)} %get-tuple-element.168), channel_id=1, source_target_pairs={{0,3},{1,0},{2,1},{3,2},{4,7},{5,4},{6,5},{7,6},{8,11},{9,8},{10,9... | collective-permute-start | bytes 270344 | tf_op jit(solution)/shard_map/ppermute | solution.py:611
  863.3 44.0 %collective-permute-start.12 = (bf16[64,704]{0,1:T(8,128)(2,1)}, bf16[64,704]{0,1:T(8,128)(2,1)}, u32[]{:S(2)}, u32[]{:S(2)}) collective-permute-start(bf16[64,704]{0,1:T(8,128)(2,1)} %get-tuple-element.168), channel_id=1, source_target_pairs={{0,2},{1,3},{2,0},{3,1},{4,6},{5,7},{6,4},{7,5},{8,10},{9,11},{10,... | collective-permute-start | bytes 270344 | tf_op jit(solution)/shard_map/ppermute | solution.py:611
  863.3 39.9 %collective-permute-start.11 = (bf16[64,704]{0,1:T(8,128)(2,1)}, bf16[64,704]{0,1:T(8,128)(2,1)}, u32[]{:S(2)}, u32[]{:S(2)}) collective-permute-start(bf16[64,704]{0,1:T(8,128)(2,1)} %get-tuple-element.168), channel_id=1, source_target_pairs={{0,1},{1,2},{2,3},{3,0},{4,5},{5,6},{6,7},{7,4},{8,9},{9,10},{10,1... | collective-permute-start | bytes 270344 | tf_op jit(solution)/shard_map/ppermute | solution.py:611
  (37 other events, 101.2 us)
Sparse Core Ops, SparseCore 0:
  95.7 94.2 all-reduce.6
  519.1 87.7 all-reduce.8
  665.8 85.7 all-reduce.10
  754.4 140.2 all-reduce.12
Sparse Core Ops, SparseCore 1:
  98.1 97.3 all-gather.2
  202.2 90.2 all-gather.4
  296.8 72.5 reduce-scatter.5
  391.8 116.1 reduce-scatter.7
  523.8 117.0 reduce-scatter.9
  688.5 83.7 reduce-scatter.13
  775.5 48.6 reduce-scatter.11

commit v4 on v3

--- a/solution.py
+++ b/solution.py
@@ -546,6 +546,73 @@
     )(rows, gate_t, up_t, back, slot, slot_gates)
 
 
+def norm_kernel(x_ref, add_ref, gain_ref, sum_ref, o_ref):
+    x = x_ref[...].astype(F32) + add_ref[...].astype(F32)
+    sum_ref[...] = x
+    scale = lax.rsqrt(jnp.mean(x * x, axis=-1, keepdims=True) + epsilon)
+    o_ref[...] = (x * scale * gain_ref[...]).astype(BF)
+
+
+def norm_sum(values, added, gain):
+    rows, width = values.shape
+    block = pl.BlockSpec((rows // 4, width), lambda i: (i, 0))
+    return pl.pallas_call(
+        norm_kernel,
+        name="norm_sum",
+        grid=(4,),
+        in_specs=[block, block, fixed((1, width))],
+        out_specs=[block, block],
+        out_shape=[
+            jax.ShapeDtypeStruct((rows, width), F32),
+            jax.ShapeDtypeStruct((rows, width), BF),
+        ],
+        compiler_params=params(),
+        cost_estimate=cost(8 * rows * width, 10 * rows * width),
+    )(values, added, gain.reshape(1, width))
+
+
+def norm_back_kernel(x_ref, up_ref, res_ref, gain_ref, *outs):
+    x = x_ref[...].astype(F32)
+    up = up_ref[...].astype(F32)
+    scale = lax.rsqrt(jnp.mean(x * x, axis=-1, keepdims=True) + epsilon)
+    scaled = x * scale
+    if len(outs) > 1:
+
+        @pl.when(pl.program_id(0) == 0)
+        def _():
+            outs[2][...] = jnp.zeros_like(outs[2])
+
+        outs[2][...] += jnp.sum(up * scaled, axis=0, keepdims=True)
+    up = up * gain_ref[...]
+    back = scale * (up - scaled * jnp.mean(up * scaled, axis=-1, keepdims=True))
+    total = res_ref[...].astype(F32) + back
+    outs[0][...] = total.astype(BF)
+    if len(outs) > 1:
+        outs[1][...] = total
+
+
+def norm_back(values, upstream, residual, gain, last):
+    rows, width = values.shape
+    block = pl.BlockSpec((rows // 4, width), lambda i: (i, 0))
+    specs = [block] if last else [block, block, fixed((1, width))]
+    shapes = [jax.ShapeDtypeStruct((rows, width), BF)]
+    if not last:
+        shapes += [
+            jax.ShapeDtypeStruct((rows, width), F32),
+            jax.ShapeDtypeStruct((1, width), F32),
+        ]
+    return pl.pallas_call(
+        norm_back_kernel,
+        name="norm_back",
+        grid=(4,),
+        in_specs=[block, block, block, fixed((1, width))],
+        out_specs=specs,
+        out_shape=shapes,
+        compiler_params=params(),
+        cost_estimate=cost(12 * rows * width, 12 * rows * width),
+    )(values, upstream, residual, gain.reshape(1, width))
+
+
 def dot(eq, a, b):
     return jnp.einsum(eq, a, b, preferred_element_type=F32)
 
@@ -592,6 +659,10 @@
     frequency = 10000.0 ** (-(jnp.arange(DR // 2, dtype=F32) * 2.0) / DR)
     angle = position[:, None] * frequency[None, :]
     return jnp.cos(angle), jnp.sin(angle)
+
+
+def swapped(value):
+    return lax.ppermute(value, "dp", [(i, i ^ 1) for i in range(lax.axis_size("dp"))])
 
 
 def after(value, *others):
@@ -615,12 +686,9 @@
     for by in range(1, peers):
         total = total + turn(piece((rank + by) % peers), by).astype(F32)
     mine = total.astype(BF)
-    out = jnp.zeros(value.shape, F32)
-    out = lax.dynamic_update_slice_in_dim(out, total, rank * rows, 0)
-    for by in range(1, peers):
-        other = turn(mine, by).astype(F32)
-        out = lax.dynamic_update_slice_in_dim(out, other, (rank - by) % peers * rows, 0)
-    return out
+    around = [turn(mine, by) for by in range(peers - 1, 0, -1)] + [mine]
+    both = jnp.concatenate(around + around[:-1], axis=0)
+    return lax.dynamic_slice_in_dim(both, (peers - 1 - rank) * rows, value.shape[0], 0)
 
 
 def shards(
@@ -650,8 +718,6 @@
     all_experts = w_router.shape[1]
     ff_local = expert_gate.shape[2]
     heads_local = w_query.shape[1] // (DN + DR)
-    reach = min(REACH, devices - 1)
-    window = (reach + 1) * tok_rows
 
     cot_all = lax.all_gather(cotangent, "dp", tiled=True)
     route_all = lax.all_gather(route_ids, "dp", tiled=True)
@@ -659,14 +725,19 @@
     index_here = rank_dp * tok_rows + jnp.arange(tok_rows, dtype=jnp.int32)
     seq_here = lax.dynamic_slice_in_dim(seq_ids, rank_dp * tok_rows, tok_rows, 0)
     cosine, sine = rope_tables(seq_ids, seq_here, index_here)
-    key_index = (rank_dp - reach) * tok_rows + jnp.arange(window, dtype=jnp.int32)
-    seq_padded = jnp.concatenate([jnp.full((reach * tok_rows,), -1, jnp.int32), seq_ids])
-    seq_keys = lax.dynamic_slice_in_dim(seq_padded, rank_dp * tok_rows, window, 0)
+    odd = rank_dp % 2
+    blocks = [rank_dp - 4, rank_dp - 2, (rank_dp - 2) ^ 1, rank_dp - 3 + 2 * odd, rank_dp]
+    seq_padded = jnp.concatenate([jnp.full((4 * tok_rows,), -1, jnp.int32), seq_ids])
+    seq_keys = jnp.concatenate(
+        [lax.dynamic_slice_in_dim(seq_padded, (at + 4) * tok_rows, tok_rows, 0) for at in blocks]
+    )
+    key_index = jnp.concatenate(
+        [at * tok_rows + jnp.arange(tok_rows, dtype=jnp.int32) for at in blocks]
+    )
     place_q = jnp.stack([seq_here, index_here], axis=1)
     place_k = jnp.stack([seq_keys, key_index], axis=0)
 
     token_features = tokens.astype(F32)
-    grad_output = cotangent.astype(F32)
     hidden_in = normed(token_features, input_gain).astype(BF)
     latent_full = jnp.dot(hidden_in, w_latent, preferred_element_type=F32)
     latent_raw = latent_full[:, :KVR]
@@ -674,15 +745,22 @@
     rope_key = rotate(latent_full[:, KVR:], cosine, sine).astype(BF)
     fill = jnp.zeros((tok_rows, -(KVR + DR) % 128), BF)
     own_keys = jnp.concatenate([latent, rope_key, fill], axis=1)
-    keys = [passed_along(own_keys, "dp", back) for back in range(reach, 0, -1)] + [own_keys]
+    before_two = passed_along(own_keys, "dp", 2)
+    before_four = passed_along(own_keys, "dp", 4)
+    keys = [
+        before_four,
+        before_two,
+        swapped(before_two),
+        swapped(jnp.where(odd == 0, own_keys, before_four)),
+        own_keys,
+    ]
     query_pre = jnp.dot(hidden_in, w_query, preferred_element_type=F32)
     attended, lse = attend(query_pre, cosine, sine, w_expand, place_q, place_k, keys)
     attention = lax.psum(
         jnp.dot(attended, w_out, preferred_element_type=F32).astype(BF), "tensor"
     )
     attention = after(attention, cot_all)
-    middle = token_features + attention.astype(F32)
-    hidden_mid = normed(middle, middle_gain).astype(BF)
+    middle, hidden_mid = norm_sum(tokens, attention, middle_gain)
     hidden_all = lax.all_gather(hidden_mid, "dp", tiled=True)
 
     local_ids = rank_dp * experts_local + jnp.arange(experts_local, dtype=jnp.int32)
@@ -748,26 +826,29 @@
     grad_expert_gate = dot("ecd,ecf->edf", rows_flat, gate_val_grad[..., :ff_local])
     grad_expert_up = dot("ecd,ecf->edf", rows_flat, up_val_grad[..., :ff_local])
 
-    routed_block = scatter_sum(after(routed_part, mid_block))
-    mid_block = after(
-        mid_block, routed_part, grad_router, grad_expert_down, grad_expert_gate, grad_expert_up
-    )
+    routed_block = scatter_sum(routed_part)
+    mid_block = after(mid_block, routed_part, grad_router, grad_expert_down)
     mid_grad = lax.psum((mid_block.astype(F32) + mid_from_shared).astype(BF), "tensor")
-    routed_block = after(routed_block, mid_grad)
-    mid_grad = mid_grad.astype(F32)
-
-    middle_from_norm, grad_middle_gain = norm_backward(middle, middle_gain, mid_grad)
-    middle_grad = grad_output + middle_from_norm
-    middle_low = middle_grad.astype(BF)
+    mid_grad = after(mid_grad, grad_expert_gate, grad_expert_up)
+
+    middle_low, middle_grad, grad_middle_gain = norm_back(
+        middle, mid_grad, cotangent, middle_gain, False
+    )
     attended_grad = dot("td,cd->tc", middle_low, w_out).astype(BF)
     query_grad, grad_expand, *window_grads = attend_back(
         query_pre, cosine, sine, w_expand, place_q, place_k, lse, attended_grad, keys
     )
+    routed_block = after(routed_block, grad_expand)
     ff_part = (routed_block.astype(F32) + shared_result).astype(BF)
     window_grads = lax.optimization_barrier((*window_grads, ff_part))[:-1]
-    keys_grad = window_grads[-1]
-    for step in range(reach, 0, -1):
-        keys_grad = keys_grad + passed_along(window_grads[reach - step], "dp", -step).astype(F32)
+    four_grad, two_grad, pair_grad, last_grad, keys_grad = window_grads
+    pair_grad = swapped(pair_grad)
+    last_grad = swapped(last_grad).astype(F32)
+    two_grad = (two_grad.astype(F32) + pair_grad.astype(F32)).astype(BF)
+    four_grad = (four_grad.astype(F32) + jnp.where(odd == 1, last_grad, 0.0)).astype(BF)
+    keys_grad = keys_grad + jnp.where(odd == 0, last_grad, 0.0)
+    keys_grad = keys_grad + passed_along(two_grad, "dp", -2).astype(F32)
+    keys_grad = keys_grad + passed_along(four_grad, "dp", -4).astype(F32)
     latent_raw_grad, grad_latent_gain = norm_backward(latent_raw, latent_gain, keys_grad[:, :KVR])
     rope_raw_grad = rotate_back(keys_grad[:, KVR : KVR + DR], cosine, sine)
     latent_full_grad = jnp.concatenate([latent_raw_grad, rope_raw_grad], axis=-1).astype(BF)
@@ -780,35 +861,34 @@
     output = (middle + feedforward.astype(F32)).astype(BF)
     input_part, grad_input_gain = lax.optimization_barrier((input_part.astype(BF), grad_input_gain))
     input_part = after(input_part, feedforward)
-    input_grad = lax.psum(input_part, "tensor").astype(F32)
+    input_grad = lax.psum(input_part, "tensor")
     tensors = lax.axis_size("tensor")
     query_width = heads_local * (DN + DR)
     out_width = heads_local * DV
     expand_width = w_expand.shape[1] * KVR // width
     latent_width = KVR + DR
+    gains = jnp.concatenate(
+        [
+            grad_middle_gain / tensors,
+            grad_input_gain[None, :],
+            jnp.repeat(grad_latent_gain, width // KVR)[None, :],
+            jnp.zeros((125, width), F32),
+        ],
+        axis=0,
+    )
+    parts = scatter_sum(
+        [dot("td,tc->dc", hidden_in, latent_full_grad).astype(BF), grad_router, gains.astype(BF).T]
+    )
     late = scatter_sum(
         [
             dot("td,tc->dc", middle_low, attended).astype(BF),
             dot("td,tc->dc", hidden_in, query_grad).astype(BF),
-            grad_expand.reshape(width, expand_width),
+            after(grad_expand, keys_grad).reshape(width, expand_width),
         ]
     )
-    gains = jnp.concatenate(
-        [
-            grad_middle_gain[None, :] / tensors,
-            grad_input_gain[None, :],
-            jnp.repeat(grad_latent_gain, width // KVR)[None, :],
-            jnp.zeros((61, width), F32),
-        ],
-        axis=0,
-    )
-    parts = scatter_sum(
-        [dot("td,tc->dc", hidden_in, latent_full_grad).astype(BF), grad_router, gains.astype(BF).T]
-    )
-    parts = tensor_sum(parts)
+    parts = tensor_sum(parts).astype(F32)
     input_grad = after(input_grad, parts)
-    token_from_norm, _ = norm_backward(token_features, input_gain, input_grad)
-    token_grad = (middle_grad + token_from_norm).astype(BF)
+    (token_grad,) = norm_back(tokens, input_grad, middle_grad, input_gain, True)
     sw = shared_gate.shape[1]
     gain_at = latent_width + all_experts
     return (

time: 948 us -> 897 us (0.946)
  waiting for transfers between devices: 388 us -> 346 us
  Pallas kernels: 244 us -> 264 us
  other arithmetic: 71.6 us -> 52.2 us
  local copies, waits for them, and re-layouts: 43.9 us -> 27.6 us
    reduce_scatter x4, waiting for transfers between devices: 67.8 us -> 0.06 us  [scatter_sum(): return lax.psum_scatter(joined, 'dp', scatter_dimension=0, tiled=True)]
    psum x1, waiting for transfers between devices: 87.1 us -> 32.5 us  [shards(): lax.psum((mid_block.astype(F32) + mid_from_shared).astype(BF), 'tensor')]
    reduce_scatter x1, waiting for transfers between devices: 0.01 us -> 39 us  [shards(): lax.psum_scatter(mid_part, 'dp', scatter_dimension=0, tiled=True)]
    psum x1, waiting for transfers between devices: 18.7 us -> 53.1 us  [shards(): feedforward = lax.psum(ff_part, 'tensor')]
    ppermute x6, waiting for transfers between devices: 29.6 us -> 50.2 us  [tensor_sum(): lax.ppermute(piece, 'tensor', [(i, (i + by) % peers) for i in range(peers)])]
    pallas_call x0 -> x3, Pallas kernels: none -> 19.6 us  [the longest x2 14 us: norm_back(): pl.pallas_call(norm_back_kernel, name='norm_back', grid=(4,), in_specs=[b...]
    dynamic_update_slice x4 -> x0, local copies, waits for them, and re-layouts: 13.1 us -> none  [the longest x3 9.64 us: tensor_sum(): lax.dynamic_update_slice_in_dim(out, other, (rank - by) % peers * rows, 0)]
    ppermute x8 -> x4, waiting for transfers between devices: 44.2 us -> 39 us  [passed_along(): return lax.ppermute(shard, axis, pairs)]
  transfers between devices with their start and end apart: 25 -> 25, of which waited for: 16 -> 16; matrix products, arithmetic and copies ran while one was open for 21% -> 21% of each run, Pallas kernels for 24% -> 27%
where the time goes in v4:
time: 897 us; the launch traced here: 891 us
  waiting for transfers between devices  346 us (39%)
  Pallas kernels  264 us (29%)
  matrix products  150 us (17%)
  other arithmetic  52.2 us (6%)
  local copies, waits for them, and re-layouts  27.6 us (3%)
  starting transfers between devices  25.7 us (3%)
  between operations  16.6 us (2%)
  blocking collectives  9.55 us (1%)
    dot_general x18, matrix products, dot(): return jnp.einsum(eq, a, b, preferred_element_type=F32)  126 us
    psum x1, waiting for transfers between devices, shards(): lax.psum(jnp.dot(attended, w_out, preferred_element_type=F32).astype(BF),...  87.3 us
    psum x1, waiting for transfers between devices, shards(): feedforward = lax.psum(ff_part, 'tensor')  53.1 us
    ppermute x6, waiting for transfers between devices, tensor_sum(): lax.ppermute(piece, 'tensor', [(i, (i + by) % peers) for i in range(peers)])  50.2 us
    pallas_call x1, Pallas kernels, expert_step(): pl.pallas_call(expert_kernel, name='expert_step', grid=(experts,), in_spe...  49.6 us
    pallas_call x1, Pallas kernels, attend_back(): pl.pallas_call(functools.partial(attend_back_kernel, heads, rows // 2, co...  43.5 us
    ppermute x4, waiting for transfers between devices, passed_along(): return lax.ppermute(shard, axis, pairs)  39 us
    reduce_scatter x1, waiting for transfers between devices, shards(): lax.psum_scatter(mid_part, 'dp', scatter_dimension=0, tiled=True)  39 us
  transfers between devices with their start and end apart: 25, of which 16 were waited for; matrix products, arithmetic and copies ran while one was open for 21% of the time, Pallas kernels for 27%

profile of v4, /device:TPU:0, one launch (start us, length us, event | category | flops | bytes accessed | tf_op | source)
XLA Modules:
  0.0 890.6 jit_solution(2597184514915902218)
XLA Ops:
  13.3 4.2 fusion.69
  21.4 8.4 collective-permute-start
  29.9 4.8 collective-permute-start.1
  35.3 22.1 %collective-permute-done.rest_0_ = bf16[512,640]{1,0:T(8,128)(2,1)} collective-permute-done((bf16[512,640]{1,0:T(8,128)(2,1)}, bf16[512,640]{1,0:T(8,128)(2,1)}, u32[]{:S(2)}, u32[]{:S(2)}) %collective-permute-start) | collective-permute-done | bytes 655392 | tf_op jit(solution)/shard_map/ppermute | solution.py:623
  60.9 4.6 fusion.71.qp_ref
  65.6 20.8 %attend.1 = (bf16[512,512]{1,0:T(8,128)(2,1)}, f32[4,512,1]{2,1,0:T(8,128)}) custom-call(f32[512,768]{1,0:T(8,128)} %fusion.71.qp_ref, f32[512,32]{1,0:T(8,128)} %get-tuple-element.200.cos_ref, f32[512,32]{1,0:T(8,128)} %get-tuple-element.199.sin_ref, bf16[512,1024]{1,0:T(8,128)(2,1)} %wx_ref.3, s32[512,2]{1,0:T(8,128)} %copy.89.sq_ref, ...), custom_call_target="tpu_custom_call" | custom-call | flops 6710886400 | bytes 3276800 | tf_op jit(solution)/shard_map/attend/pallas_call | solution.py:111
  86.3 4.3 convolution_convert_fusion.6
  91.3 87.3 %all-reduce.7.cloned.1.call-done.add_ref = bf16[512,2048]{1,0:T(8,128)(2,1)} async-done(((bf16[512,2048]{1,0:T(8,128)(2,1)}), bf16[512,2048]{1,0:T(8,128)(2,1)}) %all-reduce.7.cloned.1.call-update) | async-done | bytes 2097168 | tf_op jit(solution)/shard_map/psum | solution.py:759
  178.7 5.6 all-gather.3.cloned.1.call-done.x_ref
  184.3 5.5 norm_sum.1
  190.1 4.3 fusion.79
  204.0 4.1 pad_maximum_fusion
  208.9 9.6 %all_gather.10 = s32[4096,6]{0,1:T(8,128)S(1)} all-gather(s32[512,6]{0,1:T(8,128)S(1)} %copy-done.25), channel_id=1, replica_groups=mesh['dp'=8,'tensor'=4] {'dp'}, dimensions={0}, use_global_device_ids=true | all-gather | bytes 110592 | tf_op jit(solution)/shard_map/all_gather | solution.py:723
  220.6 3.9 compare_convert_fusion.place_ref
  224.4 19.5 %pick.1.x_ref = bf16[8,8,80,2048]{3,2,1,0:T(8,128)(2,1)} custom-call(s32[8,8,1,512]{3,2,1,0:T(1,128)} %broadcast_in_dim.61.slot_ref, bf16[4096,2048]{1,0:T(8,128)(2,1)} %all-gather.3.cloned.1.call-done.x_ref), custom_call_target="tpu_custom_call" | custom-call | flops 10737418240 | bytes 37748736 | tf_op jit(solution)/shard_map/pick/pallas_call | solution.py:278
  244.0 19.2 %down_back.1.back_ref = f32[8,640,384]{2,1,0:T(8,128)} custom-call(bf16[8,8,80,2048]{3,2,1,0:T(8,128)(2,1)} %pick.1.x_ref, bf16[8,352,2048]{2,1,0:T(8,128)(2,1)} %w_ref.3), custom_call_target="tpu_custom_call" | custom-call | flops 7381975040 | bytes 40370176 | tf_op jit(solution)/shard_map/down_back/pallas_call | solution.py:423
  263.1 17.0 %all-gather.5.cloned.1.call-done.x_ref = bf16[4096,2048]{1,0:T(8,128)(2,1)} async-done(((bf16[512,2048]{1,0:T(8,128)(2,1)}), bf16[4096,2048]{1,0:T(8,128)(2,1)}) %all-gather.5.cloned.1.call-update) | async-done | bytes 16777232 | tf_op jit(solution)/shard_map/all_gather | solution.py:764
  280.2 25.1 %pick_route.1 = (bf16[8,8,80,2048]{3,2,1,0:T(8,128)(2,1)}, f32[4096,128]{1,0:T(8,128)}, f32[8,8,80,1]{3,2,1,0:T(8,128)}) custom-call(s32[1]{0:T(128)} %bitcast.5.first_ref, s32[8,8,1,512]{3,2,1,0:T(1,128)} %broadcast_in_dim.61.slot_ref, bf16[4096,2048]{1,0:T(8,128)(2,1)} %all-gather.5.cloned.1.call-done.x_ref, bf16[128,2048]{1,0:T(8,128)(2,1)} %pad.5.w_ref), custom_call_target="tpu_custom_call" | custom-call | flops 10737418240 | bytes 37748736 | tf_op jit(solution)/shard_map/pick_route/pallas_call | solution.py:300
  305.3 49.6 %expert_step.1 = (bf16[8,640,384]{2,1,0:T(8,128)(2,1)}, bf16[8,640,384]{2,1,0:T(8,128)(2,1)}, bf16[8,640,384]{2,1,0:T(8,128)(2,1)}, bf16[8,8,80,2048]{3,2,1,0:T(8,128)(2,1)}, f32[8,8,1,512]{3,2,1,0:T(1,128)}) custom-call(bf16[8,8,80,2048]{3,2,1,0:T(8,128)(2,1)} %get-tuple-element.61.x_ref, bf16[8,352,2048]{2,1,0:T(8,128)(2,1)} %bitcast.89, ...), custom_call_target="tpu_custom_call" | custom-call | flops 32212254720 | bytes 86769664 | tf_op jit(solution)/shard_map/expert_step/pallas_call | solution.py:519
  354.8 24.8 %put_route.1 = (bf16[4096,2048]{1,0:T(8,128)(2,1)}, bf16[4096,128]{1,0:T(8,128)(2,1)}) custom-call(s32[1]{0:T(128)} %bitcast.5.first_ref, bf16[8,512,640]{2,1,0:T(8,128)(2,1)} %compare_convert_fusion.place_ref, bf16[8,8,80,2048]{3,2,1,0:T(8,128)(2,1)} %get-tuple-element.65.r_ref, f32[4096,128]{1,0:T(8,128)} %get-tuple-element.66.p_ref, ...), custom_call_target="tpu_custom_call" | custom-call | flops 10737418240 | bytes 37748736 | tf_op jit(solution)/shard_map/put_route/pallas_call | solution.py:385
  380.1 6.0 fusion.80
  386.1 20.3 %row_out.1.r_ref = bf16[8,8,80,2048]{3,2,1,0:T(8,128)(2,1)} custom-call(bf16[8,640,384]{2,1,0:T(8,128)(2,1)} %get-tuple-element.63.x_ref, bf16[8,352,2048]{2,1,0:T(8,128)(2,1)} %w_ref.3), custom_call_target="tpu_custom_call" | custom-call | flops 7381975040 | bytes 36438016 | tf_op jit(solution)/shard_map/row_out/pallas_call | solution.py:450
  406.4 21.3 %put.1 = bf16[4096,2048]{1,0:T(8,128)(2,1)} custom-call(bf16[8,512,640]{2,1,0:T(8,128)(2,1)} %compare_convert_fusion.place_ref, bf16[8,8,80,2048]{3,2,1,0:T(8,128)(2,1)} %row_out.1.r_ref), custom_call_target="tpu_custom_call" | custom-call | flops 10737418240 | bytes 37748736 | tf_op jit(solution)/shard_map/put/pallas_call | solution.py:369
  427.6 9.6 %convolution_convert_fusion.7 = bf16[2048,64]{0,1:T(8,128)(2,1)S(1)} fusion(bf16[4096,2048]{1,0:T(8,128)(2,1)} %all-gather.5.cloned.1.call-done.x_ref, bf16[4096,128]{1,0:T(8,128)(2,1)} %get-tuple-element.70), kind=kOutput, calls=%fused_computation.30 | convolution fusion | flops 1073872896 | bytes 18087936 | tf_op jit(solution)/shard_map/td,te->de/dot_general | solution.py:617
  437.3 19.4 %fusion.9 = f32[8,352,2048]{2,1,0:T(8,128)} fusion(bf16[8,640,2048]{2,1,0:T(8,128)(2,1)} %bitcast.78, bf16[8,640,384]{2,1,0:T(8,128)(2,1)} %get-tuple-element.63.x_ref), kind=kOutput, calls=%fused_computation.18 | convolution fusion | flops 7381975040 | bytes 47972352 | tf_op jit(solution)/shard_map/ecf,ecd->efd/dot_general | solution.py:617
  456.7 39.0 %reduce-scatter.10.cloned.1.call-done = bf16[512,2048]{1,0:T(8,128)(2,1)} async-done(((bf16[4096,2048]{1,0:T(8,128)(2,1)}), bf16[512,2048]{1,0:T(8,128)(2,1)}) %reduce-scatter.10.cloned.1.call-update) | async-done | bytes 2097168 | tf_op jit(solution)/shard_map/reduce_scatter | solution.py:817
  495.7 7.1 add_convert_fusion.2
  503.8 6.0 fusion.81
  509.8 25.2 %fusion.7 = f32[8,2048,352]{1,2,0:T(8,128)} fusion(bf16[8,640,2048]{2,1,0:T(8,128)(2,1)} %bitcast.79, bf16[8,640,384]{2,1,0:T(8,128)(2,1)S(1)} %copy-done.9), kind=kOutput, calls=%fused_computation.16 | convolution fusion | flops 7381975040 | bytes 47972352 | tf_op jit(solution)/shard_map/ecd,ecf->edf/dot_general | solution.py:617
  535.0 22.0 %fusion.5 = f32[8,2048,352]{1,2,0:T(8,128)} fusion(bf16[8,640,2048]{2,1,0:T(8,128)(2,1)} %bitcast.80, bf16[8,640,384]{2,1,0:T(8,128)(2,1)S(1)} %copy-done.8), kind=kOutput, calls=%fused_computation.14 | convolution fusion | flops 7381975040 | bytes 47972352 | tf_op jit(solution)/shard_map/ecd,ecf->edf/dot_general | solution.py:617
  556.9 32.5 %all-reduce.9.cloned.1.call-done.up_ref = bf16[512,2048]{1,0:T(8,128)(2,1)} async-done(((bf16[512,2048]{1,0:T(8,128)(2,1)}), bf16[512,2048]{1,0:T(8,128)(2,1)}) %all-reduce.9.cloned.1.call-update) | async-done | bytes 2097168 | tf_op jit(solution)/shard_map/psum | solution.py:831
  589.5 8.0 norm_back.2
  597.5 4.4 convolution_convert_fusion.8.do_ref
  601.8 43.5 %attend_back.1 = (bf16[512,768]{1,0:T(8,128)(2,1)}, bf16[512,1024]{1,0:T(8,128)(2,1)}, bf16[512,640]{1,0:T(8,128)(2,1)}, bf16[512,640]{1,0:T(8,128)(2,1)}, bf16[...) custom-call(f32[512,768]{1,0:T(8,128)} %fusion.71.qp_ref, ...), custom_call_target="tpu_custom_call" | custom-call | flops 18790481920 | bytes 6553600 | tf_op jit(solution)/shard_map/attend_back/pallas_call | solution.py:206
  645.4 4.9 add_convert_fusion.1
  660.7 13.4 %collective-permute-done.7 = bf16[512,640]{1,0:T(8,128)(2,1)} collective-permute-done((bf16[512,640]{1,0:T(8,128)(2,1)}, bf16[512,640]{1,0:T(8,128)(2,1)}, u32[]{:S(2)}, u32[]{:S(2)}) %collective-permute-start.7) | collective-permute-done | bytes 655392 | tf_op jit(solution)/shard_map/ppermute | solution.py:623
  683.5 3.9 fusion.47
  687.5 4.0 fusion.3
  697.6 53.1 %all-reduce.11.cloned.1.call-done = bf16[512,2048]{1,0:T(8,128)(2,1)} async-done(((bf16[512,2048]{1,0:T(8,128)(2,1)}), bf16[512,2048]{1,0:T(8,128)(2,1)}) %all-reduce.11.cloned.1.call-update) | async-done | bytes 2097168 | tf_op jit(solution)/shard_map/psum | solution.py:860
  750.8 4.5 convolution_convert_fusion.5
  763.9 5.9 pad_maximum_fusion.1
  777.9 7.3 collective-permute-done.8
  785.3 6.6 collective-permute-done.10
  791.8 18.4 %collective-permute-done.9 = bf16[64,768]{0,1:T(8,128)(2,1)S(1)} collective-permute-done((bf16[64,768]{0,1:T(8,128)(2,1)S(1)}, bf16[64,768]{0,1:T(8,128)(2,1)S(1)}, u32[]{:S(2)}, u32[]{:S(2)}) %collective-permute-start.9) | collective-permute-done | bytes 98336 | tf_op jit(solution)/shard_map/ppermute | solution.py:682
  815.2 3.8 add_convert_fusion
  821.1 15.8 %collective-permute-done.12 = bf16[64,768]{0,1:T(8,128)(2,1)S(1)} collective-permute-done((bf16[64,768]{0,1:T(8,128)(2,1)S(1)}, bf16[64,768]{0,1:T(8,128)(2,1)S(1)}, u32[]{:S(2)}, u32[]{:S(2)}) %collective-permute-start.12) | collective-permute-done | bytes 98336 | tf_op jit(solution)/shard_map/ppermute | solution.py:682
  847.5 18.6 %all-reduce.13.cloned.1.call-done.up_ref = bf16[512,2048]{1,0:T(8,128)(2,1)} async-done(((bf16[512,2048]{1,0:T(8,128)(2,1)}), bf16[512,2048]{1,0:T(8,128)(2,1)}) %all-reduce.13.cloned.1.call-update) | async-done | bytes 2097168 | tf_op jit(solution)/shard_map/psum | solution.py:864
  866.1 6.1 norm_back.3
  (200 shorter events, 99.0 us)
Async XLA Ops:
  8.0 52.9 %copy-start = (bf16[2048,768]{1,0:T(8,128)(2,1)S(1)}, bf16[2048,768]{1,0:T(8,128)(2,1)}, u32[]{:S(2)}) copy-start(bf16[2048,768]{1,0:T(8,128)(2,1)} %param.23) | copy-start | bytes 9437188
  8.0 170.6 %all-reduce.7.cloned.1.call-start = ((), (), s32[]{:S(2)}) async-start(), calls=%async_computation.5 | async-start | bytes 4194304 | tf_op jit(solution)/shard_map/psum | solution.py:759
  8.1 10.4 %copy-start.32 = (f32[32]{0:T(128)}, f32[32]{0:T(128)S(1)}, u32[]{:S(2)}) copy-start(f32[32]{0:T(128)S(1)} %multiply_power_fusion) | copy-start | bytes 388
  10.4 50.5 %copy-start.29 = (f32[512]{0:T(512)}, f32[512]{0:T(512)S(1)}, u32[]{:S(2)}) copy-start(f32[512]{0:T(512)S(1)} %add_rsqrt_fusion) | copy-start | bytes 6148
  13.3 5.0 copy-start.23
  18.3 11.6 %copy-start.19 = (f32[512]{0:T(512)}, f32[512]{0:T(512)S(1)}, u32[]{:S(2)}) copy-start(f32[512]{0:T(512)S(1)} %get-tuple-element.203) | copy-start | bytes 6148
  18.5 42.4 %copy-start.27 = (f32[2048]{0:T(1024)S(1)}, f32[2048]{0:T(1024)}, u32[]{:S(2)}) copy-start(f32[2048]{0:T(1024)} %param.22) | copy-start | bytes 24580
  21.4 35.9 %collective-permute-start = (bf16[512,640]{1,0:T(8,128)(2,1)}, bf16[512,640]{1,0:T(8,128)(2,1)}, u32[]{:S(2)}, u32[]{:S(2)}) collective-permute-start(bf16[512,640]{1,0:T(8,128)(2,1)} %maximum_maximum_fusion.rest_4_), channel_id=1, source_target_pairs={{0,16},{4,20},{8,24},{12,28},{1,17},{5,21},{9,25},{13,29},{2,18},{... | collective-permute-start | bytes 1966088 | tf_op jit(solution)/shard_map/ppermute | solution.py:623
  29.9 29.6 %collective-permute-start.1 = (bf16[512,640]{1,0:T(8,128)(2,1)}, bf16[512,640]{1,0:T(8,128)(2,1)}, u32[]{:S(2)}, u32[]{:S(2)}) collective-permute-start(bf16[512,640]{1,0:T(8,128)(2,1)} %maximum_maximum_fusion.rest_4_), channel_id=1, source_target_pairs={{0,8},{4,12},{8,16},{12,20},{16,24},{20,28},{1,9},{5,13},{9,17},{1... | collective-permute-start | bytes 1966088 | tf_op jit(solution)/shard_map/ppermute | solution.py:623
  59.5 6.0 collective-permute-start.3
  59.5 6.0 collective-permute-start.2
  90.7 93.5 %all-gather.3.cloned.1.call-start = ((), (), s32[]{:S(2)}) async-start(), calls=%async_computation.6 | async-start | bytes 18874368 | tf_op jit(solution)/shard_map/all_gather | solution.py:722
  91.3 188.8 %all-gather.5.cloned.1.call-start = ((), (), s32[]{:S(2)}) async-start(), calls=%async_computation.7 | async-start | bytes 18874368 | tf_op jit(solution)/shard_map/all_gather | solution.py:764
  189.8 189.8 %reduce-scatter.8.cloned.1.call-start = ((), (), s32[]{:S(2)}) async-start(), calls=%async_computation.9 | async-start | bytes 9732096 | tf_op jit(solution)/shard_map/reduce_scatter | solution.py:674
  190.0 4.3 copy-start.11
  208.2 11.6 %copy-start.15 = (bf16[2048,64]{0,1:T(8,128)(2,1)S(1)}, bf16[2048,64]{0,1:T(8,128)(2,1)}, u32[]{:S(2)}) copy-start(bf16[2048,64]{0,1:T(8,128)(2,1)} %param.29) | copy-start | bytes 786436
  208.2 287.5 %reduce-scatter.10.cloned.1.call-start = ((), (), s32[]{:S(2)}) async-start(), calls=%async_computation.10 | async-start | bytes 18874368 | tf_op jit(solution)/shard_map/reduce_scatter | solution.py:817
  379.6 209.8 %all-reduce.9.cloned.1.call-start = ((), (), s32[]{:S(2)}) async-start(), calls=%async_computation.11 | async-start | bytes 4194304 | tf_op jit(solution)/shard_map/psum | solution.py:831
  502.8 142.6 %reduce-scatter.6.cloned.1.call-start = ((), (), s32[]{:S(2)}) async-start(), calls=%async_computation.8 | async-start | bytes 18874368 | tf_op jit(solution)/shard_map/reduce_scatter | solution.py:674
  503.6 247.1 %all-reduce.11.cloned.1.call-start = ((), (), s32[]{:S(2)}) async-start(), calls=%async_computation.12 | async-start | bytes 4194304 | tf_op jit(solution)/shard_map/psum | solution.py:860
  503.8 6.0 copy-start.9
  509.8 25.2 %copy-start.8 = (bf16[8,640,384]{2,1,0:T(8,128)(2,1)S(1)}, bf16[8,640,384]{2,1,0:T(8,128)(2,1)}, u32[]{:S(2)}) copy-start(bf16[8,640,384]{2,1,0:T(8,128)(2,1)} %get-tuple-element.73) | copy-start | bytes 11796484
  650.3 2.4 collective-permute-start.4
  650.4 5.9 collective-permute-start.5
  650.8 9.8 %copy-start.26 = (f32[1,2048]{1,0:T(1,128)S(1)}, f32[1,2048]{1,0:T(1,128)}, u32[]{:S(2)}) copy-start(f32[1,2048]{1,0:T(1,128)} %get-tuple-element.91) | copy-start | bytes 24580
  655.1 19.0 %collective-permute-start.7 = (bf16[512,640]{1,0:T(8,128)(2,1)}, bf16[512,640]{1,0:T(8,128)(2,1)}, u32[]{:S(2)}, u32[]{:S(2)}) collective-permute-start(bf16[512,640]{1,0:T(8,128)(2,1)} %fusion.20), channel_id=1, source_target_pairs={{16,0},{20,4},{24,8},{28,12},{17,1},{21,5},{25,9},{29,13},{18,2},{... | collective-permute-start | bytes 1966088 | tf_op jit(solution)/shard_map/ppermute | solution.py:623
  658.6 19.0 %collective-permute-start.6 = (bf16[512,640]{1,0:T(8,128)(2,1)}, bf16[512,640]{1,0:T(8,128)(2,1)}, u32[]{:S(2)}, u32[]{:S(2)}) collective-permute-start(bf16[512,640]{1,0:T(8,128)(2,1)} %add_convert_fusion.3), channel_id=1, source_target_pairs={{8,0},{12,4},{16,8},{20,12},{24,16},{28,20},{9,1},{13,5},{17,9},{2... | collective-permute-start | bytes 1966088 | tf_op jit(solution)/shard_map/ppermute | solution.py:623
  660.5 19.3 %copy-start.18 = (f32[512]{0:T(512)S(1)}, f32[512]{0:T(512)}, u32[]{:S(2)}) copy-start(f32[512]{0:T(512)} %copy-done.17) | copy-start | bytes 6148
  660.5 19.3 %copy-start.24 = (f32[512]{0:T(512)S(1)}, f32[512]{0:T(512)}, u32[]{:S(2)}) copy-start(f32[512]{0:T(512)} %param.25) | copy-start | bytes 6148
  660.6 109.3 %reduce-scatter.12.cloned.1.call-start = ((), (), s32[]{:S(2)}) async-start(), calls=%async_computation.14 | async-start | bytes 3538944 | tf_op jit(solution)/shard_map/reduce_scatter | solution.py:674
  660.6 19.2 %copy-start.4 = (f32[512,576]{1,0:T(8,128)S(1)}, f32[512,576]{1,0:T(8,128)}, u32[]{:S(2)}) copy-start(f32[512,576]{1,0:T(8,128)} %copy-done.3) | copy-start | bytes 3538948
  660.7 19.5 %copy-start.20 = (f32[512]{0:T(512)S(1)}, f32[512]{0:T(512)}, u32[]{:S(2)}) copy-start(f32[512]{0:T(512)} %copy-done.19) | copy-start | bytes 6148
  660.7 19.5 %copy-start.33 = (f32[32]{0:T(128)S(1)}, f32[32]{0:T(128)}, u32[]{:S(2)}) copy-start(f32[32]{0:T(128)} %copy-done.32) | copy-start | bytes 388
  660.7 21.4 %copy-start.22 = (f32[512]{0:T(512)S(1)}, f32[512]{0:T(512)}, u32[]{:S(2)}) copy-start(f32[512]{0:T(512)} %copy-done.21) | copy-start | bytes 6148
  687.4 4.7 copy-start.16
  697.6 168.5 %all-reduce.13.cloned.1.call-start = ((), (), s32[]{:S(2)}) async-start(), calls=%async_computation.13 | async-start | bytes 4194304 | tf_op jit(solution)/shard_map/psum | solution.py:864
  750.7 4.6 copy-start.28
  750.7 4.6 copy-start.31
  750.7 122.8 %reduce-scatter.14.cloned.1.call-start = ((), (), s32[]{:S(2)}) async-start(), calls=%async_computation.15 | async-start | bytes 7077888 | tf_op jit(solution)/shard_map/reduce_scatter | solution.py:674
  750.8 4.5 copy-start.2
  750.8 4.5 copy-start.37
  769.9 45.3 %copy-start.5 = (f32[512,2048]{1,0:T(8,128)S(1)}, f32[512,2048]{1,0:T(8,128)}, u32[]{:S(2)}) copy-start(f32[512,2048]{1,0:T(8,128)} %get-tuple-element.58.x_ref) | copy-start | bytes 12582916
  771.4 13.8 %collective-permute-start.8 = (bf16[64,768]{0,1:T(8,128)(2,1)S(1)}, bf16[64,768]{0,1:T(8,128)(2,1)S(1)}, u32[]{:S(2)}, u32[]{:S(2)}) collective-permute-start(bf16[64,768]{0,1:T(8,128)(2,1)S(1)} %get-tuple-element.192), channel_id=1, source_target_pairs={{0,1},{1,2},{2,3},{3,0},{4,5},{5,6},{6,7},{7,4},{8,9},{9,10},{10,1... | collective-permute-start | bytes 294920 | tf_op jit(solution)/shard_map/ppermute | solution.py:682
  771.6 20.3 %collective-permute-start.10 = (bf16[64,768]{0,1:T(8,128)(2,1)S(1)}, bf16[64,768]{0,1:T(8,128)(2,1)S(1)}, u32[]{:S(2)}, u32[]{:S(2)}) collective-permute-start(bf16[64,768]{0,1:T(8,128)(2,1)S(1)} %get-tuple-element.193), channel_id=1, source_target_pairs={{0,3},{1,0},{2,1},{3,2},{4,7},{5,4},{6,5},{7,6},{8,11},{9,8},{10,9... | collective-permute-start | bytes 294920 | tf_op jit(solution)/shard_map/ppermute | solution.py:682
  775.3 35.0 %collective-permute-start.9 = (bf16[64,768]{0,1:T(8,128)(2,1)S(1)}, bf16[64,768]{0,1:T(8,128)(2,1)S(1)}, u32[]{:S(2)}, u32[]{:S(2)}) collective-permute-start(bf16[64,768]{0,1:T(8,128)(2,1)S(1)} %get-tuple-element.194), channel_id=1, source_target_pairs={{0,2},{1,3},{2,0},{3,1},{4,6},{5,7},{6,4},{7,5},{8,10},{9,11},{10,... | collective-permute-start | bytes 294920 | tf_op jit(solution)/shard_map/ppermute | solution.py:682
  811.4 9.7 %collective-permute-start.13 = (bf16[64,768]{0,1:T(8,128)(2,1)S(1)}, bf16[64,768]{0,1:T(8,128)(2,1)S(1)}, u32[]{:S(2)}, u32[]{:S(2)}) collective-permute-start(bf16[64,768]{0,1:T(8,128)(2,1)S(1)} %add_convert_fusion.4), channel_id=1, source_target_pairs={{0,1},{1,2},{2,3},{3,0},{4,5},{5,6},{6,7},{7,4},{8,9},{9,10},{10,1... | collective-permute-start | bytes 294920 | tf_op jit(solution)/shard_map/ppermute | solution.py:682
  811.4 25.5 %collective-permute-start.12 = (bf16[64,768]{0,1:T(8,128)(2,1)S(1)}, bf16[64,768]{0,1:T(8,128)(2,1)S(1)}, u32[]{:S(2)}, u32[]{:S(2)}) collective-permute-start(bf16[64,768]{0,1:T(8,128)(2,1)S(1)} %add_convert_fusion.4), channel_id=1, source_target_pairs={{0,2},{1,3},{2,0},{3,1},{4,6},{5,7},{6,4},{7,5},{8,10},{9,11},{10,... | collective-permute-start | bytes 294920 | tf_op jit(solution)/shard_map/ppermute | solution.py:682
  812.8 24.9 %collective-permute-start.11 = (bf16[64,768]{0,1:T(8,128)(2,1)S(1)}, bf16[64,768]{0,1:T(8,128)(2,1)}, u32[]{:S(2)}, u32[]{:S(2)}) collective-permute-start(bf16[64,768]{0,1:T(8,128)(2,1)S(1)} %add_convert_fusion.4), channel_id=1, source_target_pairs={{0,3},{1,0},{2,1},{3,2},{4,7},{5,4},{6,5},{7,6},{8,11},{9,8},{10,9... | collective-permute-start | bytes 294920 | tf_op jit(solution)/shard_map/ppermute | solution.py:682
  (16 other events, 39.1 us)
Sparse Core Ops, SparseCore 0:
  90.8 87.7 all-reduce.6
  502.9 86.4 all-reduce.8
  660.7 89.9 all-reduce.10
  752.9 113.1 all-reduce.12
Sparse Core Ops, SparseCore 1:
  93.2 91.0 all-gather.2
  189.9 90.2 all-gather.4
  284.0 72.5 reduce-scatter.7
  379.7 115.9 reduce-scatter.9
  507.6 115.8 reduce-scatter.5
  697.6 55.1 reduce-scatter.11
  769.9 60.6 reduce-scatter.13

commit v5 on v4

--- a/solution.py
+++ b/solution.py
@@ -247,89 +247,104 @@
     )
 
 
-def pick_kernel(slot_ref, x_ref, o_ref):
+def pick_kernel(order_ref, slot_ref, x_ref, o_ref):
     o_ref[...] = mm(one_hot(slot_ref), x_ref[...], 1, 0).astype(BF).reshape(o_ref.shape)
 
 
-def pick_route_kernel(count, first_ref, slot_ref, x_ref, w_ref, o_ref, p_ref, g_ref):
-    x = x_ref[...]
-    logits = mm(x, w_ref[...], 1, 1)
-    lane = lax.broadcasted_iota(jnp.int32, logits.shape, 1)
-    logits = jnp.where(lane < count, logits, -1e30)
-    e = jnp.exp(logits - jnp.max(logits, axis=-1, keepdims=True))
-    probs = e / jnp.sum(e, axis=-1, keepdims=True)
-    p_ref[...] = probs
-    high = probs.astype(BF)
-    low = (probs - high.astype(F32)).astype(BF)
-    chosen = one_hot(slot_ref)
-    o_ref[...] = mm(chosen, x, 1, 0).astype(BF).reshape(o_ref.shape)
-    taken = mm(chosen, high, 1, 0) + mm(chosen, low, 1, 0)
-    lane = lax.broadcasted_iota(jnp.int32, (SLOTS, taken.shape[1]), 1)
-    for i in range(slot_ref.shape[0]):
-        part = taken[i * SLOTS : (i + 1) * SLOTS, :]
-        g_ref[i, 0] = jnp.sum(
-            jnp.where(lane == first_ref[0] + i, part, 0.0), axis=-1, keepdims=True
-        )
-
-
-def pick(slot, values):
+def pick(order, slot, values):
     experts, blocks, _, rows = slot.shape
     width = values.shape[1]
     return pl.pallas_call(
         pick_kernel,
         name="pick",
-        grid=(blocks,),
-        in_specs=[
-            pl.BlockSpec((experts, 1, 1, rows), lambda b: (0, b, 0, 0)),
-            pl.BlockSpec((rows, width), lambda b: (b, 0)),
-        ],
-        out_specs=pl.BlockSpec((experts, 1, SLOTS, width), lambda b: (0, b, 0, 0)),
+        grid_spec=pltpu.PrefetchScalarGridSpec(
+            num_scalar_prefetch=1,
+            grid=(blocks,),
+            in_specs=[
+                pl.BlockSpec((experts, 1, 1, rows), lambda b, o: (0, b, 0, 0)),
+                pl.BlockSpec((rows, width), lambda b, o: (o[b], 0)),
+            ],
+            out_specs=pl.BlockSpec((experts, 1, SLOTS, width), lambda b, o: (0, b, 0, 0)),
+        ),
         out_shape=jax.ShapeDtypeStruct((experts, blocks, SLOTS, width), BF),
         compiler_params=params(),
         cost_estimate=cost(
             2 * experts * blocks * SLOTS * rows * width,
             2 * blocks * width * (rows + experts * SLOTS),
         ),
-    )(slot, values)
-
-
-def pick_route(first, slot, values, router_rows, count):
+    )(order, slot, values)
+
+
+def pick_route_kernel(count, pieces, first_ref, slot_ref, w_ref, *refs):
+    o_ref, p_ref, g_ref = refs[-3:]
+    experts, rows = slot_ref.shape[0], slot_ref.shape[3]
+    for n in range(pieces):
+        x = refs[n][...]
+        logits = mm(x, w_ref[...], 1, 1)
+        lane = lax.broadcasted_iota(jnp.int32, logits.shape, 1)
+        logits = jnp.where(lane < count, logits, -1e30)
+        e = jnp.exp(logits - jnp.max(logits, axis=-1, keepdims=True))
+        probs = e / jnp.sum(e, axis=-1, keepdims=True)
+        p_ref[n * rows : (n + 1) * rows, :] = probs
+        high = probs.astype(BF)
+        low = (probs - high.astype(F32)).astype(BF)
+        place = lax.broadcasted_iota(jnp.int32, (SLOTS, rows), 0)
+        chosen = jnp.concatenate(
+            [(slot_ref[i, n] == place).astype(F32).astype(BF) for i in range(experts)], axis=0
+        )
+        picked = mm(chosen, x, 1, 0).astype(BF)
+        o_ref[:, n] = picked.reshape(experts, SLOTS, -1)
+        taken = mm(chosen, high, 1, 0) + mm(chosen, low, 1, 0)
+        lane = lax.broadcasted_iota(jnp.int32, (SLOTS, taken.shape[1]), 1)
+        for i in range(experts):
+            part = taken[i * SLOTS : (i + 1) * SLOTS, :]
+            g_ref[i, n] = jnp.sum(
+                jnp.where(lane == first_ref[0] + i, part, 0.0), axis=-1, keepdims=True
+            )
+
+
+def pick_route(first, slot, values, router_rows, count, at, steps, earlier):
     experts, blocks, _, rows = slot.shape
-    width = values.shape[1]
+    pieces = len(values)
+    width = values[0].shape[1]
     lanes = router_rows.shape[0]
-    return pl.pallas_call(
-        functools.partial(pick_route_kernel, count),
+    at = at // pieces
+    whole = pl.BlockSpec(memory_space=pl.ANY)
+    return pl.pallas_call(
+        functools.partial(pick_route_kernel, count, pieces),
         name="pick_route",
-        grid=(blocks,),
+        grid=(steps,),
         in_specs=[
             smem(),
-            pl.BlockSpec((experts, 1, 1, rows), lambda b: (0, b, 0, 0)),
-            pl.BlockSpec((rows, width), lambda b: (b, 0)),
+            pl.BlockSpec((experts, pieces, 1, rows), lambda b: (0, at + b, 0, 0)),
             fixed(router_rows.shape),
-        ],
+        ]
+        + [pl.BlockSpec((rows, width), lambda b: (b, 0)) for _ in values]
+        + [whole for _ in earlier],
         out_specs=[
-            pl.BlockSpec((experts, 1, SLOTS, width), lambda b: (0, b, 0, 0)),
-            pl.BlockSpec((rows, lanes), lambda b: (b, 0)),
-            pl.BlockSpec((experts, 1, SLOTS, 1), lambda b: (0, b, 0, 0)),
+            pl.BlockSpec((experts, pieces, SLOTS, width), lambda b: (0, at + b, 0, 0)),
+            pl.BlockSpec((pieces * rows, lanes), lambda b: (at + b, 0)),
+            pl.BlockSpec((experts, pieces, SLOTS, 1), lambda b: (0, at + b, 0, 0)),
         ],
         out_shape=[
             jax.ShapeDtypeStruct((experts, blocks, SLOTS, width), BF),
             jax.ShapeDtypeStruct((blocks * rows, lanes), F32),
             jax.ShapeDtypeStruct((experts, blocks, SLOTS, 1), F32),
         ],
+        input_output_aliases={3 + pieces + i: i for i in range(len(earlier))},
         compiler_params=params(),
         cost_estimate=cost(
-            2 * experts * blocks * SLOTS * rows * width,
-            2 * blocks * width * (rows + experts * SLOTS),
+            pieces * steps * rows * width,
+            pieces * steps * width * rows,
         ),
-    )(first, slot, values, router_rows)
-
-
-def put_kernel(place_ref, r_ref, o_ref):
+    )(first, slot, router_rows, *values, *earlier)
+
+
+def put_kernel(order_ref, place_ref, r_ref, o_ref):
     o_ref[...] = mm(place_ref[0], r_ref[...].reshape(-1, r_ref.shape[-1]), 1, 0).astype(BF)
 
 
-def put_route_kernel(first_ref, place_ref, r_ref, p_ref, pg_ref, w_ref, o_ref, lg_ref):
+def put_route_kernel(order_ref, first_ref, place_ref, r_ref, p_ref, pg_ref, w_ref, o_ref, lg_ref):
     experts, rows = pg_ref.shape[0], pg_ref.shape[3]
     by_expert = jnp.concatenate(
         [pg_ref[i, 0] for i in range(experts)] + [jnp.zeros((1, rows), F32)] * (-experts % 8), axis=0
@@ -353,8 +368,8 @@
     blocks, rows, slots = places.shape
     experts, width = picked.shape[0], picked.shape[3]
     return [
-        pl.BlockSpec((1, rows, slots), lambda b: (b, 0, 0)),
-        pl.BlockSpec((experts, 1, SLOTS, width), lambda b: (0, b, 0, 0)),
+        pl.BlockSpec((1, rows, slots), lambda b, o: (b, 0, 0)),
+        pl.BlockSpec((experts, 1, SLOTS, width), lambda b, o: (0, b, 0, 0)),
     ]
 
 
@@ -363,47 +378,53 @@
     return cost(2 * blocks * slots * rows * width, 2 * blocks * width * (rows + slots))
 
 
-def put(places, picked):
+def put(order, places, picked):
     blocks, rows, _ = places.shape
     width = picked.shape[3]
     return pl.pallas_call(
         put_kernel,
         name="put",
-        grid=(blocks,),
-        in_specs=put_specs(places, picked),
-        out_specs=pl.BlockSpec((rows, width), lambda b: (b, 0)),
+        grid_spec=pltpu.PrefetchScalarGridSpec(
+            num_scalar_prefetch=1,
+            grid=(blocks,),
+            in_specs=put_specs(places, picked),
+            out_specs=pl.BlockSpec((rows, width), lambda b, o: (o[b], 0)),
+        ),
         out_shape=jax.ShapeDtypeStruct((blocks * rows, width), BF),
         compiler_params=params(),
         cost_estimate=put_cost(places, width),
-    )(places, picked)
-
-
-def put_route(first, places, picked, probs, probs_grad, router_rows):
+    )(order, places, picked)
+
+
+def put_route(order, first, places, picked, probs, probs_grad, router_rows):
     blocks, rows, _ = places.shape
     experts, width = picked.shape[0], picked.shape[3]
     lanes = probs.shape[1]
     return pl.pallas_call(
         put_route_kernel,
         name="put_route",
-        grid=(blocks,),
-        in_specs=[smem()]
-        + put_specs(places, picked)
-        + [
-            pl.BlockSpec((rows, lanes), lambda b: (b, 0)),
-            pl.BlockSpec((experts, 1, 1, rows), lambda b: (0, b, 0, 0)),
-            fixed(router_rows.shape),
-        ],
-        out_specs=[
-            pl.BlockSpec((rows, width), lambda b: (b, 0)),
-            pl.BlockSpec((rows, lanes), lambda b: (b, 0)),
-        ],
+        grid_spec=pltpu.PrefetchScalarGridSpec(
+            num_scalar_prefetch=1,
+            grid=(blocks,),
+            in_specs=[smem()]
+            + put_specs(places, picked)
+            + [
+                pl.BlockSpec((rows, lanes), lambda b, o: (b, 0)),
+                pl.BlockSpec((experts, 1, 1, rows), lambda b, o: (0, b, 0, 0)),
+                fixed(router_rows.shape),
+            ],
+            out_specs=[
+                pl.BlockSpec((rows, width), lambda b, o: (o[b], 0)),
+                pl.BlockSpec((rows, lanes), lambda b, o: (b, 0)),
+            ],
+        ),
         out_shape=[
             jax.ShapeDtypeStruct((blocks * rows, width), BF),
             jax.ShapeDtypeStruct((blocks * rows, lanes), BF),
         ],
         compiler_params=params(),
         cost_estimate=put_cost(places, width),
-    )(first, places, picked, probs, probs_grad, router_rows)
+    )(order, first, places, picked, probs, probs_grad, router_rows)
 
 
 def down_back_kernel(x_ref, w_ref, o_ref):
@@ -432,8 +453,8 @@
         out_shape=jax.ShapeDtypeStruct((experts, count, wide), F32),
         compiler_params=params(),
         cost_estimate=cost(
-            2 * experts * count * width * ff,
-            experts * (2 * count * width + 2 * ff * width + 4 * count * wide),
+            experts * count * width,
+            experts * count * ff,
         ),
     )(rows, down)
 
@@ -613,6 +634,42 @@
     )(values, upstream, residual, gain.reshape(1, width))
 
 
+def shared_kernel(x_ref, up_ref, wg_ref, wu_ref, wd_ref, act_ref, dg_ref, du_ref, grad_ref):
+    ff = wd_ref.shape[0]
+    x = x_ref[...]
+    upstream = up_ref[...]
+    a = mm(x, wg_ref[...], 1, 1)
+    b = mm(x, wu_ref[...], 1, 1)
+    back = mm(upstream, wd_ref[...], 1, 1)
+    sig = jax.nn.sigmoid(a)
+    swish = a * sig
+    active = (swish * b).astype(BF)
+    dg = (back * b * (sig + swish * (1.0 - sig))).astype(BF)
+    du = (back * swish).astype(BF)
+    act_ref[...] = active
+    dg_ref[...] = dg
+    du_ref[...] = du
+    grad_ref[:ff, :] = mm(active, upstream, 0, 0).astype(BF)
+    grad_ref[ff : 2 * ff, :] = mm(dg, x, 0, 0).astype(BF)
+    grad_ref[2 * ff :, :] = mm(du, x, 0, 0).astype(BF)
+
+
+def shared_step(values, upstream, gate_t, up_t, down):
+    rows, width = values.shape
+    ff = down.shape[0]
+    inner = jax.ShapeDtypeStruct((rows, ff), BF)
+    return pl.pallas_call(
+        shared_kernel,
+        name="shared_step",
+        grid=(1,),
+        in_specs=[fixed((rows, width))] * 2 + [fixed((ff, width))] * 3,
+        out_specs=[fixed((rows, ff))] * 3 + [fixed((3 * ff, width))],
+        out_shape=[inner, inner, inner, jax.ShapeDtypeStruct((3 * ff, width), BF)],
+        compiler_params=params(),
+        cost_estimate=cost(rows * width, rows * width),
+    )(values, upstream, gate_t, up_t, down)
+
+
 def dot(eq, a, b):
     return jnp.einsum(eq, a, b, preferred_element_type=F32)
 
@@ -661,8 +718,12 @@
     return jnp.cos(angle), jnp.sin(angle)
 
 
+def turned(value, by):
+    return lax.ppermute(value, "dp", [(i, i ^ by) for i in range(lax.axis_size("dp"))])
+
+
 def swapped(value):
-    return lax.ppermute(value, "dp", [(i, i ^ 1) for i in range(lax.axis_size("dp"))])
+    return turned(value, 1)
 
 
 def after(value, *others):
@@ -672,23 +733,6 @@
 def scatter_sum(parts):
     joined = parts if not isinstance(parts, list) else jnp.concatenate(parts, axis=1)
     return lax.psum_scatter(joined, "dp", scatter_dimension=0, tiled=True)
-
-
-def tensor_sum(value):
-    peers = lax.axis_size("tensor")
-    rank = lax.axis_index("tensor")
-    rows = value.shape[0] // peers
-    piece = lambda at: lax.dynamic_slice_in_dim(value, at * rows, rows, 0)
-    turn = lambda piece, by: lax.ppermute(
-        piece, "tensor", [(i, (i + by) % peers) for i in range(peers)]
-    )
-    total = piece(rank).astype(F32)
-    for by in range(1, peers):
-        total = total + turn(piece((rank + by) % peers), by).astype(F32)
-    mine = total.astype(BF)
-    around = [turn(mine, by) for by in range(peers - 1, 0, -1)] + [mine]
-    both = jnp.concatenate(around + around[:-1], axis=0)
-    return lax.dynamic_slice_in_dim(both, (peers - 1 - rank) * rows, value.shape[0], 0)
 
 
 def shards(
@@ -719,8 +763,9 @@
     ff_local = expert_gate.shape[2]
     heads_local = w_query.shape[1] // (DN + DR)
 
-    cot_all = lax.all_gather(cotangent, "dp", tiled=True)
-    route_all = lax.all_gather(route_ids, "dp", tiled=True)
+    direct = devices == 8
+    apart = jnp.array([0, 1, 2, 4, 3, 5, 6, 7] if direct else list(range(devices)), jnp.int32)
+    order = (rank_dp ^ apart) if direct else apart
 
     index_here = rank_dp * tok_rows + jnp.arange(tok_rows, dtype=jnp.int32)
     seq_here = lax.dynamic_slice_in_dim(seq_ids, rank_dp * tok_rows, tok_rows, 0)
@@ -754,18 +799,16 @@
         swapped(jnp.where(odd == 0, own_keys, before_four)),
         own_keys,
     ]
+    cot_all = lax.all_gather(after(cotangent, before_two, before_four), "dp", tiled=True)
     query_pre = jnp.dot(hidden_in, w_query, preferred_element_type=F32)
     attended, lse = attend(query_pre, cosine, sine, w_expand, place_q, place_k, keys)
-    attention = lax.psum(
-        jnp.dot(attended, w_out, preferred_element_type=F32).astype(BF), "tensor"
-    )
-    attention = after(attention, cot_all)
-    middle, hidden_mid = norm_sum(tokens, attention, middle_gain)
-    hidden_all = lax.all_gather(hidden_mid, "dp", tiled=True)
-
+    attention_part = jnp.dot(attended, w_out, preferred_element_type=F32).astype(BF)
+    attention = lax.psum(attention_part, "tensor")
+
+    route_all = lax.all_gather(after(route_ids, attention_part), "dp", tiled=True)
     local_ids = rank_dp * experts_local + jnp.arange(experts_local, dtype=jnp.int32)
-    named = jnp.any(route_all[:, :, None] == local_ids[None, None, :], axis=1)
-    named_block = named.reshape(devices, tok_rows, experts_local)
+    routes = jnp.take(route_all.reshape(devices, tok_rows, -1), order, axis=0)
+    named_block = jnp.any(routes[..., None] == local_ids, axis=2)
     before = jnp.tril(jnp.ones((tok_rows, tok_rows), BF), -1)
     rank_within = dot("ts,bse->bte", before, named_block.astype(BF))
     slot_of = jnp.where(named_block, rank_within, -1.0)
@@ -779,44 +822,62 @@
     ).astype(BF)
     gate_t = expert_gate.swapaxes(1, 2)
     up_t = expert_up.swapaxes(1, 2)
-    cot_rows = pick(slot, cot_all)
+    cot_rows = pick(order, slot, cot_all)
     back = down_back(cot_rows, expert_down)
 
-    shared_gate_val = jnp.dot(hidden_mid, shared_gate, preferred_element_type=F32)
-    shared_up_val = jnp.dot(hidden_mid, shared_up, preferred_element_type=F32)
-    shared_active = silu_gate(shared_gate_val, shared_up_val).astype(BF)
+    attention = after(attention, cot_rows, places)
+    middle, hidden_mid = norm_sum(tokens, attention, middle_gain)
+    first = (rank_dp * experts_local).astype(jnp.int32).reshape(1)
+    router_rows = jnp.pad(w_router.T, ((0, -all_experts % 128), (0, 0)))
+    if direct:
+        half = tok_rows // 2
+        pair = swapped(hidden_mid)
+        by_x = turned(hidden_mid, 2)
+        by_y = turned(hidden_mid, 4)
+        held = pick_route(first, slot, [hidden_mid, pair], router_rows, all_experts, 0, 1, [])
+    else:
+        hidden_all = lax.all_gather(hidden_mid, "dp", tiled=True)
+
+    hidden_shared = after(hidden_mid, pair) if direct else hidden_mid
+    shared_active, shared_gate_grad, shared_up_grad, shared_grads = shared_step(
+        hidden_shared, cotangent, shared_gate.T, shared_up.T, shared_down
+    )
     shared_result = jnp.dot(shared_active, shared_down, preferred_element_type=F32)
-    shared_active_grad = dot("td,fd->tf", cotangent, shared_down)
-    shared_gate_grad, shared_up_grad = silu_backward(
-        shared_gate_val, shared_up_val, shared_active_grad
-    )
-    shared_gate_grad = shared_gate_grad.astype(BF)
-    shared_up_grad = shared_up_grad.astype(BF)
     mid_from_shared = dot("tf,df->td", shared_gate_grad, shared_gate) + dot(
         "tf,df->td", shared_up_grad, shared_up
     )
-    shared_grads = jnp.concatenate(
-        [
-            dot("td,tf->df", cotangent, shared_active).astype(BF),
-            dot("td,tf->df", hidden_mid, shared_gate_grad).astype(BF),
-            dot("td,tf->df", hidden_mid, shared_up_grad).astype(BF),
-        ],
-        axis=1,
-    )
-
-    hidden_all = after(hidden_all, back, shared_grads)
-    first = (rank_dp * experts_local).astype(jnp.int32).reshape(1)
-    router_rows = jnp.pad(w_router.T, ((0, -all_experts % 128), (0, 0)))
-    rows, router_probs, slot_gates = pick_route(first, slot, hidden_all, router_rows, all_experts)
-    shared_sums = scatter_sum(shared_grads)
+    if direct:
+        by_x, by_y = lax.optimization_barrier((by_x, by_y, held[0], back, shared_grads))[:2]
+        pair_x, pair_y = swapped(by_x), swapped(by_y)
+        top = turned(by_y[:half], 2)
+        bottom = turned(by_x[half:], 4)
+        held = pick_route(first, slot, [by_x, by_y], router_rows, all_experts, 2, 1, held)
+        held = pick_route(first, slot, [pair_x, pair_y], router_rows, all_experts, 4, 1, held)
+        corner = jnp.concatenate([after(top, held[0]), bottom], axis=0)
+        pair_corner = swapped(corner)
+        held = pick_route(first, slot, [corner], router_rows, all_experts, 6, 1, held)
+        held = pick_route(first, slot, [pair_corner], router_rows, all_experts, 7, 1, held)
+        rows, router_probs, slot_gates = held
+        hidden_all = jnp.concatenate(
+            [hidden_mid, pair, by_x, by_y, pair_x, pair_y, after(corner, rows), pair_corner], axis=0
+        )
+    else:
+        rows, router_probs, slot_gates = pick_route(
+            first, slot, [hidden_all], router_rows, all_experts, 0, devices, []
+        )
+    shared_sums = lax.psum_scatter(
+        after(shared_grads, rows), "dp", scatter_dimension=1, tiled=True
+    )
     gated_active, gate_val_grad, up_val_grad, row_grad, probs_grad = expert_step(
         rows, gate_t, up_t, back, slot, slot_gates
     )
-    mid_part, logit_grad = put_route(first, places, row_grad, router_probs, probs_grad, router_rows)
+    mid_part, logit_grad = put_route(
+        order, first, places, row_grad, router_probs, probs_grad, router_rows
+    )
     mid_part = after(mid_part, shared_sums)
     mid_block = lax.psum_scatter(mid_part, "dp", scatter_dimension=0, tiled=True)
     grad_router = dot("td,te->de", hidden_all, logit_grad[:, :all_experts]).astype(BF)
-    routed_part = put(places, row_out(gated_active, expert_down, devices))
+    routed_part = put(order, places, row_out(gated_active, expert_down, devices))
     rows_flat = rows.reshape(experts_local, -1, width)
     grad_expert_down = dot(
         "ecf,ecd->efd",
@@ -861,7 +922,6 @@
     output = (middle + feedforward.astype(F32)).astype(BF)
     input_part, grad_input_gain = lax.optimization_barrier((input_part.astype(BF), grad_input_gain))
     input_part = after(input_part, feedforward)
-    input_grad = lax.psum(input_part, "tensor")
     tensors = lax.axis_size("tensor")
     query_width = heads_local * (DN + DR)
     out_width = heads_local * DV
@@ -886,8 +946,8 @@
             after(grad_expand, keys_grad).reshape(width, expand_width),
         ]
     )
-    parts = tensor_sum(parts).astype(F32)
-    input_grad = after(input_grad, parts)
+    input_grad, parts = lax.psum((input_part, parts), "tensor")
+    parts = parts.astype(F32)
     (token_grad,) = norm_back(tokens, input_grad, middle_grad, input_gain, True)
     sw = shared_gate.shape[1]
     gain_at = latent_width + all_experts
@@ -905,9 +965,9 @@
         grad_expert_gate,
         grad_expert_up,
         grad_expert_down,
-        shared_sums[:, sw : 2 * sw].astype(F32),
-        shared_sums[:, 2 * sw :].astype(F32),
-        shared_sums[:, :sw].astype(F32).T,
+        shared_sums[sw : 2 * sw].astype(F32).T,
+        shared_sums[2 * sw :].astype(F32).T,
+        shared_sums[:sw].astype(F32),
     )
 
 

time: 897 us -> 865 us (0.964)
  waiting for transfers between devices: 346 us -> 274 us
  Pallas kernels: 264 us -> 300 us
  local copies, waits for them, and re-layouts: 27.6 us -> 58.5 us
  matrix products: 150 us -> 132 us
    ppermute x10 -> x12, waiting for transfers between devices: 52.2 us -> 4.64 us  [turned(): lax.ppermute(value, 'dp', [(i, i ^ by) for i in range(lax.axis_size('dp'))])]
    pallas_call x4 -> x9, Pallas kernels: 90.7 us -> 128 us  [the longest x5 42.1 us: pick_route(): pl.pallas_call(functools.partial(pick_route_kernel, count, pieces), name=...]
    unnamed x83 -> x87, local copies, waits for them, and re-layouts: 5.08 us -> 30.9 us
    reduce_scatter x1, waiting for transfers between devices: 39 us -> 14.6 us  [shards(): lax.psum_scatter(mid_part, 'dp', scatter_dimension=0, tiled=True)]
    psum x2, waiting for transfers between devices: 106 us -> 87.2 us  [the longest x1 75.5 us: shards(): input_grad, parts = lax.psum((input_part, parts), 'tensor')]
    all_gather x2 -> x1, waiting for transfers between devices: 22.6 us -> 39.1 us  [shards(): lax.all_gather(after(cotangent, before_two, before_four), 'dp', tiled=True)]
    dot_general x18 -> x14, matrix products: 126 us -> 113 us  [dot(): return jnp.einsum(eq, a, b, preferred_element_type=F32)]
  transfers between devices with their start and end apart: 25 -> 26, of which waited for: 16 -> 13; matrix products, arithmetic and copies ran while one was open for 21% -> 23% of each run, Pallas kernels for 27% -> 34%
where the time goes in v5:
time: 865 us; the launch traced here: 859 us
  Pallas kernels  300 us (35%)
  waiting for transfers between devices  274 us (32%)
  matrix products  132 us (15%)
  local copies, waits for them, and re-layouts  58.5 us (7%)
  other arithmetic  45.2 us (5%)
  starting transfers between devices  20.9 us (2%)
  between operations  16.8 us (2%)
  blocking collectives  10.9 us (1%)
    dot_general x14, matrix products, dot(): return jnp.einsum(eq, a, b, preferred_element_type=F32)  113 us
    psum x1, waiting for transfers between devices, shards(): input_grad, parts = lax.psum((input_part, parts), 'tensor')  75.5 us
    psum x1, waiting for transfers between devices, shards(): feedforward = lax.psum(ff_part, 'tensor')  55.2 us
    pallas_call x1, Pallas kernels, expert_step(): pl.pallas_call(expert_kernel, name='expert_step', grid=(experts,), in_spe...  49.6 us
    pallas_call x1, Pallas kernels, attend_back(): pl.pallas_call(functools.partial(attend_back_kernel, heads, rows // 2, co...  43.6 us
    pallas_call x5, Pallas kernels, pick_route(): pl.pallas_call(functools.partial(pick_route_kernel, count, pieces), name=...  42.1 us
    ppermute x4, waiting for transfers between devices, passed_along(): return lax.ppermute(shard, axis, pairs)  40.8 us
    all_gather x1, waiting for transfers between devices, shards(): lax.all_gather(after(cotangent, before_two, before_four), 'dp', tiled=True)  39.1 us
  transfers between devices with their start and end apart: 26, of which 13 were waited for; matrix products, arithmetic and copies ran while one was open for 23% of the time, Pallas kernels for 34%

profile of v5, /device:TPU:0, one launch (start us, length us, event | category | flops | bytes accessed | tf_op | source)
XLA Modules:
  0.0 858.5 jit_solution(11918017013865360969)
XLA Ops:
  13.3 4.2 fusion.65
  20.7 6.2 collective-permute-start.1
  26.9 5.6 collective-permute-start
  32.5 9.0 %collective-permute-done.1.rest_1_ = bf16[512,640]{1,0:T(8,128)(2,1)S(1)} collective-permute-done((bf16[512,640]{1,0:T(8,128)(2,1)S(1)}, bf16[512,640]{1,0:T(8,128)(2,1)S(1)}, u32[]{:S(2)}, u32[]{:S(2)}) %collective-permute-start.1) | collective-permute-done | bytes 655392 | tf_op jit(solution)/shard_map/ppermute | solution.py:680
  42.4 14.8 %collective-permute-done.rest_0_ = bf16[512,640]{1,0:T(8,128)(2,1)} collective-permute-done((bf16[512,640]{1,0:T(8,128)(2,1)S(1)}, bf16[512,640]{1,0:T(8,128)(2,1)}, u32[]{:S(2)}, u32[]{:S(2)}) %collective-permute-start) | collective-permute-done | bytes 655392 | tf_op jit(solution)/shard_map/ppermute | solution.py:680
  62.4 4.6 fusion.67.qp_ref
  67.0 21.6 %attend.1 = (bf16[512,512]{1,0:T(8,128)(2,1)}, f32[4,512,1]{2,1,0:T(8,128)}) custom-call(f32[512,768]{1,0:T(8,128)} %fusion.67.qp_ref, f32[512,32]{1,0:T(8,128)} %get-tuple-element.240.cos_ref, f32[512,32]{1,0:T(8,128)} %get-tuple-element.239.sin_ref, bf16[512,1024]{1,0:T(8,128)(2,1)} %wx_ref.3, s32[512,2]{1,0:T(8,128)} %copy.108.sq_ref, ...), custom_call_target="tpu_custom_call" | custom-call | flops 6710886400 | bytes 3276800 | tf_op jit(solution)/shard_map/attend/pallas_call | solution.py:111
  88.6 4.4 convolution_convert_fusion.3
  93.0 10.9 %all_gather.6 = s32[4096,6]{0,1:T(8,128)S(1)} all-gather(s32[512,6]{0,1:T(8,128)S(1)} %copy-done.23), channel_id=1, replica_groups=mesh['dp'=8,'tensor'=4] {'dp'}, dimensions={0}, use_global_device_ids=true | all-gather | bytes 110592 | tf_op jit(solution)/shard_map/all_gather | solution.py:808
  106.0 3.9 compare_convert_fusion.place_ref
  109.9 39.1 %all-gather.2.cloned.1.call-done.x_ref = bf16[4096,2048]{1,0:T(8,128)(2,1)} async-done(((bf16[512,2048]{1,0:T(8,128)(2,1)}), bf16[4096,2048]{1,0:T(8,128)(2,1)}) %all-gather.2.cloned.1.call-update) | async-done | bytes 16777232 | tf_op jit(solution)/shard_map/all_gather | solution.py:802
  149.0 19.7 %pick.1.x_ref = bf16[8,8,80,2048]{3,2,1,0:T(8,128)(2,1)} custom-call(s32[8]{0:T(128)} %broadcast_xor_fusion.order_ref, s32[8,8,1,512]{3,2,1,0:T(1,128)} %broadcast_in_dim.78.slot_ref, bf16[4096,2048]{1,0:T(8,128)(2,1)} %all-gather.2.cloned.1.call-done.x_ref), custom_call_target="tpu_custom_call" | custom-call | flops 10737418240 | bytes 37748736 | tf_op jit(solution)/shard_map/pick/pallas_call | solution.py:257
  168.7 11.7 %all-reduce.8.cloned.1.call-done.add_ref = bf16[512,2048]{1,0:T(8,128)(2,1)} async-done(((bf16[512,2048]{1,0:T(8,128)(2,1)}), bf16[512,2048]{1,0:T(8,128)(2,1)}) %all-reduce.8.cloned.1.call-update) | async-done | bytes 2097168 | tf_op jit(solution)/shard_map/psum | solution.py:806
  180.4 5.5 norm_sum.1
  189.7 19.0 %down_back.1.back_ref = f32[8,640,384]{2,1,0:T(8,128)} custom-call(bf16[8,8,80,2048]{3,2,1,0:T(8,128)(2,1)} %pick.1.x_ref, bf16[8,352,2048]{2,1,0:T(8,128)(2,1)} %w_ref.3), custom_call_target="tpu_custom_call" | custom-call | flops 10485760 | bytes 1802240 | tf_op jit(solution)/shard_map/down_back/pallas_call | solution.py:444
  208.7 18.1 %shared_step.1 = (bf16[512,704]{1,0:T(8,128)(2,1)}, bf16[512,704]{1,0:T(8,128)(2,1)}, bf16[512,704]{1,0:T(8,128)(2,1)}, bf16[2112,2048]{1,0:T(8,128)(2,1)}) custom-call(bf16[512,2048]{1,0:T(8,128)(2,1)} %get-tuple-element.85.refs_0_.x_ref, bf16[512,2048]{1,0:T(8,128)(2,1)} %res_ref.1, bf16[704,2048]{1,0:T(8,128)(2,1)} %bitcast.67, ...), custom_call_target="tpu_custom_call" | custom-call | flops 1048576 | bytes 1048576 | tf_op jit(solution)/shard_map/shared_step/pallas_call | solution.py:661
  226.9 10.0 %pick_route.5 = (bf16[8,8,80,2048]{3,2,1,0:T(8,128)(2,1)}, f32[4096,128]{1,0:T(8,128)}, f32[8,8,80,1]{3,2,1,0:T(8,128)}) custom-call(s32[1]{0:T(128)} %bitcast.8.first_ref, s32[8,8,1,512]{3,2,1,0:T(1,128)} %broadcast_in_dim.78.slot_ref, bf16[128,2048]{1,0:T(8,128)(2,1)} %pad.5.w_ref, bf16[512,2048]{1,0:T(8,128)(2,1)} %get-tuple-element.85.refs_0_.x_ref, ...), custom_call_target="tpu_custom_call" | custom-call | flops 2097152 | bytes 2097152 | tf_op jit(solution)/shard_map/pick_route/pallas_call | solution.py:313
  243.2 9.8 %pick_route.6 = (bf16[8,8,80,2048]{3,2,1,0:T(8,128)(2,1)}, f32[4096,128]{1,0:T(8,128)}, f32[8,8,80,1]{3,2,1,0:T(8,128)}) custom-call(s32[1]{0:T(128)} %bitcast.8.first_ref, s32[8,8,1,512]{3,2,1,0:T(1,128)} %broadcast_in_dim.78.slot_ref, bf16[128,2048]{1,0:T(8,128)(2,1)} %pad.5.w_ref, ...), custom_call_target="tpu_custom_call", output_to_operand_aliasing={{0}: (5, {}), {1}: (6, {}), {2}: (7, {})} | custom-call | flops 2097152 | bytes 2097152 | tf_op jit(solution)/shard_map/pick_route/pallas_call | solution.py:313
  253.0 9.8 %pick_route.7 = (bf16[8,8,80,2048]{3,2,1,0:T(8,128)(2,1)}, f32[4096,128]{1,0:T(8,128)}, f32[8,8,80,1]{3,2,1,0:T(8,128)}) custom-call(s32[1]{0:T(128)} %bitcast.8.first_ref, s32[8,8,1,512]{3,2,1,0:T(1,128)} %broadcast_in_dim.78.slot_ref, bf16[128,2048]{1,0:T(8,128)(2,1)} %pad.5.w_ref, ...), custom_call_target="tpu_custom_call", output_to_operand_aliasing={{0}: (5, {}), {1}: (6, {}), {2}: (7, {})} | custom-call | flops 2097152 | bytes 2097152 | tf_op jit(solution)/shard_map/pick_route/pallas_call | solution.py:313
  270.1 6.0 pick_route.8
  276.1 6.5 pick_route.9
  282.7 49.6 %expert_step.1 = (bf16[8,640,384]{2,1,0:T(8,128)(2,1)}, bf16[8,640,384]{2,1,0:T(8,128)(2,1)}, bf16[8,640,384]{2,1,0:T(8,128)(2,1)}, bf16[8,8,80,2048]{3,2,1,0:T(8,128)(2,1)}, f32[8,8,1,512]{3,2,1,0:T(1,128)}) custom-call(bf16[8,8,80,2048]{3,2,1,0:T(8,128)(2,1)} %get-tuple-element.101.x_ref, bf16[8,352,2048]{2,1,0:T(8,128)(2,1)} %bitcast.76, ...), custom_call_target="tpu_custom_call" | custom-call | flops 32212254720 | bytes 86769664 | tf_op jit(solution)/shard_map/expert_step/pallas_call | solution.py:540
  332.2 25.6 %put_route.1 = (bf16[4096,2048]{1,0:T(8,128)(2,1)}, bf16[4096,128]{1,0:T(8,128)(2,1)}) custom-call(s32[8]{0:T(128)} %broadcast_xor_fusion.order_ref, s32[1]{0:T(128)} %bitcast.8.first_ref, bf16[8,512,640]{2,1,0:T(8,128)(2,1)} %compare_convert_fusion.place_ref, bf16[8,8,80,2048]{3,2,1,0:T(8,128)(2,1)} %get-tuple-element.105.r_ref, ...), custom_call_target="tpu_custom_call" | custom-call | flops 10737418240 | bytes 37748736 | tf_op jit(solution)/shard_map/put_route/pallas_call | solution.py:403
  367.7 3.7 constant_dynamic-update-slice_fusion.8
  372.0 4.0 fusion.70
  389.7 18.9 %row_out.1.r_ref = bf16[8,8,80,2048]{3,2,1,0:T(8,128)(2,1)} custom-call(bf16[8,640,384]{2,1,0:T(8,128)(2,1)} %get-tuple-element.103.x_ref, bf16[8,352,2048]{2,1,0:T(8,128)(2,1)} %w_ref.3), custom_call_target="tpu_custom_call" | custom-call | flops 7381975040 | bytes 36438016 | tf_op jit(solution)/shard_map/row_out/pallas_call | solution.py:471
  408.5 22.2 %put.1 = bf16[4096,2048]{1,0:T(8,128)(2,1)} custom-call(s32[8]{0:T(128)} %broadcast_xor_fusion.order_ref, bf16[8,512,640]{2,1,0:T(8,128)(2,1)} %compare_convert_fusion.place_ref, bf16[8,8,80,2048]{3,2,1,0:T(8,128)(2,1)} %row_out.1.r_ref), custom_call_target="tpu_custom_call" | custom-call | flops 10737418240 | bytes 37748736 | tf_op jit(solution)/shard_map/put/pallas_call | solution.py:384
  430.8 9.4 %convolution_convert_fusion.4 = bf16[2048,64]{0,1:T(8,128)(2,1)S(1)} fusion(bf16[4096,2048]{1,0:T(8,128)(2,1)} %constant_dynamic-update-slice_fusion.4, bf16[4096,128]{1,0:T(8,128)(2,1)} %get-tuple-element.112), kind=kOutput, calls=%fused_computation.26 | convolution fusion | flops 1073872896 | bytes 18087936 | tf_op jit(solution)/shard_map/td,te->de/dot_general | solution.py:674
  440.2 19.1 %fusion.9 = f32[8,352,2048]{2,1,0:T(8,128)} fusion(bf16[8,640,2048]{2,1,0:T(8,128)(2,1)} %bitcast.65, bf16[8,640,384]{2,1,0:T(8,128)(2,1)} %get-tuple-element.103.x_ref), kind=kOutput, calls=%fused_computation.18 | convolution fusion | flops 7381975040 | bytes 47972352 | tf_op jit(solution)/shard_map/ecf,ecd->efd/dot_general | solution.py:674
  459.2 14.6 %reduce-scatter.10.cloned.1.call-done = bf16[512,2048]{1,0:T(8,128)(2,1)} async-done(((bf16[4096,2048]{1,0:T(8,128)(2,1)}), bf16[512,2048]{1,0:T(8,128)(2,1)}) %reduce-scatter.10.cloned.1.call-update) | async-done | bytes 2097168 | tf_op jit(solution)/shard_map/reduce_scatter | solution.py:878
  473.9 7.0 add_convert_fusion.2
  481.5 6.0 fusion.71
  487.5 25.2 %fusion.7 = f32[8,2048,352]{1,2,0:T(8,128)} fusion(bf16[8,640,2048]{2,1,0:T(8,128)(2,1)} %bitcast.63, bf16[8,640,384]{2,1,0:T(8,128)(2,1)S(1)} %copy-done.7), kind=kOutput, calls=%fused_computation.16 | convolution fusion | flops 7381975040 | bytes 47972352 | tf_op jit(solution)/shard_map/ecd,ecf->edf/dot_general | solution.py:674
  512.7 22.0 %fusion.5 = f32[8,2048,352]{1,2,0:T(8,128)} fusion(bf16[8,640,2048]{2,1,0:T(8,128)(2,1)} %bitcast.64, bf16[8,640,384]{2,1,0:T(8,128)(2,1)S(1)} %copy-done.6), kind=kOutput, calls=%fused_computation.14 | convolution fusion | flops 7381975040 | bytes 47972352 | tf_op jit(solution)/shard_map/ecd,ecf->edf/dot_general | solution.py:674
  534.7 32.2 %all-reduce.10.cloned.1.call-done.up_ref = bf16[512,2048]{1,0:T(8,128)(2,1)} async-done(((bf16[512,2048]{1,0:T(8,128)(2,1)}), bf16[512,2048]{1,0:T(8,128)(2,1)}) %all-reduce.10.cloned.1.call-update) | async-done | bytes 2097168 | tf_op jit(solution)/shard_map/psum | solution.py:892
  567.0 8.0 norm_back.2
  575.0 4.6 convolution_convert_fusion.5.do_ref
  579.6 43.6 %attend_back.1 = (bf16[512,768]{1,0:T(8,128)(2,1)}, bf16[512,1024]{1,0:T(8,128)(2,1)}, bf16[512,640]{1,0:T(8,128)(2,1)}, bf16[512,640]{1,0:T(8,128)(2,1)}, bf16[...) custom-call(f32[512,768]{1,0:T(8,128)} %fusion.67.qp_ref, ...), custom_call_target="tpu_custom_call" | custom-call | flops 18790481920 | bytes 6553600 | tf_op jit(solution)/shard_map/attend_back/pallas_call | solution.py:206
  623.2 4.9 add_convert_fusion.1
  638.5 13.4 %collective-permute-done.15 = bf16[512,640]{1,0:T(8,128)(2,1)} collective-permute-done((bf16[512,640]{1,0:T(8,128)(2,1)}, bf16[512,640]{1,0:T(8,128)(2,1)}, u32[]{:S(2)}, u32[]{:S(2)}) %collective-permute-start.15) | collective-permute-done | bytes 655392 | tf_op jit(solution)/shard_map/ppermute | solution.py:680
  661.4 3.9 fusion.41
  672.5 55.2 %all-reduce.12.cloned.1.call-done = bf16[512,2048]{1,0:T(8,128)(2,1)} async-done(((bf16[512,2048]{1,0:T(8,128)(2,1)}), bf16[512,2048]{1,0:T(8,128)(2,1)}) %all-reduce.12.cloned.1.call-update) | async-done | bytes 2097168 | tf_op jit(solution)/shard_map/psum | solution.py:921
  727.8 4.4 convolution_convert_fusion.2
  732.2 3.7 convolution_convert_fusion
  740.8 5.9 pad_maximum_fusion
  749.5 4.3 add_convert_fusion
  753.8 75.5 %all-reduce.14.cloned.1.call-done = (bf16[256,768]{0,1:T(8,128)(2,1)}, bf16[512,2048]{1,0:T(8,128)(2,1)}) async-done(((bf16[256,768]{0,1:T(8,128)(2,1)}, bf16[512,2048]{1,0:T(8,128)(2,1)}), (bf16[256,768]{0,1:T(8,128)(2,1)}, bf16[512,2048]{1,0:T(8,128)(2,1)})) %all-reduce.14.cloned.1.call-update) | async-done | bytes 2490384 | tf_op jit(solution)/shard_map/psum | solution.py:949
  833.8 6.1 norm_back.3
  (209 shorter events, 108.2 us)
Async XLA Ops:
  8.0 54.4 %copy-start = (bf16[2048,768]{1,0:T(8,128)(2,1)S(1)}, bf16[2048,768]{1,0:T(8,128)(2,1)}, u32[]{:S(2)}) copy-start(bf16[2048,768]{1,0:T(8,128)(2,1)} %param.24) | copy-start | bytes 9437188
  8.0 140.9 %all-gather.2.cloned.1.call-start = ((), (), s32[]{:S(2)}) async-start(), calls=%async_computation.6 | async-start | bytes 18874368 | tf_op jit(solution)/shard_map/all_gather | solution.py:802
  8.1 10.4 %copy-start.29 = (f32[32]{0:T(128)}, f32[32]{0:T(128)S(1)}, u32[]{:S(2)}) copy-start(f32[32]{0:T(128)S(1)} %multiply_power_fusion) | copy-start | bytes 388
  10.4 52.0 %copy-start.27 = (f32[512]{0:T(512)}, f32[512]{0:T(512)S(1)}, u32[]{:S(2)}) copy-start(f32[512]{0:T(512)S(1)} %add_rsqrt_fusion) | copy-start | bytes 6148
  13.3 5.1 copy-start.21
  18.3 39.3 %copy-start.32 = (s32[8]{0:T(128)S(1)}, s32[8]{0:T(128)}, u32[]{:S(2)}) copy-start(s32[8]{0:T(128)} %constant.113.clone) | copy-start | bytes 100
  20.4 41.9 %copy-start.25 = (f32[2048]{0:T(1024)S(1)}, f32[2048]{0:T(1024)}, u32[]{:S(2)}) copy-start(f32[2048]{0:T(1024)} %param.23) | copy-start | bytes 24580
  20.6 6.3 copy-start.10
  20.7 20.9 %collective-permute-start.1 = (bf16[512,640]{1,0:T(8,128)(2,1)S(1)}, bf16[512,640]{1,0:T(8,128)(2,1)S(1)}, u32[]{:S(2)}, u32[]{:S(2)}) collective-permute-start(bf16[512,640]{1,0:T(8,128)(2,1)S(1)} %maximum_maximum_fusion.rest_4_), channel_id=1, source_target_pairs={{0,8},{4,12},{8,16},{12,20},{16,24},{20,28},{1,9},{5,13},{9,17},{1... | collective-permute-start | bytes 1966088 | tf_op jit(solution)/shard_map/ppermute | solution.py:680
  26.9 30.3 %collective-permute-start = (bf16[512,640]{1,0:T(8,128)(2,1)S(1)}, bf16[512,640]{1,0:T(8,128)(2,1)}, u32[]{:S(2)}, u32[]{:S(2)}) collective-permute-start(bf16[512,640]{1,0:T(8,128)(2,1)S(1)} %maximum_maximum_fusion.rest_4_), channel_id=1, source_target_pairs={{0,16},{4,20},{8,24},{12,28},{1,17},{5,21},{9,25},{13,29},{2,18},{... | collective-permute-start | bytes 1966088 | tf_op jit(solution)/shard_map/ppermute | solution.py:680
  57.2 123.2 %all-reduce.8.cloned.1.call-start = ((), (), s32[]{:S(2)}) async-start(), calls=%async_computation.5 | async-start | bytes 4194304 | tf_op jit(solution)/shard_map/psum | solution.py:806
  61.0 6.0 collective-permute-start.3
  61.2 5.8 collective-permute-start.2
  88.6 4.4 copy-start.23
  93.0 264.9 %reduce-scatter.8.cloned.1.call-start = ((), (), s32[]{:S(2)}) async-start(), calls=%async_computation.8 | async-start | bytes 9732096 | tf_op jit(solution)/shard_map/reduce_scatter | solution.py:868
  168.6 20.3 %copy-start.12 = (bf16[2048,64]{0,1:T(8,128)(2,1)S(1)}, bf16[2048,64]{0,1:T(8,128)(2,1)}, u32[]{:S(2)}) copy-start(bf16[2048,64]{0,1:T(8,128)(2,1)} %param.30) | copy-start | bytes 786436
  185.9 22.8 %collective-permute-start.6 = (bf16[512,2048]{1,0:T(8,128)(2,1)}, bf16[512,2048]{1,0:T(8,128)(2,1)}, u32[]{:S(2)}, u32[]{:S(2)}) collective-permute-start(bf16[512,2048]{1,0:T(8,128)(2,1)} %get-tuple-element.85.refs_0_.x_ref), channel_id=1, source_target_pairs={{0,4},{4,0},{8,12},{12,8},{16,20},{20,16},{24,28},{28,24},{1,5},{5... | collective-permute-start | bytes 6291464 | tf_op jit(solution)/shard_map/ppermute | solution.py:722
  185.9 51.0 %collective-permute-start.5 = (bf16[512,2048]{1,0:T(8,128)(2,1)}, bf16[512,2048]{1,0:T(8,128)(2,1)}, u32[]{:S(2)}, u32[]{:S(2)}) collective-permute-start(bf16[512,2048]{1,0:T(8,128)(2,1)} %get-tuple-element.85.refs_0_.x_ref), channel_id=1, source_target_pairs={{0,16},{4,20},{8,24},{12,28},{16,0},{20,4},{24,8},{28,12},{1,17},{... | collective-permute-start | bytes 6291464 | tf_op jit(solution)/shard_map/ppermute | solution.py:722
  187.4 49.5 %collective-permute-start.4 = (bf16[512,2048]{1,0:T(8,128)(2,1)}, bf16[512,2048]{1,0:T(8,128)(2,1)}, u32[]{:S(2)}, u32[]{:S(2)}) collective-permute-start(bf16[512,2048]{1,0:T(8,128)(2,1)} %get-tuple-element.85.refs_0_.x_ref), channel_id=1, source_target_pairs={{0,8},{4,12},{8,0},{12,4},{16,24},{20,28},{24,16},{28,20},{1,9},{5... | collective-permute-start | bytes 6291464 | tf_op jit(solution)/shard_map/ppermute | solution.py:722
  236.9 16.1 %collective-permute-start.9 = (bf16[512,2048]{1,0:T(8,128)(2,1)}, bf16[512,2048]{1,0:T(8,128)(2,1)}, u32[]{:S(2)}, u32[]{:S(2)}) collective-permute-start(bf16[512,2048]{1,0:T(8,128)(2,1)} %collective-permute-done.5.refs_1_), channel_id=1, source_target_pairs={{0,4},{4,0},{8,12},{12,8},{16,20},{20,16},{24,28},{28,24},{1,5},{5... | collective-permute-start | bytes 6291464 | tf_op jit(solution)/shard_map/ppermute | solution.py:722
  237.0 16.0 %collective-permute-start.8 = (bf16[512,2048]{1,0:T(8,128)(2,1)}, bf16[512,2048]{1,0:T(8,128)(2,1)}, u32[]{:S(2)}, u32[]{:S(2)}) collective-permute-start(bf16[512,2048]{1,0:T(8,128)(2,1)} %collective-permute-done.4.refs_0_), channel_id=1, source_target_pairs={{0,4},{4,0},{8,12},{12,8},{16,20},{20,16},{24,28},{28,24},{1,5},{5... | collective-permute-start | bytes 6291464 | tf_op jit(solution)/shard_map/ppermute | solution.py:722
  239.8 25.5 %collective-permute-start.7 = (bf16[256,2048]{1,0:T(8,128)(2,1)}, bf16[256,2048]{1,0:T(8,128)(2,1)}, u32[]{:S(2)}, u32[]{:S(2)}) collective-permute-start(bf16[256,2048]{1,0:T(8,128)(2,1)} %slice.78), channel_id=1, source_target_pairs={{0,8},{4,12},{8,0},{12,4},{16,24},{20,28},{24,16},{28,20},{1,9},{5... | collective-permute-start | bytes 3145736 | tf_op jit(solution)/shard_map/ppermute | solution.py:722
  242.7 25.2 %collective-permute-start.10 = (bf16[256,2048]{1,0:T(8,128)(2,1)}, bf16[256,2048]{1,0:T(8,128)(2,1)}, u32[]{:S(2)}, u32[]{:S(2)}) collective-permute-start(bf16[256,2048]{1,0:T(8,128)(2,1)} %slice.79), channel_id=1, source_target_pairs={{0,16},{4,20},{8,24},{12,28},{16,0},{20,4},{24,8},{28,12},{1,17},{... | collective-permute-start | bytes 3145736 | tf_op jit(solution)/shard_map/ppermute | solution.py:722
  270.1 6.0 collective-permute-start.11
  282.6 191.2 %reduce-scatter.10.cloned.1.call-start = ((), (), s32[]{:S(2)}) async-start(), calls=%async_computation.9 | async-start | bytes 18874368 | tf_op jit(solution)/shard_map/reduce_scatter | solution.py:878
  357.9 209.1 %all-reduce.10.cloned.1.call-start = ((), (), s32[]{:S(2)}) async-start(), calls=%async_computation.10 | async-start | bytes 4194304 | tf_op jit(solution)/shard_map/psum | solution.py:892
  367.7 4.4 copy-start.33
  480.9 142.3 %reduce-scatter.6.cloned.1.call-start = ((), (), s32[]{:S(2)}) async-start(), calls=%async_computation.7 | async-start | bytes 18874368 | tf_op jit(solution)/shard_map/reduce_scatter | solution.py:735
  481.5 246.2 %all-reduce.12.cloned.1.call-start = ((), (), s32[]{:S(2)}) async-start(), calls=%async_computation.11 | async-start | bytes 4194304 | tf_op jit(solution)/shard_map/psum | solution.py:921
  481.5 6.0 copy-start.7
  487.5 25.2 %copy-start.6 = (bf16[8,640,384]{2,1,0:T(8,128)(2,1)S(1)}, bf16[8,640,384]{2,1,0:T(8,128)(2,1)}, u32[]{:S(2)}) copy-start(bf16[8,640,384]{2,1,0:T(8,128)(2,1)} %get-tuple-element.117) | copy-start | bytes 11796484
  628.2 2.4 collective-permute-start.12
  628.2 6.0 collective-permute-start.13
  628.7 9.8 %copy-start.24 = (f32[1,2048]{1,0:T(1,128)S(1)}, f32[1,2048]{1,0:T(1,128)}, u32[]{:S(2)}) copy-start(f32[1,2048]{1,0:T(1,128)} %get-tuple-element.137) | copy-start | bytes 24580
  632.9 19.0 %collective-permute-start.15 = (bf16[512,640]{1,0:T(8,128)(2,1)}, bf16[512,640]{1,0:T(8,128)(2,1)}, u32[]{:S(2)}, u32[]{:S(2)}) collective-permute-start(bf16[512,640]{1,0:T(8,128)(2,1)} %fusion.15), channel_id=1, source_target_pairs={{16,0},{20,4},{24,8},{28,12},{17,1},{21,5},{25,9},{29,13},{18,2},{... | collective-permute-start | bytes 1966088 | tf_op jit(solution)/shard_map/ppermute | solution.py:680
  636.5 19.0 %collective-permute-start.14 = (bf16[512,640]{1,0:T(8,128)(2,1)}, bf16[512,640]{1,0:T(8,128)(2,1)}, u32[]{:S(2)}, u32[]{:S(2)}) collective-permute-start(bf16[512,640]{1,0:T(8,128)(2,1)} %add_convert_fusion.3), channel_id=1, source_target_pairs={{8,0},{12,4},{16,8},{20,12},{24,16},{28,20},{9,1},{13,5},{17,9},{2... | collective-permute-start | bytes 1966088 | tf_op jit(solution)/shard_map/ppermute | solution.py:680
  638.4 19.3 %copy-start.16 = (f32[512]{0:T(512)S(1)}, f32[512]{0:T(512)}, u32[]{:S(2)}) copy-start(f32[512]{0:T(512)} %copy-done.15) | copy-start | bytes 6148
  638.4 19.3 %copy-start.22 = (f32[512]{0:T(512)S(1)}, f32[512]{0:T(512)}, u32[]{:S(2)}) copy-start(f32[512]{0:T(512)} %param.26) | copy-start | bytes 6148
  638.4 89.2 %reduce-scatter.12.cloned.1.call-start = ((), (), s32[]{:S(2)}) async-start(), calls=%async_computation.12 | async-start | bytes 3538944 | tf_op jit(solution)/shard_map/reduce_scatter | solution.py:735
  638.5 19.2 %copy-start.4 = (f32[512,576]{1,0:T(8,128)S(1)}, f32[512,576]{1,0:T(8,128)}, u32[]{:S(2)}) copy-start(f32[512,576]{1,0:T(8,128)} %copy-done.3) | copy-start | bytes 3538948
  638.5 19.5 %copy-start.18 = (f32[512]{0:T(512)S(1)}, f32[512]{0:T(512)}, u32[]{:S(2)}) copy-start(f32[512]{0:T(512)} %copy-done.17) | copy-start | bytes 6148
  638.5 19.5 %copy-start.30 = (f32[32]{0:T(128)S(1)}, f32[32]{0:T(128)}, u32[]{:S(2)}) copy-start(f32[32]{0:T(128)} %copy-done.29) | copy-start | bytes 388
  638.5 21.4 %copy-start.20 = (f32[512]{0:T(512)S(1)}, f32[512]{0:T(512)}, u32[]{:S(2)}) copy-start(f32[512]{0:T(512)} %copy-done.19) | copy-start | bytes 6148
  661.3 4.0 copy-start.28
  672.4 156.9 %all-reduce.14.cloned.1.call-start = ((), (), s32[]{:S(2)}) async-start(), calls=%async_computation.14 | async-start | bytes 4980736 | tf_op jit(solution)/shard_map/psum | solution.py:949
  727.7 113.5 %reduce-scatter.14.cloned.1.call-start = ((), (), s32[]{:S(2)}) async-start(), calls=%async_computation.13 | async-start | bytes 7077888 | tf_op jit(solution)/shard_map/reduce_scatter | solution.py:735
  727.7 4.5 copy-start.2
  727.7 4.5 copy-start.36
  (15 other events, 39.1 us)
Sparse Core Ops, SparseCore 0:
  57.3 91.6 all-gather.1
  282.7 70.8 reduce-scatter.7
  358.0 115.7 reduce-scatter.9
  485.4 115.9 reduce-scatter.5
  672.6 54.9 reduce-scatter.11
  746.9 61.7 reduce-scatter.13
Sparse Core Ops, SparseCore 1:
  93.1 87.3 all-reduce.7
  481.0 85.9 all-reduce.9
  638.5 89.1 all-reduce.11
  730.3 99.0 all-reduce.13

commit v6 on v5

--- a/solution.py
+++ b/solution.py
@@ -40,8 +40,7 @@
 
 
 def attend_setup(
-    head, heads, step, qp_ref, cos_ref, sin_ref, wx_ref, sq_ref, sk_ref, keys,
-    q_ref, key_ref, v_ref, bias_ref,
+    head, heads, step, qp_ref, cos_ref, sin_ref, at_ref, sq_ref, seq_ref, keys, q_ref, key_ref, bias_ref
 ):
     rows = qp_ref.shape[0]
 
@@ -49,10 +48,13 @@
     def _():
         for at in range(0, rows, step):
             part = pl.ds(at, step)
-            allowed = (sq_ref[part, 0:1] == sk_ref[0:1, :]) & (
-                sk_ref[1:2, :] <= sq_ref[part, 1:2]
-            )
-            bias_ref[part, :] = jnp.where(allowed, 0.0, -1e30).astype(BF)
+            for i in range(len(keys)):
+                block = at_ref[i]
+                where = pl.multiple_of(jnp.maximum(block, 0) * rows, 128)
+                sequence = jnp.where(block >= 0, seq_ref[0:1, pl.ds(where, rows)], -1)
+                position = block * rows + lax.broadcasted_iota(jnp.int32, (1, rows), 1)
+                allowed = (sq_ref[part, 0:1] == sequence) & (position <= sq_ref[part, 1:2])
+                bias_ref[part, i * rows : (i + 1) * rows] = jnp.where(allowed, 0.0, -1e30).astype(BF)
         for i, key in enumerate(keys):
             key_ref[i * rows : (i + 1) * rows, DN:] = key[:, KVR : KVR + DR]
 
@@ -68,46 +70,47 @@
             q_ref[:, DN : DN + DR // 2] = (front * cosine - back * sine).astype(BF)
             q_ref[:, DN + DR // 2 :] = (back * cosine + front * sine).astype(BF)
 
-    for i, key in enumerate(keys):
-        kv = mm(key[:, :KVR], wx_ref[...], 1, 0).astype(BF)
-        key_ref[i * rows : (i + 1) * rows, :DN] = kv[:, :DN]
-        v_ref[i * rows : (i + 1) * rows, :] = kv[:, DN:]
-
-
-def attend_kernel(heads, step, qp_ref, cos_ref, sin_ref, wx_ref, sq_ref, sk_ref, *rest):
-    keys, (o_ref, lse_ref, q_ref, key_ref, v_ref, bias_ref) = rest[:-6], rest[-6:]
+
+def attend_kernel(heads, step, qp_ref, cos_ref, sin_ref, wx_ref, at_ref, sq_ref, seq_ref, *rest):
+    keys, (o_ref, lse_ref, kv_ref, q_ref, key_ref, bias_ref) = rest[:-6], rest[-6:]
     rows = qp_ref.shape[0]
     scale = (DN + DR) ** (-0.5)
     attend_setup(
-        pl.program_id(0), heads, step, qp_ref, cos_ref, sin_ref, wx_ref, sq_ref, sk_ref, keys,
-        q_ref, key_ref, v_ref, bias_ref,
-    )
+        pl.program_id(0), heads, step, qp_ref, cos_ref, sin_ref, at_ref, sq_ref, seq_ref, keys,
+        q_ref, key_ref, bias_ref,
+    )
+    for i, key in enumerate(keys):
+        part = pl.ds(i * rows, rows)
+        kv = mm(key[:, :KVR], wx_ref[...], 1, 0).astype(BF)
+        kv_ref[part, :] = kv
+        key_ref[part, :DN] = kv[:, :DN]
     for at in range(0, rows, step):
         part = pl.ds(at, step)
         s = mm(q_ref[part, :], key_ref[...], 1, 1) * scale + bias_ref[part, :].astype(F32)
         top = jnp.max(s, axis=-1, keepdims=True)
         p = jnp.exp(s - top)
         total = jnp.sum(p, axis=-1, keepdims=True)
-        o_ref[part, :] = mm((p * (1.0 / total)).astype(BF), v_ref[...], 1, 0).astype(BF)
+        o_ref[part, :] = mm((p * (1.0 / total)).astype(BF), kv_ref[:, DN:], 1, 0).astype(BF)
         lse_ref[0, part, :] = top + jnp.log(total)
 
 
-def attend_specs(query_pre, cosine, w_expand, place_q, place_k, keys):
+def attend_specs(query_pre, cosine, w_expand, blocks, place_q, sequences, keys):
     return [
         fixed(query_pre.shape),
         fixed(cosine.shape),
         fixed(cosine.shape),
         pl.BlockSpec((KVR, DN + DV), lambda h: (0, h)),
+        smem(),
         fixed(place_q.shape),
-        fixed(place_k.shape),
+        fixed(sequences.shape),
     ], [fixed(keys[0].shape) for _ in keys]
 
 
-def attend(query_pre, cosine, sine, w_expand, place_q, place_k, keys):
+def attend(query_pre, cosine, sine, w_expand, blocks, place_q, sequences, keys):
     rows = query_pre.shape[0]
     heads = query_pre.shape[1] // (DN + DR)
     window = rows * len(keys)
-    specs, key_specs = attend_specs(query_pre, cosine, w_expand, place_q, place_k, keys)
+    specs, key_specs = attend_specs(query_pre, cosine, w_expand, blocks, place_q, sequences, keys)
     return pl.pallas_call(
         functools.partial(attend_kernel, heads, rows // 2),
         name="attend",
@@ -116,38 +119,40 @@
         out_specs=[
             pl.BlockSpec((rows, DV), lambda h: (0, h)),
             pl.BlockSpec((1, rows, 1), lambda h: (h, 0, 0)),
+            pl.BlockSpec((window, DN + DV), lambda h: (0, h)),
         ],
         out_shape=[
             jax.ShapeDtypeStruct((rows, heads * DV), BF),
             jax.ShapeDtypeStruct((heads, rows, 1), F32),
+            jax.ShapeDtypeStruct((window, heads * (DN + DV)), BF),
         ],
         scratch_shapes=[
             pltpu.VMEM((rows, DN + DR), BF),
             pltpu.VMEM((window, DN + DR), BF),
-            pltpu.VMEM((window, DV), BF),
             pltpu.VMEM((rows, window), BF),
         ],
         compiler_params=params(),
         cost_estimate=cost(
             2 * heads * window * (rows * 384 + KVR * 256), 2 * window * 640, heads * rows * window
         ),
-    )(query_pre, cosine, sine, w_expand, place_q, place_k, *keys)
+    )(query_pre, cosine, sine, w_expand, blocks, place_q, sequences, *keys)
 
 
 def attend_back_kernel(
-    heads, step, count, qp_ref, cos_ref, sin_ref, wx_ref, sq_ref, sk_ref, lse_ref, do_ref, *rest
+    heads, step, count, qp_ref, cos_ref, sin_ref, wx_ref, at_ref, sq_ref, seq_ref, lse_ref, do_ref, kv_ref,
+    *rest
 ):
     keys, rest = rest[:count], rest[count:]
-    dq_ref, gx_ref = rest[:2]
+    dq_ref, dkv_ref = rest[:2]
     grads = rest[2 : 2 + count]
-    q_ref, key_ref, v_ref, bias_ref, dk_ref, dv_ref, dkv_ref, acc_ref, dqs_ref = rest[2 + count :]
+    q_ref, key_ref, bias_ref, dk_ref, dv_ref, acc_ref, dqs_ref = rest[2 + count :]
     rows = qp_ref.shape[0]
     head = pl.program_id(0)
     scale = (DN + DR) ** (-0.5)
     attend_setup(
-        head, heads, step, qp_ref, cos_ref, sin_ref, wx_ref, sq_ref, sk_ref, keys,
-        q_ref, key_ref, v_ref, bias_ref,
-    )
+        head, heads, step, qp_ref, cos_ref, sin_ref, at_ref, sq_ref, seq_ref, keys, q_ref, key_ref, bias_ref
+    )
+    key_ref[:, :DN] = kv_ref[:, :DN]
 
     @pl.when(head == 0)
     def _():
@@ -159,7 +164,7 @@
         do = do_ref[part, :]
         s = mm(q, key_ref[...], 1, 1) * scale + bias_ref[part, :].astype(F32)
         p = jnp.exp(s - lse_ref[0, part, :])
-        dp = mm(do, v_ref[...], 1, 1)
+        dp = mm(do, kv_ref[:, DN:], 1, 1)
         ds = (p * (dp - jnp.sum(p * dp, axis=-1, keepdims=True))).astype(BF)
         dqs_ref[part, :] = mm(ds, key_ref[...], 1, 0) * scale
         dk = mm(ds, q, 0, 0) * scale
@@ -174,10 +179,6 @@
     dkv_ref[:, DN:] = dv_ref[...].astype(BF)
     acc_ref[:, :KVR] += mm(dkv_ref[...], wx_ref[...], 1, 1)
     acc_ref[:, KVR : KVR + DR] += dk_ref[:, DN:]
-    expand_grad = jnp.zeros((KVR, DN + DV), F32)
-    for i, key in enumerate(keys):
-        expand_grad += mm(key[:, :KVR], dkv_ref[i * rows : (i + 1) * rows, :], 0, 0)
-    gx_ref[...] = expand_grad.astype(BF)
     for k in range(heads):
 
         @pl.when(head == k)
@@ -196,12 +197,12 @@
             grad[...] = acc_ref[i * rows : (i + 1) * rows, :].astype(grad.dtype)
 
 
-def attend_back(query_pre, cosine, sine, w_expand, place_q, place_k, lse, attended_grad, keys):
+def attend_back(query_pre, cosine, sine, w_expand, blocks, place_q, sequences, lse, attended_grad, kv, keys):
     rows = query_pre.shape[0]
     heads = query_pre.shape[1] // (DN + DR)
     window = rows * len(keys)
     count = len(keys)
-    specs, key_specs = attend_specs(query_pre, cosine, w_expand, place_q, place_k, keys)
+    specs, key_specs = attend_specs(query_pre, cosine, w_expand, blocks, place_q, sequences, keys)
     wide = keys[0].shape[1]
     return pl.pallas_call(
         functools.partial(attend_back_kernel, heads, rows // 2, count),
@@ -211,24 +212,23 @@
         + [
             pl.BlockSpec((1, rows, 1), lambda h: (h, 0, 0)),
             pl.BlockSpec((rows, DV), lambda h: (0, h)),
+            pl.BlockSpec((window, DN + DV), lambda h: (0, h)),
         ]
         + key_specs,
-        out_specs=[fixed(query_pre.shape), pl.BlockSpec((KVR, DN + DV), lambda h: (0, h))]
+        out_specs=[fixed(query_pre.shape), pl.BlockSpec((window, DN + DV), lambda h: (0, h))]
         + [fixed((rows, wide)) for _ in keys],
         out_shape=[
             jax.ShapeDtypeStruct(query_pre.shape, BF),
-            jax.ShapeDtypeStruct(w_expand.shape, BF),
+            jax.ShapeDtypeStruct((window, w_expand.shape[1]), BF),
         ]
         + [jax.ShapeDtypeStruct((rows, wide), BF) for _ in keys[1:]]
         + [jax.ShapeDtypeStruct((rows, wide), F32)],
         scratch_shapes=[
             pltpu.VMEM((rows, DN + DR), BF),
             pltpu.VMEM((window, DN + DR), BF),
-            pltpu.VMEM((window, DV), BF),
             pltpu.VMEM((rows, window), BF),
             pltpu.VMEM((window, DN + DR), F32),
             pltpu.VMEM((window, DV), F32),
-            pltpu.VMEM((window, DN + DV), BF),
             pltpu.VMEM((window, wide), F32),
             pltpu.VMEM((rows, DN + DR), F32),
         ],
@@ -236,7 +236,7 @@
         cost_estimate=cost(
             2 * heads * window * (rows * 1024 + KVR * 768), 4 * window * 640, heads * rows * window
         ),
-    )(query_pre, cosine, sine, w_expand, place_q, place_k, lse, attended_grad, *keys)
+    )(query_pre, cosine, sine, w_expand, blocks, place_q, sequences, lse, attended_grad, kv, *keys)
 
 
 def one_hot(slot_ref):
@@ -275,26 +275,30 @@
     )(order, slot, values)
 
 
-def pick_route_kernel(count, pieces, first_ref, slot_ref, w_ref, *refs):
+def pick_route_kernel(count, pieces, parts, first_ref, slot_ref, w_ref, *refs):
     o_ref, p_ref, g_ref = refs[-3:]
     experts, rows = slot_ref.shape[0], slot_ref.shape[3]
+    size = rows // parts
     for n in range(pieces):
-        x = refs[n][...]
-        logits = mm(x, w_ref[...], 1, 1)
-        lane = lax.broadcasted_iota(jnp.int32, logits.shape, 1)
-        logits = jnp.where(lane < count, logits, -1e30)
-        e = jnp.exp(logits - jnp.max(logits, axis=-1, keepdims=True))
-        probs = e / jnp.sum(e, axis=-1, keepdims=True)
-        p_ref[n * rows : (n + 1) * rows, :] = probs
-        high = probs.astype(BF)
-        low = (probs - high.astype(F32)).astype(BF)
         place = lax.broadcasted_iota(jnp.int32, (SLOTS, rows), 0)
         chosen = jnp.concatenate(
             [(slot_ref[i, n] == place).astype(F32).astype(BF) for i in range(experts)], axis=0
         )
-        picked = mm(chosen, x, 1, 0).astype(BF)
-        o_ref[:, n] = picked.reshape(experts, SLOTS, -1)
-        taken = mm(chosen, high, 1, 0) + mm(chosen, low, 1, 0)
+        picked, taken = 0.0, 0.0
+        for m in range(parts):
+            x = refs[n * parts + m][...]
+            logits = mm(x, w_ref[...], 1, 1)
+            lane = lax.broadcasted_iota(jnp.int32, logits.shape, 1)
+            logits = jnp.where(lane < count, logits, -1e30)
+            e = jnp.exp(logits - jnp.max(logits, axis=-1, keepdims=True))
+            probs = e / jnp.sum(e, axis=-1, keepdims=True)
+            p_ref[n * rows + m * size : n * rows + (m + 1) * size, :] = probs
+            high = probs.astype(BF)
+            low = (probs - high.astype(F32)).astype(BF)
+            part = chosen[:, m * size : (m + 1) * size]
+            picked += mm(part, x, 1, 0)
+            taken += mm(part, high, 1, 0) + mm(part, low, 1, 0)
+        o_ref[:, n] = picked.astype(BF).reshape(experts, SLOTS, -1)
         lane = lax.broadcasted_iota(jnp.int32, (SLOTS, taken.shape[1]), 1)
         for i in range(experts):
             part = taken[i * SLOTS : (i + 1) * SLOTS, :]
@@ -305,13 +309,15 @@
 
 def pick_route(first, slot, values, router_rows, count, at, steps, earlier):
     experts, blocks, _, rows = slot.shape
+    parts = len(values[0])
     pieces = len(values)
+    values = [part for value in values for part in value]
     width = values[0].shape[1]
     lanes = router_rows.shape[0]
     at = at // pieces
     whole = pl.BlockSpec(memory_space=pl.ANY)
     return pl.pallas_call(
-        functools.partial(pick_route_kernel, count, pieces),
+        functools.partial(pick_route_kernel, count, pieces, parts),
         name="pick_route",
         grid=(steps,),
         in_specs=[
@@ -319,7 +325,7 @@
             pl.BlockSpec((experts, pieces, 1, rows), lambda b: (0, at + b, 0, 0)),
             fixed(router_rows.shape),
         ]
-        + [pl.BlockSpec((rows, width), lambda b: (b, 0)) for _ in values]
+        + [pl.BlockSpec((rows // parts, width), lambda b: (b, 0)) for _ in values]
         + [whole for _ in earlier],
         out_specs=[
             pl.BlockSpec((experts, pieces, SLOTS, width), lambda b: (0, at + b, 0, 0)),
@@ -331,20 +337,68 @@
             jax.ShapeDtypeStruct((blocks * rows, lanes), F32),
             jax.ShapeDtypeStruct((experts, blocks, SLOTS, 1), F32),
         ],
-        input_output_aliases={3 + pieces + i: i for i in range(len(earlier))},
-        compiler_params=params(),
-        cost_estimate=cost(
-            pieces * steps * rows * width,
-            pieces * steps * width * rows,
-        ),
+        input_output_aliases={3 + len(values) + i: i for i in range(len(earlier))},
+        compiler_params=params(),
+        cost_estimate=cost(pieces * steps * rows * width, pieces * steps * width * rows),
     )(first, slot, router_rows, *values, *earlier)
+
+
+def route_grad_kernel(count, *refs):
+    total = 0.0
+    grads, values = refs[:count], refs[count:-1]
+    which, at = 0, 0
+    for ref in values:
+        size = ref.shape[0]
+        total += mm(grads[which][at : at + size, :], ref[...], 0, 0)
+        at += size
+        if at == grads[which].shape[0]:
+            which, at = which + 1, 0
+    refs[-1][...] = total.astype(BF)
+
+
+def route_grad(grads, values):
+    width = values[0].shape[1]
+    lanes = grads[0].shape[1]
+    return pl.pallas_call(
+        functools.partial(route_grad_kernel, len(grads)),
+        name="route_grad",
+        grid=(1,),
+        in_specs=[fixed(array.shape) for array in [*grads, *values]],
+        out_specs=fixed((lanes, width)),
+        out_shape=jax.ShapeDtypeStruct((lanes, width), BF),
+        compiler_params=params(),
+        cost_estimate=cost(lanes * width, lanes * width),
+    )(*grads, *values)
+
+
+def parts_kernel(lg_ref, x_ref, route_ref, gain_ref, o_ref):
+    inner = lg_ref.shape[1]
+    count = o_ref.shape[0] - inner - gain_ref.shape[0]
+    o_ref[:inner, :] = mm(lg_ref[...], x_ref[...], 0, 0).astype(BF)
+    o_ref[inner : inner + count, :] = route_ref[:count, :]
+    o_ref[inner + count :, :] = gain_ref[...].astype(BF)
+
+
+def parts_rows(latent_grad, values, route, gains, count):
+    width = values.shape[1]
+    shape = (latent_grad.shape[1] + count + gains.shape[0], width)
+    return pl.pallas_call(
+        parts_kernel,
+        name="parts_rows",
+        grid=(1,),
+        in_specs=[fixed(array.shape) for array in (latent_grad, values, route, gains)],
+        out_specs=fixed(shape),
+        out_shape=jax.ShapeDtypeStruct(shape, BF),
+        compiler_params=params(),
+        cost_estimate=cost(width, width),
+    )(latent_grad, values, route, gains)
 
 
 def put_kernel(order_ref, place_ref, r_ref, o_ref):
     o_ref[...] = mm(place_ref[0], r_ref[...].reshape(-1, r_ref.shape[-1]), 1, 0).astype(BF)
 
 
-def put_route_kernel(order_ref, first_ref, place_ref, r_ref, p_ref, pg_ref, w_ref, o_ref, lg_ref):
+def returned(first_ref, place_ref, r_ref, p_ref, pg_ref, w_ref):
     experts, rows = pg_ref.shape[0], pg_ref.shape[3]
     by_expert = jnp.concatenate(
         [pg_ref[i, 0] for i in range(experts)] + [jnp.zeros((1, rows), F32)] * (-experts % 8), axis=0
@@ -359,9 +413,45 @@
     spread = spread.astype(F32).astype(BF)
     grad = mm(high, spread, 0, 0) + mm(low, spread, 0, 0)
     back = (probs * (grad - jnp.sum(probs * grad, axis=-1, keepdims=True))).astype(BF)
+    total = mm(place_ref[0], r_ref[...].reshape(-1, r_ref.shape[-1]), 1, 0)
+    return total + mm(back, w_ref[...], 1, 0), back
+
+
+def put_route_kernel(
+    order_ref, first_ref, place_ref, r_ref, p_ref, pg_ref, w_ref, *rest
+):
+    total, back = returned(first_ref, place_ref, r_ref, p_ref, pg_ref, w_ref)
+    if len(rest) == 3:
+        total += rest[0][...].astype(F32)
+    rest[-2][...] = total.astype(BF)
+    rest[-1][...] = back
+
+
+def put_cross_kernel(
+    order_ref, first_ref, place_ref, r_ref, p_ref, pg_ref, w_ref, add_ref,
+    sx_ref, sy_ref, keep_ref, lg_ref,
+):
+    total, back = returned(first_ref, place_ref, r_ref, p_ref, pg_ref, w_ref)
     lg_ref[...] = back
-    total = mm(place_ref[0], r_ref[...].reshape(-1, r_ref.shape[-1]), 1, 0)
-    o_ref[...] = (total + mm(back, w_ref[...], 1, 0)).astype(BF)
+    total = (total + add_ref[...].astype(F32)).astype(BF)
+    half = total.shape[0] // 2
+    top, bottom = total[:half], total[half:]
+    step = pl.program_id(0)
+
+    @pl.when(step == 0)
+    def _():
+        sx_ref[half:, :] = top
+        keep_ref[half:, :] = bottom
+
+    @pl.when(step == 1)
+    def _():
+        sy_ref[half:, :] = bottom
+        keep_ref[:half, :] = top
+
+    @pl.when(step == 2)
+    def _():
+        sx_ref[:half, :] = top
+        sy_ref[:half, :] = bottom
 
 
 def put_specs(places, picked):
@@ -371,11 +461,6 @@
         pl.BlockSpec((1, rows, slots), lambda b, o: (b, 0, 0)),
         pl.BlockSpec((experts, 1, SLOTS, width), lambda b, o: (0, b, 0, 0)),
     ]
-
-
-def put_cost(places, width):
-    blocks, rows, slots = places.shape
-    return cost(2 * blocks * slots * rows * width, 2 * blocks * width * (rows + slots))
 
 
 def put(order, places, picked):
@@ -392,39 +477,44 @@
         ),
         out_shape=jax.ShapeDtypeStruct((blocks * rows, width), BF),
         compiler_params=params(),
-        cost_estimate=put_cost(places, width),
+        cost_estimate=cost(blocks * rows * width, blocks * rows * width),
     )(order, places, picked)
 
 
-def put_route(order, first, places, picked, probs, probs_grad, router_rows):
-    blocks, rows, _ = places.shape
+def put_route(order, absolute, first, places, picked, probs, probs_grad, router_rows, added):
+    _, rows, slots = places.shape
+    blocks = order.shape[0]
     experts, width = picked.shape[0], picked.shape[3]
     lanes = probs.shape[1]
-    return pl.pallas_call(
-        put_route_kernel,
+    come = (lambda b, o: b) if absolute else (lambda b, o: o[b])
+    go = (lambda b, o: o[b]) if absolute else (lambda b, o: b)
+    cross = added is not None and blocks == 3
+    whole = pl.BlockSpec((rows, width), lambda b, o: (0, 0))
+    out_specs = [whole] * 3 if cross else [pl.BlockSpec((rows, width), lambda b, o: (go(b, o), 0))]
+    sizes = [rows] * 3 if cross else [blocks * rows]
+    more = [] if added is None else [added]
+    return pl.pallas_call(
+        put_cross_kernel if cross else put_route_kernel,
         name="put_route",
         grid_spec=pltpu.PrefetchScalarGridSpec(
             num_scalar_prefetch=1,
             grid=(blocks,),
-            in_specs=[smem()]
-            + put_specs(places, picked)
-            + [
-                pl.BlockSpec((rows, lanes), lambda b, o: (b, 0)),
-                pl.BlockSpec((experts, 1, 1, rows), lambda b, o: (0, b, 0, 0)),
+            in_specs=[
+                smem(),
+                pl.BlockSpec((1, rows, slots), lambda b, o: (come(b, o), 0, 0)),
+                pl.BlockSpec((experts, 1, SLOTS, width), lambda b, o: (0, come(b, o), 0, 0)),
+                pl.BlockSpec((rows, lanes), lambda b, o: (come(b, o), 0)),
+                pl.BlockSpec((experts, 1, 1, rows), lambda b, o: (0, come(b, o), 0, 0)),
                 fixed(router_rows.shape),
-            ],
-            out_specs=[
-                pl.BlockSpec((rows, width), lambda b, o: (o[b], 0)),
-                pl.BlockSpec((rows, lanes), lambda b, o: (b, 0)),
-            ],
+            ]
+            + [pl.BlockSpec((rows, width), lambda b, o: (b, 0)) for _ in more],
+            out_specs=out_specs + [pl.BlockSpec((rows, lanes), lambda b, o: (b, 0))],
         ),
-        out_shape=[
-            jax.ShapeDtypeStruct((blocks * rows, width), BF),
-            jax.ShapeDtypeStruct((blocks * rows, lanes), BF),
-        ],
-        compiler_params=params(),
-        cost_estimate=put_cost(places, width),
-    )(order, first, places, picked, probs, probs_grad, router_rows)
+        out_shape=[jax.ShapeDtypeStruct((size, width), BF) for size in sizes]
+        + [jax.ShapeDtypeStruct((blocks * rows, lanes), BF)],
+        compiler_params=params(),
+        cost_estimate=cost(blocks * rows * width, blocks * rows * width),
+    )(order, first, places, picked, probs, probs_grad, router_rows, *more)
 
 
 def down_back_kernel(x_ref, w_ref, o_ref):
@@ -479,10 +569,7 @@
         out_specs=pl.BlockSpec((1, blocks, slots, width), lambda e: (e, 0, 0, 0)),
         out_shape=jax.ShapeDtypeStruct((experts, blocks, slots, width), BF),
         compiler_params=params(),
-        cost_estimate=cost(
-            2 * experts * count * width * ff,
-            2 * experts * (count * width + ff * width + count * wide),
-        ),
+        cost_estimate=cost(count * width, count * width),
     )(active, down)
 
 
@@ -567,76 +654,103 @@
     )(rows, gate_t, up_t, back, slot, slot_gates)
 
 
-def norm_kernel(x_ref, add_ref, gain_ref, sum_ref, o_ref):
+def norm_kernel(x_ref, add_ref, gain_ref, sum_ref, top_ref, bottom_ref):
     x = x_ref[...].astype(F32) + add_ref[...].astype(F32)
     sum_ref[...] = x
     scale = lax.rsqrt(jnp.mean(x * x, axis=-1, keepdims=True) + epsilon)
-    o_ref[...] = (x * scale * gain_ref[...]).astype(BF)
+    out = (x * scale * gain_ref[...]).astype(BF)
+
+    @pl.when(pl.program_id(0) < 2)
+    def _():
+        top_ref[...] = out
+
+    @pl.when(pl.program_id(0) >= 2)
+    def _():
+        bottom_ref[...] = out
 
 
 def norm_sum(values, added, gain):
     rows, width = values.shape
     block = pl.BlockSpec((rows // 4, width), lambda i: (i, 0))
+    half = jax.ShapeDtypeStruct((rows // 2, width), BF)
     return pl.pallas_call(
         norm_kernel,
         name="norm_sum",
         grid=(4,),
         in_specs=[block, block, fixed((1, width))],
-        out_specs=[block, block],
-        out_shape=[
-            jax.ShapeDtypeStruct((rows, width), F32),
-            jax.ShapeDtypeStruct((rows, width), BF),
+        out_specs=[
+            block,
+            pl.BlockSpec((rows // 4, width), lambda i: (jnp.minimum(i, 1), 0)),
+            pl.BlockSpec((rows // 4, width), lambda i: (jnp.maximum(i - 2, 0), 0)),
         ],
+        out_shape=[jax.ShapeDtypeStruct((rows, width), F32), half, half],
         compiler_params=params(),
         cost_estimate=cost(8 * rows * width, 10 * rows * width),
     )(values, added, gain.reshape(1, width))
 
 
-def norm_back_kernel(x_ref, up_ref, res_ref, gain_ref, *outs):
+def norm_back_kernel(x_ref, up_ref, res_ref, gain_ref, *rest):
     x = x_ref[...].astype(F32)
     up = up_ref[...].astype(F32)
     scale = lax.rsqrt(jnp.mean(x * x, axis=-1, keepdims=True) + epsilon)
     scaled = x * scale
-    if len(outs) > 1:
+    if len(rest) > 1:
+        gain_grad_ref = rest[4]
 
         @pl.when(pl.program_id(0) == 0)
         def _():
-            outs[2][...] = jnp.zeros_like(outs[2])
-
-        outs[2][...] += jnp.sum(up * scaled, axis=0, keepdims=True)
+            gain_grad_ref[...] = jnp.zeros_like(gain_grad_ref)
+
+        gain_grad_ref[...] += jnp.sum(up * scaled, axis=0, keepdims=True)
     up = up * gain_ref[...]
     back = scale * (up - scaled * jnp.mean(up * scaled, axis=-1, keepdims=True))
     total = res_ref[...].astype(F32) + back
-    outs[0][...] = total.astype(BF)
-    if len(outs) > 1:
-        outs[1][...] = total
-
-
-def norm_back(values, upstream, residual, gain, last):
+    if len(rest) == 1:
+        rest[0][...] = total.astype(BF)
+        return
+    w_ref, low_ref, total_ref, out_ref = rest[:4]
+    low = total.astype(BF)
+    low_ref[...] = low
+    total_ref[...] = total
+    out_ref[...] = mm(low, w_ref[...], 1, 1).astype(BF)
+
+
+def norm_back(values, upstream, residual, gain, weight):
     rows, width = values.shape
     block = pl.BlockSpec((rows // 4, width), lambda i: (i, 0))
-    specs = [block] if last else [block, block, fixed((1, width))]
+    in_specs = [block, block, block, fixed((1, width))]
+    out_specs = [block]
     shapes = [jax.ShapeDtypeStruct((rows, width), BF)]
-    if not last:
+    more = []
+    if weight is not None:
+        inner = weight.shape[0]
+        more = [weight]
+        in_specs += [fixed(weight.shape)]
+        out_specs += [
+            block,
+            pl.BlockSpec((rows // 4, inner), lambda i: (i, 0)),
+            fixed((1, width)),
+        ]
         shapes += [
             jax.ShapeDtypeStruct((rows, width), F32),
+            jax.ShapeDtypeStruct((rows, inner), BF),
             jax.ShapeDtypeStruct((1, width), F32),
         ]
     return pl.pallas_call(
         norm_back_kernel,
         name="norm_back",
         grid=(4,),
-        in_specs=[block, block, block, fixed((1, width))],
-        out_specs=specs,
+        in_specs=in_specs,
+        out_specs=out_specs,
         out_shape=shapes,
         compiler_params=params(),
         cost_estimate=cost(12 * rows * width, 12 * rows * width),
-    )(values, upstream, residual, gain.reshape(1, width))
-
-
-def shared_kernel(x_ref, up_ref, wg_ref, wu_ref, wd_ref, act_ref, dg_ref, du_ref, grad_ref):
+    )(values, upstream, residual, gain.reshape(1, width), *more)
+
+
+def shared_kernel(top_ref, bottom_ref, up_ref, wg_ref, wu_ref, wd_ref, act_ref, dg_ref, du_ref, grad_ref):
     ff = wd_ref.shape[0]
-    x = x_ref[...]
+    x = jnp.concatenate([top_ref[...], bottom_ref[...]], axis=0)
     upstream = up_ref[...]
     a = mm(x, wg_ref[...], 1, 1)
     b = mm(x, wu_ref[...], 1, 1)
@@ -654,20 +768,49 @@
     grad_ref[2 * ff :, :] = mm(du, x, 0, 0).astype(BF)
 
 
-def shared_step(values, upstream, gate_t, up_t, down):
-    rows, width = values.shape
+def shared_step(top, bottom, upstream, gate_t, up_t, down):
+    rows, width = upstream.shape
     ff = down.shape[0]
     inner = jax.ShapeDtypeStruct((rows, ff), BF)
     return pl.pallas_call(
         shared_kernel,
         name="shared_step",
         grid=(1,),
-        in_specs=[fixed((rows, width))] * 2 + [fixed((ff, width))] * 3,
+        in_specs=[fixed(top.shape)] * 2 + [fixed((rows, width))] + [fixed((ff, width))] * 3,
         out_specs=[fixed((rows, ff))] * 3 + [fixed((3 * ff, width))],
         out_shape=[inner, inner, inner, jax.ShapeDtypeStruct((3 * ff, width), BF)],
         compiler_params=params(),
         cost_estimate=cost(rows * width, rows * width),
-    )(values, upstream, gate_t, up_t, down)
+    )(top, bottom, upstream, gate_t, up_t, down)
+
+
+def finals_kernel(x_ref, proj_ref, query_ref, expand_ref):
+    inner, rows = proj_ref.shape
+    wide = query_ref.shape[1]
+    part = x_ref.shape[1] - inner - wide
+    count = expand_ref.shape[0]
+    proj_ref[...] = x_ref[:, :inner].astype(F32).T
+    query_ref[...] = x_ref[:, inner : inner + wide].astype(F32)
+    for i in range(rows // count):
+        expand_ref[:, i * part : (i + 1) * part] = x_ref[
+            i * count : (i + 1) * count, inner + wide :
+        ].astype(F32)
+
+
+def finals(joined, inner, wide, count):
+    rows = joined.shape[0]
+    part = joined.shape[1] - inner - wide
+    shapes = [(inner, rows), (rows, wide), (count, rows // count * part)]
+    return pl.pallas_call(
+        finals_kernel,
+        name="finals",
+        grid=(1,),
+        in_specs=[fixed(joined.shape)],
+        out_specs=[fixed(shape) for shape in shapes],
+        out_shape=[jax.ShapeDtypeStruct(shape, F32) for shape in shapes],
+        compiler_params=params(),
+        cost_estimate=cost(rows, rows),
+    )(joined)
 
 
 def dot(eq, a, b):
@@ -770,18 +913,6 @@
     index_here = rank_dp * tok_rows + jnp.arange(tok_rows, dtype=jnp.int32)
     seq_here = lax.dynamic_slice_in_dim(seq_ids, rank_dp * tok_rows, tok_rows, 0)
     cosine, sine = rope_tables(seq_ids, seq_here, index_here)
-    odd = rank_dp % 2
-    blocks = [rank_dp - 4, rank_dp - 2, (rank_dp - 2) ^ 1, rank_dp - 3 + 2 * odd, rank_dp]
-    seq_padded = jnp.concatenate([jnp.full((4 * tok_rows,), -1, jnp.int32), seq_ids])
-    seq_keys = jnp.concatenate(
-        [lax.dynamic_slice_in_dim(seq_padded, (at + 4) * tok_rows, tok_rows, 0) for at in blocks]
-    )
-    key_index = jnp.concatenate(
-        [at * tok_rows + jnp.arange(tok_rows, dtype=jnp.int32) for at in blocks]
-    )
-    place_q = jnp.stack([seq_here, index_here], axis=1)
-    place_k = jnp.stack([seq_keys, key_index], axis=0)
-
     token_features = tokens.astype(F32)
     hidden_in = normed(token_features, input_gain).astype(BF)
     latent_full = jnp.dot(hidden_in, w_latent, preferred_element_type=F32)
@@ -790,18 +921,20 @@
     rope_key = rotate(latent_full[:, KVR:], cosine, sine).astype(BF)
     fill = jnp.zeros((tok_rows, -(KVR + DR) % 128), BF)
     own_keys = jnp.concatenate([latent, rope_key, fill], axis=1)
+    odd = rank_dp % 2
+    blocks = jnp.stack(
+        [rank_dp - 4, rank_dp - 2, (rank_dp - 2) ^ 1, rank_dp - 3 + 2 * odd, rank_dp]
+    ).astype(jnp.int32)
+    place_q = jnp.stack([seq_here, index_here], axis=1)
+    sequences = seq_ids.reshape(1, -1)
     before_two = passed_along(own_keys, "dp", 2)
     before_four = passed_along(own_keys, "dp", 4)
-    keys = [
-        before_four,
-        before_two,
-        swapped(before_two),
-        swapped(jnp.where(odd == 0, own_keys, before_four)),
-        own_keys,
-    ]
+    query_pre = jnp.dot(hidden_in, w_query, preferred_element_type=F32)
+    from_pair = swapped(jnp.where(odd == 0, own_keys, before_four))
+    before_two = after(before_two, query_pre, from_pair, place_q)
+    keys = [before_four, before_two, swapped(before_two), from_pair, own_keys]
     cot_all = lax.all_gather(after(cotangent, before_two, before_four), "dp", tiled=True)
-    query_pre = jnp.dot(hidden_in, w_query, preferred_element_type=F32)
-    attended, lse = attend(query_pre, cosine, sine, w_expand, place_q, place_k, keys)
+    attended, lse, kv = attend(query_pre, cosine, sine, w_expand, blocks, place_q, sequences, keys)
     attention_part = jnp.dot(attended, w_out, preferred_element_type=F32).astype(BF)
     attention = lax.psum(attention_part, "tensor")
 
@@ -826,80 +959,108 @@
     back = down_back(cot_rows, expert_down)
 
     attention = after(attention, cot_rows, places)
-    middle, hidden_mid = norm_sum(tokens, attention, middle_gain)
+    middle, *hidden_mid = norm_sum(tokens, attention, middle_gain)
     first = (rank_dp * experts_local).astype(jnp.int32).reshape(1)
     router_rows = jnp.pad(w_router.T, ((0, -all_experts % 128), (0, 0)))
     if direct:
-        half = tok_rows // 2
-        pair = swapped(hidden_mid)
-        by_x = turned(hidden_mid, 2)
-        by_y = turned(hidden_mid, 4)
+        pair = [swapped(part) for part in hidden_mid]
+        by_x = [turned(part, 2) for part in hidden_mid]
+        by_y = [turned(part, 4) for part in hidden_mid]
         held = pick_route(first, slot, [hidden_mid, pair], router_rows, all_experts, 0, 1, [])
     else:
-        hidden_all = lax.all_gather(hidden_mid, "dp", tiled=True)
-
-    hidden_shared = after(hidden_mid, pair) if direct else hidden_mid
+        hidden_all = lax.all_gather(jnp.concatenate(hidden_mid, axis=0), "dp", tiled=True)
+
+    top, bottom = hidden_mid
+    if direct:
+        top = after(top, pair[0])
     shared_active, shared_gate_grad, shared_up_grad, shared_grads = shared_step(
-        hidden_shared, cotangent, shared_gate.T, shared_up.T, shared_down
+        top, bottom, cotangent, shared_gate.T, shared_up.T, shared_down
     )
     shared_result = jnp.dot(shared_active, shared_down, preferred_element_type=F32)
     mid_from_shared = dot("tf,df->td", shared_gate_grad, shared_gate) + dot(
         "tf,df->td", shared_up_grad, shared_up
     )
     if direct:
-        by_x, by_y = lax.optimization_barrier((by_x, by_y, held[0], back, shared_grads))[:2]
-        pair_x, pair_y = swapped(by_x), swapped(by_y)
-        top = turned(by_y[:half], 2)
-        bottom = turned(by_x[half:], 4)
+        x_top, x_bottom, y_top, y_bottom = lax.optimization_barrier(
+            (*by_x, *by_y, held[0], back, shared_grads)
+        )[:4]
+        by_x, by_y = [x_top, x_bottom], [y_top, y_bottom]
+        corner = [turned(y_top, 2), turned(x_bottom, 4)]
+        pair_x = [swapped(part) for part in by_x]
+        pair_y = [swapped(part) for part in by_y]
         held = pick_route(first, slot, [by_x, by_y], router_rows, all_experts, 2, 1, held)
         held = pick_route(first, slot, [pair_x, pair_y], router_rows, all_experts, 4, 1, held)
-        corner = jnp.concatenate([after(top, held[0]), bottom], axis=0)
-        pair_corner = swapped(corner)
+        corner[0] = after(corner[0], held[0])
+        pair_corner = [swapped(part) for part in corner]
         held = pick_route(first, slot, [corner], router_rows, all_experts, 6, 1, held)
         held = pick_route(first, slot, [pair_corner], router_rows, all_experts, 7, 1, held)
         rows, router_probs, slot_gates = held
-        hidden_all = jnp.concatenate(
-            [hidden_mid, pair, by_x, by_y, pair_x, pair_y, after(corner, rows), pair_corner], axis=0
-        )
+        hidden_parts = [*hidden_mid, *pair, *by_x, *by_y, *corner, *pair_x, *pair_y, *pair_corner]
     else:
         rows, router_probs, slot_gates = pick_route(
-            first, slot, [hidden_all], router_rows, all_experts, 0, devices, []
+            first, slot, [[hidden_all]], router_rows, all_experts, 0, devices, []
         )
+        hidden_parts = [hidden_all]
     shared_sums = lax.psum_scatter(
         after(shared_grads, rows), "dp", scatter_dimension=1, tiled=True
     )
     gated_active, gate_val_grad, up_val_grad, row_grad, probs_grad = expert_step(
         rows, gate_t, up_t, back, slot, slot_gates
     )
-    mid_part, logit_grad = put_route(
-        order, first, places, row_grad, router_probs, probs_grad, router_rows
-    )
-    mid_part = after(mid_part, shared_sums)
-    mid_block = lax.psum_scatter(mid_part, "dp", scatter_dimension=0, tiled=True)
-    grad_router = dot("td,te->de", hidden_all, logit_grad[:, :all_experts]).astype(BF)
-    routed_part = put(order, places, row_out(gated_active, expert_down, devices))
-    rows_flat = rows.reshape(experts_local, -1, width)
     grad_expert_down = dot(
         "ecf,ecd->efd",
         gated_active[..., :ff_local],
         cot_rows.reshape(experts_local, -1, width),
     )
+    if direct:
+        put_args = (first, places, row_grad, router_probs, probs_grad, router_rows)
+        some = lambda *at: jnp.array(at, jnp.int32)
+        to_pair, logits_pair = put_route(some(4, 5, 7), False, *put_args, None)
+        from_pair = swapped(to_pair)
+        to_sibling, logits_sibling = put_route(some(1), False, *put_args, None)
+        from_sibling = swapped(to_sibling)
+        send_x, send_y, kept, logits_cross = put_route(some(2, 3, 6), False, *put_args, from_pair)
+        send_x, shared_sums = lax.optimization_barrier((send_x, shared_sums))
+        got_x = turned(send_x, 2)
+        got_y = turned(send_y, 4)
+        own, logits_own = put_route(some(0), False, *put_args, from_sibling)
+        routed_part = put(order, places, row_out(gated_active, expert_down, devices))
+        got_x, got_y, own, routed_part, mid_from_shared = lax.optimization_barrier(
+            (got_x, got_y, own, routed_part, mid_from_shared)
+        )
+        half = tok_rows // 2
+        plus = lambda *terms: sum(term.astype(F32) for term in terms)
+        last_y = turned(plus(kept[:half], got_x[:half]).astype(BF), 4)
+        last_x = turned(plus(kept[half:], got_y[:half]).astype(BF), 2)
+        last_y, last_x = lax.optimization_barrier((last_y, last_x, grad_expert_down))[:2]
+        mid_block = jnp.concatenate(
+            [plus(own[:half], got_x[half:], last_y), plus(own[half:], got_y[half:], last_x)], axis=0
+        )
+        logit_grads = [logits_own, logits_sibling, logits_cross, logits_pair]
+    else:
+        mid_part, logit_grad = put_route(
+            order, True, first, places, row_grad, router_probs, probs_grad, router_rows, None
+        )
+        mid_block = scatter_sum(after(mid_part, shared_sums)).astype(F32)
+        routed_part = put(order, places, row_out(gated_active, expert_down, devices))
+        mid_block = after(mid_block, routed_part, grad_expert_down)
+        logit_grads = [logit_grad]
+    mid_sum = (mid_block + mid_from_shared).astype(BF)
+    routed_block = scatter_sum(after(routed_part, mid_sum))
+    mid_grad = lax.psum(mid_sum, "tensor")
+    rows_flat = rows.reshape(experts_local, -1, width)
     grad_expert_gate = dot("ecd,ecf->edf", rows_flat, gate_val_grad[..., :ff_local])
     grad_expert_up = dot("ecd,ecf->edf", rows_flat, up_val_grad[..., :ff_local])
-
-    routed_block = scatter_sum(routed_part)
-    mid_block = after(mid_block, routed_part, grad_router, grad_expert_down)
-    mid_grad = lax.psum((mid_block.astype(F32) + mid_from_shared).astype(BF), "tensor")
-    mid_grad = after(mid_grad, grad_expert_gate, grad_expert_up)
-
-    middle_low, middle_grad, grad_middle_gain = norm_back(
-        middle, mid_grad, cotangent, middle_gain, False
-    )
-    attended_grad = dot("td,cd->tc", middle_low, w_out).astype(BF)
-    query_grad, grad_expand, *window_grads = attend_back(
-        query_pre, cosine, sine, w_expand, place_q, place_k, lse, attended_grad, keys
-    )
-    routed_block = after(routed_block, grad_expand)
+    grad_router = route_grad(logit_grads, hidden_parts)
+    mid_grad = after(mid_grad, grad_expert_gate, grad_expert_up, grad_router)
+
+    middle_low, middle_grad, attended_grad, grad_middle_gain = norm_back(
+        middle, mid_grad, cotangent, middle_gain, w_out
+    )
+    query_grad, expanded_grad, *window_grads = attend_back(
+        query_pre, cosine, sine, w_expand, blocks, place_q, sequences, lse, attended_grad, kv, keys
+    )
+    routed_block = after(routed_block, expanded_grad)
     ff_part = (routed_block.astype(F32) + shared_result).astype(BF)
     window_grads = lax.optimization_barrier((*window_grads, ff_part))[:-1]
     four_grad, two_grad, pair_grad, last_grad, keys_grad = window_grads
@@ -932,36 +1093,44 @@
             grad_middle_gain / tensors,
             grad_input_gain[None, :],
             jnp.repeat(grad_latent_gain, width // KVR)[None, :],
-            jnp.zeros((125, width), F32),
+            jnp.zeros((13, width), F32),
         ],
         axis=0,
     )
-    parts = scatter_sum(
-        [dot("td,tc->dc", hidden_in, latent_full_grad).astype(BF), grad_router, gains.astype(BF).T]
+    parts = parts_rows(latent_full_grad, hidden_in, grad_router, gains, all_experts)
+    parts = lax.psum_scatter(parts, "dp", scatter_dimension=1, tiled=True)
+    latents = jnp.concatenate([key[:, :KVR] for key in keys], axis=0)
+    grad_expand = dot("wk,wc->kc", latents, after(expanded_grad, keys_grad)).astype(BF)
+    share = KVR // devices
+    grad_expand = (
+        grad_expand.reshape(devices, share, -1, expand_width)
+        .transpose(0, 2, 1, 3)
+        .reshape(width, expand_width)
     )
     late = scatter_sum(
         [
             dot("td,tc->dc", middle_low, attended).astype(BF),
             dot("td,tc->dc", hidden_in, query_grad).astype(BF),
-            after(grad_expand, keys_grad).reshape(width, expand_width),
+            grad_expand,
         ]
     )
+    grad_out_proj, grad_query, grad_expand = finals(late, out_width, query_width, share)
     input_grad, parts = lax.psum((input_part, parts), "tensor")
     parts = parts.astype(F32)
-    (token_grad,) = norm_back(tokens, input_grad, middle_grad, input_gain, True)
+    (token_grad,) = norm_back(tokens, input_grad, middle_grad, input_gain, None)
     sw = shared_gate.shape[1]
     gain_at = latent_width + all_experts
     return (
         output,
         token_grad,
-        parts[:, gain_at + 1],
-        late[:, out_width : out_width + query_width].astype(F32),
-        parts[:, :latent_width],
-        parts[:: width // KVR, gain_at + 2],
-        late[:, out_width + query_width :].astype(F32).reshape(KVR // devices, -1),
-        late[:, :out_width].astype(F32).T,
-        parts[:, gain_at],
-        parts[:, latent_width:gain_at],
+        parts[gain_at + 1],
+        grad_query,
+        parts[:latent_width].T,
+        parts[gain_at + 2, :: width // KVR],
+        grad_expand,
+        grad_out_proj,
+        parts[gain_at],
+        parts[latent_width:gain_at].T,
         grad_expert_gate,
         grad_expert_up,
         grad_expert_down,

time: 865 us -> 836 us (0.966)
  local copies, waits for them, and re-layouts: 58.5 us -> 24 us
  Pallas kernels: 300 us -> 330 us
  waiting for transfers between devices: 274 us -> 252 us
  matrix products: 132 us -> 115 us
    pallas_call x8 -> x14, Pallas kernels: 81.8 us -> 119 us  [the longest x5 46 us: pick_route(): pl.pallas_call(functools.partial(pick_route_kernel, count, pieces, parts)...]
    unnamed x87 -> x82, local copies, waits for them, and re-layouts: 30.9 us -> 10.6 us
    reduce_scatter x1, waiting for transfers between devices: 14.6 us -> 0.01 us  [shards(): parts = lax.psum_scatter(parts, 'dp', scatter_dimension=1, tiled=True)]
    dot_general x14 -> x12, matrix products: 113 us -> 98 us  [dot(): return jnp.einsum(eq, a, b, preferred_element_type=F32)]
    psum x1, waiting for transfers between devices: 32.2 us -> 19 us  [shards(): mid_grad = lax.psum(mid_sum, 'tensor')]
    ppermute x12 -> x24, waiting for transfers between devices: 4.64 us -> 15.6 us  [turned(): lax.ppermute(value, 'dp', [(i, i ^ by) for i in range(lax.axis_size('dp'))])]
    psum x1, waiting for transfers between devices: 75.5 us -> 66.7 us  [shards(): input_grad, parts = lax.psum((input_part, parts), 'tensor')]
  transfers between devices with their start and end apart: 26 -> 37, of which waited for: 13 -> 16; matrix products, arithmetic and copies ran while one was open for 23% -> 19% of each run, Pallas kernels for 34% -> 38%
where the time goes in v6:
time: 836 us; the launch traced here: 828 us
  Pallas kernels  330 us (39%)
  waiting for transfers between devices  252 us (30%)
  matrix products  115 us (14%)
  other arithmetic  52.8 us (6%)
  starting transfers between devices  27.8 us (3%)
  local copies, waits for them, and re-layouts  24 us (3%)
  between operations  16.4 us (2%)
  blocking collectives  10.5 us (1%)
    dot_general x12, matrix products, dot(): return jnp.einsum(eq, a, b, preferred_element_type=F32)  98 us
    psum x1, waiting for transfers between devices, shards(): input_grad, parts = lax.psum((input_part, parts), 'tensor')  66.7 us
    pallas_call x1, Pallas kernels, expert_step(): pl.pallas_call(expert_kernel, name='expert_step', grid=(experts,), in_spe...  49.6 us
    psum x1, waiting for transfers between devices, shards(): feedforward = lax.psum(ff_part, 'tensor')  48.3 us
    pallas_call x5, Pallas kernels, pick_route(): pl.pallas_call(functools.partial(pick_route_kernel, count, pieces, parts)...  46 us
    all_gather x1, waiting for transfers between devices, shards(): lax.all_gather(after(cotangent, before_two, before_four), 'dp', tiled=True)  44.2 us
    pallas_call x4, Pallas kernels, put_route(): pl.pallas_call(put_cross_kernel if cross else put_route_kernel, name='put...  40.8 us
    ppermute x4, waiting for transfers between devices, passed_along(): return lax.ppermute(shard, axis, pairs)  40.7 us
  transfers between devices with their start and end apart: 37, of which 16 were waited for; matrix products, arithmetic and copies ran while one was open for 19% of the time, Pallas kernels for 38%

profile of v6, /device:TPU:0, one launch (start us, length us, event | category | flops | bytes accessed | tf_op | source)
XLA Modules:
  0.0 828.3 jit_solution(8786100033940499364)
XLA Ops:
  21.0 5.7 collective-permute-start
  26.7 4.3 collective-permute-start.1
  31.0 23.3 %collective-permute-done.rest_0_ = bf16[512,640]{1,0:T(8,128)(2,1)} collective-permute-done((bf16[512,640]{1,0:T(8,128)(2,1)}, bf16[512,640]{1,0:T(8,128)(2,1)}, u32[]{:S(2)}, u32[]{:S(2)}) %collective-permute-start) | collective-permute-done | bytes 655392 | tf_op jit(solution)/shard_map/ppermute | solution.py:823
  55.7 4.6 fusion.61.qp_ref
  65.6 21.2 %attend.1 = (bf16[512,512]{1,0:T(8,128)(2,1)}, f32[4,512,1]{2,1,0:T(8,128)}, bf16[2560,1024]{1,0:T(8,128)(2,1)}) custom-call(f32[512,768]{1,0:T(8,128)} %fusion.61.qp_ref, f32[512,32]{1,0:T(8,128)} %get-tuple-element.210.cos_ref, f32[512,32]{1,0:T(8,128)} %get-tuple-element.209.sin_ref, bf16[512,1024]{1,0:T(8,128)(2,1)} %wx_ref.3, s32[5]{0:T(128)} %stack.28.at_ref, ...), custom_call_target="tpu_custom_call" | custom-call | flops 6710886400 | bytes 3276800 | tf_op jit(solution)/shard_map/attend/pallas_call | solution.py:114
  86.8 4.4 convolution_convert_fusion.2
  91.2 10.5 %all_gather.6 = s32[4096,6]{0,1:T(8,128)S(1)} all-gather(s32[512,6]{0,1:T(8,128)S(1)} %copy-done.26), channel_id=1, replica_groups=mesh['dp'=8,'tensor'=4] {'dp'}, dimensions={0}, use_global_device_ids=true | all-gather | bytes 110592 | tf_op jit(solution)/shard_map/all_gather | solution.py:941
  107.7 44.2 %all-gather.2.cloned.1.call-done.x_ref = bf16[4096,2048]{1,0:T(8,128)(2,1)} async-done(((bf16[512,2048]{1,0:T(8,128)(2,1)}), bf16[4096,2048]{1,0:T(8,128)(2,1)}) %all-gather.2.cloned.1.call-update) | async-done | bytes 16777232 | tf_op jit(solution)/shard_map/all_gather | solution.py:936
  151.9 19.7 %pick.1.x_ref = bf16[8,8,80,2048]{3,2,1,0:T(8,128)(2,1)} custom-call(s32[8]{0:T(128)} %broadcast_xor_fusion.order_ref, s32[8,8,1,512]{3,2,1,0:T(1,128)} %broadcast_in_dim.79.slot_ref, bf16[4096,2048]{1,0:T(8,128)(2,1)} %all-gather.2.cloned.1.call-done.x_ref), custom_call_target="tpu_custom_call" | custom-call | flops 10737418240 | bytes 37748736 | tf_op jit(solution)/shard_map/pick/pallas_call | solution.py:257
  171.5 16.7 %all-reduce.7.cloned.1.call-done.add_ref = bf16[512,2048]{1,0:T(8,128)(2,1)} async-done(((bf16[512,2048]{1,0:T(8,128)(2,1)}), bf16[512,2048]{1,0:T(8,128)(2,1)}) %all-reduce.7.cloned.1.call-update) | async-done | bytes 2097168 | tf_op jit(solution)/shard_map/psum | solution.py:939
  188.2 5.9 norm_sum.1
  199.5 19.1 %down_back.1.back_ref = f32[8,640,384]{2,1,0:T(8,128)} custom-call(bf16[8,8,80,2048]{3,2,1,0:T(8,128)(2,1)} %pick.1.x_ref, bf16[8,352,2048]{2,1,0:T(8,128)(2,1)} %w_ref.3), custom_call_target="tpu_custom_call" | custom-call | flops 10485760 | bytes 1802240 | tf_op jit(solution)/shard_map/down_back/pallas_call | solution.py:534
  218.6 18.2 %shared_step.1 = (bf16[512,704]{1,0:T(8,128)(2,1)}, bf16[512,704]{1,0:T(8,128)(2,1)}, bf16[512,704]{1,0:T(8,128)(2,1)}, bf16[2112,2048]{1,0:T(8,128)(2,1)}) custom-call(bf16[256,2048]{1,0:T(8,128)(2,1)} %get-tuple-element.111.refs_0_.top_ref.refs_4_, bf16[256,2048]{1,0:T(8,128)(2,1)} %get-tuple-element.109.refs_1_.bottom_ref.refs_5_, ...), custom_call_target="tpu_custom_call" | custom-call | flops 1048576 | bytes 1048576 | tf_op jit(solution)/shard_map/shared_step/pallas_call | solution.py:775
  236.8 11.1 %pick_route.5 = (bf16[8,8,80,2048]{3,2,1,0:T(8,128)(2,1)}, f32[4096,128]{1,0:T(8,128)}, f32[8,8,80,1]{3,2,1,0:T(8,128)}) custom-call(s32[1]{0:T(128)} %bitcast.14.first_ref, s32[8,8,1,512]{3,2,1,0:T(1,128)} %broadcast_in_dim.79.slot_ref, bf16[128,2048]{1,0:T(8,128)(2,1)} %pad.4.w_ref, bf16[256,2048]{1,0:T(8,128)(2,1)} %get-tuple-element.111.refs_0_.top_ref.refs_4_, ...), custom_call_target="tpu_custom_call" | custom-call | flops 2097152 | bytes 2097152 | tf_op jit(solution)/shard_map/pick_route/pallas_call | solution.py:319
  252.4 10.6 %pick_route.6 = (bf16[8,8,80,2048]{3,2,1,0:T(8,128)(2,1)}, f32[4096,128]{1,0:T(8,128)}, f32[8,8,80,1]{3,2,1,0:T(8,128)}) custom-call(s32[1]{0:T(128)} %bitcast.14.first_ref, s32[8,8,1,512]{3,2,1,0:T(1,128)} %broadcast_in_dim.79.slot_ref, bf16[128,2048]{1,0:T(8,128)(2,1)} %pad.4.w_ref, ...), custom_call_target="tpu_custom_call", output_to_operand_aliasing={{0}: (7, {}), {1}: (8, {}), {2}: (9, {})} | custom-call | flops 2097152 | bytes 2097152 | tf_op jit(solution)/shard_map/pick_route/pallas_call | solution.py:319
  263.1 10.8 %pick_route.7 = (bf16[8,8,80,2048]{3,2,1,0:T(8,128)(2,1)}, f32[4096,128]{1,0:T(8,128)}, f32[8,8,80,1]{3,2,1,0:T(8,128)}) custom-call(s32[1]{0:T(128)} %bitcast.14.first_ref, s32[8,8,1,512]{3,2,1,0:T(1,128)} %broadcast_in_dim.79.slot_ref, bf16[128,2048]{1,0:T(8,128)(2,1)} %pad.4.w_ref, ...), custom_call_target="tpu_custom_call", output_to_operand_aliasing={{0}: (7, {}), {1}: (8, {}), {2}: (9, {})} | custom-call | flops 2097152 | bytes 2097152 | tf_op jit(solution)/shard_map/pick_route/pallas_call | solution.py:319
  276.5 6.7 pick_route.8
  283.2 6.7 pick_route.9
  290.0 49.6 %expert_step.1 = (bf16[8,640,384]{2,1,0:T(8,128)(2,1)}, bf16[8,640,384]{2,1,0:T(8,128)(2,1)}, bf16[8,640,384]{2,1,0:T(8,128)(2,1)}, bf16[8,8,80,2048]{3,2,1,0:T(8,128)(2,1)}, f32[8,8,1,512]{3,2,1,0:T(1,128)}) custom-call(bf16[8,8,80,2048]{3,2,1,0:T(8,128)(2,1)} %get-tuple-element.129.x_ref, bf16[8,352,2048]{2,1,0:T(8,128)(2,1)} %bitcast.93, ...), custom_call_target="tpu_custom_call" | custom-call | flops 32212254720 | bytes 86769664 | tf_op jit(solution)/shard_map/expert_step/pallas_call | solution.py:627
  339.6 12.7 %put_route.4 = (bf16[1536,2048]{1,0:T(8,128)(2,1)}, bf16[1536,128]{1,0:T(8,128)(2,1)}) custom-call(s32[3]{0:T(128)} %constant.115.clone.order_ref, s32[1]{0:T(128)} %bitcast.14.first_ref, bf16[8,512,640]{2,1,0:T(8,128)(2,1)} %compare_convert_fusion.place_ref, bf16[8,8,80,2048]{3,2,1,0:T(8,128)(2,1)} %get-tuple-element.131.r_ref, ...), custom_call_target="tpu_custom_call" | custom-call | flops 3145728 | bytes 3145728 | tf_op jit(solution)/shard_map/put_route/pallas_call | solution.py:496
  352.6 6.1 put_route.6
  358.8 3.9 collective-permute-done.18.add_ref
  362.8 15.2 %put_route.5 = (bf16[512,2048]{1,0:T(8,128)(2,1)}, bf16[512,2048]{1,0:T(8,128)(2,1)}, bf16[512,2048]{1,0:T(8,128)(2,1)}, bf16[1536,128]{1,0:T(8,128)(2,1)}) custom-call(s32[3]{0:T(128)} %constant.117.clone.order_ref, s32[1]{0:T(128)} %bitcast.14.first_ref, bf16[8,512,640]{2,1,0:T(8,128)(2,1)} %compare_convert_fusion.place_ref, ...), custom_call_target="tpu_custom_call" | custom-call | flops 3145728 | bytes 3145728 | tf_op jit(solution)/shard_map/put_route/pallas_call | solution.py:496
  381.1 4.0 fusion.63
  388.8 18.4 %row_out.1.r_ref = bf16[8,8,80,2048]{3,2,1,0:T(8,128)(2,1)} custom-call(bf16[8,640,384]{2,1,0:T(8,128)(2,1)} %get-tuple-element.141.x_ref, bf16[8,352,2048]{2,1,0:T(8,128)(2,1)} %w_ref.3), custom_call_target="tpu_custom_call" | custom-call | flops 1310720 | bytes 1310720 | tf_op jit(solution)/shard_map/row_out/pallas_call | solution.py:561
  407.2 21.6 %put.1 = bf16[4096,2048]{1,0:T(8,128)(2,1)} custom-call(s32[8]{0:T(128)} %broadcast_xor_fusion.order_ref, bf16[8,512,640]{2,1,0:T(8,128)(2,1)} %compare_convert_fusion.place_ref, bf16[8,8,80,2048]{3,2,1,0:T(8,128)(2,1)} %row_out.1.r_ref), custom_call_target="tpu_custom_call" | custom-call | flops 8388608 | bytes 8388608 | tf_op jit(solution)/shard_map/put/pallas_call | solution.py:469
  428.8 6.8 put_route.7
  435.6 4.4 add_convert_fusion.2
  441.1 19.1 %fusion.10 = f32[8,352,2048]{2,1,0:T(8,128)} fusion(bf16[8,640,2048]{2,1,0:T(8,128)(2,1)} %bitcast.78, bf16[8,640,384]{2,1,0:T(8,128)(2,1)} %get-tuple-element.141.x_ref), kind=kOutput, calls=%fused_computation.19 | convolution fusion | flops 7381975040 | bytes 47972352 | tf_op jit(solution)/shard_map/ecf,ecd->efd/dot_general | solution.py:817
  460.3 5.0 collective-permute-done.22
  465.5 4.2 convert_add_fusion.1
  472.4 5.9 fusion.64
  478.4 25.8 %fusion.8 = f32[8,2048,352]{1,2,0:T(8,128)} fusion(bf16[8,640,2048]{2,1,0:T(8,128)(2,1)} %bitcast.76, bf16[8,640,384]{2,1,0:T(8,128)(2,1)S(1)} %copy-done.10), kind=kOutput, calls=%fused_computation.17 | convolution fusion | flops 7381975040 | bytes 47972352 | tf_op jit(solution)/shard_map/ecd,ecf->edf/dot_general | solution.py:817
  504.2 22.2 %fusion.6 = f32[8,2048,352]{1,2,0:T(8,128)} fusion(bf16[8,640,2048]{2,1,0:T(8,128)(2,1)} %bitcast.77, bf16[8,640,384]{2,1,0:T(8,128)(2,1)S(1)} %copy-done.9), kind=kOutput, calls=%fused_computation.15 | convolution fusion | flops 7381975040 | bytes 47972352 | tf_op jit(solution)/shard_map/ecd,ecf->edf/dot_general | solution.py:817
  526.5 9.9 %route_grad.1.route_ref = bf16[128,2048]{1,0:T(8,128)(2,1)} custom-call(bf16[512,128]{1,0:T(8,128)(2,1)} %get-tuple-element.156.refs_0_, bf16[512,128]{1,0:T(8,128)(2,1)} %get-tuple-element.157.refs_1_, bf16[1536,128]{1,0:T(8,128)(2,1)} %get-tuple-element.158.refs_2_, bf16[1536,128]{1,0:T(8,128)(2,1)} %get-tuple-element.159.refs_3_, ...), custom_call_target="tpu_custom_call" | custom-call | flops 262144 | bytes 262144 | tf_op jit(solution)/shard_map/route_grad/pallas_call | solution.py:362
  536.3 19.0 %all-reduce.9.cloned.1.call-done.up_ref = bf16[512,2048]{1,0:T(8,128)(2,1)} async-done(((bf16[512,2048]{1,0:T(8,128)(2,1)}), bf16[512,2048]{1,0:T(8,128)(2,1)}) %all-reduce.9.cloned.1.call-update) | async-done | bytes 2097168 | tf_op jit(solution)/shard_map/psum | solution.py:1050
  555.4 8.6 %norm_back.2 = (bf16[512,2048]{1,0:T(8,128)(2,1)}, f32[512,2048]{1,0:T(8,128)}, bf16[512,512]{1,0:T(8,128)(2,1)}, f32[1,2048]{1,0:T(1,128)}) custom-call(f32[512,2048]{1,0:T(8,128)} %get-tuple-element.107.x_ref, bf16[512,2048]{1,0:T(8,128)(2,1)} %all-reduce.9.cloned.1.call-done.up_ref, bf16[512,2048]{1,0:T(8,128)(2,1)} %res_ref.1, f32[1,2048]{1,0:T(1,128)} %bitcast.85, ...), custom_call_target="tpu_custom_call" | custom-call | flops 12582912 | bytes 12582912 | tf_op jit(solution)/shard_map/norm_back/pallas_call | solution.py:739
  563.9 37.9 %attend_back.1 = (bf16[512,768]{1,0:T(8,128)(2,1)}, bf16[2560,1024]{1,0:T(8,128)(2,1)}, bf16[512,640]{1,0:T(8,128)(2,1)}, bf16[512,640]{1,0:T(8,128)(2,1)}, bf16...) custom-call(f32[512,768]{1,0:T(8,128)} %fusion.61.qp_ref, ...), custom_call_target="tpu_custom_call" | custom-call | flops 18790481920 | bytes 6553600 | tf_op jit(solution)/shard_map/attend_back/pallas_call | solution.py:207
  601.9 4.9 add_convert_fusion.1
  616.6 13.9 %collective-permute-done.27 = bf16[512,640]{1,0:T(8,128)(2,1)} collective-permute-done((bf16[512,640]{1,0:T(8,128)(2,1)}, bf16[512,640]{1,0:T(8,128)(2,1)}, u32[]{:S(2)}, u32[]{:S(2)}) %collective-permute-start.27) | collective-permute-done | bytes 655392 | tf_op jit(solution)/shard_map/ppermute | solution.py:823
  645.6 4.9 parts_rows.1
  658.1 48.3 %all-reduce.11.cloned.1.call-done = bf16[512,2048]{1,0:T(8,128)(2,1)} async-done(((bf16[512,2048]{1,0:T(8,128)(2,1)}), bf16[512,2048]{1,0:T(8,128)(2,1)}) %all-reduce.11.cloned.1.call-update) | async-done | bytes 2097168 | tf_op jit(solution)/shard_map/psum | solution.py:1082
  708.9 4.4 convolution_convert_fusion.1
  716.9 5.6 convolution_convert_fusion.3
  727.1 5.0 pad_maximum_fusion
  734.8 4.7 add_convert_fusion
  739.5 66.7 %all-reduce.13.cloned.1.call-done = (bf16[512,2048]{1,0:T(8,128)(2,1)}, bf16[656,256]{1,0:T(8,128)(2,1)}) async-done(((bf16[512,2048]{1,0:T(8,128)(2,1)}, bf16[656,256]{1,0:T(8,128)(2,1)}), (bf16[512,2048]{1,0:T(8,128)(2,1)}, bf16[656,256]{1,0:T(8,128)(2,1)})) %all-reduce.13.cloned.1.call-update) | async-done | bytes 2433040 | tf_op jit(solution)/shard_map/psum | solution.py:1118
  809.4 6.1 norm_back.3
  (218 shorter events, 103.6 us)
Async XLA Ops:
  8.0 47.7 %copy-start = (bf16[2048,768]{1,0:T(8,128)(2,1)S(1)}, bf16[2048,768]{1,0:T(8,128)(2,1)}, u32[]{:S(2)}) copy-start(bf16[2048,768]{1,0:T(8,128)(2,1)} %param.28) | copy-start | bytes 9437188
  8.0 143.8 %all-gather.2.cloned.1.call-start = ((), (), s32[]{:S(2)}) async-start(), calls=%async_computation.5 | async-start | bytes 18874368 | tf_op jit(solution)/shard_map/all_gather | solution.py:936
  8.1 9.1 %copy-start.30 = (f32[32]{0:T(128)}, f32[32]{0:T(128)S(1)}, u32[]{:S(2)}) copy-start(f32[32]{0:T(128)S(1)} %multiply_power_fusion) | copy-start | bytes 388
  21.0 33.2 %collective-permute-start = (bf16[512,640]{1,0:T(8,128)(2,1)}, bf16[512,640]{1,0:T(8,128)(2,1)}, u32[]{:S(2)}, u32[]{:S(2)}) collective-permute-start(bf16[512,640]{1,0:T(8,128)(2,1)} %maximum_maximum_fusion.rest_4_), channel_id=1, source_target_pairs={{0,16},{4,20},{8,24},{12,28},{1,17},{5,21},{9,25},{13,29},{2,18},{... | collective-permute-start | bytes 1966088 | tf_op jit(solution)/shard_map/ppermute | solution.py:823
  26.7 33.5 %collective-permute-start.1 = (bf16[512,640]{1,0:T(8,128)(2,1)}, bf16[512,640]{1,0:T(8,128)(2,1)}, u32[]{:S(2)}, u32[]{:S(2)}) collective-permute-start(bf16[512,640]{1,0:T(8,128)(2,1)} %maximum_maximum_fusion.rest_4_), channel_id=1, source_target_pairs={{0,8},{4,12},{8,16},{12,20},{16,24},{20,28},{1,9},{5,13},{9,17},{1... | collective-permute-start | bytes 1966088 | tf_op jit(solution)/shard_map/ppermute | solution.py:823
  55.6 4.7 collective-permute-start.2
  60.3 127.9 %all-reduce.7.cloned.1.call-start = ((), (), s32[]{:S(2)}) async-start(), calls=%async_computation.4 | async-start | bytes 4194304 | tf_op jit(solution)/shard_map/psum | solution.py:939
  62.3 2.4 collective-permute-start.3
  101.7 277.9 %reduce-scatter.5.cloned.1.call-start = ((), (), s32[]{:S(2)}) async-start(), calls=%async_computation.6 | async-start | bytes 9732096 | tf_op jit(solution)/shard_map/reduce_scatter | solution.py:1004
  171.5 27.1 %copy-start.17 = (bf16[2048,64]{0,1:T(8,128)(2,1)S(1)}, bf16[2048,64]{0,1:T(8,128)(2,1)}, u32[]{:S(2)}) copy-start(bf16[2048,64]{0,1:T(8,128)(2,1)} %param.34) | copy-start | bytes 786436
  194.1 4.0 collective-permute-start.8
  194.1 42.7 %collective-permute-start.9 = (bf16[256,2048]{1,0:T(8,128)(2,1)}, bf16[256,2048]{1,0:T(8,128)(2,1)}, u32[]{:S(2)}, u32[]{:S(2)}) collective-permute-start(bf16[256,2048]{1,0:T(8,128)(2,1)} %get-tuple-element.109.refs_1_.bottom_ref.refs_5_), channel_id=1, source_target_pairs={{0,4},{4,0},{8,12},{12,8},{16,20},{20,16},{24,28},{28,24},{1,5},{5... | collective-permute-start | bytes 3145736 | tf_op jit(solution)/shard_map/ppermute | solution.py:865
  194.6 53.2 %collective-permute-start.4 = (bf16[256,2048]{1,0:T(8,128)(2,1)}, bf16[256,2048]{1,0:T(8,128)(2,1)}, u32[]{:S(2)}, u32[]{:S(2)}) collective-permute-start(bf16[256,2048]{1,0:T(8,128)(2,1)} %get-tuple-element.111.refs_0_.top_ref.refs_4_), channel_id=1, source_target_pairs={{0,8},{4,12},{8,0},{12,4},{16,24},{20,28},{24,16},{28,20},{1,9},{5... | collective-permute-start | bytes 3145736 | tf_op jit(solution)/shard_map/ppermute | solution.py:865
  196.1 51.8 %collective-permute-start.5 = (bf16[256,2048]{1,0:T(8,128)(2,1)}, bf16[256,2048]{1,0:T(8,128)(2,1)}, u32[]{:S(2)}, u32[]{:S(2)}) collective-permute-start(bf16[256,2048]{1,0:T(8,128)(2,1)} %get-tuple-element.109.refs_1_.bottom_ref.refs_5_), channel_id=1, source_target_pairs={{0,8},{4,12},{8,0},{12,4},{16,24},{20,28},{24,16},{28,20},{1,9},{5... | collective-permute-start | bytes 3145736 | tf_op jit(solution)/shard_map/ppermute | solution.py:865
  196.6 51.2 %collective-permute-start.6 = (bf16[256,2048]{1,0:T(8,128)(2,1)}, bf16[256,2048]{1,0:T(8,128)(2,1)}, u32[]{:S(2)}, u32[]{:S(2)}) collective-permute-start(bf16[256,2048]{1,0:T(8,128)(2,1)} %get-tuple-element.111.refs_0_.top_ref.refs_4_), channel_id=1, source_target_pairs={{0,16},{4,20},{8,24},{12,28},{16,0},{20,4},{24,8},{28,12},{1,17},{... | collective-permute-start | bytes 3145736 | tf_op jit(solution)/shard_map/ppermute | solution.py:865
  198.1 49.8 %collective-permute-start.7 = (bf16[256,2048]{1,0:T(8,128)(2,1)}, bf16[256,2048]{1,0:T(8,128)(2,1)}, u32[]{:S(2)}, u32[]{:S(2)}) collective-permute-start(bf16[256,2048]{1,0:T(8,128)(2,1)} %get-tuple-element.109.refs_1_.bottom_ref.refs_5_), channel_id=1, source_target_pairs={{0,16},{4,20},{8,24},{12,28},{16,0},{20,4},{24,8},{28,12},{1,17},{... | collective-permute-start | bytes 3145736 | tf_op jit(solution)/shard_map/ppermute | solution.py:865
  247.9 3.1 collective-permute-start.11
  248.0 15.1 %collective-permute-start.12 = (bf16[256,2048]{1,0:T(8,128)(2,1)}, bf16[256,2048]{1,0:T(8,128)(2,1)}, u32[]{:S(2)}, u32[]{:S(2)}) collective-permute-start(bf16[256,2048]{1,0:T(8,128)(2,1)} %collective-permute-done.5.refs_1_.refs_9_), channel_id=1, source_target_pairs={{0,4},{4,0},{8,12},{12,8},{16,20},{20,16},{24,28},{28,24},{1,5},{5... | collective-permute-start | bytes 3145736 | tf_op jit(solution)/shard_map/ppermute | solution.py:865
  248.5 14.6 %collective-permute-start.13 = (bf16[256,2048]{1,0:T(8,128)(2,1)}, bf16[256,2048]{1,0:T(8,128)(2,1)}, u32[]{:S(2)}, u32[]{:S(2)}) collective-permute-start(bf16[256,2048]{1,0:T(8,128)(2,1)} %collective-permute-done.6.refs_2_.refs_10_), channel_id=1, source_target_pairs={{0,4},{4,0},{8,12},{12,8},{16,20},{20,16},{24,28},{28,24},{1,5},{5... | collective-permute-start | bytes 3145736 | tf_op jit(solution)/shard_map/ppermute | solution.py:865
  248.5 14.6 %collective-permute-start.14 = (bf16[256,2048]{1,0:T(8,128)(2,1)}, bf16[256,2048]{1,0:T(8,128)(2,1)}, u32[]{:S(2)}, u32[]{:S(2)}) collective-permute-start(bf16[256,2048]{1,0:T(8,128)(2,1)} %collective-permute-done.7.refs_3_.refs_11_), channel_id=1, source_target_pairs={{0,4},{4,0},{8,12},{12,8},{16,20},{20,16},{24,28},{28,24},{1,5},{5... | collective-permute-start | bytes 3145736 | tf_op jit(solution)/shard_map/ppermute | solution.py:865
  249.0 25.5 %collective-permute-start.10 = (bf16[256,2048]{1,0:T(8,128)(2,1)}, bf16[256,2048]{1,0:T(8,128)(2,1)}, u32[]{:S(2)}, u32[]{:S(2)}) collective-permute-start(bf16[256,2048]{1,0:T(8,128)(2,1)} %collective-permute-done.6.refs_2_.refs_10_), channel_id=1, source_target_pairs={{0,8},{4,12},{8,0},{12,4},{16,24},{20,28},{24,16},{28,20},{1,9},{5... | collective-permute-start | bytes 3145736 | tf_op jit(solution)/shard_map/ppermute | solution.py:865
  250.9 25.5 %collective-permute-start.16 = (bf16[256,2048]{1,0:T(8,128)(2,1)}, bf16[256,2048]{1,0:T(8,128)(2,1)}, u32[]{:S(2)}, u32[]{:S(2)}) collective-permute-start(bf16[256,2048]{1,0:T(8,128)(2,1)} %collective-permute-done.5.refs_1_.refs_9_), channel_id=1, source_target_pairs={{0,16},{4,20},{8,24},{12,28},{16,0},{20,4},{24,8},{28,12},{1,17},{... | collective-permute-start | bytes 3145736 | tf_op jit(solution)/shard_map/ppermute | solution.py:865
  274.4 8.8 %collective-permute-start.15 = (bf16[256,2048]{1,0:T(8,128)(2,1)}, bf16[256,2048]{1,0:T(8,128)(2,1)}, u32[]{:S(2)}, u32[]{:S(2)}) collective-permute-start(bf16[256,2048]{1,0:T(8,128)(2,1)} %collective-permute-done.10.refs_0_.refs_12_), channel_id=1, source_target_pairs={{0,4},{4,0},{8,12},{12,8},{16,20},{20,16},{24,28},{28,24},{1,5},{5... | collective-permute-start | bytes 3145736 | tf_op jit(solution)/shard_map/ppermute | solution.py:865
  276.5 6.7 collective-permute-start.17
  289.9 265.4 %all-reduce.9.cloned.1.call-start = ((), (), s32[]{:S(2)}) async-start(), calls=%async_computation.8 | async-start | bytes 4194304 | tf_op jit(solution)/shard_map/psum | solution.py:1050
  352.3 10.5 %collective-permute-start.18 = (bf16[1536,2048]{1,0:T(8,128)(2,1)}, bf16[1536,2048]{1,0:T(8,128)(2,1)}, u32[]{:S(2)}, u32[]{:S(2)}) collective-permute-start(bf16[1536,2048]{1,0:T(8,128)(2,1)} %get-tuple-element.134), channel_id=1, source_target_pairs={{0,4},{4,0},{8,12},{12,8},{16,20},{20,16},{24,28},{28,24},{1,5},{5... | collective-permute-start | bytes 18874376 | tf_op jit(solution)/shard_map/ppermute | solution.py:865
  358.8 70.1 %collective-permute-start.21 = (bf16[512,2048]{1,0:T(8,128)(2,1)}, bf16[512,2048]{1,0:T(8,128)(2,1)}, u32[]{:S(2)}, u32[]{:S(2)}) collective-permute-start(bf16[512,2048]{1,0:T(8,128)(2,1)} %get-tuple-element.139), channel_id=1, source_target_pairs={{0,4},{4,0},{8,12},{12,8},{16,20},{20,16},{24,28},{28,24},{1,5},{5... | collective-permute-start | bytes 6291464 | tf_op jit(solution)/shard_map/ppermute | solution.py:865
  377.9 57.7 %collective-permute-start.20 = (bf16[512,2048]{1,0:T(8,128)(2,1)}, bf16[512,2048]{1,0:T(8,128)(2,1)}, u32[]{:S(2)}, u32[]{:S(2)}) collective-permute-start(bf16[512,2048]{1,0:T(8,128)(2,1)} %get-tuple-element.138), channel_id=1, source_target_pairs={{0,16},{4,20},{8,24},{12,28},{16,0},{20,4},{24,8},{28,12},{1,17},{... | collective-permute-start | bytes 6291464 | tf_op jit(solution)/shard_map/ppermute | solution.py:865
  379.6 56.0 %collective-permute-start.19 = (bf16[512,2048]{1,0:T(8,128)(2,1)}, bf16[512,2048]{1,0:T(8,128)(2,1)}, u32[]{:S(2)}, u32[]{:S(2)}) collective-permute-start(bf16[512,2048]{1,0:T(8,128)(2,1)} %get-tuple-element.137), channel_id=1, source_target_pairs={{0,8},{4,12},{8,0},{12,4},{16,24},{20,28},{24,16},{28,20},{1,9},{5... | collective-permute-start | bytes 6291464 | tf_op jit(solution)/shard_map/ppermute | solution.py:865
  440.1 25.1 %collective-permute-start.22 = (bf16[256,2048]{1,0:T(8,128)(2,1)}, bf16[256,2048]{1,0:T(8,128)(2,1)}, u32[]{:S(2)}, u32[]{:S(2)}) collective-permute-start(bf16[256,2048]{1,0:T(8,128)(2,1)} %get-tuple-element.199), channel_id=1, source_target_pairs={{0,16},{4,20},{8,24},{12,28},{16,0},{20,4},{24,8},{28,12},{1,17},{... | collective-permute-start | bytes 3145736 | tf_op jit(solution)/shard_map/ppermute | solution.py:865
  440.8 24.7 %collective-permute-start.23 = (bf16[256,2048]{1,0:T(8,128)(2,1)}, bf16[256,2048]{1,0:T(8,128)(2,1)}, u32[]{:S(2)}, u32[]{:S(2)}) collective-permute-start(bf16[256,2048]{1,0:T(8,128)(2,1)} %get-tuple-element.198), channel_id=1, source_target_pairs={{0,8},{4,12},{8,0},{12,4},{16,24},{20,28},{24,16},{28,20},{1,9},{5... | collective-permute-start | bytes 3145736 | tf_op jit(solution)/shard_map/ppermute | solution.py:865
  471.7 130.2 %reduce-scatter.7.cloned.1.call-start = ((), (), s32[]{:S(2)}) async-start(), calls=%async_computation.7 | async-start | bytes 18874368 | tf_op jit(solution)/shard_map/reduce_scatter | solution.py:878
  472.4 234.0 %all-reduce.11.cloned.1.call-start = ((), (), s32[]{:S(2)}) async-start(), calls=%async_computation.9 | async-start | bytes 4194304 | tf_op jit(solution)/shard_map/psum | solution.py:1082
  478.4 25.8 %copy-start.9 = (bf16[8,640,384]{2,1,0:T(8,128)(2,1)S(1)}, bf16[8,640,384]{2,1,0:T(8,128)(2,1)}, u32[]{:S(2)}) copy-start(bf16[8,640,384]{2,1,0:T(8,128)(2,1)} %get-tuple-element.155) | copy-start | bytes 11796484
  606.8 9.7 %copy-start.29 = (f32[1,2048]{1,0:T(1,128)S(1)}, f32[1,2048]{1,0:T(1,128)}, u32[]{:S(2)}) copy-start(f32[1,2048]{1,0:T(1,128)} %get-tuple-element.180) | copy-start | bytes 24580
  606.8 2.4 collective-permute-start.24
  606.8 6.0 collective-permute-start.25
  611.5 19.0 %collective-permute-start.27 = (bf16[512,640]{1,0:T(8,128)(2,1)}, bf16[512,640]{1,0:T(8,128)(2,1)}, u32[]{:S(2)}, u32[]{:S(2)}) collective-permute-start(bf16[512,640]{1,0:T(8,128)(2,1)} %fusion.16), channel_id=1, source_target_pairs={{16,0},{20,4},{24,8},{28,12},{17,1},{21,5},{25,9},{29,13},{18,2},{... | collective-permute-start | bytes 1966088 | tf_op jit(solution)/shard_map/ppermute | solution.py:823
  615.1 19.0 %collective-permute-start.26 = (bf16[512,640]{1,0:T(8,128)(2,1)}, bf16[512,640]{1,0:T(8,128)(2,1)}, u32[]{:S(2)}, u32[]{:S(2)}) collective-permute-start(bf16[512,640]{1,0:T(8,128)(2,1)} %add_convert_fusion.4), channel_id=1, source_target_pairs={{8,0},{12,4},{16,8},{20,12},{24,16},{28,20},{9,1},{13,5},{17,9},{2... | collective-permute-start | bytes 1966088 | tf_op jit(solution)/shard_map/ppermute | solution.py:823
  616.5 19.7 %copy-start.23 = (f32[512]{0:T(512)S(1)}, f32[512]{0:T(512)}, u32[]{:S(2)}) copy-start(f32[512]{0:T(512)} %copy-done.22) | copy-start | bytes 6148
  616.5 19.7 %copy-start.31 = (f32[32]{0:T(128)S(1)}, f32[32]{0:T(128)}, u32[]{:S(2)}) copy-start(f32[32]{0:T(128)} %copy-done.30) | copy-start | bytes 388
  616.5 21.0 %copy-start.19 = (f32[512]{0:T(512)S(1)}, f32[512]{0:T(512)}, u32[]{:S(2)}) copy-start(f32[512]{0:T(512)} %copy-done.18) | copy-start | bytes 6148
  616.5 21.0 %copy-start.21 = (f32[512]{0:T(512)S(1)}, f32[512]{0:T(512)}, u32[]{:S(2)}) copy-start(f32[512]{0:T(512)} %param.30) | copy-start | bytes 6148
  616.6 21.3 %copy-start.25 = (f32[512]{0:T(512)S(1)}, f32[512]{0:T(512)}, u32[]{:S(2)}) copy-start(f32[512]{0:T(512)} %copy-done.24) | copy-start | bytes 6148
  616.6 89.9 %reduce-scatter.9.cloned.1.call-start = ((), (), s32[]{:S(2)}) async-start(), calls=%async_computation.10 | async-start | bytes 3022848 | tf_op jit(solution)/shard_map/reduce_scatter | solution.py:1101
  616.6 20.9 %copy-start.3 = (f32[512,576]{1,0:T(8,128)S(1)}, f32[512,576]{1,0:T(8,128)}, u32[]{:S(2)}) copy-start(f32[512,576]{1,0:T(8,128)} %copy-done.2) | copy-start | bytes 3538948
  650.6 155.6 %all-reduce.13.cloned.1.call-start = ((), (), s32[]{:S(2)}) async-start(), calls=%async_computation.12 | async-start | bytes 4866048 | tf_op jit(solution)/shard_map/psum | solution.py:1118
  706.5 111.9 %reduce-scatter.11.cloned.1.call-start = ((), (), s32[]{:S(2)}) async-start(), calls=%async_computation.11 | async-start | bytes 7077888 | tf_op jit(solution)/shard_map/reduce_scatter | solution.py:878
  (28 other events, 114.8 us)
Sparse Core Ops, SparseCore 0:
  60.4 91.4 all-gather.1
  290.1 71.8 reduce-scatter.4
  476.5 113.6 reduce-scatter.6
  650.7 53.9 reduce-scatter.8
  732.2 60.7 reduce-scatter.10
Sparse Core Ops, SparseCore 1:
  101.8 86.3 all-reduce.6
  471.7 83.6 all-reduce.8
  616.6 89.8 all-reduce.10
  708.9 97.2 all-reduce.12

commit v7 on v6

--- a/solution.py
+++ b/solution.py
@@ -233,9 +233,7 @@
             pltpu.VMEM((rows, DN + DR), F32),
         ],
         compiler_params=params(),
-        cost_estimate=cost(
-            2 * heads * window * (rows * 1024 + KVR * 768), 4 * window * 640, heads * rows * window
-        ),
+        cost_estimate=cost(window * rows, window * rows),
     )(query_pre, cosine, sine, w_expand, blocks, place_q, sequences, lse, attended_grad, kv, *keys)
 
 
@@ -878,6 +876,23 @@
     return lax.psum_scatter(joined, "dp", scatter_dimension=0, tiled=True)
 
 
+def tensor_sum(value):
+    peers = lax.axis_size("tensor")
+    rank = lax.axis_index("tensor")
+    size = value.shape[0] // peers
+    piece = lambda at: lax.dynamic_slice_in_dim(value, at * size, size, 0)
+    turn = lambda piece, by: lax.ppermute(
+        piece, "tensor", [(i, (i + by) % peers) for i in range(peers)]
+    )
+    total = piece(rank).astype(F32)
+    for by in range(1, peers):
+        total = total + turn(piece((rank + by) % peers), by).astype(F32)
+    mine = total.astype(BF)
+    around = [turn(mine, by) for by in range(peers - 1, 0, -1)] + [mine]
+    both = jnp.concatenate(around + around[:-1], axis=0)
+    return lax.dynamic_slice_in_dim(both, (peers - 1 - rank) * size, value.shape[0], 0)
+
+
 def shards(
     tokens,
     seq_ids,
@@ -930,15 +945,15 @@
     before_two = passed_along(own_keys, "dp", 2)
     before_four = passed_along(own_keys, "dp", 4)
     query_pre = jnp.dot(hidden_in, w_query, preferred_element_type=F32)
+    route_all = lax.all_gather(after(route_ids, own_keys), "dp", tiled=True)
+    before_four = after(before_four, query_pre, place_q, route_all)
     from_pair = swapped(jnp.where(odd == 0, own_keys, before_four))
-    before_two = after(before_two, query_pre, from_pair, place_q)
     keys = [before_four, before_two, swapped(before_two), from_pair, own_keys]
     cot_all = lax.all_gather(after(cotangent, before_two, before_four), "dp", tiled=True)
     attended, lse, kv = attend(query_pre, cosine, sine, w_expand, blocks, place_q, sequences, keys)
     attention_part = jnp.dot(attended, w_out, preferred_element_type=F32).astype(BF)
     attention = lax.psum(attention_part, "tensor")
 
-    route_all = lax.all_gather(after(route_ids, attention_part), "dp", tiled=True)
     local_ids = rank_dp * experts_local + jnp.arange(experts_local, dtype=jnp.int32)
     routes = jnp.take(route_all.reshape(devices, tok_rows, -1), order, axis=0)
     named_block = jnp.any(routes[..., None] == local_ids, axis=2)
@@ -1046,29 +1061,26 @@
         mid_block = after(mid_block, routed_part, grad_expert_down)
         logit_grads = [logit_grad]
     mid_sum = (mid_block + mid_from_shared).astype(BF)
-    routed_block = scatter_sum(after(routed_part, mid_sum))
+    routed_block = scatter_sum(routed_part)
     mid_grad = lax.psum(mid_sum, "tensor")
-    rows_flat = rows.reshape(experts_local, -1, width)
-    grad_expert_gate = dot("ecd,ecf->edf", rows_flat, gate_val_grad[..., :ff_local])
-    grad_expert_up = dot("ecd,ecf->edf", rows_flat, up_val_grad[..., :ff_local])
     grad_router = route_grad(logit_grads, hidden_parts)
-    mid_grad = after(mid_grad, grad_expert_gate, grad_expert_up, grad_router)
+    ff_part = (routed_block.astype(F32) + shared_result).astype(BF)
+    feedforward = lax.psum(after(ff_part, mid_grad), "tensor")
+    mid_grad = after(mid_grad, grad_router, ff_part)
 
     middle_low, middle_grad, attended_grad, grad_middle_gain = norm_back(
         middle, mid_grad, cotangent, middle_gain, w_out
     )
+    attended_grad = after(attended_grad, ff_part)
     query_grad, expanded_grad, *window_grads = attend_back(
         query_pre, cosine, sine, w_expand, blocks, place_q, sequences, lse, attended_grad, kv, keys
     )
-    routed_block = after(routed_block, expanded_grad)
-    ff_part = (routed_block.astype(F32) + shared_result).astype(BF)
-    window_grads = lax.optimization_barrier((*window_grads, ff_part))[:-1]
     four_grad, two_grad, pair_grad, last_grad, keys_grad = window_grads
     pair_grad = swapped(pair_grad)
     last_grad = swapped(last_grad).astype(F32)
     two_grad = (two_grad.astype(F32) + pair_grad.astype(F32)).astype(BF)
     four_grad = (four_grad.astype(F32) + jnp.where(odd == 1, last_grad, 0.0)).astype(BF)
-    keys_grad = keys_grad + jnp.where(odd == 0, last_grad, 0.0)
+    keys_grad = after(keys_grad, feedforward) + jnp.where(odd == 0, last_grad, 0.0)
     keys_grad = keys_grad + passed_along(two_grad, "dp", -2).astype(F32)
     keys_grad = keys_grad + passed_along(four_grad, "dp", -4).astype(F32)
     latent_raw_grad, grad_latent_gain = norm_backward(latent_raw, latent_gain, keys_grad[:, :KVR])
@@ -1079,7 +1091,6 @@
     )
     _, grad_input_gain = norm_backward(token_features, input_gain, input_part)
 
-    feedforward = lax.psum(ff_part, "tensor")
     output = (middle + feedforward.astype(F32)).astype(BF)
     input_part, grad_input_gain = lax.optimization_barrier((input_part.astype(BF), grad_input_gain))
     input_part = after(input_part, feedforward)
@@ -1093,7 +1104,7 @@
             grad_middle_gain / tensors,
             grad_input_gain[None, :],
             jnp.repeat(grad_latent_gain, width // KVR)[None, :],
-            jnp.zeros((13, width), F32),
+            jnp.zeros((61, width), F32),
         ],
         axis=0,
     )
@@ -1107,16 +1118,22 @@
         .transpose(0, 2, 1, 3)
         .reshape(width, expand_width)
     )
-    late = scatter_sum(
+    late = jnp.concatenate(
         [
             dot("td,tc->dc", middle_low, attended).astype(BF),
             dot("td,tc->dc", hidden_in, query_grad).astype(BF),
             grad_expand,
-        ]
-    )
+        ],
+        axis=1,
+    )
+    rows_late = after(rows, late).reshape(experts_local, -1, width)
+    grad_expert_gate = dot("ecd,ecf->edf", rows_late, gate_val_grad[..., :ff_local])
+    grad_expert_up = dot("ecd,ecf->edf", rows_late, up_val_grad[..., :ff_local])
+    late = scatter_sum(late)
     grad_out_proj, grad_query, grad_expand = finals(late, out_width, query_width, share)
-    input_grad, parts = lax.psum((input_part, parts), "tensor")
-    parts = parts.astype(F32)
+    input_grad = lax.psum(input_part, "tensor")
+    input_grad = after(input_grad, grad_expert_gate, grad_expert_up)
+    parts = tensor_sum(after(parts, input_grad)).astype(F32)
     (token_grad,) = norm_back(tokens, input_grad, middle_grad, input_gain, None)
     sw = shared_gate.shape[1]
     gain_at = latent_width + all_experts

time: 836 us -> 795 us (0.951)
  waiting for transfers between devices: 252 us -> 194 us
  blocking collectives: 10.5 us -> 28.5 us
    psum x2, waiting for transfers between devices: 115 us -> 47.9 us  [the longest x1 37.6 us: shards(): feedforward = lax.psum(after(ff_part, mid_grad), 'tensor')]
    reduce_scatter x2, waiting for transfers between devices: 0.02 us -> 60.7 us  [scatter_sum(): return lax.psum_scatter(joined, 'dp', scatter_dimension=0, tiled=True)]
    ppermute x4, waiting for transfers between devices: 40.7 us -> 0.01 us  [passed_along(): return lax.ppermute(shard, axis, pairs)]
    all_gather x1, blocking collectives: 10.5 us -> 28.5 us  [shards(): route_all = lax.all_gather(after(route_ids, own_keys), 'dp', tiled=True)]
    psum x1, waiting for transfers between devices: 19 us -> 1.87 us  [shards(): mid_grad = lax.psum(mid_sum, 'tensor')]
    ppermute x0 -> x6, waiting for transfers between devices: none -> 10 us  [tensor_sum(): lax.ppermute(piece, 'tensor', [(i, (i + by) % peers) for i in range(peers)])]
  transfers between devices with their start and end apart: 37 -> 43, of which waited for: 16 -> 16; matrix products, arithmetic and copies ran while one was open for 19% -> 20% of each run, Pallas kernels for 38% -> 39%
where the time goes in v7:
time: 795 us; the launch traced here: 788 us
  Pallas kernels  331 us (42%)
  waiting for transfers between devices  194 us (24%)
  matrix products  108 us (14%)
  other arithmetic  50.2 us (6%)
  starting transfers between devices  35.5 us (4%)
  blocking collectives  28.5 us (4%)
  local copies, waits for them, and re-layouts  24.2 us (3%)
  between operations  16.5 us (2%)
    dot_general x12, matrix products, dot(): return jnp.einsum(eq, a, b, preferred_element_type=F32)  93 us
    reduce_scatter x2, waiting for transfers between devices, scatter_sum(): return lax.psum_scatter(joined, 'dp', scatter_dimension=0, tiled=True)  60.7 us
    all_gather x1, waiting for transfers between devices, shards(): lax.all_gather(after(cotangent, before_two, before_four), 'dp', tiled=True)  51.3 us
    pallas_call x1, Pallas kernels, expert_step(): pl.pallas_call(expert_kernel, name='expert_step', grid=(experts,), in_spe...  49.6 us
    pallas_call x5, Pallas kernels, pick_route(): pl.pallas_call(functools.partial(pick_route_kernel, count, pieces, parts)...  45.8 us
    pallas_call x4, Pallas kernels, put_route(): pl.pallas_call(put_cross_kernel if cross else put_route_kernel, name='put...  40.8 us
    psum x1, waiting for transfers between devices, shards(): feedforward = lax.psum(after(ff_part, mid_grad), 'tensor')  37.6 us
    pallas_call x1, Pallas kernels, attend_back(): pl.pallas_call(functools.partial(attend_back_kernel, heads, rows // 2, co...  37.6 us
  transfers between devices with their start and end apart: 43, of which 16 were waited for; matrix products, arithmetic and copies ran while one was open for 20% of the time, Pallas kernels for 39%

profile of v7, /device:TPU:0, one launch (start us, length us, event | category | flops | bytes accessed | tf_op | source)
XLA Modules:
  0.0 788.0 jit_solution(11919290983448778770)
XLA Ops:
  20.4 5.7 collective-permute-start
  26.1 4.3 collective-permute-start.1
  30.3 28.5 %all_gather.6 = s32[4096,6]{0,1:T(8,128)S(1)} all-gather(s32[512,6]{0,1:T(8,128)S(1)} %copy-done.25), channel_id=1, replica_groups=mesh['dp'=8,'tensor'=4] {'dp'}, dimensions={0}, use_global_device_ids=true | all-gather | bytes 110592 | tf_op jit(solution)/shard_map/all_gather | solution.py:948
  68.7 22.1 %attend.1 = (bf16[512,512]{1,0:T(8,128)(2,1)}, f32[4,512,1]{2,1,0:T(8,128)}, bf16[2560,1024]{1,0:T(8,128)(2,1)}) custom-call(f32[512,768]{1,0:T(8,128)} %fusion.61.qp_ref, f32[512,32]{1,0:T(8,128)} %get-tuple-element.209.cos_ref, f32[512,32]{1,0:T(8,128)} %get-tuple-element.208.sin_ref, bf16[512,1024]{1,0:T(8,128)(2,1)} %wx_ref.3, s32[5]{0:T(128)} %stack.28.at_ref, ...), custom_call_target="tpu_custom_call" | custom-call | flops 6710886400 | bytes 3276800 | tf_op jit(solution)/shard_map/attend/pallas_call | solution.py:114
  90.9 4.3 convolution_convert_fusion.2
  97.0 3.9 compare_convert_fusion.place_ref
  100.9 51.3 %all-gather.2.cloned.1.call-done.x_ref = bf16[4096,2048]{1,0:T(8,128)(2,1)} async-done(((bf16[512,2048]{1,0:T(8,128)(2,1)}), bf16[4096,2048]{1,0:T(8,128)(2,1)}) %all-gather.2.cloned.1.call-update) | async-done | bytes 16777232 | tf_op jit(solution)/shard_map/all_gather | solution.py:952
  152.2 19.7 %pick.1.x_ref = bf16[8,8,80,2048]{3,2,1,0:T(8,128)(2,1)} custom-call(s32[8]{0:T(128)} %broadcast_xor_fusion.order_ref, s32[8,8,1,512]{3,2,1,0:T(1,128)} %broadcast_in_dim.79.slot_ref, bf16[4096,2048]{1,0:T(8,128)(2,1)} %all-gather.2.cloned.1.call-done.x_ref), custom_call_target="tpu_custom_call" | custom-call | flops 10737418240 | bytes 37748736 | tf_op jit(solution)/shard_map/pick/pallas_call | solution.py:255
  171.9 9.8 %all-reduce.6.cloned.1.call-done.add_ref = bf16[512,2048]{1,0:T(8,128)(2,1)} async-done(((bf16[512,2048]{1,0:T(8,128)(2,1)}), bf16[512,2048]{1,0:T(8,128)(2,1)}) %all-reduce.6.cloned.1.call-update) | async-done | bytes 2097168 | tf_op jit(solution)/shard_map/psum | solution.py:955
  181.7 5.9 norm_sum.1
  193.0 19.4 %down_back.1.back_ref = f32[8,640,384]{2,1,0:T(8,128)} custom-call(bf16[8,8,80,2048]{3,2,1,0:T(8,128)(2,1)} %pick.1.x_ref, bf16[8,352,2048]{2,1,0:T(8,128)(2,1)} %w_ref.3), custom_call_target="tpu_custom_call" | custom-call | flops 10485760 | bytes 1802240 | tf_op jit(solution)/shard_map/down_back/pallas_call | solution.py:532
  212.3 18.2 %shared_step.1 = (bf16[512,704]{1,0:T(8,128)(2,1)}, bf16[512,704]{1,0:T(8,128)(2,1)}, bf16[512,704]{1,0:T(8,128)(2,1)}, bf16[2112,2048]{1,0:T(8,128)(2,1)}) custom-call(bf16[256,2048]{1,0:T(8,128)(2,1)} %get-tuple-element.110.refs_0_.top_ref.refs_4_, bf16[256,2048]{1,0:T(8,128)(2,1)} %get-tuple-element.108.refs_1_.bottom_ref.refs_5_, ...), custom_call_target="tpu_custom_call" | custom-call | flops 1048576 | bytes 1048576 | tf_op jit(solution)/shard_map/shared_step/pallas_call | solution.py:773
  230.6 10.8 %pick_route.5 = (bf16[8,8,80,2048]{3,2,1,0:T(8,128)(2,1)}, f32[4096,128]{1,0:T(8,128)}, f32[8,8,80,1]{3,2,1,0:T(8,128)}) custom-call(s32[1]{0:T(128)} %bitcast.14.first_ref, s32[8,8,1,512]{3,2,1,0:T(1,128)} %broadcast_in_dim.79.slot_ref, bf16[128,2048]{1,0:T(8,128)(2,1)} %pad.4.w_ref, bf16[256,2048]{1,0:T(8,128)(2,1)} %get-tuple-element.110.refs_0_.top_ref.refs_4_, ...), custom_call_target="tpu_custom_call" | custom-call | flops 2097152 | bytes 2097152 | tf_op jit(solution)/shard_map/pick_route/pallas_call | solution.py:317
  246.0 10.6 %pick_route.6 = (bf16[8,8,80,2048]{3,2,1,0:T(8,128)(2,1)}, f32[4096,128]{1,0:T(8,128)}, f32[8,8,80,1]{3,2,1,0:T(8,128)}) custom-call(s32[1]{0:T(128)} %bitcast.14.first_ref, s32[8,8,1,512]{3,2,1,0:T(1,128)} %broadcast_in_dim.79.slot_ref, bf16[128,2048]{1,0:T(8,128)(2,1)} %pad.4.w_ref, ...), custom_call_target="tpu_custom_call", output_to_operand_aliasing={{0}: (7, {}), {1}: (8, {}), {2}: (9, {})} | custom-call | flops 2097152 | bytes 2097152 | tf_op jit(solution)/shard_map/pick_route/pallas_call | solution.py:317
  256.6 10.8 %pick_route.7 = (bf16[8,8,80,2048]{3,2,1,0:T(8,128)(2,1)}, f32[4096,128]{1,0:T(8,128)}, f32[8,8,80,1]{3,2,1,0:T(8,128)}) custom-call(s32[1]{0:T(128)} %bitcast.14.first_ref, s32[8,8,1,512]{3,2,1,0:T(1,128)} %broadcast_in_dim.79.slot_ref, bf16[128,2048]{1,0:T(8,128)(2,1)} %pad.4.w_ref, ...), custom_call_target="tpu_custom_call", output_to_operand_aliasing={{0}: (7, {}), {1}: (8, {}), {2}: (9, {})} | custom-call | flops 2097152 | bytes 2097152 | tf_op jit(solution)/shard_map/pick_route/pallas_call | solution.py:317
  270.0 6.7 pick_route.8
  276.7 6.7 pick_route.9
  283.5 49.6 %expert_step.1 = (bf16[8,640,384]{2,1,0:T(8,128)(2,1)}, bf16[8,640,384]{2,1,0:T(8,128)(2,1)}, bf16[8,640,384]{2,1,0:T(8,128)(2,1)}, bf16[8,8,80,2048]{3,2,1,0:T(8,128)(2,1)}, f32[8,8,1,512]{3,2,1,0:T(1,128)}) custom-call(bf16[8,8,80,2048]{3,2,1,0:T(8,128)(2,1)} %get-tuple-element.174.x_ref, bf16[8,352,2048]{2,1,0:T(8,128)(2,1)} %bitcast.93, ...), custom_call_target="tpu_custom_call" | custom-call | flops 32212254720 | bytes 86769664 | tf_op jit(solution)/shard_map/expert_step/pallas_call | solution.py:625
  333.1 12.7 %put_route.4 = (bf16[1536,2048]{1,0:T(8,128)(2,1)}, bf16[1536,128]{1,0:T(8,128)(2,1)}) custom-call(s32[3]{0:T(128)} %constant.141.clone.order_ref, s32[1]{0:T(128)} %bitcast.14.first_ref, bf16[8,512,640]{2,1,0:T(8,128)(2,1)} %compare_convert_fusion.place_ref, bf16[8,8,80,2048]{3,2,1,0:T(8,128)(2,1)} %get-tuple-element.130.r_ref, ...), custom_call_target="tpu_custom_call" | custom-call | flops 3145728 | bytes 3145728 | tf_op jit(solution)/shard_map/put_route/pallas_call | solution.py:494
  346.2 6.1 put_route.6
  352.4 3.9 collective-permute-done.18.add_ref
  356.3 15.2 %put_route.5 = (bf16[512,2048]{1,0:T(8,128)(2,1)}, bf16[512,2048]{1,0:T(8,128)(2,1)}, bf16[512,2048]{1,0:T(8,128)(2,1)}, bf16[1536,128]{1,0:T(8,128)(2,1)}) custom-call(s32[3]{0:T(128)} %constant.143.clone.order_ref, s32[1]{0:T(128)} %bitcast.14.first_ref, bf16[8,512,640]{2,1,0:T(8,128)(2,1)} %compare_convert_fusion.place_ref, ...), custom_call_target="tpu_custom_call" | custom-call | flops 3145728 | bytes 3145728 | tf_op jit(solution)/shard_map/put_route/pallas_call | solution.py:494
  374.6 4.0 fusion.63
  378.7 3.8 convolution_add_fusion.1
  382.4 18.4 %row_out.1.r_ref = bf16[8,8,80,2048]{3,2,1,0:T(8,128)(2,1)} custom-call(bf16[8,640,384]{2,1,0:T(8,128)(2,1)} %get-tuple-element.140.x_ref, bf16[8,352,2048]{2,1,0:T(8,128)(2,1)} %w_ref.3), custom_call_target="tpu_custom_call" | custom-call | flops 1310720 | bytes 1310720 | tf_op jit(solution)/shard_map/row_out/pallas_call | solution.py:559
  400.8 21.6 %put.1 = bf16[4096,2048]{1,0:T(8,128)(2,1)} custom-call(s32[8]{0:T(128)} %broadcast_xor_fusion.order_ref, bf16[8,512,640]{2,1,0:T(8,128)(2,1)} %compare_convert_fusion.place_ref, bf16[8,8,80,2048]{3,2,1,0:T(8,128)(2,1)} %row_out.1.r_ref), custom_call_target="tpu_custom_call" | custom-call | flops 8388608 | bytes 8388608 | tf_op jit(solution)/shard_map/put/pallas_call | solution.py:467
  422.4 6.8 put_route.7
  429.3 4.4 add_convert_fusion.2
  434.8 22.4 %fusion.10 = f32[8,352,2048]{2,1,0:T(8,128)} fusion(bf16[8,640,2048]{2,1,0:T(8,128)(2,1)} %bitcast.78, bf16[8,640,384]{2,1,0:T(8,128)(2,1)} %get-tuple-element.140.x_ref), kind=kOutput, calls=%fused_computation.19 | convolution fusion | flops 7381975040 | bytes 47972352 | tf_op jit(solution)/shard_map/ecf,ecd->efd/dot_general | solution.py:815
  459.1 4.2 convert_add_fusion.1
  465.9 5.9 fusion.64
  471.8 9.9 %route_grad.1.route_ref = bf16[128,2048]{1,0:T(8,128)(2,1)} custom-call(bf16[512,128]{1,0:T(8,128)(2,1)} %get-tuple-element.154.refs_0_, bf16[512,128]{1,0:T(8,128)(2,1)} %get-tuple-element.155.refs_1_, bf16[1536,128]{1,0:T(8,128)(2,1)} %get-tuple-element.156.refs_2_, bf16[1536,128]{1,0:T(8,128)(2,1)} %get-tuple-element.157.refs_3_, ...), custom_call_target="tpu_custom_call" | custom-call | flops 262144 | bytes 262144 | tf_op jit(solution)/shard_map/route_grad/pallas_call | solution.py:360
  481.6 60.7 %reduce-scatter.7.cloned.1.call-done = bf16[512,2048]{1,0:T(8,128)(2,1)} async-done(((bf16[4096,2048]{1,0:T(8,128)(2,1)}), bf16[512,2048]{1,0:T(8,128)(2,1)}) %reduce-scatter.7.cloned.1.call-update) | async-done | bytes 2097168 | tf_op jit(solution)/shard_map/reduce_scatter | solution.py:876
  542.3 4.9 add_convert_fusion.1
  549.1 8.5 %norm_back.2 = (bf16[512,2048]{1,0:T(8,128)(2,1)}, f32[512,2048]{1,0:T(8,128)}, bf16[512,512]{1,0:T(8,128)(2,1)}, f32[1,2048]{1,0:T(1,128)}) custom-call(f32[512,2048]{1,0:T(8,128)} %get-tuple-element.106.x_ref, bf16[512,2048]{1,0:T(8,128)(2,1)} %all-reduce.8.cloned.1.call-done.up_ref, bf16[512,2048]{1,0:T(8,128)(2,1)} %res_ref.1, f32[1,2048]{1,0:T(1,128)} %bitcast.85, ...), custom_call_target="tpu_custom_call" | custom-call | flops 12582912 | bytes 12582912 | tf_op jit(solution)/shard_map/norm_back/pallas_call | solution.py:737
  557.6 37.6 %attend_back.1 = (bf16[512,768]{1,0:T(8,128)(2,1)}, bf16[2560,1024]{1,0:T(8,128)(2,1)}, bf16[512,640]{1,0:T(8,128)(2,1)}, bf16[512,640]{1,0:T(8,128)(2,1)}, bf16...) custom-call(f32[512,768]{1,0:T(8,128)} %fusion.61.qp_ref, ...), custom_call_target="tpu_custom_call" | custom-call | flops 1310720 | bytes 1310720 | tf_op jit(solution)/shard_map/attend_back/pallas_call | solution.py:207
  605.1 37.6 %all-reduce.10.cloned.1.call-done = bf16[512,2048]{1,0:T(8,128)(2,1)} async-done(((bf16[512,2048]{1,0:T(8,128)(2,1)}), bf16[512,2048]{1,0:T(8,128)(2,1)}) %all-reduce.10.cloned.1.call-update) | async-done | bytes 2097168 | tf_op jit(solution)/shard_map/psum | solution.py:1068
  654.7 5.0 parts_rows.1
  667.5 3.5 convolution_convert_fusion
  671.0 3.9 convolution_convert_fusion.3
  679.5 5.2 pad_maximum_fusion
  684.8 20.2 %fusion.8 = f32[8,2048,352]{1,2,0:T(8,128)} fusion(bf16[8,640,2048]{2,1,0:T(8,128)(2,1)} %bitcast.76, bf16[8,640,384]{2,1,0:T(8,128)(2,1)} %get-tuple-element.175), kind=kOutput, calls=%fused_computation.17 | convolution fusion | flops 7381975040 | bytes 47972352 | tf_op jit(solution)/shard_map/ecd,ecf->edf/dot_general | solution.py:815
  705.1 23.1 %fusion.6 = f32[8,2048,352]{1,2,0:T(8,128)} fusion(bf16[8,640,2048]{2,1,0:T(8,128)(2,1)} %bitcast.77, bf16[8,640,384]{2,1,0:T(8,128)(2,1)S(1)} %copy-done.11), kind=kOutput, calls=%fused_computation.15 | convolution fusion | flops 7381975040 | bytes 47972352 | tf_op jit(solution)/shard_map/ecd,ecf->edf/dot_general | solution.py:815
  728.2 10.3 %all-reduce.12.cloned.1.call-done.up_ref = bf16[512,2048]{1,0:T(8,128)(2,1)} async-done(((bf16[512,2048]{1,0:T(8,128)(2,1)}), bf16[512,2048]{1,0:T(8,128)(2,1)}) %all-reduce.12.cloned.1.call-update) | async-done | bytes 2097168 | tf_op jit(solution)/shard_map/psum | solution.py:1134
  745.7 4.2 collective-permute-done.29
  752.6 3.7 add_convert_fusion
  756.3 6.4 norm_back.3
  765.1 5.8 collective-permute-done.32
  (241 shorter events, 103.2 us)
Async XLA Ops:
  8.0 50.8 %copy-start = (bf16[2048,768]{1,0:T(8,128)(2,1)S(1)}, bf16[2048,768]{1,0:T(8,128)(2,1)}, u32[]{:S(2)}) copy-start(bf16[2048,768]{1,0:T(8,128)(2,1)} %param.28) | copy-start | bytes 9437188
  8.0 144.2 %all-gather.2.cloned.1.call-start = ((), (), s32[]{:S(2)}) async-start(), calls=%async_computation.5 | async-start | bytes 18874368 | tf_op jit(solution)/shard_map/all_gather | solution.py:952
  15.1 43.7 %copy-start.8 = (bf16[512,2048]{1,0:T(8,128)(2,1)}, bf16[512,2048]{1,0:T(8,128)(2,1)S(1)}, u32[]{:S(2)}) copy-start(bf16[512,2048]{1,0:T(8,128)(2,1)S(1)} %fusion.2.x_ref) | copy-start | bytes 6291460
  20.0 41.8 %copy-start.10 = (bf16[512,512]{1,0:T(8,128)(2,1)}, bf16[512,512]{1,0:T(8,128)(2,1)S(1)}, u32[]{:S(2)}) copy-start(bf16[512,512]{1,0:T(8,128)(2,1)S(1)} %multiply_convert_fusion) | copy-start | bytes 1572868
  20.3 41.5 %copy-start.13 = (bf16[512,640]{1,0:T(8,128)(2,1)}, bf16[512,640]{1,0:T(8,128)(2,1)S(1)}, u32[]{:S(2)}) copy-start(bf16[512,640]{1,0:T(8,128)(2,1)S(1)} %maximum_maximum_fusion.rest_4_) | copy-start | bytes 1966084
  20.4 41.5 %collective-permute-start = (bf16[512,640]{1,0:T(8,128)(2,1)S(1)}, bf16[512,640]{1,0:T(8,128)(2,1)}, u32[]{:S(2)}, u32[]{:S(2)}) collective-permute-start(bf16[512,640]{1,0:T(8,128)(2,1)S(1)} %maximum_maximum_fusion.rest_4_), channel_id=1, source_target_pairs={{0,16},{4,20},{8,24},{12,28},{1,17},{5,21},{9,25},{13,29},{2,18},{... | collective-permute-start | bytes 1966088 | tf_op jit(solution)/shard_map/ppermute | solution.py:821
  26.1 35.8 %collective-permute-start.1 = (bf16[512,640]{1,0:T(8,128)(2,1)S(1)}, bf16[512,640]{1,0:T(8,128)(2,1)}, u32[]{:S(2)}, u32[]{:S(2)}) collective-permute-start(bf16[512,640]{1,0:T(8,128)(2,1)S(1)} %maximum_maximum_fusion.rest_4_), channel_id=1, source_target_pairs={{0,8},{4,12},{8,16},{12,20},{16,24},{20,28},{1,9},{5,13},{9,17},{1... | collective-permute-start | bytes 1966088 | tf_op jit(solution)/shard_map/ppermute | solution.py:821
  61.9 119.8 %all-reduce.6.cloned.1.call-start = ((), (), s32[]{:S(2)}) async-start(), calls=%async_computation.4 | async-start | bytes 4194304 | tf_op jit(solution)/shard_map/psum | solution.py:955
  65.2 3.6 collective-permute-start.3
  65.7 3.0 collective-permute-start.2
  95.3 277.9 %reduce-scatter.5.cloned.1.call-start = ((), (), s32[]{:S(2)}) async-start(), calls=%async_computation.6 | async-start | bytes 9732096 | tf_op jit(solution)/shard_map/reduce_scatter | solution.py:1019
  187.6 4.0 collective-permute-start.8
  187.6 43.0 %collective-permute-start.9 = (bf16[256,2048]{1,0:T(8,128)(2,1)}, bf16[256,2048]{1,0:T(8,128)(2,1)}, u32[]{:S(2)}, u32[]{:S(2)}) collective-permute-start(bf16[256,2048]{1,0:T(8,128)(2,1)} %get-tuple-element.108.refs_1_.bottom_ref.refs_5_), channel_id=1, source_target_pairs={{0,4},{4,0},{8,12},{12,8},{16,20},{20,16},{24,28},{28,24},{1,5},{5... | collective-permute-start | bytes 3145736 | tf_op jit(solution)/shard_map/ppermute | solution.py:863
  188.1 53.3 %collective-permute-start.4 = (bf16[256,2048]{1,0:T(8,128)(2,1)}, bf16[256,2048]{1,0:T(8,128)(2,1)}, u32[]{:S(2)}, u32[]{:S(2)}) collective-permute-start(bf16[256,2048]{1,0:T(8,128)(2,1)} %get-tuple-element.110.refs_0_.top_ref.refs_4_), channel_id=1, source_target_pairs={{0,8},{4,12},{8,0},{12,4},{16,24},{20,28},{24,16},{28,20},{1,9},{5... | collective-permute-start | bytes 3145736 | tf_op jit(solution)/shard_map/ppermute | solution.py:863
  189.6 51.8 %collective-permute-start.5 = (bf16[256,2048]{1,0:T(8,128)(2,1)}, bf16[256,2048]{1,0:T(8,128)(2,1)}, u32[]{:S(2)}, u32[]{:S(2)}) collective-permute-start(bf16[256,2048]{1,0:T(8,128)(2,1)} %get-tuple-element.108.refs_1_.bottom_ref.refs_5_), channel_id=1, source_target_pairs={{0,8},{4,12},{8,0},{12,4},{16,24},{20,28},{24,16},{28,20},{1,9},{5... | collective-permute-start | bytes 3145736 | tf_op jit(solution)/shard_map/ppermute | solution.py:863
  190.1 51.3 %collective-permute-start.6 = (bf16[256,2048]{1,0:T(8,128)(2,1)}, bf16[256,2048]{1,0:T(8,128)(2,1)}, u32[]{:S(2)}, u32[]{:S(2)}) collective-permute-start(bf16[256,2048]{1,0:T(8,128)(2,1)} %get-tuple-element.110.refs_0_.top_ref.refs_4_), channel_id=1, source_target_pairs={{0,16},{4,20},{8,24},{12,28},{16,0},{20,4},{24,8},{28,12},{1,17},{... | collective-permute-start | bytes 3145736 | tf_op jit(solution)/shard_map/ppermute | solution.py:863
  191.6 49.8 %collective-permute-start.7 = (bf16[256,2048]{1,0:T(8,128)(2,1)}, bf16[256,2048]{1,0:T(8,128)(2,1)}, u32[]{:S(2)}, u32[]{:S(2)}) collective-permute-start(bf16[256,2048]{1,0:T(8,128)(2,1)} %get-tuple-element.108.refs_1_.bottom_ref.refs_5_), channel_id=1, source_target_pairs={{0,16},{4,20},{8,24},{12,28},{16,0},{20,4},{24,8},{28,12},{1,17},{... | collective-permute-start | bytes 3145736 | tf_op jit(solution)/shard_map/ppermute | solution.py:863
  241.4 3.1 collective-permute-start.11
  241.5 15.1 %collective-permute-start.12 = (bf16[256,2048]{1,0:T(8,128)(2,1)}, bf16[256,2048]{1,0:T(8,128)(2,1)}, u32[]{:S(2)}, u32[]{:S(2)}) collective-permute-start(bf16[256,2048]{1,0:T(8,128)(2,1)} %collective-permute-done.5.refs_1_.refs_9_), channel_id=1, source_target_pairs={{0,4},{4,0},{8,12},{12,8},{16,20},{20,16},{24,28},{28,24},{1,5},{5... | collective-permute-start | bytes 3145736 | tf_op jit(solution)/shard_map/ppermute | solution.py:863
  242.0 14.6 %collective-permute-start.13 = (bf16[256,2048]{1,0:T(8,128)(2,1)}, bf16[256,2048]{1,0:T(8,128)(2,1)}, u32[]{:S(2)}, u32[]{:S(2)}) collective-permute-start(bf16[256,2048]{1,0:T(8,128)(2,1)} %collective-permute-done.6.refs_2_.refs_10_), channel_id=1, source_target_pairs={{0,4},{4,0},{8,12},{12,8},{16,20},{20,16},{24,28},{28,24},{1,5},{5... | collective-permute-start | bytes 3145736 | tf_op jit(solution)/shard_map/ppermute | solution.py:863
  242.1 14.5 %collective-permute-start.14 = (bf16[256,2048]{1,0:T(8,128)(2,1)}, bf16[256,2048]{1,0:T(8,128)(2,1)}, u32[]{:S(2)}, u32[]{:S(2)}) collective-permute-start(bf16[256,2048]{1,0:T(8,128)(2,1)} %collective-permute-done.7.refs_3_.refs_11_), channel_id=1, source_target_pairs={{0,4},{4,0},{8,12},{12,8},{16,20},{20,16},{24,28},{28,24},{1,5},{5... | collective-permute-start | bytes 3145736 | tf_op jit(solution)/shard_map/ppermute | solution.py:863
  242.5 25.5 %collective-permute-start.10 = (bf16[256,2048]{1,0:T(8,128)(2,1)}, bf16[256,2048]{1,0:T(8,128)(2,1)}, u32[]{:S(2)}, u32[]{:S(2)}) collective-permute-start(bf16[256,2048]{1,0:T(8,128)(2,1)} %collective-permute-done.6.refs_2_.refs_10_), channel_id=1, source_target_pairs={{0,8},{4,12},{8,0},{12,4},{16,24},{20,28},{24,16},{28,20},{1,9},{5... | collective-permute-start | bytes 3145736 | tf_op jit(solution)/shard_map/ppermute | solution.py:863
  244.5 25.5 %collective-permute-start.16 = (bf16[256,2048]{1,0:T(8,128)(2,1)}, bf16[256,2048]{1,0:T(8,128)(2,1)}, u32[]{:S(2)}, u32[]{:S(2)}) collective-permute-start(bf16[256,2048]{1,0:T(8,128)(2,1)} %collective-permute-done.5.refs_1_.refs_9_), channel_id=1, source_target_pairs={{0,16},{4,20},{8,24},{12,28},{16,0},{20,4},{24,8},{28,12},{1,17},{... | collective-permute-start | bytes 3145736 | tf_op jit(solution)/shard_map/ppermute | solution.py:863
  268.0 8.8 %collective-permute-start.15 = (bf16[256,2048]{1,0:T(8,128)(2,1)}, bf16[256,2048]{1,0:T(8,128)(2,1)}, u32[]{:S(2)}, u32[]{:S(2)}) collective-permute-start(bf16[256,2048]{1,0:T(8,128)(2,1)} %collective-permute-done.10.refs_0_.refs_12_), channel_id=1, source_target_pairs={{0,4},{4,0},{8,12},{12,8},{16,20},{20,16},{24,28},{28,24},{1,5},{5... | collective-permute-start | bytes 3145736 | tf_op jit(solution)/shard_map/ppermute | solution.py:863
  270.0 6.7 collective-permute-start.17
  283.5 258.8 %reduce-scatter.7.cloned.1.call-start = ((), (), s32[]{:S(2)}) async-start(), calls=%async_computation.7 | async-start | bytes 18874368 | tf_op jit(solution)/shard_map/reduce_scatter | solution.py:876
  345.8 10.5 %collective-permute-start.18 = (bf16[1536,2048]{1,0:T(8,128)(2,1)}, bf16[1536,2048]{1,0:T(8,128)(2,1)}, u32[]{:S(2)}, u32[]{:S(2)}) collective-permute-start(bf16[1536,2048]{1,0:T(8,128)(2,1)} %get-tuple-element.133), channel_id=1, source_target_pairs={{0,4},{4,0},{8,12},{12,8},{16,20},{20,16},{24,28},{28,24},{1,5},{5... | collective-permute-start | bytes 18874376 | tf_op jit(solution)/shard_map/ppermute | solution.py:863
  352.3 70.1 %collective-permute-start.21 = (bf16[512,2048]{1,0:T(8,128)(2,1)}, bf16[512,2048]{1,0:T(8,128)(2,1)}, u32[]{:S(2)}, u32[]{:S(2)}) collective-permute-start(bf16[512,2048]{1,0:T(8,128)(2,1)} %get-tuple-element.138), channel_id=1, source_target_pairs={{0,4},{4,0},{8,12},{12,8},{16,20},{20,16},{24,28},{28,24},{1,5},{5... | collective-permute-start | bytes 6291464 | tf_op jit(solution)/shard_map/ppermute | solution.py:863
  371.5 57.7 %collective-permute-start.20 = (bf16[512,2048]{1,0:T(8,128)(2,1)}, bf16[512,2048]{1,0:T(8,128)(2,1)}, u32[]{:S(2)}, u32[]{:S(2)}) collective-permute-start(bf16[512,2048]{1,0:T(8,128)(2,1)} %get-tuple-element.137), channel_id=1, source_target_pairs={{0,16},{4,20},{8,24},{12,28},{16,0},{20,4},{24,8},{28,12},{1,17},{... | collective-permute-start | bytes 6291464 | tf_op jit(solution)/shard_map/ppermute | solution.py:863
  373.2 56.0 %collective-permute-start.19 = (bf16[512,2048]{1,0:T(8,128)(2,1)}, bf16[512,2048]{1,0:T(8,128)(2,1)}, u32[]{:S(2)}, u32[]{:S(2)}) collective-permute-start(bf16[512,2048]{1,0:T(8,128)(2,1)} %get-tuple-element.136), channel_id=1, source_target_pairs={{0,8},{4,12},{8,0},{12,4},{16,24},{20,28},{24,16},{28,20},{1,9},{5... | collective-permute-start | bytes 6291464 | tf_op jit(solution)/shard_map/ppermute | solution.py:863
  429.2 119.8 %all-reduce.8.cloned.1.call-start = ((), (), s32[]{:S(2)}) async-start(), calls=%async_computation.8 | async-start | bytes 4194304 | tf_op jit(solution)/shard_map/psum | solution.py:1065
  433.7 25.1 %collective-permute-start.22 = (bf16[256,2048]{1,0:T(8,128)(2,1)}, bf16[256,2048]{1,0:T(8,128)(2,1)}, u32[]{:S(2)}, u32[]{:S(2)}) collective-permute-start(bf16[256,2048]{1,0:T(8,128)(2,1)} %get-tuple-element.195), channel_id=1, source_target_pairs={{0,16},{4,20},{8,24},{12,28},{16,0},{20,4},{24,8},{28,12},{1,17},{... | collective-permute-start | bytes 3145736 | tf_op jit(solution)/shard_map/ppermute | solution.py:863
  434.4 24.7 %collective-permute-start.23 = (bf16[256,2048]{1,0:T(8,128)(2,1)}, bf16[256,2048]{1,0:T(8,128)(2,1)}, u32[]{:S(2)}, u32[]{:S(2)}) collective-permute-start(bf16[256,2048]{1,0:T(8,128)(2,1)} %get-tuple-element.194), channel_id=1, source_target_pairs={{0,8},{4,12},{8,0},{12,4},{16,24},{20,28},{24,16},{28,20},{1,9},{5... | collective-permute-start | bytes 3145736 | tf_op jit(solution)/shard_map/ppermute | solution.py:863
  465.8 176.9 %all-reduce.10.cloned.1.call-start = ((), (), s32[]{:S(2)}) async-start(), calls=%async_computation.9 | async-start | bytes 4194304 | tf_op jit(solution)/shard_map/psum | solution.py:1068
  557.6 180.8 %all-reduce.12.cloned.1.call-start = ((), (), s32[]{:S(2)}) async-start(), calls=%async_computation.10 | async-start | bytes 4194304 | tf_op jit(solution)/shard_map/psum | solution.py:1134
  595.2 2.5 collective-permute-start.24
  595.3 6.0 collective-permute-start.25
  600.1 42.6 %collective-permute-start.27 = (bf16[512,640]{1,0:T(8,128)(2,1)}, bf16[512,640]{1,0:T(8,128)(2,1)}, u32[]{:S(2)}, u32[]{:S(2)}) collective-permute-start(bf16[512,640]{1,0:T(8,128)(2,1)} %fusion.16), channel_id=1, source_target_pairs={{16,0},{20,4},{24,8},{28,12},{17,1},{21,5},{25,9},{29,13},{18,2},{... | collective-permute-start | bytes 1966088 | tf_op jit(solution)/shard_map/ppermute | solution.py:821
  603.6 41.4 %copy-start.30 = (f32[32]{0:T(128)S(1)}, f32[32]{0:T(128)}, u32[]{:S(2)}) copy-start(f32[32]{0:T(128)} %copy-done.29) | copy-start | bytes 388
  603.6 39.1 %collective-permute-start.26 = (bf16[512,640]{1,0:T(8,128)(2,1)}, bf16[512,640]{1,0:T(8,128)(2,1)}, u32[]{:S(2)}, u32[]{:S(2)}) collective-permute-start(bf16[512,640]{1,0:T(8,128)(2,1)} %add_convert_fusion.4), channel_id=1, source_target_pairs={{8,0},{12,4},{16,8},{20,12},{24,16},{28,20},{9,1},{13,5},{17,9},{2... | collective-permute-start | bytes 1966088 | tf_op jit(solution)/shard_map/ppermute | solution.py:821
  653.3 85.1 %reduce-scatter.9.cloned.1.call-start = ((), (), s32[]{:S(2)}) async-start(), calls=%async_computation.11 | async-start | bytes 3244032 | tf_op jit(solution)/shard_map/reduce_scatter | solution.py:1112
  659.7 118.3 %reduce-scatter.11.cloned.1.call-start = ((), (), s32[]{:S(2)}) async-start(), calls=%async_computation.12 | async-start | bytes 7077888 | tf_op jit(solution)/shard_map/reduce_scatter | solution.py:876
  739.6 6.1 collective-permute-start.30
  741.2 8.7 %collective-permute-start.29 = (bf16[176,256]{1,0:T(8,128)(2,1)S(1)}, bf16[176,256]{1,0:T(8,128)(2,1)S(1)}, u32[]{:S(2)}, u32[]{:S(2)}) collective-permute-start(bf16[176,256]{1,0:T(8,128)(2,1)S(1)} %get-tuple-element.207), channel_id=1, source_target_pairs={{0,2},{1,3},{2,0},{3,1},{4,6},{5,7},{6,4},{7,5},{8,10},{9,11},{10,... | collective-permute-start | bytes 270344 | tf_op jit(solution)/shard_map/ppermute | solution.py:884
  741.5 8.4 %collective-permute-start.28 = (bf16[176,256]{1,0:T(8,128)(2,1)S(1)}, bf16[176,256]{1,0:T(8,128)(2,1)S(1)}, u32[]{:S(2)}, u32[]{:S(2)}) collective-permute-start(bf16[176,256]{1,0:T(8,128)(2,1)S(1)} %get-tuple-element.205), channel_id=1, source_target_pairs={{0,1},{1,2},{2,3},{3,0},{4,5},{5,6},{6,7},{7,4},{8,9},{9,10},{10,1... | collective-permute-start | bytes 270344 | tf_op jit(solution)/shard_map/ppermute | solution.py:884
  750.9 14.3 %collective-permute-start.31 = (bf16[176,256]{1,0:T(8,128)(2,1)S(1)}, bf16[176,256]{1,0:T(8,128)(2,1)S(1)}, u32[]{:S(2)}, u32[]{:S(2)}) collective-permute-start(bf16[176,256]{1,0:T(8,128)(2,1)S(1)} %add_convert_fusion.5), channel_id=1, source_target_pairs={{0,3},{1,0},{2,1},{3,2},{4,7},{5,4},{6,5},{7,6},{8,11},{9,8},{10,9... | collective-permute-start | bytes 270344 | tf_op jit(solution)/shard_map/ppermute | solution.py:884
  762.7 8.3 %collective-permute-start.32 = (bf16[176,256]{1,0:T(8,128)(2,1)S(1)}, bf16[176,256]{1,0:T(8,128)(2,1)S(1)}, u32[]{:S(2)}, u32[]{:S(2)}) collective-permute-start(bf16[176,256]{1,0:T(8,128)(2,1)S(1)} %add_convert_fusion.5), channel_id=1, source_target_pairs={{0,2},{1,3},{2,0},{3,1},{4,6},{5,7},{6,4},{7,5},{8,10},{9,11},{10,... | collective-permute-start | bytes 270344 | tf_op jit(solution)/shard_map/ppermute | solution.py:884
  763.2 7.7 collective-permute-start.33
  (35 other events, 218.6 us)
Sparse Core Ops, SparseCore 0:
  62.0 90.1 all-gather.1
  283.6 71.8 reduce-scatter.4
  429.4 112.8 reduce-scatter.6
  659.8 43.9 reduce-scatter.8
  707.0 61.7 reduce-scatter.10
Sparse Core Ops, SparseCore 1:
  95.3 86.3 all-reduce.5
  465.9 83.1 all-reduce.7
  557.7 85.0 all-reduce.9
  653.4 85.0 all-reduce.11

commit v8 on v7

--- a/solution.py
+++ b/solution.py
@@ -811,6 +811,51 @@
     )(joined)
 
 
+def weight_grad_kernel(a_ref, x_ref, o_ref):
+    ff = o_ref.shape[1]
+    x = x_ref[...].reshape(-1, x_ref.shape[-1])
+    o_ref[0] = mm(a_ref[0, :, :ff], x, 0, 0)
+
+
+def weight_grad(active, rows, ff):
+    experts, blocks, slots, width = rows.shape
+    count, wide = active.shape[1:]
+    return pl.pallas_call(
+        weight_grad_kernel,
+        name="weight_grad",
+        grid=(experts,),
+        in_specs=[
+            pl.BlockSpec((1, count, wide), lambda e: (e, 0, 0)),
+            pl.BlockSpec((1, blocks, slots, width), lambda e: (e, 0, 0, 0)),
+        ],
+        out_specs=pl.BlockSpec((1, ff, width), lambda e: (e, 0, 0)),
+        out_shape=jax.ShapeDtypeStruct((experts, ff, width), F32),
+        compiler_params=params(),
+        cost_estimate=cost(count * width, count * width),
+    )(active, rows)
+
+
+def split_kernel(x_ref, *outs):
+    at = 0
+    for out in outs:
+        out[...] = x_ref[at : at + out.shape[0], :].astype(F32)
+        at += out.shape[0]
+
+
+def split_rows(joined, sizes):
+    width = joined.shape[1]
+    return pl.pallas_call(
+        split_kernel,
+        name="split_rows",
+        grid=(1,),
+        in_specs=[fixed(joined.shape)],
+        out_specs=[fixed((size, width)) for size in sizes],
+        out_shape=[jax.ShapeDtypeStruct((size, width), F32) for size in sizes],
+        compiler_params=params(),
+        cost_estimate=cost(width, width),
+    )(joined)
+
+
 def dot(eq, a, b):
     return jnp.einsum(eq, a, b, preferred_element_type=F32)
 
@@ -876,7 +921,7 @@
     return lax.psum_scatter(joined, "dp", scatter_dimension=0, tiled=True)
 
 
-def tensor_sum(value):
+def tensor_sum(value, first):
     peers = lax.axis_size("tensor")
     rank = lax.axis_index("tensor")
     size = value.shape[0] // peers
@@ -887,7 +932,7 @@
     total = piece(rank).astype(F32)
     for by in range(1, peers):
         total = total + turn(piece((rank + by) % peers), by).astype(F32)
-    mine = total.astype(BF)
+    mine = after(total.astype(BF), first)
     around = [turn(mine, by) for by in range(peers - 1, 0, -1)] + [mine]
     both = jnp.concatenate(around + around[:-1], axis=0)
     return lax.dynamic_slice_in_dim(both, (peers - 1 - rank) * size, value.shape[0], 0)
@@ -945,7 +990,7 @@
     before_two = passed_along(own_keys, "dp", 2)
     before_four = passed_along(own_keys, "dp", 4)
     query_pre = jnp.dot(hidden_in, w_query, preferred_element_type=F32)
-    route_all = lax.all_gather(after(route_ids, own_keys), "dp", tiled=True)
+    route_all = lax.all_gather(after(route_ids, query_pre), "dp", tiled=True)
     before_four = after(before_four, query_pre, place_q, route_all)
     from_pair = swapped(jnp.where(odd == 0, own_keys, before_four))
     keys = [before_four, before_two, swapped(before_two), from_pair, own_keys]
@@ -992,9 +1037,6 @@
         top, bottom, cotangent, shared_gate.T, shared_up.T, shared_down
     )
     shared_result = jnp.dot(shared_active, shared_down, preferred_element_type=F32)
-    mid_from_shared = dot("tf,df->td", shared_gate_grad, shared_gate) + dot(
-        "tf,df->td", shared_up_grad, shared_up
-    )
     if direct:
         x_top, x_bottom, y_top, y_bottom = lax.optimization_barrier(
             (*by_x, *by_y, held[0], back, shared_grads)
@@ -1022,11 +1064,6 @@
     gated_active, gate_val_grad, up_val_grad, row_grad, probs_grad = expert_step(
         rows, gate_t, up_t, back, slot, slot_gates
     )
-    grad_expert_down = dot(
-        "ecf,ecd->efd",
-        gated_active[..., :ff_local],
-        cot_rows.reshape(experts_local, -1, width),
-    )
     if direct:
         put_args = (first, places, row_grad, router_probs, probs_grad, router_rows)
         some = lambda *at: jnp.array(at, jnp.int32)
@@ -1038,16 +1075,20 @@
         send_x, shared_sums = lax.optimization_barrier((send_x, shared_sums))
         got_x = turned(send_x, 2)
         got_y = turned(send_y, 4)
+        routed_part = put(order, places, row_out(gated_active, expert_down, devices))
+        got_x, got_y, routed_part, from_sibling = lax.optimization_barrier(
+            (got_x, got_y, routed_part, from_sibling)
+        )
+        shared_gate_grad = after(shared_gate_grad, routed_part)
+        mid_from_shared = dot("tf,df->td", shared_gate_grad, shared_gate) + dot(
+            "tf,df->td", shared_up_grad, shared_up
+        )
         own, logits_own = put_route(some(0), False, *put_args, from_sibling)
-        routed_part = put(order, places, row_out(gated_active, expert_down, devices))
-        got_x, got_y, own, routed_part, mid_from_shared = lax.optimization_barrier(
-            (got_x, got_y, own, routed_part, mid_from_shared)
-        )
         half = tok_rows // 2
         plus = lambda *terms: sum(term.astype(F32) for term in terms)
         last_y = turned(plus(kept[:half], got_x[:half]).astype(BF), 4)
         last_x = turned(plus(kept[half:], got_y[:half]).astype(BF), 2)
-        last_y, last_x = lax.optimization_barrier((last_y, last_x, grad_expert_down))[:2]
+        last_y, last_x = lax.optimization_barrier((last_y, last_x, own, mid_from_shared))[:2]
         mid_block = jnp.concatenate(
             [plus(own[:half], got_x[half:], last_y), plus(own[half:], got_y[half:], last_x)], axis=0
         )
@@ -1058,7 +1099,11 @@
         )
         mid_block = scatter_sum(after(mid_part, shared_sums)).astype(F32)
         routed_part = put(order, places, row_out(gated_active, expert_down, devices))
-        mid_block = after(mid_block, routed_part, grad_expert_down)
+        mid_block = after(mid_block, routed_part)
+        shared_gate_grad = after(shared_gate_grad, routed_part)
+        mid_from_shared = dot("tf,df->td", shared_gate_grad, shared_gate) + dot(
+            "tf,df->td", shared_up_grad, shared_up
+        )
         logit_grads = [logit_grad]
     mid_sum = (mid_block + mid_from_shared).astype(BF)
     routed_block = scatter_sum(routed_part)
@@ -1066,7 +1111,8 @@
     grad_router = route_grad(logit_grads, hidden_parts)
     ff_part = (routed_block.astype(F32) + shared_result).astype(BF)
     feedforward = lax.psum(after(ff_part, mid_grad), "tensor")
-    mid_grad = after(mid_grad, grad_router, ff_part)
+    grad_expert_down = weight_grad(after(gated_active, mid_sum), cot_rows, ff_local)
+    mid_grad = after(mid_grad, grad_router, ff_part, grad_expert_down)
 
     middle_low, middle_grad, attended_grad, grad_middle_gain = norm_back(
         middle, mid_grad, cotangent, middle_gain, w_out
@@ -1133,21 +1179,23 @@
     grad_out_proj, grad_query, grad_expand = finals(late, out_width, query_width, share)
     input_grad = lax.psum(input_part, "tensor")
     input_grad = after(input_grad, grad_expert_gate, grad_expert_up)
-    parts = tensor_sum(after(parts, input_grad)).astype(F32)
     (token_grad,) = norm_back(tokens, input_grad, middle_grad, input_gain, None)
+    parts = tensor_sum(after(parts, input_grad), token_grad)
+    latent_part, router_part, gain_part = split_rows(
+        parts, [latent_width, all_experts, gains.shape[0]]
+    )
     sw = shared_gate.shape[1]
-    gain_at = latent_width + all_experts
     return (
         output,
         token_grad,
-        parts[gain_at + 1],
+        gain_part[1],
         grad_query,
-        parts[:latent_width].T,
-        parts[gain_at + 2, :: width // KVR],
+        latent_part.T,
+        gain_part[2, :: width // KVR],
         grad_expand,
         grad_out_proj,
-        parts[gain_at],
-        parts[latent_width:gain_at].T,
+        gain_part[0],
+        router_part.T,
         grad_expert_gate,
         grad_expert_up,
         grad_expert_down,

time: 795 us -> 778 us (0.979)
  Pallas kernels: 331 us -> 357 us
  matrix products: 108 us -> 83.8 us
  waiting for transfers between devices: 194 us -> 183 us
    pallas_call x0 -> x2, Pallas kernels: none -> 24.6 us  [the longest x1 22.7 us: weight_grad(): pl.pallas_call(weight_grad_kernel, name='weight_grad', grid=(experts,), i...]
    dot_general x12 -> x11, matrix products: 93 us -> 68.8 us  [dot(): return jnp.einsum(eq, a, b, preferred_element_type=F32)]
    reduce_scatter x2, waiting for transfers between devices: 60.7 us -> 40.7 us  [scatter_sum(): return lax.psum_scatter(joined, 'dp', scatter_dimension=0, tiled=True)]
    ppermute x24, waiting for transfers between devices: 12.4 us -> 25.4 us  [turned(): lax.ppermute(value, 'dp', [(i, i ^ by) for i in range(lax.axis_size('dp'))])]
  transfers between devices with their start and end apart: 43 -> 43, of which waited for: 16 -> 18; matrix products, arithmetic and copies ran while one was open for 20% -> 17% of each run, Pallas kernels for 39% -> 43%
where the time goes in v8:
time: 778 us; the launch traced here: 771 us
  Pallas kernels  357 us (46%)
  waiting for transfers between devices  183 us (24%)
  matrix products  83.8 us (11%)
  other arithmetic  48.3 us (6%)
  starting transfers between devices  36.7 us (5%)
  blocking collectives  25.6 us (3%)
  local copies, waits for them, and re-layouts  20.6 us (3%)
  between operations  16.5 us (2%)
    dot_general x11, matrix products, dot(): return jnp.einsum(eq, a, b, preferred_element_type=F32)  68.8 us
    all_gather x1, waiting for transfers between devices, shards(): lax.all_gather(after(cotangent, before_two, before_four), 'dp', tiled=True)  51.3 us
    pallas_call x1, Pallas kernels, expert_step(): pl.pallas_call(expert_kernel, name='expert_step', grid=(experts,), in_spe...  49.6 us
    pallas_call x5, Pallas kernels, pick_route(): pl.pallas_call(functools.partial(pick_route_kernel, count, pieces, parts)...  46 us
    pallas_call x4, Pallas kernels, put_route(): pl.pallas_call(put_cross_kernel if cross else put_route_kernel, name='put...  41.6 us
    reduce_scatter x2, waiting for transfers between devices, scatter_sum(): return lax.psum_scatter(joined, 'dp', scatter_dimension=0, tiled=True)  40.7 us
    psum x1, waiting for transfers between devices, shards(): feedforward = lax.psum(after(ff_part, mid_grad), 'tensor')  38 us
    pallas_call x1, Pallas kernels, attend_back(): pl.pallas_call(functools.partial(attend_back_kernel, heads, rows // 2, co...  37.6 us
  transfers between devices with their start and end apart: 43, of which 18 were waited for; matrix products, arithmetic and copies ran while one was open for 17% of the time, Pallas kernels for 43%

profile of v8, /device:TPU:0, one launch (start us, length us, event | category | flops | bytes accessed | tf_op | source)
XLA Modules:
  0.0 771.1 jit_solution(15336363265389484666)
XLA Ops:
  20.3 5.8 collective-permute-start
  26.1 4.2 collective-permute-start.1
  33.3 25.6 %all_gather.6 = s32[4096,6]{0,1:T(8,128)S(1)} all-gather(s32[512,6]{0,1:T(8,128)S(1)} %copy-done.25), channel_id=1, replica_groups=mesh['dp'=8,'tensor'=4] {'dp'}, dimensions={0}, use_global_device_ids=true | all-gather | bytes 110592 | tf_op jit(solution)/shard_map/all_gather | solution.py:993
  65.8 22.2 %attend.1 = (bf16[512,512]{1,0:T(8,128)(2,1)}, f32[4,512,1]{2,1,0:T(8,128)}, bf16[2560,1024]{1,0:T(8,128)(2,1)}) custom-call(f32[512,768]{1,0:T(8,128)} %fusion.59.qp_ref, f32[512,32]{1,0:T(8,128)} %get-tuple-element.219.cos_ref, f32[512,32]{1,0:T(8,128)} %get-tuple-element.218.sin_ref, bf16[512,1024]{1,0:T(8,128)(2,1)} %wx_ref.3, s32[5]{0:T(128)} %stack.28.at_ref, ...), custom_call_target="tpu_custom_call" | custom-call | flops 6710886400 | bytes 3276800 | tf_op jit(solution)/shard_map/attend/pallas_call | solution.py:114
  87.9 4.3 convolution_convert_fusion.2
  94.1 3.9 compare_convert_fusion.place_ref
  98.0 51.3 %all-gather.2.cloned.1.call-done.x_ref = bf16[4096,2048]{1,0:T(8,128)(2,1)} async-done(((bf16[512,2048]{1,0:T(8,128)(2,1)}), bf16[4096,2048]{1,0:T(8,128)(2,1)}) %all-gather.2.cloned.1.call-update) | async-done | bytes 16777232 | tf_op jit(solution)/shard_map/all_gather | solution.py:997
  149.3 19.7 %pick.1.x_ref = bf16[8,8,80,2048]{3,2,1,0:T(8,128)(2,1)} custom-call(s32[8]{0:T(128)} %broadcast_xor_fusion.order_ref, s32[8,8,1,512]{3,2,1,0:T(1,128)} %broadcast_in_dim.79.slot_ref, bf16[4096,2048]{1,0:T(8,128)(2,1)} %all-gather.2.cloned.1.call-done.x_ref), custom_call_target="tpu_custom_call" | custom-call | flops 10737418240 | bytes 37748736 | tf_op jit(solution)/shard_map/pick/pallas_call | solution.py:255
  169.0 9.8 %all-reduce.6.cloned.1.call-done.add_ref = bf16[512,2048]{1,0:T(8,128)(2,1)} async-done(((bf16[512,2048]{1,0:T(8,128)(2,1)}), bf16[512,2048]{1,0:T(8,128)(2,1)}) %all-reduce.6.cloned.1.call-update) | async-done | bytes 2097168 | tf_op jit(solution)/shard_map/psum | solution.py:1000
  178.7 5.9 norm_sum.1
  190.0 19.3 %down_back.1.back_ref = f32[8,640,384]{2,1,0:T(8,128)} custom-call(bf16[8,8,80,2048]{3,2,1,0:T(8,128)(2,1)} %pick.1.x_ref, bf16[8,352,2048]{2,1,0:T(8,128)(2,1)} %w_ref.3), custom_call_target="tpu_custom_call" | custom-call | flops 10485760 | bytes 1802240 | tf_op jit(solution)/shard_map/down_back/pallas_call | solution.py:532
  209.3 18.2 %shared_step.1 = (bf16[512,704]{1,0:T(8,128)(2,1)}, bf16[512,704]{1,0:T(8,128)(2,1)}, bf16[512,704]{1,0:T(8,128)(2,1)}, bf16[2112,2048]{1,0:T(8,128)(2,1)}) custom-call(bf16[256,2048]{1,0:T(8,128)(2,1)} %get-tuple-element.115.refs_0_.top_ref.refs_4_, bf16[256,2048]{1,0:T(8,128)(2,1)} %get-tuple-element.113.refs_1_.bottom_ref.refs_5_, ...), custom_call_target="tpu_custom_call" | custom-call | flops 1048576 | bytes 1048576 | tf_op jit(solution)/shard_map/shared_step/pallas_call | solution.py:773
  227.5 10.8 %pick_route.5 = (bf16[8,8,80,2048]{3,2,1,0:T(8,128)(2,1)}, f32[4096,128]{1,0:T(8,128)}, f32[8,8,80,1]{3,2,1,0:T(8,128)}) custom-call(s32[1]{0:T(128)} %bitcast.14.first_ref, s32[8,8,1,512]{3,2,1,0:T(1,128)} %broadcast_in_dim.79.slot_ref, bf16[128,2048]{1,0:T(8,128)(2,1)} %pad.4.w_ref, bf16[256,2048]{1,0:T(8,128)(2,1)} %get-tuple-element.115.refs_0_.top_ref.refs_4_, ...), custom_call_target="tpu_custom_call" | custom-call | flops 2097152 | bytes 2097152 | tf_op jit(solution)/shard_map/pick_route/pallas_call | solution.py:317
  242.9 10.7 %pick_route.6 = (bf16[8,8,80,2048]{3,2,1,0:T(8,128)(2,1)}, f32[4096,128]{1,0:T(8,128)}, f32[8,8,80,1]{3,2,1,0:T(8,128)}) custom-call(s32[1]{0:T(128)} %bitcast.14.first_ref, s32[8,8,1,512]{3,2,1,0:T(1,128)} %broadcast_in_dim.79.slot_ref, bf16[128,2048]{1,0:T(8,128)(2,1)} %pad.4.w_ref, ...), custom_call_target="tpu_custom_call", output_to_operand_aliasing={{0}: (7, {}), {1}: (8, {}), {2}: (9, {})} | custom-call | flops 2097152 | bytes 2097152 | tf_op jit(solution)/shard_map/pick_route/pallas_call | solution.py:317
  253.6 11.1 %pick_route.7 = (bf16[8,8,80,2048]{3,2,1,0:T(8,128)(2,1)}, f32[4096,128]{1,0:T(8,128)}, f32[8,8,80,1]{3,2,1,0:T(8,128)}) custom-call(s32[1]{0:T(128)} %bitcast.14.first_ref, s32[8,8,1,512]{3,2,1,0:T(1,128)} %broadcast_in_dim.79.slot_ref, bf16[128,2048]{1,0:T(8,128)(2,1)} %pad.4.w_ref, ...), custom_call_target="tpu_custom_call", output_to_operand_aliasing={{0}: (7, {}), {1}: (8, {}), {2}: (9, {})} | custom-call | flops 2097152 | bytes 2097152 | tf_op jit(solution)/shard_map/pick_route/pallas_call | solution.py:317
  267.0 6.7 pick_route.8
  273.7 6.7 pick_route.9
  280.5 49.6 %expert_step.1 = (bf16[8,640,384]{2,1,0:T(8,128)(2,1)}, bf16[8,640,384]{2,1,0:T(8,128)(2,1)}, bf16[8,640,384]{2,1,0:T(8,128)(2,1)}, bf16[8,8,80,2048]{3,2,1,0:T(8,128)(2,1)}, f32[8,8,1,512]{3,2,1,0:T(1,128)}) custom-call(bf16[8,8,80,2048]{3,2,1,0:T(8,128)(2,1)} %get-tuple-element.180.x_ref, bf16[8,352,2048]{2,1,0:T(8,128)(2,1)} %bitcast.88, ...), custom_call_target="tpu_custom_call" | custom-call | flops 32212254720 | bytes 86769664 | tf_op jit(solution)/shard_map/expert_step/pallas_call | solution.py:625
  330.1 12.7 %put_route.4 = (bf16[1536,2048]{1,0:T(8,128)(2,1)}, bf16[1536,128]{1,0:T(8,128)(2,1)}) custom-call(s32[3]{0:T(128)} %constant.141.clone.order_ref, s32[1]{0:T(128)} %bitcast.14.first_ref, bf16[8,512,640]{2,1,0:T(8,128)(2,1)} %compare_convert_fusion.place_ref, bf16[8,8,80,2048]{3,2,1,0:T(8,128)(2,1)} %get-tuple-element.135.r_ref, ...), custom_call_target="tpu_custom_call" | custom-call | flops 3145728 | bytes 3145728 | tf_op jit(solution)/shard_map/put_route/pallas_call | solution.py:494
  343.2 6.2 put_route.6
  349.4 3.9 collective-permute-done.18.add_ref
  353.3 14.8 %put_route.5 = (bf16[512,2048]{1,0:T(8,128)(2,1)}, bf16[512,2048]{1,0:T(8,128)(2,1)}, bf16[512,2048]{1,0:T(8,128)(2,1)}, bf16[1536,128]{1,0:T(8,128)(2,1)}) custom-call(s32[3]{0:T(128)} %constant.143.clone.order_ref, s32[1]{0:T(128)} %bitcast.14.first_ref, bf16[8,512,640]{2,1,0:T(8,128)(2,1)} %compare_convert_fusion.place_ref, ...), custom_call_target="tpu_custom_call" | custom-call | flops 3145728 | bytes 3145728 | tf_op jit(solution)/shard_map/put_route/pallas_call | solution.py:494
  371.1 18.4 %row_out.1.r_ref = bf16[8,8,80,2048]{3,2,1,0:T(8,128)(2,1)} custom-call(bf16[8,640,384]{2,1,0:T(8,128)(2,1)} %get-tuple-element.163.x_ref.a_ref, bf16[8,352,2048]{2,1,0:T(8,128)(2,1)} %w_ref.3), custom_call_target="tpu_custom_call" | custom-call | flops 1310720 | bytes 1310720 | tf_op jit(solution)/shard_map/row_out/pallas_call | solution.py:559
  389.5 21.8 %put.1 = bf16[4096,2048]{1,0:T(8,128)(2,1)} custom-call(s32[8]{0:T(128)} %broadcast_xor_fusion.order_ref, bf16[8,512,640]{2,1,0:T(8,128)(2,1)} %compare_convert_fusion.place_ref, bf16[8,8,80,2048]{3,2,1,0:T(8,128)(2,1)} %row_out.1.r_ref), custom_call_target="tpu_custom_call" | custom-call | flops 8388608 | bytes 8388608 | tf_op jit(solution)/shard_map/put/pallas_call | solution.py:467
  411.3 5.0 collective-permute-done.20
  417.7 4.4 add_convert_fusion.2
  424.1 7.9 %put_route.7 = (bf16[512,2048]{1,0:T(8,128)(2,1)}, bf16[512,128]{1,0:T(8,128)(2,1)}) custom-call(s32[1]{0:T(128)} %constant.144.clone.order_ref, s32[1]{0:T(128)} %bitcast.14.first_ref, bf16[8,512,640]{2,1,0:T(8,128)(2,1)} %compare_convert_fusion.place_ref, bf16[8,8,80,2048]{3,2,1,0:T(8,128)(2,1)} %get-tuple-element.135.r_ref, ...), custom_call_target="tpu_custom_call" | custom-call | flops 1048576 | bytes 1048576 | tf_op jit(solution)/shard_map/put_route/pallas_call | solution.py:494
  432.0 4.3 fusion.62
  438.2 8.5 %collective-permute-done.22 = bf16[256,2048]{1,0:T(8,128)(2,1)} collective-permute-done((bf16[256,2048]{1,0:T(8,128)(2,1)}, bf16[256,2048]{1,0:T(8,128)(2,1)}, u32[]{:S(2)}, u32[]{:S(2)}) %collective-permute-start.22) | collective-permute-done | bytes 1048608 | tf_op jit(solution)/shard_map/ppermute | solution.py:908
  452.3 5.9 fusion.61
  458.2 9.8 %route_grad.1.route_ref = bf16[128,2048]{1,0:T(8,128)(2,1)} custom-call(bf16[512,128]{1,0:T(8,128)(2,1)} %get-tuple-element.159.refs_0_, bf16[512,128]{1,0:T(8,128)(2,1)} %get-tuple-element.160.refs_1_, bf16[1536,128]{1,0:T(8,128)(2,1)} %get-tuple-element.161.refs_2_, bf16[1536,128]{1,0:T(8,128)(2,1)} %get-tuple-element.162.refs_3_, ...), custom_call_target="tpu_custom_call" | custom-call | flops 262144 | bytes 262144 | tf_op jit(solution)/shard_map/route_grad/pallas_call | solution.py:360
  468.0 22.7 %weight_grad.1 = f32[8,352,2048]{2,1,0:T(8,128)} custom-call(bf16[8,640,384]{2,1,0:T(8,128)(2,1)} %get-tuple-element.163.x_ref.a_ref, bf16[8,8,80,2048]{3,2,1,0:T(8,128)(2,1)} %pick.1.x_ref), custom_call_target="tpu_custom_call" | custom-call | flops 1310720 | bytes 1310720 | tf_op jit(solution)/shard_map/weight_grad/pallas_call | solution.py:823
  490.8 40.7 %reduce-scatter.7.cloned.1.call-done = bf16[512,2048]{1,0:T(8,128)(2,1)} async-done(((bf16[4096,2048]{1,0:T(8,128)(2,1)}), bf16[512,2048]{1,0:T(8,128)(2,1)}) %reduce-scatter.7.cloned.1.call-update) | async-done | bytes 2097168 | tf_op jit(solution)/shard_map/reduce_scatter | solution.py:921
  531.4 4.9 add_convert_fusion.1
  536.8 8.5 %norm_back.2 = (bf16[512,2048]{1,0:T(8,128)(2,1)}, f32[512,2048]{1,0:T(8,128)}, bf16[512,512]{1,0:T(8,128)(2,1)}, f32[1,2048]{1,0:T(1,128)}) custom-call(f32[512,2048]{1,0:T(8,128)} %get-tuple-element.111.x_ref, bf16[512,2048]{1,0:T(8,128)(2,1)} %all-reduce.8.cloned.1.call-done.up_ref, bf16[512,2048]{1,0:T(8,128)(2,1)} %res_ref.1, f32[1,2048]{1,0:T(1,128)} %bitcast.80, ...), custom_call_target="tpu_custom_call" | custom-call | flops 12582912 | bytes 12582912 | tf_op jit(solution)/shard_map/norm_back/pallas_call | solution.py:737
  545.4 37.6 %attend_back.1 = (bf16[512,768]{1,0:T(8,128)(2,1)}, bf16[2560,1024]{1,0:T(8,128)(2,1)}, bf16[512,640]{1,0:T(8,128)(2,1)}, bf16[512,640]{1,0:T(8,128)(2,1)}, bf16...) custom-call(f32[512,768]{1,0:T(8,128)} %fusion.59.qp_ref, ...), custom_call_target="tpu_custom_call" | custom-call | flops 1310720 | bytes 1310720 | tf_op jit(solution)/shard_map/attend_back/pallas_call | solution.py:207
  593.0 38.0 %all-reduce.10.cloned.1.call-done = bf16[512,2048]{1,0:T(8,128)(2,1)} async-done(((bf16[512,2048]{1,0:T(8,128)(2,1)}), bf16[512,2048]{1,0:T(8,128)(2,1)}) %all-reduce.10.cloned.1.call-update) | async-done | bytes 2097168 | tf_op jit(solution)/shard_map/psum | solution.py:1113
  638.2 3.3 fusion.3
  642.9 5.1 parts_rows.1
  655.6 3.5 convolution_convert_fusion
  659.2 3.9 convolution_convert_fusion.3
  667.6 5.1 pad_maximum_fusion
  672.8 20.2 %fusion.8 = f32[8,2048,352]{1,2,0:T(8,128)} fusion(bf16[8,640,2048]{2,1,0:T(8,128)(2,1)} %bitcast.72, bf16[8,640,384]{2,1,0:T(8,128)(2,1)} %get-tuple-element.181), kind=kOutput, calls=%fused_computation.17 | convolution fusion | flops 7381975040 | bytes 47972352 | tf_op jit(solution)/shard_map/ecd,ecf->edf/dot_general | solution.py:860
  693.0 23.0 %fusion.6 = f32[8,2048,352]{1,2,0:T(8,128)} fusion(bf16[8,640,2048]{2,1,0:T(8,128)(2,1)} %bitcast.73, bf16[8,640,384]{2,1,0:T(8,128)(2,1)S(1)} %copy-done.10), kind=kOutput, calls=%fused_computation.15 | convolution fusion | flops 7381975040 | bytes 47972352 | tf_op jit(solution)/shard_map/ecd,ecf->edf/dot_general | solution.py:860
  716.0 10.7 %all-reduce.12.cloned.1.call-done.up_ref = bf16[512,2048]{1,0:T(8,128)(2,1)} async-done(((bf16[512,2048]{1,0:T(8,128)(2,1)}), bf16[512,2048]{1,0:T(8,128)(2,1)}) %all-reduce.12.cloned.1.call-update) | async-done | bytes 2097168 | tf_op jit(solution)/shard_map/psum | solution.py:1180
  731.2 6.1 norm_back.3
  746.2 5.8 collective-permute-done.32
  752.9 3.7 add_convert_fusion
  (242 shorter events, 102.5 us)
Async XLA Ops:
  8.0 22.3 %copy-start = (bf16[2048,768]{1,0:T(8,128)(2,1)S(1)}, bf16[2048,768]{1,0:T(8,128)(2,1)}, u32[]{:S(2)}) copy-start(bf16[2048,768]{1,0:T(8,128)(2,1)} %param.28) | copy-start | bytes 9437188
  8.0 141.3 %all-gather.2.cloned.1.call-start = ((), (), s32[]{:S(2)}) async-start(), calls=%async_computation.5 | async-start | bytes 18874368 | tf_op jit(solution)/shard_map/all_gather | solution.py:997
  20.3 39.8 %copy-start.31 = (s32[8]{0:T(128)S(1)}, s32[8]{0:T(128)}, u32[]{:S(2)}) copy-start(s32[8]{0:T(128)} %constant.140.clone) | copy-start | bytes 100
  20.3 38.6 %collective-permute-start = (bf16[512,640]{1,0:T(8,128)(2,1)S(1)}, bf16[512,640]{1,0:T(8,128)(2,1)}, u32[]{:S(2)}, u32[]{:S(2)}) collective-permute-start(bf16[512,640]{1,0:T(8,128)(2,1)S(1)} %maximum_maximum_fusion.rest_4_), channel_id=1, source_target_pairs={{0,16},{4,20},{8,24},{12,28},{1,17},{5,21},{9,25},{13,29},{2,18},{... | collective-permute-start | bytes 1966088 | tf_op jit(solution)/shard_map/ppermute | solution.py:866
  26.1 32.8 %collective-permute-start.1 = (bf16[512,640]{1,0:T(8,128)(2,1)S(1)}, bf16[512,640]{1,0:T(8,128)(2,1)}, u32[]{:S(2)}, u32[]{:S(2)}) collective-permute-start(bf16[512,640]{1,0:T(8,128)(2,1)S(1)} %maximum_maximum_fusion.rest_4_), channel_id=1, source_target_pairs={{0,8},{4,12},{8,16},{12,20},{16,24},{20,28},{1,9},{5,13},{9,17},{1... | collective-permute-start | bytes 1966088 | tf_op jit(solution)/shard_map/ppermute | solution.py:866
  59.0 119.8 %all-reduce.6.cloned.1.call-start = ((), (), s32[]{:S(2)}) async-start(), calls=%async_computation.4 | async-start | bytes 4194304 | tf_op jit(solution)/shard_map/psum | solution.py:1000
  62.2 3.6 collective-permute-start.3
  62.8 3.0 collective-permute-start.2
  92.3 277.4 %reduce-scatter.5.cloned.1.call-start = ((), (), s32[]{:S(2)}) async-start(), calls=%async_computation.6 | async-start | bytes 9732096 | tf_op jit(solution)/shard_map/reduce_scatter | solution.py:1061
  168.9 20.2 %copy-start.16 = (bf16[2048,64]{0,1:T(8,128)(2,1)S(1)}, bf16[2048,64]{0,1:T(8,128)(2,1)}, u32[]{:S(2)}) copy-start(bf16[2048,64]{0,1:T(8,128)(2,1)} %param.34) | copy-start | bytes 786436
  184.6 4.0 collective-permute-start.8
  184.6 42.9 %collective-permute-start.9 = (bf16[256,2048]{1,0:T(8,128)(2,1)}, bf16[256,2048]{1,0:T(8,128)(2,1)}, u32[]{:S(2)}, u32[]{:S(2)}) collective-permute-start(bf16[256,2048]{1,0:T(8,128)(2,1)} %get-tuple-element.113.refs_1_.bottom_ref.refs_5_), channel_id=1, source_target_pairs={{0,4},{4,0},{8,12},{12,8},{16,20},{20,16},{24,28},{28,24},{1,5},{5... | collective-permute-start | bytes 3145736 | tf_op jit(solution)/shard_map/ppermute | solution.py:908
  185.1 53.2 %collective-permute-start.4 = (bf16[256,2048]{1,0:T(8,128)(2,1)}, bf16[256,2048]{1,0:T(8,128)(2,1)}, u32[]{:S(2)}, u32[]{:S(2)}) collective-permute-start(bf16[256,2048]{1,0:T(8,128)(2,1)} %get-tuple-element.115.refs_0_.top_ref.refs_4_), channel_id=1, source_target_pairs={{0,8},{4,12},{8,0},{12,4},{16,24},{20,28},{24,16},{28,20},{1,9},{5... | collective-permute-start | bytes 3145736 | tf_op jit(solution)/shard_map/ppermute | solution.py:908
  186.6 51.8 %collective-permute-start.5 = (bf16[256,2048]{1,0:T(8,128)(2,1)}, bf16[256,2048]{1,0:T(8,128)(2,1)}, u32[]{:S(2)}, u32[]{:S(2)}) collective-permute-start(bf16[256,2048]{1,0:T(8,128)(2,1)} %get-tuple-element.113.refs_1_.bottom_ref.refs_5_), channel_id=1, source_target_pairs={{0,8},{4,12},{8,0},{12,4},{16,24},{20,28},{24,16},{28,20},{1,9},{5... | collective-permute-start | bytes 3145736 | tf_op jit(solution)/shard_map/ppermute | solution.py:908
  187.2 51.2 %collective-permute-start.6 = (bf16[256,2048]{1,0:T(8,128)(2,1)}, bf16[256,2048]{1,0:T(8,128)(2,1)}, u32[]{:S(2)}, u32[]{:S(2)}) collective-permute-start(bf16[256,2048]{1,0:T(8,128)(2,1)} %get-tuple-element.115.refs_0_.top_ref.refs_4_), channel_id=1, source_target_pairs={{0,16},{4,20},{8,24},{12,28},{16,0},{20,4},{24,8},{28,12},{1,17},{... | collective-permute-start | bytes 3145736 | tf_op jit(solution)/shard_map/ppermute | solution.py:908
  188.6 49.8 %collective-permute-start.7 = (bf16[256,2048]{1,0:T(8,128)(2,1)}, bf16[256,2048]{1,0:T(8,128)(2,1)}, u32[]{:S(2)}, u32[]{:S(2)}) collective-permute-start(bf16[256,2048]{1,0:T(8,128)(2,1)} %get-tuple-element.113.refs_1_.bottom_ref.refs_5_), channel_id=1, source_target_pairs={{0,16},{4,20},{8,24},{12,28},{16,0},{20,4},{24,8},{28,12},{1,17},{... | collective-permute-start | bytes 3145736 | tf_op jit(solution)/shard_map/ppermute | solution.py:908
  238.4 3.1 collective-permute-start.11
  238.5 15.1 %collective-permute-start.12 = (bf16[256,2048]{1,0:T(8,128)(2,1)}, bf16[256,2048]{1,0:T(8,128)(2,1)}, u32[]{:S(2)}, u32[]{:S(2)}) collective-permute-start(bf16[256,2048]{1,0:T(8,128)(2,1)} %collective-permute-done.5.refs_1_.refs_9_), channel_id=1, source_target_pairs={{0,4},{4,0},{8,12},{12,8},{16,20},{20,16},{24,28},{28,24},{1,5},{5... | collective-permute-start | bytes 3145736 | tf_op jit(solution)/shard_map/ppermute | solution.py:908
  239.0 14.6 %collective-permute-start.13 = (bf16[256,2048]{1,0:T(8,128)(2,1)}, bf16[256,2048]{1,0:T(8,128)(2,1)}, u32[]{:S(2)}, u32[]{:S(2)}) collective-permute-start(bf16[256,2048]{1,0:T(8,128)(2,1)} %collective-permute-done.6.refs_2_.refs_10_), channel_id=1, source_target_pairs={{0,4},{4,0},{8,12},{12,8},{16,20},{20,16},{24,28},{28,24},{1,5},{5... | collective-permute-start | bytes 3145736 | tf_op jit(solution)/shard_map/ppermute | solution.py:908
  239.0 14.6 %collective-permute-start.14 = (bf16[256,2048]{1,0:T(8,128)(2,1)}, bf16[256,2048]{1,0:T(8,128)(2,1)}, u32[]{:S(2)}, u32[]{:S(2)}) collective-permute-start(bf16[256,2048]{1,0:T(8,128)(2,1)} %collective-permute-done.7.refs_3_.refs_11_), channel_id=1, source_target_pairs={{0,4},{4,0},{8,12},{12,8},{16,20},{20,16},{24,28},{28,24},{1,5},{5... | collective-permute-start | bytes 3145736 | tf_op jit(solution)/shard_map/ppermute | solution.py:908
  239.5 25.5 %collective-permute-start.10 = (bf16[256,2048]{1,0:T(8,128)(2,1)}, bf16[256,2048]{1,0:T(8,128)(2,1)}, u32[]{:S(2)}, u32[]{:S(2)}) collective-permute-start(bf16[256,2048]{1,0:T(8,128)(2,1)} %collective-permute-done.6.refs_2_.refs_10_), channel_id=1, source_target_pairs={{0,8},{4,12},{8,0},{12,4},{16,24},{20,28},{24,16},{28,20},{1,9},{5... | collective-permute-start | bytes 3145736 | tf_op jit(solution)/shard_map/ppermute | solution.py:908
  241.5 25.5 %collective-permute-start.16 = (bf16[256,2048]{1,0:T(8,128)(2,1)}, bf16[256,2048]{1,0:T(8,128)(2,1)}, u32[]{:S(2)}, u32[]{:S(2)}) collective-permute-start(bf16[256,2048]{1,0:T(8,128)(2,1)} %collective-permute-done.5.refs_1_.refs_9_), channel_id=1, source_target_pairs={{0,16},{4,20},{8,24},{12,28},{16,0},{20,4},{24,8},{28,12},{1,17},{... | collective-permute-start | bytes 3145736 | tf_op jit(solution)/shard_map/ppermute | solution.py:908
  264.9 8.8 %collective-permute-start.15 = (bf16[256,2048]{1,0:T(8,128)(2,1)}, bf16[256,2048]{1,0:T(8,128)(2,1)}, u32[]{:S(2)}, u32[]{:S(2)}) collective-permute-start(bf16[256,2048]{1,0:T(8,128)(2,1)} %collective-permute-done.10.refs_0_.refs_12_), channel_id=1, source_target_pairs={{0,4},{4,0},{8,12},{12,8},{16,20},{20,16},{24,28},{28,24},{1,5},{5... | collective-permute-start | bytes 3145736 | tf_op jit(solution)/shard_map/ppermute | solution.py:908
  267.0 6.7 collective-permute-start.17
  280.4 251.0 %reduce-scatter.7.cloned.1.call-start = ((), (), s32[]{:S(2)}) async-start(), calls=%async_computation.7 | async-start | bytes 18874368 | tf_op jit(solution)/shard_map/reduce_scatter | solution.py:921
  342.8 10.5 %collective-permute-start.18 = (bf16[1536,2048]{1,0:T(8,128)(2,1)}, bf16[1536,2048]{1,0:T(8,128)(2,1)}, u32[]{:S(2)}, u32[]{:S(2)}) collective-permute-start(bf16[1536,2048]{1,0:T(8,128)(2,1)} %get-tuple-element.138), channel_id=1, source_target_pairs={{0,4},{4,0},{8,12},{12,8},{16,20},{20,16},{24,28},{28,24},{1,5},{5... | collective-permute-start | bytes 18874376 | tf_op jit(solution)/shard_map/ppermute | solution.py:908
  349.3 61.9 %collective-permute-start.21 = (bf16[512,2048]{1,0:T(8,128)(2,1)}, bf16[512,2048]{1,0:T(8,128)(2,1)}, u32[]{:S(2)}, u32[]{:S(2)}) collective-permute-start(bf16[512,2048]{1,0:T(8,128)(2,1)} %get-tuple-element.144), channel_id=1, source_target_pairs={{0,4},{4,0},{8,12},{12,8},{16,20},{20,16},{24,28},{28,24},{1,5},{5... | collective-permute-start | bytes 6291464 | tf_op jit(solution)/shard_map/ppermute | solution.py:908
  368.1 48.2 %collective-permute-start.20 = (bf16[512,2048]{1,0:T(8,128)(2,1)}, bf16[512,2048]{1,0:T(8,128)(2,1)}, u32[]{:S(2)}, u32[]{:S(2)}) collective-permute-start(bf16[512,2048]{1,0:T(8,128)(2,1)} %get-tuple-element.142), channel_id=1, source_target_pairs={{0,16},{4,20},{8,24},{12,28},{16,0},{20,4},{24,8},{28,12},{1,17},{... | collective-permute-start | bytes 6291464 | tf_op jit(solution)/shard_map/ppermute | solution.py:908
  369.7 47.9 %collective-permute-start.19 = (bf16[512,2048]{1,0:T(8,128)(2,1)}, bf16[512,2048]{1,0:T(8,128)(2,1)}, u32[]{:S(2)}, u32[]{:S(2)}) collective-permute-start(bf16[512,2048]{1,0:T(8,128)(2,1)} %get-tuple-element.141), channel_id=1, source_target_pairs={{0,8},{4,12},{8,0},{12,4},{16,24},{20,28},{24,16},{28,20},{1,9},{5... | collective-permute-start | bytes 6291464 | tf_op jit(solution)/shard_map/ppermute | solution.py:908
  417.6 119.2 %all-reduce.8.cloned.1.call-start = ((), (), s32[]{:S(2)}) async-start(), calls=%async_computation.8 | async-start | bytes 4194304 | tf_op jit(solution)/shard_map/psum | solution.py:1110
  422.1 24.6 %collective-permute-start.22 = (bf16[256,2048]{1,0:T(8,128)(2,1)}, bf16[256,2048]{1,0:T(8,128)(2,1)}, u32[]{:S(2)}, u32[]{:S(2)}) collective-permute-start(bf16[256,2048]{1,0:T(8,128)(2,1)} %get-tuple-element.205), channel_id=1, source_target_pairs={{0,16},{4,20},{8,24},{12,28},{16,0},{20,4},{24,8},{28,12},{1,17},{... | collective-permute-start | bytes 3145736 | tf_op jit(solution)/shard_map/ppermute | solution.py:908
  422.5 24.5 %collective-permute-start.23 = (bf16[256,2048]{1,0:T(8,128)(2,1)}, bf16[256,2048]{1,0:T(8,128)(2,1)}, u32[]{:S(2)}, u32[]{:S(2)}) collective-permute-start(bf16[256,2048]{1,0:T(8,128)(2,1)} %get-tuple-element.204), channel_id=1, source_target_pairs={{0,8},{4,12},{8,0},{12,4},{16,24},{20,28},{24,16},{28,20},{1,9},{5... | collective-permute-start | bytes 3145736 | tf_op jit(solution)/shard_map/ppermute | solution.py:908
  452.3 178.7 %all-reduce.10.cloned.1.call-start = ((), (), s32[]{:S(2)}) async-start(), calls=%async_computation.9 | async-start | bytes 4194304 | tf_op jit(solution)/shard_map/psum | solution.py:1113
  545.3 181.3 %all-reduce.12.cloned.1.call-start = ((), (), s32[]{:S(2)}) async-start(), calls=%async_computation.10 | async-start | bytes 4194304 | tf_op jit(solution)/shard_map/psum | solution.py:1180
  583.0 2.5 collective-permute-start.24
  583.0 6.0 collective-permute-start.25
  587.8 43.2 %collective-permute-start.27 = (bf16[512,640]{1,0:T(8,128)(2,1)}, bf16[512,640]{1,0:T(8,128)(2,1)}, u32[]{:S(2)}, u32[]{:S(2)}) collective-permute-start(bf16[512,640]{1,0:T(8,128)(2,1)} %fusion.14), channel_id=1, source_target_pairs={{16,0},{20,4},{24,8},{28,12},{17,1},{21,5},{25,9},{29,13},{18,2},{... | collective-permute-start | bytes 1966088 | tf_op jit(solution)/shard_map/ppermute | solution.py:866
  591.4 41.9 %copy-start.22 = (f32[512]{0:T(512)S(1)}, f32[512]{0:T(512)}, u32[]{:S(2)}) copy-start(f32[512]{0:T(512)} %copy-done.21) | copy-start | bytes 6148
  591.4 41.9 %copy-start.30 = (f32[32]{0:T(128)S(1)}, f32[32]{0:T(128)}, u32[]{:S(2)}) copy-start(f32[32]{0:T(128)} %copy-done.29) | copy-start | bytes 388
  591.4 39.6 %collective-permute-start.26 = (bf16[512,640]{1,0:T(8,128)(2,1)}, bf16[512,640]{1,0:T(8,128)(2,1)}, u32[]{:S(2)}, u32[]{:S(2)}) collective-permute-start(bf16[512,640]{1,0:T(8,128)(2,1)} %add_convert_fusion.4), channel_id=1, source_target_pairs={{8,0},{12,4},{16,8},{20,12},{24,16},{28,20},{9,1},{13,5},{17,9},{2... | collective-permute-start | bytes 1966088 | tf_op jit(solution)/shard_map/ppermute | solution.py:866
  641.6 85.1 %reduce-scatter.9.cloned.1.call-start = ((), (), s32[]{:S(2)}) async-start(), calls=%async_computation.11 | async-start | bytes 3244032 | tf_op jit(solution)/shard_map/reduce_scatter | solution.py:1158
  648.0 113.1 %reduce-scatter.11.cloned.1.call-start = ((), (), s32[]{:S(2)}) async-start(), calls=%async_computation.12 | async-start | bytes 7077888 | tf_op jit(solution)/shard_map/reduce_scatter | solution.py:921
  727.7 9.6 %collective-permute-start.30 = (bf16[176,256]{1,0:T(8,128)(2,1)S(1)}, bf16[176,256]{1,0:T(8,128)(2,1)S(1)}, u32[]{:S(2)}, u32[]{:S(2)}) collective-permute-start(bf16[176,256]{1,0:T(8,128)(2,1)S(1)} %get-tuple-element.214), channel_id=1, source_target_pairs={{0,3},{1,0},{2,1},{3,2},{4,7},{5,4},{6,5},{7,6},{8,11},{9,8},{10,9... | collective-permute-start | bytes 270344 | tf_op jit(solution)/shard_map/ppermute | solution.py:929
  729.3 8.8 %collective-permute-start.29 = (bf16[176,256]{1,0:T(8,128)(2,1)S(1)}, bf16[176,256]{1,0:T(8,128)(2,1)}, u32[]{:S(2)}, u32[]{:S(2)}) collective-permute-start(bf16[176,256]{1,0:T(8,128)(2,1)S(1)} %get-tuple-element.215), channel_id=1, source_target_pairs={{0,2},{1,3},{2,0},{3,1},{4,6},{5,7},{6,4},{7,5},{8,10},{9,11},{10,... | collective-permute-start | bytes 270344 | tf_op jit(solution)/shard_map/ppermute | solution.py:929
  729.6 8.6 %collective-permute-start.28 = (bf16[176,256]{1,0:T(8,128)(2,1)S(1)}, bf16[176,256]{1,0:T(8,128)(2,1)}, u32[]{:S(2)}, u32[]{:S(2)}) collective-permute-start(bf16[176,256]{1,0:T(8,128)(2,1)S(1)} %get-tuple-element.213), channel_id=1, source_target_pairs={{0,1},{1,2},{2,3},{3,0},{4,5},{5,6},{6,7},{7,4},{8,9},{9,10},{10,1... | collective-permute-start | bytes 270344 | tf_op jit(solution)/shard_map/ppermute | solution.py:929
  739.2 7.1 collective-permute-start.31
  743.4 8.5 %collective-permute-start.32 = (bf16[176,256]{1,0:T(8,128)(2,1)S(1)}, bf16[176,256]{1,0:T(8,128)(2,1)S(1)}, u32[]{:S(2)}, u32[]{:S(2)}) collective-permute-start(bf16[176,256]{1,0:T(8,128)(2,1)S(1)} %add_convert_fusion.5), channel_id=1, source_target_pairs={{0,2},{1,3},{2,0},{3,1},{4,6},{5,7},{6,4},{7,5},{8,10},{9,11},{10,... | collective-permute-start | bytes 270344 | tf_op jit(solution)/shard_map/ppermute | solution.py:929
  744.4 7.6 collective-permute-start.33
  (36 other events, 209.2 us)
Sparse Core Ops, SparseCore 0:
  59.1 90.1 all-gather.1
  280.6 71.8 reduce-scatter.4
  417.7 113.6 reduce-scatter.6
  648.1 43.9 reduce-scatter.8
  695.3 61.7 reduce-scatter.10
Sparse Core Ops, SparseCore 1:
  92.4 86.3 all-reduce.5
  452.4 84.4 all-reduce.7
  545.4 85.5 all-reduce.9
  641.6 85.0 all-reduce.11

commit v9 on v8

--- a/solution.py
+++ b/solution.py
@@ -1178,7 +1178,7 @@
     late = scatter_sum(late)
     grad_out_proj, grad_query, grad_expand = finals(late, out_width, query_width, share)
     input_grad = lax.psum(input_part, "tensor")
-    input_grad = after(input_grad, grad_expert_gate, grad_expert_up)
+    input_grad = after(input_grad, grad_expert_gate, grad_expert_up, output)
     (token_grad,) = norm_back(tokens, input_grad, middle_grad, input_gain, None)
     parts = tensor_sum(after(parts, input_grad), token_grad)
     latent_part, router_part, gain_part = split_rows(

time: 778 us -> 775 us (level)
  transfers between devices with their start and end apart: 43 -> 43, of which waited for: 18 -> 20; matrix products, arithmetic and copies ran while one was open for 17% -> 17% of each run, Pallas kernels for 43% -> 43%
where the time goes in v9:
time: 775 us; the launch traced here: 767 us
  Pallas kernels  357 us (46%)
  waiting for transfers between devices  176 us (23%)
  matrix products  86.2 us (11%)
  other arithmetic  48.6 us (6%)
  starting transfers between devices  36.7 us (5%)
  blocking collectives  25.6 us (3%)
  local copies, waits for them, and re-layouts  20.7 us (3%)
  between operations  16.5 us (2%)
    dot_general x11, matrix products, dot(): return jnp.einsum(eq, a, b, preferred_element_type=F32)  71.2 us
    all_gather x1, waiting for transfers between devices, shards(): lax.all_gather(after(cotangent, before_two, before_four), 'dp', tiled=True)  51.3 us
    pallas_call x1, Pallas kernels, expert_step(): pl.pallas_call(expert_kernel, name='expert_step', grid=(experts,), in_spe...  49.6 us
    pallas_call x5, Pallas kernels, pick_route(): pl.pallas_call(functools.partial(pick_route_kernel, count, pieces, parts)...  46 us
    pallas_call x4, Pallas kernels, put_route(): pl.pallas_call(put_cross_kernel if cross else put_route_kernel, name='put...  41.6 us
    reduce_scatter x2, waiting for transfers between devices, scatter_sum(): return lax.psum_scatter(joined, 'dp', scatter_dimension=0, tiled=True)  41.1 us
    psum x1, waiting for transfers between devices, shards(): feedforward = lax.psum(after(ff_part, mid_grad), 'tensor')  38 us
    pallas_call x1, Pallas kernels, attend_back(): pl.pallas_call(functools.partial(attend_back_kernel, heads, rows // 2, co...  37.6 us
  transfers between devices with their start and end apart: 43, of which 20 were waited for; matrix products, arithmetic and copies ran while one was open for 17% of the time, Pallas kernels for 43%

profile of v9, /device:TPU:0, one launch (start us, length us, event | category | flops | bytes accessed | tf_op | source)
XLA Modules:
  0.0 767.2 jit_solution(15894180812011409928)
XLA Ops:
  20.3 5.8 collective-permute-start
  26.2 4.2 collective-permute-start.1
  33.4 25.6 %all_gather.6 = s32[4096,6]{0,1:T(8,128)S(1)} all-gather(s32[512,6]{0,1:T(8,128)S(1)} %copy-done.26), channel_id=1, replica_groups=mesh['dp'=8,'tensor'=4] {'dp'}, dimensions={0}, use_global_device_ids=true | all-gather | bytes 110592 | tf_op jit(solution)/shard_map/all_gather | solution.py:993
  65.8 22.2 %attend.1 = (bf16[512,512]{1,0:T(8,128)(2,1)}, f32[4,512,1]{2,1,0:T(8,128)}, bf16[2560,1024]{1,0:T(8,128)(2,1)}) custom-call(f32[512,768]{1,0:T(8,128)} %fusion.59.qp_ref, f32[512,32]{1,0:T(8,128)} %get-tuple-element.219.cos_ref, f32[512,32]{1,0:T(8,128)} %get-tuple-element.218.sin_ref, bf16[512,1024]{1,0:T(8,128)(2,1)} %wx_ref.3, s32[5]{0:T(128)} %stack.28.at_ref, ...), custom_call_target="tpu_custom_call" | custom-call | flops 6710886400 | bytes 3276800 | tf_op jit(solution)/shard_map/attend/pallas_call | solution.py:114
  88.0 4.3 convolution_convert_fusion.2
  94.1 3.9 compare_convert_fusion.place_ref
  98.0 51.3 %all-gather.2.cloned.1.call-done.x_ref = bf16[4096,2048]{1,0:T(8,128)(2,1)} async-done(((bf16[512,2048]{1,0:T(8,128)(2,1)}), bf16[4096,2048]{1,0:T(8,128)(2,1)}) %all-gather.2.cloned.1.call-update) | async-done | bytes 16777232 | tf_op jit(solution)/shard_map/all_gather | solution.py:997
  149.4 19.7 %pick.1.x_ref = bf16[8,8,80,2048]{3,2,1,0:T(8,128)(2,1)} custom-call(s32[8]{0:T(128)} %broadcast_xor_fusion.order_ref, s32[8,8,1,512]{3,2,1,0:T(1,128)} %broadcast_in_dim.79.slot_ref, bf16[4096,2048]{1,0:T(8,128)(2,1)} %all-gather.2.cloned.1.call-done.x_ref), custom_call_target="tpu_custom_call" | custom-call | flops 10737418240 | bytes 37748736 | tf_op jit(solution)/shard_map/pick/pallas_call | solution.py:255
  169.0 9.7 %all-reduce.6.cloned.1.call-done.add_ref = bf16[512,2048]{1,0:T(8,128)(2,1)} async-done(((bf16[512,2048]{1,0:T(8,128)(2,1)}), bf16[512,2048]{1,0:T(8,128)(2,1)}) %all-reduce.6.cloned.1.call-update) | async-done | bytes 2097168 | tf_op jit(solution)/shard_map/psum | solution.py:1000
  178.8 5.9 norm_sum.1
  190.1 19.3 %down_back.1.back_ref = f32[8,640,384]{2,1,0:T(8,128)} custom-call(bf16[8,8,80,2048]{3,2,1,0:T(8,128)(2,1)} %pick.1.x_ref, bf16[8,352,2048]{2,1,0:T(8,128)(2,1)} %w_ref.3), custom_call_target="tpu_custom_call" | custom-call | flops 10485760 | bytes 1802240 | tf_op jit(solution)/shard_map/down_back/pallas_call | solution.py:532
  209.4 18.2 %shared_step.1 = (bf16[512,704]{1,0:T(8,128)(2,1)}, bf16[512,704]{1,0:T(8,128)(2,1)}, bf16[512,704]{1,0:T(8,128)(2,1)}, bf16[2112,2048]{1,0:T(8,128)(2,1)}) custom-call(bf16[256,2048]{1,0:T(8,128)(2,1)} %get-tuple-element.115.refs_0_.top_ref.refs_4_, bf16[256,2048]{1,0:T(8,128)(2,1)} %get-tuple-element.113.refs_1_.bottom_ref.refs_5_, ...), custom_call_target="tpu_custom_call" | custom-call | flops 1048576 | bytes 1048576 | tf_op jit(solution)/shard_map/shared_step/pallas_call | solution.py:773
  227.6 10.9 %pick_route.5 = (bf16[8,8,80,2048]{3,2,1,0:T(8,128)(2,1)}, f32[4096,128]{1,0:T(8,128)}, f32[8,8,80,1]{3,2,1,0:T(8,128)}) custom-call(s32[1]{0:T(128)} %bitcast.14.first_ref, s32[8,8,1,512]{3,2,1,0:T(1,128)} %broadcast_in_dim.79.slot_ref, bf16[128,2048]{1,0:T(8,128)(2,1)} %pad.4.w_ref, bf16[256,2048]{1,0:T(8,128)(2,1)} %get-tuple-element.115.refs_0_.top_ref.refs_4_, ...), custom_call_target="tpu_custom_call" | custom-call | flops 2097152 | bytes 2097152 | tf_op jit(solution)/shard_map/pick_route/pallas_call | solution.py:317
  243.0 10.7 %pick_route.6 = (bf16[8,8,80,2048]{3,2,1,0:T(8,128)(2,1)}, f32[4096,128]{1,0:T(8,128)}, f32[8,8,80,1]{3,2,1,0:T(8,128)}) custom-call(s32[1]{0:T(128)} %bitcast.14.first_ref, s32[8,8,1,512]{3,2,1,0:T(1,128)} %broadcast_in_dim.79.slot_ref, bf16[128,2048]{1,0:T(8,128)(2,1)} %pad.4.w_ref, ...), custom_call_target="tpu_custom_call", output_to_operand_aliasing={{0}: (7, {}), {1}: (8, {}), {2}: (9, {})} | custom-call | flops 2097152 | bytes 2097152 | tf_op jit(solution)/shard_map/pick_route/pallas_call | solution.py:317
  253.7 11.1 %pick_route.7 = (bf16[8,8,80,2048]{3,2,1,0:T(8,128)(2,1)}, f32[4096,128]{1,0:T(8,128)}, f32[8,8,80,1]{3,2,1,0:T(8,128)}) custom-call(s32[1]{0:T(128)} %bitcast.14.first_ref, s32[8,8,1,512]{3,2,1,0:T(1,128)} %broadcast_in_dim.79.slot_ref, bf16[128,2048]{1,0:T(8,128)(2,1)} %pad.4.w_ref, ...), custom_call_target="tpu_custom_call", output_to_operand_aliasing={{0}: (7, {}), {1}: (8, {}), {2}: (9, {})} | custom-call | flops 2097152 | bytes 2097152 | tf_op jit(solution)/shard_map/pick_route/pallas_call | solution.py:317
  267.0 6.7 pick_route.8
  273.8 6.7 pick_route.9
  280.6 49.6 %expert_step.1 = (bf16[8,640,384]{2,1,0:T(8,128)(2,1)}, bf16[8,640,384]{2,1,0:T(8,128)(2,1)}, bf16[8,640,384]{2,1,0:T(8,128)(2,1)}, bf16[8,8,80,2048]{3,2,1,0:T(8,128)(2,1)}, f32[8,8,1,512]{3,2,1,0:T(1,128)}) custom-call(bf16[8,8,80,2048]{3,2,1,0:T(8,128)(2,1)} %get-tuple-element.180.x_ref, bf16[8,352,2048]{2,1,0:T(8,128)(2,1)} %bitcast.88, ...), custom_call_target="tpu_custom_call" | custom-call | flops 32212254720 | bytes 86769664 | tf_op jit(solution)/shard_map/expert_step/pallas_call | solution.py:625
  330.1 12.7 %put_route.4 = (bf16[1536,2048]{1,0:T(8,128)(2,1)}, bf16[1536,128]{1,0:T(8,128)(2,1)}) custom-call(s32[3]{0:T(128)} %constant.141.clone.order_ref, s32[1]{0:T(128)} %bitcast.14.first_ref, bf16[8,512,640]{2,1,0:T(8,128)(2,1)} %compare_convert_fusion.place_ref, bf16[8,8,80,2048]{3,2,1,0:T(8,128)(2,1)} %get-tuple-element.135.r_ref, ...), custom_call_target="tpu_custom_call" | custom-call | flops 3145728 | bytes 3145728 | tf_op jit(solution)/shard_map/put_route/pallas_call | solution.py:494
  343.2 6.2 put_route.6
  349.5 3.9 collective-permute-done.18.add_ref
  353.4 14.8 %put_route.5 = (bf16[512,2048]{1,0:T(8,128)(2,1)}, bf16[512,2048]{1,0:T(8,128)(2,1)}, bf16[512,2048]{1,0:T(8,128)(2,1)}, bf16[1536,128]{1,0:T(8,128)(2,1)}) custom-call(s32[3]{0:T(128)} %constant.143.clone.order_ref, s32[1]{0:T(128)} %bitcast.14.first_ref, bf16[8,512,640]{2,1,0:T(8,128)(2,1)} %compare_convert_fusion.place_ref, ...), custom_call_target="tpu_custom_call" | custom-call | flops 3145728 | bytes 3145728 | tf_op jit(solution)/shard_map/put_route/pallas_call | solution.py:494
  371.2 18.4 %row_out.1.r_ref = bf16[8,8,80,2048]{3,2,1,0:T(8,128)(2,1)} custom-call(bf16[8,640,384]{2,1,0:T(8,128)(2,1)} %get-tuple-element.163.x_ref.a_ref, bf16[8,352,2048]{2,1,0:T(8,128)(2,1)} %w_ref.3), custom_call_target="tpu_custom_call" | custom-call | flops 1310720 | bytes 1310720 | tf_op jit(solution)/shard_map/row_out/pallas_call | solution.py:559
  389.6 21.8 %put.1 = bf16[4096,2048]{1,0:T(8,128)(2,1)} custom-call(s32[8]{0:T(128)} %broadcast_xor_fusion.order_ref, bf16[8,512,640]{2,1,0:T(8,128)(2,1)} %compare_convert_fusion.place_ref, bf16[8,8,80,2048]{3,2,1,0:T(8,128)(2,1)} %row_out.1.r_ref), custom_call_target="tpu_custom_call" | custom-call | flops 8388608 | bytes 8388608 | tf_op jit(solution)/shard_map/put/pallas_call | solution.py:467
  411.4 5.0 collective-permute-done.20
  417.7 4.4 add_convert_fusion.2
  424.2 7.9 %put_route.7 = (bf16[512,2048]{1,0:T(8,128)(2,1)}, bf16[512,128]{1,0:T(8,128)(2,1)}) custom-call(s32[1]{0:T(128)} %constant.144.clone.order_ref, s32[1]{0:T(128)} %bitcast.14.first_ref, bf16[8,512,640]{2,1,0:T(8,128)(2,1)} %compare_convert_fusion.place_ref, bf16[8,8,80,2048]{3,2,1,0:T(8,128)(2,1)} %get-tuple-element.135.r_ref, ...), custom_call_target="tpu_custom_call" | custom-call | flops 1048576 | bytes 1048576 | tf_op jit(solution)/shard_map/put_route/pallas_call | solution.py:494
  432.1 4.3 fusion.62
  438.3 8.5 %collective-permute-done.22 = bf16[256,2048]{1,0:T(8,128)(2,1)} collective-permute-done((bf16[256,2048]{1,0:T(8,128)(2,1)}, bf16[256,2048]{1,0:T(8,128)(2,1)}, u32[]{:S(2)}, u32[]{:S(2)}) %collective-permute-start.22) | collective-permute-done | bytes 1048608 | tf_op jit(solution)/shard_map/ppermute | solution.py:908
  447.1 3.3 convert_add_fusion.1
  452.4 5.9 fusion.61
  458.3 9.8 %route_grad.1.route_ref = bf16[128,2048]{1,0:T(8,128)(2,1)} custom-call(bf16[512,128]{1,0:T(8,128)(2,1)} %get-tuple-element.159.refs_0_, bf16[512,128]{1,0:T(8,128)(2,1)} %get-tuple-element.160.refs_1_, bf16[1536,128]{1,0:T(8,128)(2,1)} %get-tuple-element.161.refs_2_, bf16[1536,128]{1,0:T(8,128)(2,1)} %get-tuple-element.162.refs_3_, ...), custom_call_target="tpu_custom_call" | custom-call | flops 262144 | bytes 262144 | tf_op jit(solution)/shard_map/route_grad/pallas_call | solution.py:360
  468.1 22.7 %weight_grad.1 = f32[8,352,2048]{2,1,0:T(8,128)} custom-call(bf16[8,640,384]{2,1,0:T(8,128)(2,1)} %get-tuple-element.163.x_ref.a_ref, bf16[8,8,80,2048]{3,2,1,0:T(8,128)(2,1)} %pick.1.x_ref), custom_call_target="tpu_custom_call" | custom-call | flops 1310720 | bytes 1310720 | tf_op jit(solution)/shard_map/weight_grad/pallas_call | solution.py:823
  490.8 40.8 %reduce-scatter.7.cloned.1.call-done = bf16[512,2048]{1,0:T(8,128)(2,1)} async-done(((bf16[4096,2048]{1,0:T(8,128)(2,1)}), bf16[512,2048]{1,0:T(8,128)(2,1)}) %reduce-scatter.7.cloned.1.call-update) | async-done | bytes 2097168 | tf_op jit(solution)/shard_map/reduce_scatter | solution.py:921
  531.6 4.9 add_convert_fusion.1
  536.9 8.5 %norm_back.2 = (bf16[512,2048]{1,0:T(8,128)(2,1)}, f32[512,2048]{1,0:T(8,128)}, bf16[512,512]{1,0:T(8,128)(2,1)}, f32[1,2048]{1,0:T(1,128)}) custom-call(f32[512,2048]{1,0:T(8,128)} %get-tuple-element.111.x_ref, bf16[512,2048]{1,0:T(8,128)(2,1)} %all-reduce.8.cloned.1.call-done.up_ref, bf16[512,2048]{1,0:T(8,128)(2,1)} %res_ref.1, f32[1,2048]{1,0:T(1,128)} %bitcast.80, ...), custom_call_target="tpu_custom_call" | custom-call | flops 12582912 | bytes 12582912 | tf_op jit(solution)/shard_map/norm_back/pallas_call | solution.py:737
  545.5 37.6 %attend_back.1 = (bf16[512,768]{1,0:T(8,128)(2,1)}, bf16[2560,1024]{1,0:T(8,128)(2,1)}, bf16[512,640]{1,0:T(8,128)(2,1)}, bf16[512,640]{1,0:T(8,128)(2,1)}, bf16...) custom-call(f32[512,768]{1,0:T(8,128)} %fusion.59.qp_ref, ...), custom_call_target="tpu_custom_call" | custom-call | flops 1310720 | bytes 1310720 | tf_op jit(solution)/shard_map/attend_back/pallas_call | solution.py:207
  593.1 38.0 %all-reduce.10.cloned.1.call-done = bf16[512,2048]{1,0:T(8,128)(2,1)} async-done(((bf16[512,2048]{1,0:T(8,128)(2,1)}), bf16[512,2048]{1,0:T(8,128)(2,1)}) %all-reduce.10.cloned.1.call-update) | async-done | bytes 2097168 | tf_op jit(solution)/shard_map/psum | solution.py:1113
  638.4 3.3 fusion.3
  643.1 5.1 parts_rows.1
  655.8 3.5 convolution_convert_fusion
  659.3 3.9 convolution_convert_fusion.3
  667.7 5.1 pad_maximum_fusion
  672.9 5.1 add_convert_fusion
  678.0 22.4 %fusion.8 = f32[8,2048,352]{1,2,0:T(8,128)} fusion(bf16[8,640,2048]{2,1,0:T(8,128)(2,1)} %bitcast.72, bf16[8,640,384]{2,1,0:T(8,128)(2,1)S(1)} %copy-done.10), kind=kOutput, calls=%fused_computation.17 | convolution fusion | flops 7381975040 | bytes 47972352 | tf_op jit(solution)/shard_map/ecd,ecf->edf/dot_general | solution.py:860
  700.5 23.3 %fusion.6 = f32[8,2048,352]{1,2,0:T(8,128)} fusion(bf16[8,640,2048]{2,1,0:T(8,128)(2,1)} %bitcast.73, bf16[8,640,384]{2,1,0:T(8,128)(2,1)S(1)} %copy-done.9), kind=kOutput, calls=%fused_computation.15 | convolution fusion | flops 7381975040 | bytes 47972352 | tf_op jit(solution)/shard_map/ecd,ecf->edf/dot_general | solution.py:860
  731.4 6.1 norm_back.3
  744.0 6.1 collective-permute-done.32
  (244 shorter events, 101.7 us)
Async XLA Ops:
  8.0 22.4 %copy-start = (bf16[2048,768]{1,0:T(8,128)(2,1)S(1)}, bf16[2048,768]{1,0:T(8,128)(2,1)}, u32[]{:S(2)}) copy-start(bf16[2048,768]{1,0:T(8,128)(2,1)} %param.28) | copy-start | bytes 9437188
  8.0 141.3 %all-gather.2.cloned.1.call-start = ((), (), s32[]{:S(2)}) async-start(), calls=%async_computation.5 | async-start | bytes 18874368 | tf_op jit(solution)/shard_map/all_gather | solution.py:997
  20.3 39.8 %copy-start.32 = (s32[8]{0:T(128)S(1)}, s32[8]{0:T(128)}, u32[]{:S(2)}) copy-start(s32[8]{0:T(128)} %constant.140.clone) | copy-start | bytes 100
  20.3 38.6 %collective-permute-start = (bf16[512,640]{1,0:T(8,128)(2,1)S(1)}, bf16[512,640]{1,0:T(8,128)(2,1)}, u32[]{:S(2)}, u32[]{:S(2)}) collective-permute-start(bf16[512,640]{1,0:T(8,128)(2,1)S(1)} %maximum_maximum_fusion.rest_4_), channel_id=1, source_target_pairs={{0,16},{4,20},{8,24},{12,28},{1,17},{5,21},{9,25},{13,29},{2,18},{... | collective-permute-start | bytes 1966088 | tf_op jit(solution)/shard_map/ppermute | solution.py:866
  26.2 32.8 %collective-permute-start.1 = (bf16[512,640]{1,0:T(8,128)(2,1)S(1)}, bf16[512,640]{1,0:T(8,128)(2,1)}, u32[]{:S(2)}, u32[]{:S(2)}) collective-permute-start(bf16[512,640]{1,0:T(8,128)(2,1)S(1)} %maximum_maximum_fusion.rest_4_), channel_id=1, source_target_pairs={{0,8},{4,12},{8,16},{12,20},{16,24},{20,28},{1,9},{5,13},{9,17},{1... | collective-permute-start | bytes 1966088 | tf_op jit(solution)/shard_map/ppermute | solution.py:866
  59.0 119.7 %all-reduce.6.cloned.1.call-start = ((), (), s32[]{:S(2)}) async-start(), calls=%async_computation.4 | async-start | bytes 4194304 | tf_op jit(solution)/shard_map/psum | solution.py:1000
  62.3 3.6 collective-permute-start.3
  62.8 3.0 collective-permute-start.2
  92.4 277.4 %reduce-scatter.5.cloned.1.call-start = ((), (), s32[]{:S(2)}) async-start(), calls=%async_computation.6 | async-start | bytes 9732096 | tf_op jit(solution)/shard_map/reduce_scatter | solution.py:1061
  184.6 4.0 collective-permute-start.8
  184.7 42.9 %collective-permute-start.9 = (bf16[256,2048]{1,0:T(8,128)(2,1)}, bf16[256,2048]{1,0:T(8,128)(2,1)}, u32[]{:S(2)}, u32[]{:S(2)}) collective-permute-start(bf16[256,2048]{1,0:T(8,128)(2,1)} %get-tuple-element.113.refs_1_.bottom_ref.refs_5_), channel_id=1, source_target_pairs={{0,4},{4,0},{8,12},{12,8},{16,20},{20,16},{24,28},{28,24},{1,5},{5... | collective-permute-start | bytes 3145736 | tf_op jit(solution)/shard_map/ppermute | solution.py:908
  185.2 53.3 %collective-permute-start.4 = (bf16[256,2048]{1,0:T(8,128)(2,1)}, bf16[256,2048]{1,0:T(8,128)(2,1)}, u32[]{:S(2)}, u32[]{:S(2)}) collective-permute-start(bf16[256,2048]{1,0:T(8,128)(2,1)} %get-tuple-element.115.refs_0_.top_ref.refs_4_), channel_id=1, source_target_pairs={{0,8},{4,12},{8,0},{12,4},{16,24},{20,28},{24,16},{28,20},{1,9},{5... | collective-permute-start | bytes 3145736 | tf_op jit(solution)/shard_map/ppermute | solution.py:908
  186.6 51.8 %collective-permute-start.5 = (bf16[256,2048]{1,0:T(8,128)(2,1)}, bf16[256,2048]{1,0:T(8,128)(2,1)}, u32[]{:S(2)}, u32[]{:S(2)}) collective-permute-start(bf16[256,2048]{1,0:T(8,128)(2,1)} %get-tuple-element.113.refs_1_.bottom_ref.refs_5_), channel_id=1, source_target_pairs={{0,8},{4,12},{8,0},{12,4},{16,24},{20,28},{24,16},{28,20},{1,9},{5... | collective-permute-start | bytes 3145736 | tf_op jit(solution)/shard_map/ppermute | solution.py:908
  187.2 51.2 %collective-permute-start.6 = (bf16[256,2048]{1,0:T(8,128)(2,1)}, bf16[256,2048]{1,0:T(8,128)(2,1)}, u32[]{:S(2)}, u32[]{:S(2)}) collective-permute-start(bf16[256,2048]{1,0:T(8,128)(2,1)} %get-tuple-element.115.refs_0_.top_ref.refs_4_), channel_id=1, source_target_pairs={{0,16},{4,20},{8,24},{12,28},{16,0},{20,4},{24,8},{28,12},{1,17},{... | collective-permute-start | bytes 3145736 | tf_op jit(solution)/shard_map/ppermute | solution.py:908
  188.7 49.8 %collective-permute-start.7 = (bf16[256,2048]{1,0:T(8,128)(2,1)}, bf16[256,2048]{1,0:T(8,128)(2,1)}, u32[]{:S(2)}, u32[]{:S(2)}) collective-permute-start(bf16[256,2048]{1,0:T(8,128)(2,1)} %get-tuple-element.113.refs_1_.bottom_ref.refs_5_), channel_id=1, source_target_pairs={{0,16},{4,20},{8,24},{12,28},{16,0},{20,4},{24,8},{28,12},{1,17},{... | collective-permute-start | bytes 3145736 | tf_op jit(solution)/shard_map/ppermute | solution.py:908
  238.5 3.1 collective-permute-start.11
  238.5 15.1 %collective-permute-start.12 = (bf16[256,2048]{1,0:T(8,128)(2,1)}, bf16[256,2048]{1,0:T(8,128)(2,1)}, u32[]{:S(2)}, u32[]{:S(2)}) collective-permute-start(bf16[256,2048]{1,0:T(8,128)(2,1)} %collective-permute-done.5.refs_1_.refs_9_), channel_id=1, source_target_pairs={{0,4},{4,0},{8,12},{12,8},{16,20},{20,16},{24,28},{28,24},{1,5},{5... | collective-permute-start | bytes 3145736 | tf_op jit(solution)/shard_map/ppermute | solution.py:908
  239.0 14.6 %collective-permute-start.13 = (bf16[256,2048]{1,0:T(8,128)(2,1)}, bf16[256,2048]{1,0:T(8,128)(2,1)}, u32[]{:S(2)}, u32[]{:S(2)}) collective-permute-start(bf16[256,2048]{1,0:T(8,128)(2,1)} %collective-permute-done.6.refs_2_.refs_10_), channel_id=1, source_target_pairs={{0,4},{4,0},{8,12},{12,8},{16,20},{20,16},{24,28},{28,24},{1,5},{5... | collective-permute-start | bytes 3145736 | tf_op jit(solution)/shard_map/ppermute | solution.py:908
  239.1 14.6 %collective-permute-start.14 = (bf16[256,2048]{1,0:T(8,128)(2,1)}, bf16[256,2048]{1,0:T(8,128)(2,1)}, u32[]{:S(2)}, u32[]{:S(2)}) collective-permute-start(bf16[256,2048]{1,0:T(8,128)(2,1)} %collective-permute-done.7.refs_3_.refs_11_), channel_id=1, source_target_pairs={{0,4},{4,0},{8,12},{12,8},{16,20},{20,16},{24,28},{28,24},{1,5},{5... | collective-permute-start | bytes 3145736 | tf_op jit(solution)/shard_map/ppermute | solution.py:908
  239.5 25.5 %collective-permute-start.10 = (bf16[256,2048]{1,0:T(8,128)(2,1)}, bf16[256,2048]{1,0:T(8,128)(2,1)}, u32[]{:S(2)}, u32[]{:S(2)}) collective-permute-start(bf16[256,2048]{1,0:T(8,128)(2,1)} %collective-permute-done.6.refs_2_.refs_10_), channel_id=1, source_target_pairs={{0,8},{4,12},{8,0},{12,4},{16,24},{20,28},{24,16},{28,20},{1,9},{5... | collective-permute-start | bytes 3145736 | tf_op jit(solution)/shard_map/ppermute | solution.py:908
  241.5 25.5 %collective-permute-start.16 = (bf16[256,2048]{1,0:T(8,128)(2,1)}, bf16[256,2048]{1,0:T(8,128)(2,1)}, u32[]{:S(2)}, u32[]{:S(2)}) collective-permute-start(bf16[256,2048]{1,0:T(8,128)(2,1)} %collective-permute-done.5.refs_1_.refs_9_), channel_id=1, source_target_pairs={{0,16},{4,20},{8,24},{12,28},{16,0},{20,4},{24,8},{28,12},{1,17},{... | collective-permute-start | bytes 3145736 | tf_op jit(solution)/shard_map/ppermute | solution.py:908
  265.0 8.8 %collective-permute-start.15 = (bf16[256,2048]{1,0:T(8,128)(2,1)}, bf16[256,2048]{1,0:T(8,128)(2,1)}, u32[]{:S(2)}, u32[]{:S(2)}) collective-permute-start(bf16[256,2048]{1,0:T(8,128)(2,1)} %collective-permute-done.10.refs_0_.refs_12_), channel_id=1, source_target_pairs={{0,4},{4,0},{8,12},{12,8},{16,20},{20,16},{24,28},{28,24},{1,5},{5... | collective-permute-start | bytes 3145736 | tf_op jit(solution)/shard_map/ppermute | solution.py:908
  267.0 6.7 collective-permute-start.17
  280.5 251.1 %reduce-scatter.7.cloned.1.call-start = ((), (), s32[]{:S(2)}) async-start(), calls=%async_computation.7 | async-start | bytes 18874368 | tf_op jit(solution)/shard_map/reduce_scatter | solution.py:921
  342.8 10.5 %collective-permute-start.18 = (bf16[1536,2048]{1,0:T(8,128)(2,1)}, bf16[1536,2048]{1,0:T(8,128)(2,1)}, u32[]{:S(2)}, u32[]{:S(2)}) collective-permute-start(bf16[1536,2048]{1,0:T(8,128)(2,1)} %get-tuple-element.138), channel_id=1, source_target_pairs={{0,4},{4,0},{8,12},{12,8},{16,20},{20,16},{24,28},{28,24},{1,5},{5... | collective-permute-start | bytes 18874376 | tf_op jit(solution)/shard_map/ppermute | solution.py:908
  349.4 62.0 %collective-permute-start.21 = (bf16[512,2048]{1,0:T(8,128)(2,1)}, bf16[512,2048]{1,0:T(8,128)(2,1)}, u32[]{:S(2)}, u32[]{:S(2)}) collective-permute-start(bf16[512,2048]{1,0:T(8,128)(2,1)} %get-tuple-element.144), channel_id=1, source_target_pairs={{0,4},{4,0},{8,12},{12,8},{16,20},{20,16},{24,28},{28,24},{1,5},{5... | collective-permute-start | bytes 6291464 | tf_op jit(solution)/shard_map/ppermute | solution.py:908
  368.1 48.2 %collective-permute-start.20 = (bf16[512,2048]{1,0:T(8,128)(2,1)}, bf16[512,2048]{1,0:T(8,128)(2,1)}, u32[]{:S(2)}, u32[]{:S(2)}) collective-permute-start(bf16[512,2048]{1,0:T(8,128)(2,1)} %get-tuple-element.142), channel_id=1, source_target_pairs={{0,16},{4,20},{8,24},{12,28},{16,0},{20,4},{24,8},{28,12},{1,17},{... | collective-permute-start | bytes 6291464 | tf_op jit(solution)/shard_map/ppermute | solution.py:908
  369.8 47.9 %collective-permute-start.19 = (bf16[512,2048]{1,0:T(8,128)(2,1)}, bf16[512,2048]{1,0:T(8,128)(2,1)}, u32[]{:S(2)}, u32[]{:S(2)}) collective-permute-start(bf16[512,2048]{1,0:T(8,128)(2,1)} %get-tuple-element.141), channel_id=1, source_target_pairs={{0,8},{4,12},{8,0},{12,4},{16,24},{20,28},{24,16},{28,20},{1,9},{5... | collective-permute-start | bytes 6291464 | tf_op jit(solution)/shard_map/ppermute | solution.py:908
  417.7 119.2 %all-reduce.8.cloned.1.call-start = ((), (), s32[]{:S(2)}) async-start(), calls=%async_computation.8 | async-start | bytes 4194304 | tf_op jit(solution)/shard_map/psum | solution.py:1110
  422.2 24.6 %collective-permute-start.22 = (bf16[256,2048]{1,0:T(8,128)(2,1)}, bf16[256,2048]{1,0:T(8,128)(2,1)}, u32[]{:S(2)}, u32[]{:S(2)}) collective-permute-start(bf16[256,2048]{1,0:T(8,128)(2,1)} %get-tuple-element.205), channel_id=1, source_target_pairs={{0,16},{4,20},{8,24},{12,28},{16,0},{20,4},{24,8},{28,12},{1,17},{... | collective-permute-start | bytes 3145736 | tf_op jit(solution)/shard_map/ppermute | solution.py:908
  422.6 24.5 %collective-permute-start.23 = (bf16[256,2048]{1,0:T(8,128)(2,1)}, bf16[256,2048]{1,0:T(8,128)(2,1)}, u32[]{:S(2)}, u32[]{:S(2)}) collective-permute-start(bf16[256,2048]{1,0:T(8,128)(2,1)} %get-tuple-element.204), channel_id=1, source_target_pairs={{0,8},{4,12},{8,0},{12,4},{16,24},{20,28},{24,16},{28,20},{1,9},{5... | collective-permute-start | bytes 3145736 | tf_op jit(solution)/shard_map/ppermute | solution.py:908
  452.4 178.7 %all-reduce.10.cloned.1.call-start = ((), (), s32[]{:S(2)}) async-start(), calls=%async_computation.9 | async-start | bytes 4194304 | tf_op jit(solution)/shard_map/psum | solution.py:1113
  545.5 181.3 %all-reduce.12.cloned.1.call-start = ((), (), s32[]{:S(2)}) async-start(), calls=%async_computation.10 | async-start | bytes 4194304 | tf_op jit(solution)/shard_map/psum | solution.py:1180
  583.1 2.5 collective-permute-start.24
  583.2 6.0 collective-permute-start.25
  587.9 43.2 %collective-permute-start.27 = (bf16[512,640]{1,0:T(8,128)(2,1)}, bf16[512,640]{1,0:T(8,128)(2,1)}, u32[]{:S(2)}, u32[]{:S(2)}) collective-permute-start(bf16[512,640]{1,0:T(8,128)(2,1)} %fusion.14), channel_id=1, source_target_pairs={{16,0},{20,4},{24,8},{28,12},{17,1},{21,5},{25,9},{29,13},{18,2},{... | collective-permute-start | bytes 1966088 | tf_op jit(solution)/shard_map/ppermute | solution.py:866
  591.5 41.9 %copy-start.23 = (f32[512]{0:T(512)S(1)}, f32[512]{0:T(512)}, u32[]{:S(2)}) copy-start(f32[512]{0:T(512)} %copy-done.22) | copy-start | bytes 6148
  591.5 41.9 %copy-start.31 = (f32[32]{0:T(128)S(1)}, f32[32]{0:T(128)}, u32[]{:S(2)}) copy-start(f32[32]{0:T(128)} %copy-done.30) | copy-start | bytes 388
  591.5 39.6 %collective-permute-start.26 = (bf16[512,640]{1,0:T(8,128)(2,1)}, bf16[512,640]{1,0:T(8,128)(2,1)}, u32[]{:S(2)}, u32[]{:S(2)}) collective-permute-start(bf16[512,640]{1,0:T(8,128)(2,1)} %add_convert_fusion.4), channel_id=1, source_target_pairs={{8,0},{12,4},{16,8},{20,12},{24,16},{28,20},{9,1},{13,5},{17,9},{2... | collective-permute-start | bytes 1966088 | tf_op jit(solution)/shard_map/ppermute | solution.py:866
  641.7 85.1 %reduce-scatter.9.cloned.1.call-start = ((), (), s32[]{:S(2)}) async-start(), calls=%async_computation.11 | async-start | bytes 3244032 | tf_op jit(solution)/shard_map/reduce_scatter | solution.py:1158
  648.2 109.1 %reduce-scatter.11.cloned.1.call-start = ((), (), s32[]{:S(2)}) async-start(), calls=%async_computation.12 | async-start | bytes 7077888 | tf_op jit(solution)/shard_map/reduce_scatter | solution.py:921
  678.0 22.4 %copy-start.9 = (bf16[8,640,384]{2,1,0:T(8,128)(2,1)S(1)}, bf16[8,640,384]{2,1,0:T(8,128)(2,1)}, u32[]{:S(2)}) copy-start(bf16[8,640,384]{2,1,0:T(8,128)(2,1)} %get-tuple-element.182) | copy-start | bytes 11796484
  727.8 9.7 %collective-permute-start.30 = (bf16[176,256]{1,0:T(8,128)(2,1)S(1)}, bf16[176,256]{1,0:T(8,128)(2,1)S(1)}, u32[]{:S(2)}, u32[]{:S(2)}) collective-permute-start(bf16[176,256]{1,0:T(8,128)(2,1)S(1)} %get-tuple-element.214), channel_id=1, source_target_pairs={{0,3},{1,0},{2,1},{3,2},{4,7},{5,4},{6,5},{7,6},{8,11},{9,8},{10,9... | collective-permute-start | bytes 270344 | tf_op jit(solution)/shard_map/ppermute | solution.py:929
  729.5 8.8 %collective-permute-start.29 = (bf16[176,256]{1,0:T(8,128)(2,1)S(1)}, bf16[176,256]{1,0:T(8,128)(2,1)}, u32[]{:S(2)}, u32[]{:S(2)}) collective-permute-start(bf16[176,256]{1,0:T(8,128)(2,1)S(1)} %get-tuple-element.215), channel_id=1, source_target_pairs={{0,2},{1,3},{2,0},{3,1},{4,6},{5,7},{6,4},{7,5},{8,10},{9,11},{10,... | collective-permute-start | bytes 270344 | tf_op jit(solution)/shard_map/ppermute | solution.py:929
  729.7 8.5 %collective-permute-start.28 = (bf16[176,256]{1,0:T(8,128)(2,1)S(1)}, bf16[176,256]{1,0:T(8,128)(2,1)}, u32[]{:S(2)}, u32[]{:S(2)}) collective-permute-start(bf16[176,256]{1,0:T(8,128)(2,1)S(1)} %get-tuple-element.213), channel_id=1, source_target_pairs={{0,1},{1,2},{2,3},{3,0},{4,5},{5,6},{6,7},{7,4},{8,9},{9,10},{10,1... | collective-permute-start | bytes 270344 | tf_op jit(solution)/shard_map/ppermute | solution.py:929
  739.3 4.7 collective-permute-start.31
  741.0 9.2 %collective-permute-start.32 = (bf16[176,256]{1,0:T(8,128)(2,1)S(1)}, bf16[176,256]{1,0:T(8,128)(2,1)S(1)}, u32[]{:S(2)}, u32[]{:S(2)}) collective-permute-start(bf16[176,256]{1,0:T(8,128)(2,1)S(1)} %add_convert_fusion.5), channel_id=1, source_target_pairs={{0,2},{1,3},{2,0},{3,1},{4,6},{5,7},{6,4},{7,5},{8,10},{9,11},{10,... | collective-permute-start | bytes 270344 | tf_op jit(solution)/shard_map/ppermute | solution.py:929
  741.8 8.3 %collective-permute-start.33 = (bf16[176,256]{1,0:T(8,128)(2,1)S(1)}, bf16[176,256]{1,0:T(8,128)(2,1)S(1)}, u32[]{:S(2)}, u32[]{:S(2)}) collective-permute-start(bf16[176,256]{1,0:T(8,128)(2,1)S(1)} %add_convert_fusion.5), channel_id=1, source_target_pairs={{0,1},{1,2},{2,3},{3,0},{4,5},{5,6},{6,7},{7,4},{8,9},{9,10},{10,1... | collective-permute-start | bytes 270344 | tf_op jit(solution)/shard_map/ppermute | solution.py:929
  (37 other events, 211.0 us)
Sparse Core Ops, SparseCore 0:
  59.1 90.1 all-gather.1
  280.6 71.7 reduce-scatter.4
  417.8 113.7 reduce-scatter.6
  648.3 43.9 reduce-scatter.8
  695.5 61.7 reduce-scatter.10
Sparse Core Ops, SparseCore 1:
  92.4 86.3 all-reduce.5
  452.4 84.4 all-reduce.7
  545.6 85.5 all-reduce.9
  641.8 85.0 all-reduce.11
